TPU v7x, 256 devices: a whole 4x4x8 slice. The times are simulated.
256 devices in a mesh: dp: 4 (over x), gx: 16 (over y, z_lo, core), gy: 4 (over z_hi).
Axes of the slice: x: 4, y: 4, z: 8 (z_hi: 4, z_lo: 2; z = z_hi * 2 + z_lo), core: 2. Of those that a mesh axis runs over, the one named last changes fastest.
Arguments:
- field_in: bfloat16 [4, 32, 1024, 1024], P('dp', None, 'gx', 'gy'), parts along dimension 0, may hold values from -6 to 6
- spectral_weight: bfloat16 [32, 32, 2, 128, 128], P(None, None, None, ('gx', 'gy')), may hold values from -6 to 6
- conv_weight: bfloat16 [9, 32, 32], replicated, may hold values from -0.375 to 0.375
- conv_bias: float32 [32], replicated, may hold values from -3 to 3
- upstream: bfloat16 [4, 32, 1024, 1024], P('dp', None, 'gx', 'gy'), parts along dimension 0, may hold values from -6 to 6
Outputs:
- activation: float32 [4, 32, 1024, 1024], P('dp', None, 'gx', 'gy'), parts along dimension 0
- field_grad: float32 [4, 32, 1024, 1024], P('dp', None, 'gx', 'gy'), parts along dimension 0
- weight_grad: float32 [128, 32, 2, 128, 128], P('dp', None, None, ('gx', 'gy')), parts along dimension 0
There are 4 independent parts, one for each index of `dp`. A program takes and returns all parts, laid end to end along the dimension named above; an argument that names none is the same for every part. Nothing has to cross between parts.
All inputs are finite; a program needn't handle non-finite values.
Results may differ from a plain program's by a relative error of at most 0.02.
Values may be sent and summed in bfloat16 or wider, within the bound.
No kernel may reach another device: no remote copies, remote signals or barrier semaphores. Data moves between devices by JAX's collectives and lax.ppermute only.
A program may use at most 128 MiB of HBM per device.

v0:
```python
import math

import jax
import jax.numpy as jnp
from jax import lax
from jax.sharding import PartitionSpec as P

M1 = 128
M2 = 128


def padded_2(cells, sides, width):
    for axis, dim in sides:
        count = lax.axis_size(axis)
        ends = count - 1
        head = lax.slice_in_dim(cells, 0, width, axis=dim)
        tail = lax.slice_in_dim(cells, cells.shape[dim] - width, cells.shape[dim], axis=dim)
        cells = jnp.concatenate(
            [
                lax.ppermute(tail, axis, [(i, (i + 1) % count) for i in range(ends)]),
                cells,
                lax.ppermute(head, axis, [((i + 1) % count, i) for i in range(ends)]),
            ],
            axis=dim,
        )
    return cells


def kx_values(index, length, kept):
    return jnp.where(index < kept // 2, index, index + (length - kept))


def x_table(modes, positions, length):
    product = modes[:, None] * positions[None, :] % length
    angle = product.astype(jnp.float32) * (2.0 * math.pi / length)
    return jnp.stack([jnp.cos(angle), -jnp.sin(angle)], axis=1).astype(jnp.bfloat16)


def y_rows(length, kept, weighted):
    modes = jnp.arange(kept, dtype=jnp.int32)
    places = jnp.arange(length, dtype=jnp.int32)
    angle = (places[:, None] * modes[None, :] % length).astype(jnp.float32) * (
        2.0 * math.pi / length
    )
    cosine = jnp.cos(angle)
    sine = jnp.sin(angle)
    rows = jnp.stack(
        [jnp.stack([cosine, -sine], axis=1), jnp.stack([sine, cosine], axis=1)], axis=0
    )
    if weighted:
        rows = rows * jnp.where(modes == 0, 1.0, 2.0).astype(jnp.float32)
    return rows


def pdot(form, left, right):
    return jnp.einsum(form, left, right, preferred_element_type=jnp.float32)


def padded_block(field):
    return padded_2(field, (("gx", 2), ("gy", 3)), 1)


def forward_chain(field, ytab, factor):
    count_x = lax.axis_size("gx")
    strip_x = lax.axis_index("gx")
    width_x = field.shape[2]
    length_x = width_x * count_x
    positions = strip_x * width_x + jnp.arange(width_x, dtype=jnp.int32)
    modes = kx_values(
        jnp.arange(M1 // count_x * lax.axis_size("gx"), dtype=jnp.int32), length_x, M1
    )
    summed = lax.psum_scatter(
        pdot("msx,lcxy->mslcy", x_table(modes, positions, length_x), field),
        "gx",
        scatter_dimension=0,
        tiled=True,
    )
    spec_x = (summed * factor).astype(jnp.bfloat16)
    spec_x = lax.all_to_all(spec_x, "gy", split_axis=0, concat_axis=4, tiled=True)
    return pdot("mslcy,sytq->mtlcq", spec_x, ytab).astype(jnp.bfloat16)


def inverse_chain(spec, ytab, factor, width_x):
    count_x = lax.axis_size("gx")
    strip_x = lax.axis_index("gx")
    length_x = width_x * count_x
    over_y = pdot("mtldq,tqpy->mpldy", spec, ytab).astype(jnp.bfloat16)
    rows = lax.all_to_all(over_y, "gy", split_axis=4, concat_axis=0, tiled=True)
    positions = strip_x * width_x + jnp.arange(width_x, dtype=jnp.int32)
    piece = lax.all_gather(rows, "gx", axis=0, tiled=True)
    modes = kx_values(jnp.arange(piece.shape[0], dtype=jnp.int32), length_x, M1)
    total = pdot("mpldy,mpx->ldxy", piece, x_table(modes, positions, length_x))
    return (total * factor).astype(jnp.bfloat16)


def mix_modes(spec, weight):
    real_s, imag_s = (spec[:, 0], spec[:, 1])
    real_w, imag_w = (weight[:, :, 0], weight[:, :, 1])
    form = "mlcq,cdmq->mldq"
    real_v = pdot(form, real_s, real_w) - pdot(form, imag_s, imag_w)
    imag_v = pdot(form, real_s, imag_w) + pdot(form, imag_s, real_w)
    return jnp.stack([real_v, imag_v], axis=1).astype(jnp.bfloat16)


def mix_grads(spec, weight, dmixed):
    real_s, imag_s = (spec[:, 0], spec[:, 1])
    real_w, imag_w = (weight[:, :, 0], weight[:, :, 1])
    real_d, imag_d = (dmixed[:, 0], dmixed[:, 1])
    form_w = "mlcq,mldq->cdmq"
    grad_real = pdot(form_w, real_s, real_d) + pdot(form_w, imag_s, imag_d)
    grad_imag = pdot(form_w, real_s, imag_d) - pdot(form_w, imag_s, real_d)
    form_s = "cdmq,mldq->mlcq"
    dreal = pdot(form_s, real_w, real_d) + pdot(form_s, imag_w, imag_d)
    dimag = pdot(form_s, real_w, imag_d) - pdot(form_s, imag_w, real_d)
    grads = jnp.stack([grad_real, grad_imag], axis=2)
    return (grads, jnp.stack([dreal, dimag], axis=1).astype(jnp.bfloat16))


def conv_forward(padded, weight, rows, cols):
    total = jnp.zeros((padded.shape[0], weight.shape[1], rows, cols), jnp.float32)
    for row_tap in range(3):
        for col_tap in range(3):
            window = padded[:, :, row_tap : row_tap + rows, col_tap : col_tap + cols]
            total = total + pdot("dc,lcxy->ldxy", weight[3 * row_tap + col_tap], window)
    return total


def conv_backward(padded, weight, rows, cols):
    total = jnp.zeros((padded.shape[0], weight.shape[2], rows, cols), jnp.float32)
    for row_tap in range(3):
        for col_tap in range(3):
            window = padded[
                :, :, 2 - row_tap : 2 - row_tap + rows, 2 - col_tap : 2 - col_tap + cols
            ]
            total = total + pdot("dc,ldxy->lcxy", weight[3 * row_tap + col_tap], window)
    return total


def body(field_in, spectral_weight, conv_weight, conv_bias, upstream):
    width_x = field_in.shape[2]
    width_y = field_in.shape[3]
    length_y = width_y * lax.axis_size("gy")
    scale = 1.0 / (width_x * lax.axis_size("gx") * length_y)
    plain = y_rows(length_y, M2, False)
    weighted = y_rows(length_y, M2, True)
    fy_table = plain.astype(jnp.bfloat16)
    ay_table = weighted.astype(jnp.bfloat16)
    gy_table = jnp.transpose(weighted, (2, 3, 0, 1)).astype(jnp.bfloat16)
    by_table = jnp.transpose(plain, (2, 3, 0, 1)).astype(jnp.bfloat16)
    spec = forward_chain(field_in, fy_table, 1.0)
    mixed = mix_modes(spec, spectral_weight)
    spectral = inverse_chain(mixed, gy_table, scale, width_x)
    local = conv_forward(padded_block(field_in), conv_weight, width_x, width_y)
    pre = spectral.astype(jnp.float32) + local + conv_bias[None, :, None, None]
    gate = jax.nn.sigmoid(pre)
    activation = pre * gate
    dpre = (upstream.astype(jnp.float32) * gate * (1.0 + pre * (1.0 - gate))).astype(jnp.bfloat16)
    dspec = forward_chain(dpre, ay_table, scale)
    weight_grad, dmix = mix_grads(spec, spectral_weight, dspec)
    dfield = inverse_chain(dmix, by_table, 1.0, width_x)
    back_local = conv_backward(padded_block(dpre), conv_weight, width_x, width_y)
    field_grad = dfield.astype(jnp.float32) + back_local
    return (activation, field_grad, weight_grad)


def solution(mesh):
    return jax.shard_map(
        body,
        mesh=mesh,
        in_specs=(
            P("dp", None, "gx", "gy"),
            P(None, None, None, ("gx", "gy"), None),
            P(),
            P(),
            P("dp", None, "gx", "gy"),
        ),
        out_specs=(
            P("dp", None, "gx", "gy"),
            P("dp", None, "gx", "gy"),
            P("dp", None, None, ("gx", "gy"), None),
        ),
        check_vma=False,
    )
```

profile of v0, /device:TPU:1, one launch (start us, length us, event | category | flops | bytes accessed | tf_op | source)
XLA Modules:
  0.0 457.2 jit_solution(8955305337069914426)
XLA Ops:
  7.5 5.8 %convolution_bitcast_fusion.1 = f32[128,2,1,32,256]{4,0,3,1,2:T(8,128)} fusion(bf16[1,32,64,256]{3,2,1,0:T(8,128)(2,1)} %param.5, bf16[128,1,64]{0,2,1:T(8,128)(2,1)S(1)} %get-tuple-element.48, bf16[128,1,64]{0,2,1:T(8,128)(2,1)S(1)} %get-tuple-element.47), kind=kOutput, calls=%fused_computation.5 | convolution fusion | flops 268500992 | bytes 9469952 | tf_op jit(solution)/shard_map/msx,lcxy->mslcy/dot_general | solution.py:56
  15.2 100.7 %reduce-scatter.3.cloned.1.call-done = f32[8,2,1,32,256]{4,0,3,1,2:T(8,128)} async-done(((f32[128,2,1,32,256]{4,0,3,1,2:T(8,128)}), f32[8,2,1,32,256]{4,0,3,1,2:T(8,128)}) %reduce-scatter.3.cloned.1.call-update) | async-done | bytes 524304 | tf_op jit(solution)/shard_map/reduce_scatter | solution.py:72
  117.8 5.8 %all-to-all-start = ((bf16[8,2,1,32,256]{4,3,1,2,0:T(8,128)(2,1)}), bf16[8,2,1,32,256]{4,3,1,2,0:T(8,128)(2,1)S(1)}, u32[]{:S(2)}, u32[]{:S(2)}) async-start(bf16[8,2,1,32,256]{4,3,1,2,0:T(8,128)(2,1)} %copy.63), calls=%async_computation.1 | async-start | bytes 524288 | tf_op jit(solution)/shard_map/all_to_all | solution.py:79
  123.6 2.1 fusion.104
  125.9 7.2 %all-to-all-done = bf16[8,2,1,32,256]{4,3,1,2,0:T(8,128)(2,1)S(1)} async-done(((bf16[8,2,1,32,256]{4,3,1,2,0:T(8,128)(2,1)}), bf16[8,2,1,32,256]{4,3,1,2,0:T(8,128)(2,1)S(1)}, u32[]{:S(2)}, u32[]{:S(2)}) %all-to-all-start) | async-done | bytes 262176 | tf_op jit(solution)/shard_map/all_to_all | solution.py:79
  136.1 2.1 fusion.26
  140.4 11.9 %all_to_all.66 = bf16[4,2,16384]{2,1,0:T(2,128)(2,1)S(1)} all-to-all(bf16[4,2,16384]{2,1,0:T(2,128)(2,1)S(1)} %reshape.513), channel_id=1, replica_groups=mesh['dp'=4,'gx'=16,'gy'=4] {'gy'}, dimensions={0} | all-to-all | bytes 524288 | tf_op jit(solution)/shard_map/all_to_all | solution.py:88
  155.7 6.7 %collective-permute-start = (bf16[1,32,1,256]{3,1,2,0:T(8,128)(2,1)S(1)}, bf16[1,32,1,256]{3,1,2,0:T(8,128)(2,1)S(1)}, u32[]{:S(2)}, u32[]{:S(2)}) collective-permute-start(bf16[1,32,1,256]{3,1,2,0:T(8,128)(2,1)S(1)} %get-tuple-element.34), channel_id=1, source_target_pairs={{0,4},{4,8},{8,12},{12,16},{16,20},{20,24},{24,28},{28,32},{32,36}... | collective-permute-start | bytes 49160 | tf_op jit(solution)/shard_map/ppermute | solution.py:20
  162.4 2.1 collective-permute-start.1
  164.5 2.1 fusion.92
  172.1 4.9 %collective-permute-start.2 = (bf16[1,32,66,1]{2,1,3,0:T(8,128)(2,1)S(1)}, bf16[1,32,66,1]{2,1,3,0:T(8,128)(2,1)S(1)}, u32[]{:S(2)}, u32[]{:S(2)}) collective-permute-start(bf16[1,32,66,1]{2,1,3,0:T(8,128)(2,1)S(1)} %copy.71), channel_id=1, source_target_pairs={{0,1},{1,2},{2,3},{4,5},{5,6},{6,7},{8,9},{9,10},{10,11},{12,13},{... | collective-permute-start | bytes 12680 | tf_op jit(solution)/shard_map/ppermute | solution.py:20
  193.9 11.2 %all-gather.3.cloned.1.call-done = bf16[128,2,1,32,256]{4,0,1,3,2:T(8,128)(2,1)} async-done(((bf16[8,2,1,32,256]{4,0,1,3,2:T(8,128)(2,1)}), bf16[128,2,1,32,256]{4,0,1,3,2:T(8,128)(2,1)}) %all-gather.3.cloned.1.call-update) | async-done | bytes 4194320 | tf_op jit(solution)/shard_map/all_gather | solution.py:90
  205.1 26.7 %multiply_convert_fusion = (bf16[1,32,64,256]{3,2,1,0:T(8,128)(2,1)S(1)}, f32[1,32,64,256]{3,2,1,0:T(8,128)}) fusion(bf16[1,32,64,256]{3,2,1,0:T(8,128)(2,1)S(1)} %copy-done.7, f32[32]{0:T(128)S(1)} %copy-done.12, f32[64,256,32]{1,2,0:T(8,128)} %fusion.53, f32[64,256,32]{1,2,0:T(8,128)} %fusion.57, f32[64,256,32]{1,2,0:T(8,128)} %fusion.61, ...), kind=kOutput, calls=%fused_computation.32 | convolution fusion | flops 281083904 | bytes 27295872 | tf_op jit(solution)/shard_map/mpldy,mpx->ldxy/dot_general | solution.py:56
  231.8 4.5 convolution_bitcast_fusion
  236.4 97.3 %reduce-scatter.5.cloned.1.call-done = f32[8,2,1,32,256]{4,0,3,1,2:T(8,128)} async-done(((f32[128,2,1,32,256]{4,0,3,1,2:T(8,128)}), f32[8,2,1,32,256]{4,0,3,1,2:T(8,128)}) %reduce-scatter.5.cloned.1.call-update) | async-done | bytes 524304 | tf_op jit(solution)/shard_map/reduce_scatter | solution.py:72
  334.9 15.5 %all_to_all.67 = bf16[8,2,1,32,256]{4,3,1,2,0:T(8,128)(2,1)S(1)} all-to-all(bf16[8,2,1,32,256]{4,3,1,2,0:T(8,128)(2,1)S(1)} %copy.87), channel_id=1, replica_groups=mesh['dp'=4,'gx'=16,'gy'=4] {'gy'}, dimensions={0} | all-to-all | bytes 524288 | tf_op jit(solution)/shard_map/all_to_all | solution.py:79
  353.5 2.6 fusion.30
  358.3 12.0 %all_to_all.68 = bf16[4,2,16384]{2,1,0:T(2,128)(2,1)S(1)} all-to-all(bf16[4,2,16384]{2,1,0:T(2,128)(2,1)S(1)} %reshape.515), channel_id=1, replica_groups=mesh['dp'=4,'gx'=16,'gy'=4] {'gy'}, dimensions={0} | all-to-all | bytes 524288 | tf_op jit(solution)/shard_map/all_to_all | solution.py:88
  373.1 7.4 %collective-permute-start.4 = (bf16[1,32,1,256]{3,2,1,0:T(2,128)(2,1)S(1)}, bf16[1,32,1,256]{3,2,1,0:T(2,128)(2,1)S(1)}, u32[]{:S(2)}, u32[]{:S(2)}) collective-permute-start(bf16[1,32,1,256]{3,2,1,0:T(2,128)(2,1)S(1)} %get-tuple-element.31), channel_id=1, source_target_pairs={{0,4},{4,8},{8,12},{12,16},{16,20},{20,24},{24,28},{28,32},{32,36}... | collective-permute-start | bytes 49160 | tf_op jit(solution)/shard_map/ppermute | solution.py:20
  383.3 2.6 collective-permute-done.5
  389.2 2.4 collective-permute-start.7
  395.0 2.1 fusion.76
  397.1 2.1 fusion.88
  401.6 3.7 pad_maximum_fusion.2
  406.0 2.1 fusion.74
  408.1 2.2 slice_bitcast_fusion.5
  410.3 2.1 fusion.78
  412.5 2.1 fusion.80
  414.5 2.1 fusion.84
  416.6 2.1 fusion.86
  422.0 2.4 pad_maximum_fusion.1
  424.4 25.9 %bitcast_add_fusion = f32[1,32,64,256]{3,2,1,0:T(8,128)} fusion(f32[64,256,32]{1,2,0:T(8,128)} %fusion.74, f32[64,256,32]{1,2,0:T(8,128)} %fusion.76, f32[64,256,32]{1,2,0:T(8,128)} %fusion.78, f32[64,256,32]{1,2,0:T(8,128)} %fusion.80, f32[64,256,32]{1,2,0:T(8,128)S(1)} %fusion.82, f32[64,256,32]{1,2,0:T(8,128)} %fusion.84, f32[64,256,32]{1,2,0:T(8,128)} %fusion.86, ...), kind=kOutput, calls=%fused_computation.8 | convolution fusion | flops 274268160 | bytes 25198592 | tf_op jit(solution)/shard_map/mpldy,mpx->ldxy/dot_general | solution.py:56
  (117 shorter events, 60.3 us)
Async XLA Ops:
  7.2 108.8 %reduce-scatter.3.cloned.1.call-start = ((), (), s32[]{:S(2)}) async-start(), calls=%async_computation.6 | async-start | bytes 8912896 | tf_op jit(solution)/shard_map/reduce_scatter | solution.py:72
  117.8 15.3 %all-to-all-start = ((bf16[8,2,1,32,256]{4,3,1,2,0:T(8,128)(2,1)}), bf16[8,2,1,32,256]{4,3,1,2,0:T(8,128)(2,1)S(1)}, u32[]{:S(2)}, u32[]{:S(2)}) async-start(bf16[8,2,1,32,256]{4,3,1,2,0:T(8,128)(2,1)} %copy.63), calls=%async_computation.1 | async-start | bytes 524288 | tf_op jit(solution)/shard_map/all_to_all | solution.py:79
  123.6 81.5 %all-gather.3.cloned.1.call-start = ((), (), s32[]{:S(2)}) async-start(), calls=%async_computation.7 | async-start | bytes 4456448 | tf_op jit(solution)/shard_map/all_gather | solution.py:90
  125.8 12.4 %copy-start.1 = (f32[1,1024,2,128]{3,1,0,2:T(8,128)}, f32[1,1024,2,128]{3,1,0,2:T(8,128)S(1)}, u32[]{:S(2)}) copy-start(f32[1,1024,2,128]{3,1,0,2:T(8,128)S(1)} %get-tuple-element.35) | copy-start | bytes 3145732
  125.9 12.4 %copy-start.3 = (f32[1,1024,2,128]{3,1,0,2:T(8,128)}, f32[1,1024,2,128]{3,1,0,2:T(8,128)S(1)}, u32[]{:S(2)}) copy-start(f32[1,1024,2,128]{3,1,0,2:T(8,128)S(1)} %get-tuple-element.36) | copy-start | bytes 3145732
  125.9 10.2 %copy-start.5 = (bf16[32,32,2,2,128]{4,3,2,1,0:T(2,128)(2,1)S(1)}, bf16[32,32,2,2,128]{4,3,2,1,0:T(2,128)(2,1)}, u32[]{:S(2)}) copy-start(bf16[32,32,2,2,128]{4,3,2,1,0:T(2,128)(2,1)} %param.6) | copy-start | bytes 3145732
  140.4 14.7 %copy-start = (bf16[1,32,64,256]{3,2,1,0:T(8,128)(2,1)S(1)}, bf16[1,32,64,256]{3,2,1,0:T(8,128)(2,1)}, u32[]{:S(2)}) copy-start(bf16[1,32,64,256]{3,2,1,0:T(8,128)(2,1)} %param.5) | copy-start | bytes 3145732
  152.8 11.7 %copy-start.8 = (bf16[9,32,32]{2,1,0:T(8,128)(2,1)S(1)}, bf16[9,32,32]{2,1,0:T(8,128)(2,1)}, u32[]{:S(2)}) copy-start(bf16[9,32,32]{2,1,0:T(8,128)(2,1)} %param.7) | copy-start | bytes 55300
  155.0 178.7 %reduce-scatter.5.cloned.1.call-start = ((), (), s32[]{:S(2)}) async-start(), calls=%async_computation.8 | async-start | bytes 8912896 | tf_op jit(solution)/shard_map/reduce_scatter | solution.py:72
  155.7 11.0 %collective-permute-start = (bf16[1,32,1,256]{3,1,2,0:T(8,128)(2,1)S(1)}, bf16[1,32,1,256]{3,1,2,0:T(8,128)(2,1)S(1)}, u32[]{:S(2)}, u32[]{:S(2)}) collective-permute-start(bf16[1,32,1,256]{3,1,2,0:T(8,128)(2,1)S(1)} %get-tuple-element.34), channel_id=1, source_target_pairs={{0,4},{4,8},{8,12},{12,16},{16,20},{20,24},{24,28},{28,32},{32,36}... | collective-permute-start | bytes 49160 | tf_op jit(solution)/shard_map/ppermute | solution.py:20
  162.4 5.1 %collective-permute-start.1 = (bf16[1,32,1,256]{3,1,2,0:T(8,128)(2,1)S(1)}, bf16[1,32,1,256]{3,1,2,0:T(8,128)(2,1)S(1)}, u32[]{:S(2)}, u32[]{:S(2)}) collective-permute-start(bf16[1,32,1,256]{3,1,2,0:T(8,128)(2,1)S(1)} %get-tuple-element.33), channel_id=1, source_target_pairs={{4,0},{8,4},{12,8},{16,12},{20,16},{24,20},{28,24},{32,28},{36,32}... | collective-permute-start | bytes 49160 | tf_op jit(solution)/shard_map/ppermute | solution.py:22
  170.2 10.3 %collective-permute-start.3 = (bf16[1,32,66,1]{2,1,3,0:T(8,128)(2,1)S(1)}, bf16[1,32,66,1]{2,1,3,0:T(8,128)(2,1)S(1)}, u32[]{:S(2)}, u32[]{:S(2)}) collective-permute-start(bf16[1,32,66,1]{2,1,3,0:T(8,128)(2,1)S(1)} %copy.76), channel_id=1, source_target_pairs={{1,0},{2,1},{3,2},{5,4},{6,5},{7,6},{9,8},{10,9},{11,10},{13,12},{... | collective-permute-start | bytes 12680 | tf_op jit(solution)/shard_map/ppermute | solution.py:22
  172.1 9.3 %collective-permute-start.2 = (bf16[1,32,66,1]{2,1,3,0:T(8,128)(2,1)S(1)}, bf16[1,32,66,1]{2,1,3,0:T(8,128)(2,1)S(1)}, u32[]{:S(2)}, u32[]{:S(2)}) collective-permute-start(bf16[1,32,66,1]{2,1,3,0:T(8,128)(2,1)S(1)} %copy.71), channel_id=1, source_target_pairs={{0,1},{1,2},{2,3},{4,5},{5,6},{6,7},{8,9},{9,10},{10,11},{12,13},{... | collective-permute-start | bytes 12680 | tf_op jit(solution)/shard_map/ppermute | solution.py:20
  192.0 13.1 %copy-start.7 = (bf16[1,32,64,256]{3,2,1,0:T(8,128)(2,1)S(1)}, bf16[1,32,64,256]{3,2,1,0:T(8,128)(2,1)}, u32[]{:S(2)}) copy-start(bf16[1,32,64,256]{3,2,1,0:T(8,128)(2,1)} %param.9) | copy-start | bytes 3145732
  192.0 13.1 %copy-start.12 = (f32[32]{0:T(128)S(1)}, f32[32]{0:T(128)}, u32[]{:S(2)}) copy-start(f32[32]{0:T(128)} %param.8) | copy-start | bytes 388
  236.3 115.1 %copy-start.2 = (f32[1,1024,2,128]{3,1,0,2:T(8,128)S(1)}, f32[1,1024,2,128]{3,1,0,2:T(8,128)}, u32[]{:S(2)}) copy-start(f32[1,1024,2,128]{3,1,0,2:T(8,128)} %copy-done.1) | copy-start | bytes 3145732
  236.3 115.1 %copy-start.4 = (f32[1,1024,2,128]{3,1,0,2:T(8,128)S(1)}, f32[1,1024,2,128]{3,1,0,2:T(8,128)}, u32[]{:S(2)}) copy-start(f32[1,1024,2,128]{3,1,0,2:T(8,128)} %copy-done.3) | copy-start | bytes 3145732
  236.3 188.1 %all-gather.5.cloned.1.call-start = ((), (), s32[]{:S(2)}) async-start(), calls=%async_computation.9 | async-start | bytes 4456448 | tf_op jit(solution)/shard_map/all_gather | solution.py:90
  351.4 2.0 copy-start.6
  358.3 14.7 %copy-start.9 = (f32[2,128,32]{1,2,0:T(8,128)S(1)}, f32[2,128,32]{1,2,0:T(8,128)}, u32[]{:S(2)}) copy-start(f32[2,128,32]{1,2,0:T(8,128)} %get-tuple-element.43) | copy-start | bytes 98308
  373.1 10.1 %collective-permute-start.4 = (bf16[1,32,1,256]{3,2,1,0:T(2,128)(2,1)S(1)}, bf16[1,32,1,256]{3,2,1,0:T(2,128)(2,1)S(1)}, u32[]{:S(2)}, u32[]{:S(2)}) collective-permute-start(bf16[1,32,1,256]{3,2,1,0:T(2,128)(2,1)S(1)} %get-tuple-element.31), channel_id=1, source_target_pairs={{0,4},{4,8},{8,12},{12,16},{16,20},{20,24},{24,28},{28,32},{32,36}... | collective-permute-start | bytes 49160 | tf_op jit(solution)/shard_map/ppermute | solution.py:20
  380.6 5.2 %collective-permute-start.5 = (bf16[1,32,1,256]{3,2,1,0:T(2,128)(2,1)S(1)}, bf16[1,32,1,256]{3,2,1,0:T(2,128)(2,1)S(1)}, u32[]{:S(2)}, u32[]{:S(2)}) collective-permute-start(bf16[1,32,1,256]{3,2,1,0:T(2,128)(2,1)S(1)} %get-tuple-element.32), channel_id=1, source_target_pairs={{4,0},{8,4},{12,8},{16,12},{20,16},{24,20},{28,24},{32,28},{36,32}... | collective-permute-start | bytes 49160 | tf_op jit(solution)/shard_map/ppermute | solution.py:22
  389.2 10.0 %collective-permute-start.7 = (bf16[1,32,66,1]{2,1,3,0:T(8,128)(2,1)S(1)}, bf16[1,32,66,1]{2,1,3,0:T(8,128)(2,1)S(1)}, u32[]{:S(2)}, u32[]{:S(2)}) collective-permute-start(bf16[1,32,66,1]{2,1,3,0:T(8,128)(2,1)S(1)} %copy.100), channel_id=1, source_target_pairs={{0,1},{1,2},{2,3},{4,5},{5,6},{6,7},{8,9},{9,10},{10,11},{12,13},{... | collective-permute-start | bytes 12680 | tf_op jit(solution)/shard_map/ppermute | solution.py:20
  393.0 7.4 %collective-permute-start.6 = (bf16[1,32,66,1]{2,1,3,0:T(8,128)(2,1)S(1)}, bf16[1,32,66,1]{2,1,3,0:T(8,128)(2,1)S(1)}, u32[]{:S(2)}, u32[]{:S(2)}) collective-permute-start(bf16[1,32,66,1]{2,1,3,0:T(8,128)(2,1)S(1)} %copy.92), channel_id=1, source_target_pairs={{1,0},{2,1},{3,2},{5,4},{6,5},{7,6},{9,8},{10,9},{11,10},{13,12},{... | collective-permute-start | bytes 12680 | tf_op jit(solution)/shard_map/ppermute | solution.py:22
  418.6 2.1 copy-start.11
  418.6 2.1 copy-start.10
Sparse Core Ops, SparseCore 0:
  13.4 102.5 reduce-scatter.2
  155.1 49.9 all-gather.2
  236.4 97.2 reduce-scatter.4
  373.1 49.3 all-gather.4
where the time goes:
time: 466 us; the launch traced here: 457 us
  waiting for transfers between devices  219 us (47%)
  matrix products  99.8 us (21%)
  blocking collectives  39.4 us (8%)
  starting transfers between devices  34 us (7%)
  local copies, waits for them, and re-layouts  28.8 us (6%)
  other arithmetic  21.2 us (5%)
  between operations  14.7 us (3%)
    reduce_scatter x2, waiting for transfers between devices, forward_chain(): lax.psum_scatter(pdot('msx,lcxy->mslcy', x_table(modes, positions, length...  198 us
    dot_general x26, matrix products, pdot(): return jnp.einsum(form, left, right, preferred_element_type=jnp.float32)  99.8 us
    all_to_all x2, blocking collectives, inverse_chain(): rows = lax.all_to_all(over_y, 'gy', split_axis=4, concat_axis=0, tiled=True)  23.9 us
    ppermute x4, starting transfers between devices, padded_2(): lax.ppermute(tail, axis, [(i, (i + 1) % count) for i in range(ends)])  21.4 us
    all_to_all x1, blocking collectives, forward_chain(): lax.all_to_all(spec_x, 'gy', split_axis=0, concat_axis=4, tiled=True)  15.5 us
    all_gather x2, waiting for transfers between devices, inverse_chain(): piece = lax.all_gather(rows, 'gx', axis=0, tiled=True)  11.2 us
  transfers between devices with their start and end apart: 13, of which 6 were waited for; matrix products, arithmetic and copies ran while one was open for 14% of the time, Pallas kernels for 0%

commit v1 on v0

v1 whole, which is shorter than its diff:
```python
import functools
import math

import jax
import jax.numpy as jnp
import numpy as np
from jax import lax
from jax.experimental import pallas as pl
from jax.experimental.pallas import tpu as pltpu
from jax.sharding import PartitionSpec as P

M1 = 128
M2 = 128
BF = jnp.bfloat16
F32 = jnp.float32


def dot(left, right):
    return jnp.dot(left, right, preferred_element_type=F32)


@functools.lru_cache(maxsize=None)
def x_table(length, owners):
    slots = M1 // owners
    order = np.arange(M1).reshape(owners, slots).T.reshape(-1)
    modes = np.where(order < M1 // 2, order, order + length - M1)
    angle = (modes[:, None] * np.arange(length)[None, :] % length) * (2.0 * math.pi / length)
    table = np.concatenate([np.cos(angle), -np.sin(angle)], axis=0)
    return table.astype(np.float32).astype(jnp.bfloat16)


@functools.lru_cache(maxsize=None)
def y_table(length, width):
    angle = (np.arange(width)[:, None] * np.arange(M2)[None, :] % length) * (2.0 * math.pi / length)
    cosine, sine = np.cos(angle), np.sin(angle)
    table = np.concatenate(
        [np.concatenate([cosine, -sine], axis=1), np.concatenate([sine, cosine], axis=1)], axis=0
    )
    return table.astype(np.float32).astype(jnp.bfloat16)


def turn(values, quarter, sign):
    half = values.shape[1] // 2
    lane = lax.broadcasted_iota(jnp.int32, (1, 2 * half), 1)
    second = lane >= half
    q = jnp.where(second, lane - half, lane)
    step = lax.rem(q * quarter, 4)
    one = jnp.where(step == 0, 1.0, jnp.where(step == 2, -1.0, 0.0))
    imag = jnp.where(step == 1, 1.0, jnp.where(step == 3, -1.0, 0.0)) * sign
    swap = jnp.concatenate([values[:, half:], values[:, :half]], axis=1)
    return values * one + swap * jnp.where(second, imag, -imag)


def column_weight(half):
    lane = lax.broadcasted_iota(jnp.int32, (1, 2 * half), 1)
    return jnp.where((lane == 0) | (lane == half), 1.0, 2.0)


def forward_kernel(weighted, factor, block_ref, x_ref, y_ref, out_ref, rows_ref):
    step = pl.program_id(0)
    slots = out_ref.shape[1] // 4
    owners = out_ref.shape[0]
    width = block_ref.shape[3]
    block = block_ref[:, 0].reshape(-1, width)
    spec_x = dot(x_ref[...], block)
    if factor != 1.0:
        spec_x = spec_x * factor
    spec_x = spec_x.astype(BF)
    spec = dot(spec_x[:M1], y_ref[:width]) + dot(spec_x[M1:], y_ref[width:])
    spec = turn(spec, lax.axis_index("gy"), -1.0)
    if weighted:
        spec = spec * column_weight(M2)
    for slot in range(slots):
        for part in range(2):
            rows_ref[(step * slots + slot) * 2 + part] = spec[
                slot * owners : (slot + 1) * owners, part * M2 : (part + 1) * M2
            ]

    @pl.when(step == 1)
    def _():
        out_ref[...] = jnp.transpose(rows_ref[...], (1, 0, 2)).astype(BF)


def to_modes(block, weighted, factor, length_x, length_y, owners):
    strips, channels, width_x, width_y = block.shape
    slots = M1 // owners
    rows = channels * slots * 2
    return pl.pallas_call(
        functools.partial(forward_kernel, weighted, factor),
        grid=(channels,),
        in_specs=[
            pl.BlockSpec((strips, 1, width_x, width_y), lambda c: (0, c, 0, 0)),
            pl.BlockSpec((2 * M1, length_x), lambda c: (0, 0)),
            pl.BlockSpec((2 * width_y, 2 * M2), lambda c: (0, 0)),
        ],
        out_specs=pl.BlockSpec((owners, rows, M2), lambda c: (0, 0, 0)),
        out_shape=jax.ShapeDtypeStruct((owners, rows, M2), BF),
        scratch_shapes=[pltpu.VMEM((rows, owners, M2), F32)],
        name="to_modes",
    )(block, x_table(length_x, owners), y_table(length_y, width_y))


def inverse_kernel(weighted, factor, spec_ref, x_ref, y_ref, out_ref, rows_ref):
    step = pl.program_id(0)
    slots = spec_ref.shape[1] // 4
    width = out_ref.shape[3]

    @pl.when(step == 0)
    def _():
        rows_ref[...] = jnp.transpose(spec_ref[...].astype(F32), (1, 0, 2))

    spec = jnp.concatenate(
        [
            jnp.concatenate(
                [rows_ref[(step * slots + slot) * 2], rows_ref[(step * slots + slot) * 2 + 1]],
                axis=1,
            )
            for slot in range(slots)
        ],
        axis=0,
    )
    spec = turn(spec, lax.axis_index("gy"), 1.0)
    if weighted:
        spec = spec * column_weight(M2)
    over_y = dot(spec.astype(BF), y_ref[...]).astype(BF)
    over_y = jnp.concatenate([over_y[:, :width], over_y[:, width:]], axis=0)
    total = dot(x_ref[...], over_y)
    if factor != 1.0:
        total = total * factor
    out_ref[:, 0] = total.astype(BF).reshape(out_ref.shape[0], out_ref.shape[2], width)


def to_field(spec, weighted, factor, length_x, length_y, strips, width_y):
    owners, rows, _ = spec.shape
    slots = M1 // owners
    channels = rows // slots // 2
    width_x = length_x // strips
    return pl.pallas_call(
        functools.partial(inverse_kernel, weighted, factor),
        grid=(channels,),
        in_specs=[
            pl.BlockSpec((owners, rows, M2), lambda c: (0, 0, 0)),
            pl.BlockSpec((length_x, 2 * M1), lambda c: (0, 0)),
            pl.BlockSpec((2 * M2, 2 * width_y), lambda c: (0, 0)),
        ],
        out_specs=pl.BlockSpec((strips, 1, width_x, width_y), lambda c: (0, c, 0, 0)),
        out_shape=jax.ShapeDtypeStruct((strips, channels, width_x, width_y), BF),
        scratch_shapes=[pltpu.VMEM((rows, owners, M2), F32)],
        name="to_field",
    )(
        spec,
        np.ascontiguousarray(x_table(length_x, owners).T),
        np.ascontiguousarray(y_table(length_y, width_y).T),
    )


CONV_ROWS = 4


def conv_matrix(weight):
    outs, ins = weight.shape[1:]
    band = jnp.transpose(weight.reshape(3, 3, outs, ins), (1, 2, 0, 3)).reshape(3 * outs, 3 * ins)
    return jnp.concatenate(
        [
            jnp.pad(band, ((0, 0), (row * ins, (CONV_ROWS - 1 - row) * ins)))
            for row in range(CONV_ROWS)
        ],
        axis=0,
    )


def conv_kernel(matrix_ref, main_ref, side_ref, out_ref):
    step = pl.program_id(0)
    ins = matrix_ref.shape[1] // (CONV_ROWS + 2)
    outs = out_ref.shape[0]
    tall = out_ref.shape[1]
    width = out_ref.shape[2]
    window = (CONV_ROWS + 2) * ins
    pieces = []
    for part in range(tall // CONV_ROWS):
        start = pl.multiple_of((step * tall + part * CONV_ROWS) * ins, ins)
        main = dot(matrix_ref[...], main_ref[pl.ds(start, window), :])
        side = dot(matrix_ref[...], side_ref[pl.ds(start, window), :])
        taps = jnp.concatenate([main, side], axis=1)
        full = taps.shape[1]
        for row in range(CONV_ROWS):
            base = row * 3 * outs
            low = pltpu.roll(taps[base : base + outs], 1, 1)[:, :width]
            mid = taps[base + outs : base + 2 * outs, :width]
            high = pltpu.roll(taps[base + 2 * outs : base + 3 * outs], full - 1, 1)[:, :width]
            pieces.append(low + mid + high)
    out_ref[...] = jnp.transpose(jnp.stack(pieces, axis=0), (1, 0, 2))


def conv(weight, main, side, rows):
    outs = weight.shape[1]
    width = main.shape[1]
    matrix = conv_matrix(weight)
    tall = 8
    return pl.pallas_call(
        conv_kernel,
        grid=(rows // tall,),
        in_specs=[
            pl.BlockSpec(matrix.shape, lambda k: (0, 0)),
            pl.BlockSpec(main.shape, lambda k: (0, 0)),
            pl.BlockSpec(side.shape, lambda k: (0, 0)),
        ],
        out_specs=pl.BlockSpec((outs, tall, width), lambda k: (0, k, 0)),
        out_shape=jax.ShapeDtypeStruct((outs, rows, width), F32),
        name="conv",
    )(matrix, main, side)


def swap(value, axis, back=False):
    count = lax.axis_size(axis)
    pairs = [(i, i + 1) for i in range(count - 1)]
    if back:
        pairs = [(b, a) for a, b in pairs]
    return lax.ppermute(value, axis, pairs)


def halo(field):
    channels, rows, width = field.shape
    top = swap(field[:, rows - 1], "gx")
    bottom = swap(field[:, 0], "gx", back=True)
    main = jnp.concatenate([top[None], jnp.transpose(field, (1, 0, 2)), bottom[None]], axis=0)
    main = main.reshape((rows + 2) * channels, width)
    pick = np.zeros((2, width), np.float32)
    pick[0, 0] = pick[1, width - 1] = 1.0
    ends = jnp.einsum("ry,ny->rn", pick.astype(BF), main, preferred_element_type=F32).astype(BF)
    right = swap(ends[:1], "gy", back=True)
    left = swap(ends[1:], "gy")
    place = np.zeros((2, 128), np.float32)
    place[0, 0] = place[1, 127] = 1.0
    side = jnp.einsum(
        "rn,rk->nk", jnp.concatenate([right, left]), place.astype(BF), preferred_element_type=F32
    ).astype(BF)
    return main, side


def gather_modes(parts, strips):
    owners, rows, kept = parts.shape
    slots = M1 // owners
    split = parts.reshape(strips, owners // strips, rows // slots // 2, slots, 2, kept)
    total = jnp.sum(split.astype(F32), axis=1).astype(BF)
    return jnp.transpose(total, (2, 3, 0, 1, 4)).reshape(slots, 2, -1, kept)


def spread_modes(spec, strips, pieces):
    slots, _, channels, kept = spec.shape
    split = jnp.transpose(spec.reshape(slots, 2, strips, channels // strips, kept), (2, 3, 0, 1, 4))
    split = jnp.broadcast_to(
        split.reshape(strips, 1, -1, kept), (strips, pieces, 2 * slots * channels // strips, kept)
    )
    return split.reshape(strips * pieces, -1, kept)


def exchange(value, axes):
    return lax.all_to_all(value, axes, split_axis=0, concat_axis=0, tiled=True)


def pdot(form, left, right):
    return jnp.einsum(form, left, right, preferred_element_type=F32)


def mix_modes(spec, weight):
    real_s, imag_s = (spec[:, 0], spec[:, 1])
    real_w, imag_w = (weight[:, :, 0], weight[:, :, 1])
    form = "mcq,cdmq->mdq"
    real_v = pdot(form, real_s, real_w) - pdot(form, imag_s, imag_w)
    imag_v = pdot(form, real_s, imag_w) + pdot(form, imag_s, real_w)
    return jnp.stack([real_v, imag_v], axis=1).astype(BF)


def mix_grads(spec, weight, dmixed):
    real_s, imag_s = (spec[:, 0], spec[:, 1])
    real_w, imag_w = (weight[:, :, 0], weight[:, :, 1])
    real_d, imag_d = (dmixed[:, 0], dmixed[:, 1])
    form_w = "mcq,mdq->cdmq"
    grad_real = pdot(form_w, real_s, real_d) + pdot(form_w, imag_s, imag_d)
    grad_imag = pdot(form_w, real_s, imag_d) - pdot(form_w, imag_s, real_d)
    form_s = "cdmq,mdq->mcq"
    dreal = pdot(form_s, real_w, real_d) + pdot(form_s, imag_w, imag_d)
    dimag = pdot(form_s, real_w, imag_d) - pdot(form_s, imag_w, real_d)
    grads = jnp.stack([grad_real, grad_imag], axis=2)
    return (grads, jnp.stack([dreal, dimag], axis=1).astype(BF))


def body(field_in, spectral_weight, conv_weight, conv_bias, upstream):
    strips, pieces = lax.axis_size("gx"), lax.axis_size("gy")
    owners = strips * pieces
    _, channels, width_x, width_y = field_in.shape
    length_x, length_y = width_x * strips, width_y * pieces
    scale = 1.0 / (length_x * length_y)
    both = ("gx", "gy")
    share = (strips, channels // strips, width_x, width_y)
    whole = (channels, width_x, width_y)

    field = field_in[0]
    block = exchange(field.reshape(share), "gx")
    parts = to_modes(block, False, 1.0, length_x, length_y, owners)
    spec = gather_modes(exchange(parts, both), strips)
    main, side = halo(field)
    local = conv(conv_weight, main, side, width_x)
    mixed = mix_modes(spec, spectral_weight)
    arrived = exchange(spread_modes(mixed, strips, pieces), both)
    back = to_field(arrived, True, scale, length_x, length_y, strips, width_y)
    spectral = exchange(back, "gx").reshape(whole)

    pre = spectral.astype(F32) + local + conv_bias[:, None, None]
    gate = jax.nn.sigmoid(pre)
    activation = pre * gate
    dpre = (upstream[0].astype(F32) * gate * (1.0 + pre * (1.0 - gate))).astype(BF)

    dblock = exchange(dpre.reshape(share), "gx")
    dparts = to_modes(dblock, True, scale, length_x, length_y, owners)
    dspec = gather_modes(exchange(dparts, both), strips)
    dmain, dside = halo(dpre)
    back_local = conv(jnp.transpose(conv_weight[::-1], (0, 2, 1)), dmain, dside, width_x)
    weight_grad, dmix = mix_grads(spec, spectral_weight, dspec)
    darrived = exchange(spread_modes(dmix, strips, pieces), both)
    dback = to_field(darrived, False, 1.0, length_x, length_y, strips, width_y)
    dfield = exchange(dback, "gx").reshape(whole)
    field_grad = dfield.astype(F32) + back_local
    return (activation[None], field_grad[None], weight_grad)


def solution(mesh):
    return jax.shard_map(
        body,
        mesh=mesh,
        in_specs=(
            P("dp", None, "gx", "gy"),
            P(None, None, None, ("gx", "gy"), None),
            P(),
            P(),
            P("dp", None, "gx", "gy"),
        ),
        out_specs=(
            P("dp", None, "gx", "gy"),
            P("dp", None, "gx", "gy"),
            P("dp", None, None, ("gx", "gy"), None),
        ),
        check_vma=False,
    )
```

time: 466 us -> 199 us (0.43); the launches traced: 457 us -> 197 us
  waiting for transfers between devices: 219 us -> 29 us
  matrix products: 99.8 us -> 0.76 us
  blocking collectives: 39.4 us -> 66.6 us
  Pallas kernels: 0 us -> 25.2 us
  local copies, waits for them, and re-layouts: 28.8 us -> 4.47 us
  starting transfers between devices: 34 us -> 50.1 us
  between operations: 14.7 us -> 1.21 us
    reduce_scatter x2 -> x0, waiting for transfers between devices: 198 us -> none  [forward_chain(): lax.psum_scatter(pdot('msx,lcxy->mslcy', x_table(modes, positions, length...]
    dot_general x26 -> x2, matrix products: 99.8 us -> 0.76 us  [halo(): jnp.einsum('ry,ny->rn', pick.astype(BF), main, preferred_element_type=F32)]
    all_to_all x3, blocking collectives: 39.4 us -> 66.6 us  [exchange(): return lax.all_to_all(value, axes, split_axis=0, concat_axis=0, tiled=True)]
    pallas_call x0 -> x6, Pallas kernels: none -> 25.2 us  [the longest x2 13.2 us: conv(): pl.pallas_call(conv_kernel, grid=(rows // tall,), in_specs=[pl.BlockSpec(...]
    all_to_all x1 -> x5, starting transfers between devices: 5.84 us -> 26.6 us  [exchange(): return lax.all_to_all(value, axes, split_axis=0, concat_axis=0, tiled=True)]
    all_to_all x1 -> x5, waiting for transfers between devices: 7.17 us -> 19.5 us  [exchange(): return lax.all_to_all(value, axes, split_axis=0, concat_axis=0, tiled=True)]
    all_gather x2 -> x0, waiting for transfers between devices: 11.2 us -> none  [inverse_chain(): piece = lax.all_gather(rows, 'gx', axis=0, tiled=True)]
    slice x8 -> x5, local copies, waits for them, and re-layouts: 7.49 us -> 0.21 us  [the longest x1 0.06 us: halo(): top = swap(field[:, rows - 1], 'gx')]
  transfers between devices with their start and end apart: 13 -> 13, of which waited for: 6 -> 6; matrix products, arithmetic and copies ran while one was open for 14% -> 6% of each run, Pallas kernels for 0% -> 8%
where the time goes in v1:
time: 199 us; the launch traced here: 197 us
  blocking collectives  66.6 us (33%)
  starting transfers between devices  50.1 us (25%)
  waiting for transfers between devices  29 us (15%)
  Pallas kernels  25.2 us (13%)
  other arithmetic  20.1 us (10%)
  local copies, waits for them, and re-layouts  4.47 us (2%)
    all_to_all x3, blocking collectives, exchange(): return lax.all_to_all(value, axes, split_axis=0, concat_axis=0, tiled=True)  66.6 us
    all_to_all x5, starting transfers between devices, exchange(): return lax.all_to_all(value, axes, split_axis=0, concat_axis=0, tiled=True)  26.6 us
    ppermute x8, starting transfers between devices, swap(): return lax.ppermute(value, axis, pairs)  23.6 us
    all_to_all x5, waiting for transfers between devices, exchange(): return lax.all_to_all(value, axes, split_axis=0, concat_axis=0, tiled=True)  19.5 us
    pallas_call x2, Pallas kernels, conv(): pl.pallas_call(conv_kernel, grid=(rows // tall,), in_specs=[pl.BlockSpec(...  13.2 us
    ppermute x8, waiting for transfers between devices, swap(): return lax.ppermute(value, axis, pairs)  9.47 us
    pallas_call x2, Pallas kernels, to_modes(): pl.pallas_call(functools.partial(forward_kernel, weighted, factor), grid=...  6.07 us
    pallas_call x2, Pallas kernels, to_field(): pl.pallas_call(functools.partial(inverse_kernel, weighted, factor), grid=...  5.96 us
  transfers between devices with their start and end apart: 13, of which 6 were waited for; matrix products, arithmetic and copies ran while one was open for 6% of the time, Pallas kernels for 8%

profile of v1, /device:TPU:1, one launch (start us, length us, event | category | flops | bytes accessed | tf_op | source)
XLA Modules:
  0.0 197.4 jit_solution(9919858259782787009)
XLA Ops:
  0.6 23.0 %all_to_all.40.block_ref = bf16[16,2,64,256]{3,2,1,0:T(8,128)(2,1)} all-to-all(bf16[16,2,64,256]{3,2,1,0:T(8,128)(2,1)} %bitcast.163), channel_id=1, replica_groups=mesh['dp'=4,'gx'=16,'gy'=4] {'gx'}, dimensions={0} | all-to-all | bytes 2097152 | tf_op jit(solution)/shard_map/all_to_all | solution.py:259
  23.7 3.1 %to_modes.2 = bf16[64,8,128]{2,1,0:T(8,128)(2,1)} custom-call(bf16[16,2,64,256]{3,2,1,0:T(8,128)(2,1)} %all_to_all.40.block_ref, bf16[256,1024]{1,0:T(8,128)(2,1)} %constant.20.clone.x_ref, bf16[512,256]{1,0:T(8,128)(2,1)} %constant.21.clone.y_ref), custom_call_target="tpu_custom_call" | custom-call | tf_op jit(solution)/shard_map/to_modes/pallas_call | solution.py:88
  26.8 20.7 %all_to_all.41 = bf16[64,8,128]{2,1,0:T(8,128)(2,1)S(1)} all-to-all(bf16[64,8,128]{2,1,0:T(8,128)(2,1)} %to_modes.2), channel_id=1, replica_groups=mesh['dp'=4,'gx'=16,'gy'=4] {'gx','gy'}, dimensions={0} | all-to-all | bytes 262144 | tf_op jit(solution)/shard_map/all_to_all | solution.py:259
  47.8 2.1 %fusion.8 = (f32[2,128,32]{1,0,2:T(2,128)S(1)}, f32[2,128,32]{1,0,2:T(2,128)S(1)}, f32[2,128,32]{1,0,2:T(2,128)S(1)}, f32[2,128,32]{1,0,2:T(2,128)S(1)}) fusion(f32[2,128,32]{1,0,2:T(2,128)S(1)} %copy.144, bf16[32,32,2,2,128]{4,3,2,1,0:T(2,128)(2,1)S(1)} %copy-done.3, f32[2,128,32]{1,0,2:T(2,128)S(1)} %copy.145), kind=kLoop, calls=%fused_computation.28 | loop fusion | flops 2588672 | bytes 1245184
  50.7 4.5 %all-to-all-start.2 = ((bf16[64,8,128]{2,1,0:T(8,128)(2,1)}), bf16[64,8,128]{2,1,0:T(8,128)(2,1)S(1)}, u32[]{:S(2)}, u32[]{:S(2)}) async-start(bf16[64,8,128]{2,1,0:T(8,128)(2,1)} %bitcast.39), calls=%async_computation.2 | async-start | bytes 262144 | tf_op jit(solution)/shard_map/all_to_all | solution.py:259
  55.8 3.6 %collective-permute-start = (bf16[32,256]{1,0:T(8,128)(2,1)S(1)}, bf16[32,256]{1,0:T(8,128)(2,1)S(1)}, u32[]{:S(2)}, u32[]{:S(2)}) collective-permute-start(bf16[32,256]{1,0:T(8,128)(2,1)S(1)} %get-tuple-element.19), channel_id=1, source_target_pairs={{0,4},{4,8},{8,12},{12,16},{16,20},{20,24},{24,28},{28,32},{32,36}... | collective-permute-start | bytes 49160 | tf_op jit(solution)/shard_map/ppermute | solution.py:219
  59.4 1.9 collective-permute-start.1
  61.5 5.0 %all-to-all-done.2.spec_ref = bf16[64,8,128]{2,1,0:T(8,128)(2,1)S(1)} async-done(((bf16[64,8,128]{2,1,0:T(8,128)(2,1)}), bf16[64,8,128]{2,1,0:T(8,128)(2,1)S(1)}, u32[]{:S(2)}, u32[]{:S(2)}) %all-to-all-start.2) | async-done | bytes 131104 | tf_op jit(solution)/shard_map/all_to_all | solution.py:259
  67.2 3.0 %to_field.2 = bf16[16,2,64,256]{3,2,1,0:T(8,128)(2,1)} custom-call(bf16[64,8,128]{2,1,0:T(8,128)(2,1)} %copy-done.6, bf16[1024,256]{1,0:T(8,128)(2,1)} %constant.24.clone.x_ref, bf16[256,512]{1,0:T(8,128)(2,1)} %constant.25.clone.y_ref), custom_call_target="tpu_custom_call" | custom-call | tf_op jit(solution)/shard_map/to_field/pallas_call | solution.py:138
  70.1 4.7 %all-to-all-start.3 = ((bf16[16,2,64,256]{3,2,1,0:T(8,128)(2,1)}), bf16[16,2,64,256]{3,2,1,0:T(8,128)(2,1)}, u32[]{:S(2)}, u32[]{:S(2)}) async-start(bf16[16,2,64,256]{3,2,1,0:T(8,128)(2,1)} %to_field.2), calls=%async_computation.3 | async-start | bytes 2097152 | tf_op jit(solution)/shard_map/all_to_all | solution.py:259
  77.5 4.9 %collective-permute-start.3 = (bf16[1,2112]{1,0:T(2,128)(2,1)S(1)}, bf16[1,2112]{1,0:T(2,128)(2,1)S(1)}, u32[]{:S(2)}, u32[]{:S(2)}) collective-permute-start(bf16[1,2112]{1,0:T(2,128)(2,1)S(1)} %get-tuple-element.40), channel_id=1, source_target_pairs={{0,1},{1,2},{2,3},{4,5},{5,6},{6,7},{8,9},{9,10},{10,11},{12,13},{... | collective-permute-start | bytes 12680 | tf_op jit(solution)/shard_map/ppermute | solution.py:219
  82.5 4.3 %collective-permute-done.3 = bf16[1,2112]{1,0:T(2,128)(2,1)S(1)} collective-permute-done((bf16[1,2112]{1,0:T(2,128)(2,1)S(1)}, bf16[1,2112]{1,0:T(2,128)(2,1)S(1)}, u32[]{:S(2)}, u32[]{:S(2)}) %collective-permute-start.3) | collective-permute-done | bytes 4256 | tf_op jit(solution)/shard_map/ppermute | solution.py:219
  86.8 1.4 fusion.7.side_ref
  88.2 6.7 %conv.2 = f32[32,64,256]{2,1,0:T(8,128)} custom-call(bf16[384,192]{1,0:T(8,128)(2,1)} %fusion.28.matrix_ref, bf16[2112,256]{1,0:T(8,128)(2,1)} %bitcast.160, bf16[2112,128]{1,0:T(8,128)(2,1)} %fusion.7.side_ref), custom_call_target="tpu_custom_call" | custom-call | tf_op jit(solution)/shard_map/conv/pallas_call | solution.py:200
  94.9 4.3 %fusion.4 = (bf16[32,64,256]{2,1,0:T(8,128)(2,1)S(1)}, f32[1,32,64,256]{3,2,1,0:T(8,128)}) fusion(f32[32,64,256]{2,1,0:T(8,128)} %conv.2, bf16[1,32,64,256]{3,2,1,0:T(8,128)(2,1)S(1)} %copy-done.5, bf16[16,2,64,256]{3,2,1,0:T(8,128)(2,1)} %all-to-all-done.3, f32[32]{0:T(128)S(1)} %copy-done.12), kind=kLoop, calls=%fused_computation.9 | loop fusion | flops 7340032 | bytes 7340160 | tf_op jit(solution)/shard_map/convert_element_type | solution.py:313
  99.1 22.8 %all_to_all.42.block_ref = bf16[16,2,64,256]{3,2,1,0:T(8,128)(2,1)} all-to-all(bf16[16,2,64,256]{3,2,1,0:T(8,128)(2,1)S(1)} %bitcast.155), channel_id=1, replica_groups=mesh['dp'=4,'gx'=16,'gy'=4] {'gx'}, dimensions={0} | all-to-all | bytes 2097152 | tf_op jit(solution)/shard_map/all_to_all | solution.py:259
  122.0 3.0 %to_modes.3 = bf16[64,8,128]{2,1,0:T(8,128)(2,1)} custom-call(bf16[16,2,64,256]{3,2,1,0:T(8,128)(2,1)} %all_to_all.42.block_ref, bf16[256,1024]{1,0:T(8,128)(2,1)} %constant.20.clone.x_ref, bf16[512,256]{1,0:T(8,128)(2,1)} %constant.21.clone.y_ref), custom_call_target="tpu_custom_call" | custom-call | tf_op jit(solution)/shard_map/to_modes/pallas_call | solution.py:88
  125.0 6.0 %all-to-all-start.5 = ((bf16[64,8,128]{2,1,0:T(8,128)(2,1)}), bf16[64,8,128]{2,1,0:T(8,128)(2,1)S(1)}, u32[]{:S(2)}, u32[]{:S(2)}) async-start(bf16[64,8,128]{2,1,0:T(8,128)(2,1)} %to_modes.3), calls=%async_computation.5 | async-start | bytes 262144 | tf_op jit(solution)/shard_map/all_to_all | solution.py:259
  131.0 2.4 %collective-permute-start.5 = (bf16[32,256]{1,0:T(8,128)(2,1)S(1)}, bf16[32,256]{1,0:T(8,128)(2,1)S(1)}, u32[]{:S(2)}, u32[]{:S(2)}) collective-permute-start(bf16[32,256]{1,0:T(8,128)(2,1)S(1)} %bitcast.180), channel_id=1, source_target_pairs={{4,0},{8,4},{12,8},{16,12},{20,16},{24,20},{28,24},{32,28},{36,32}... | collective-permute-start | bytes 49160 | tf_op jit(solution)/shard_map/ppermute | solution.py:219
  133.4 3.4 %collective-permute-start.4 = (bf16[32,256]{1,0:T(8,128)(2,1)S(1)}, bf16[32,256]{1,0:T(8,128)(2,1)S(1)}, u32[]{:S(2)}, u32[]{:S(2)}) collective-permute-start(bf16[32,256]{1,0:T(8,128)(2,1)S(1)} %bitcast.182), channel_id=1, source_target_pairs={{0,4},{4,8},{8,12},{12,16},{16,20},{20,24},{24,28},{28,32},{32,36}... | collective-permute-start | bytes 49160 | tf_op jit(solution)/shard_map/ppermute | solution.py:219
  137.5 4.7 %all-to-all-done.5 = bf16[64,8,128]{2,1,0:T(8,128)(2,1)S(1)} async-done(((bf16[64,8,128]{2,1,0:T(8,128)(2,1)}), bf16[64,8,128]{2,1,0:T(8,128)(2,1)S(1)}, u32[]{:S(2)}, u32[]{:S(2)}) %all-to-all-start.5) | async-done | bytes 131104 | tf_op jit(solution)/shard_map/all_to_all | solution.py:259
  142.5 2.6 %fusion.12 = (f32[2,128,32]{1,0,2:T(2,128)S(1)}, f32[2,128,32]{1,0,2:T(2,128)S(1)}, f32[2,128,32]{1,0,2:T(2,128)S(1)}, f32[2,128,32]{1,0,2:T(2,128)S(1)}) fusion(f32[2,128,32]{1,0,2:T(2,128)S(1)} %copy.146, bf16[32,32,2,2,128]{4,3,2,1,0:T(2,128)(2,1)S(1)} %copy-done.3, f32[2,128,32]{1,0,2:T(2,128)S(1)} %copy.147), kind=kLoop, calls=%fused_computation.32 | loop fusion | flops 2588672 | bytes 1245184
  145.8 7.5 %all-to-all-start.6 = ((bf16[64,8,128]{2,1,0:T(8,128)(2,1)}), bf16[64,8,128]{2,1,0:T(8,128)(2,1)S(1)}, u32[]{:S(2)}, u32[]{:S(2)}) async-start(bf16[64,8,128]{2,1,0:T(8,128)(2,1)} %bitcast.74), calls=%async_computation.6 | async-start | bytes 262144 | tf_op jit(solution)/shard_map/all_to_all | solution.py:259
  154.7 9.8 %all-to-all-done.6.spec_ref = bf16[64,8,128]{2,1,0:T(8,128)(2,1)S(1)} async-done(((bf16[64,8,128]{2,1,0:T(8,128)(2,1)}), bf16[64,8,128]{2,1,0:T(8,128)(2,1)S(1)}, u32[]{:S(2)}, u32[]{:S(2)}) %all-to-all-start.6) | async-done | bytes 131104 | tf_op jit(solution)/shard_map/all_to_all | solution.py:259
  165.2 3.0 %to_field.3 = bf16[16,2,64,256]{3,2,1,0:T(8,128)(2,1)} custom-call(bf16[64,8,128]{2,1,0:T(8,128)(2,1)} %copy-done.7, bf16[1024,256]{1,0:T(8,128)(2,1)} %constant.24.clone.x_ref, bf16[256,512]{1,0:T(8,128)(2,1)} %constant.25.clone.y_ref), custom_call_target="tpu_custom_call" | custom-call | tf_op jit(solution)/shard_map/to_field/pallas_call | solution.py:138
  168.2 3.9 %all-to-all-start.7 = ((bf16[16,2,64,256]{3,2,1,0:T(8,128)(2,1)}), bf16[16,2,64,256]{3,2,1,0:T(8,128)(2,1)S(1)}, u32[]{:S(2)}, u32[]{:S(2)}) async-start(bf16[16,2,64,256]{3,2,1,0:T(8,128)(2,1)} %to_field.3), calls=%async_computation.7 | async-start | bytes 2097152 | tf_op jit(solution)/shard_map/all_to_all | solution.py:259
  174.2 4.9 %collective-permute-start.7 = (bf16[1,2112]{1,0:T(2,128)(2,1)S(1)}, bf16[1,2112]{1,0:T(2,128)(2,1)S(1)}, u32[]{:S(2)}, u32[]{:S(2)}) collective-permute-start(bf16[1,2112]{1,0:T(2,128)(2,1)S(1)} %get-tuple-element.38), channel_id=1, source_target_pairs={{0,1},{1,2},{2,3},{4,5},{5,6},{6,7},{8,9},{9,10},{10,11},{12,13},{... | collective-permute-start | bytes 12680 | tf_op jit(solution)/shard_map/ppermute | solution.py:219
  179.2 4.8 %collective-permute-done.7 = bf16[1,2112]{1,0:T(2,128)(2,1)S(1)} collective-permute-done((bf16[1,2112]{1,0:T(2,128)(2,1)S(1)}, bf16[1,2112]{1,0:T(2,128)(2,1)S(1)}, u32[]{:S(2)}, u32[]{:S(2)}) %collective-permute-start.7) | collective-permute-done | bytes 4256 | tf_op jit(solution)/shard_map/ppermute | solution.py:219
  184.0 1.4 fusion.6.side_ref
  185.5 6.5 %conv.3 = f32[32,64,256]{2,1,0:T(8,128)} custom-call(bf16[384,192]{1,0:T(8,128)(2,1)} %fusion.31.matrix_ref, bf16[2112,256]{1,0:T(8,128)(2,1)} %bitcast.158, bf16[2112,128]{1,0:T(8,128)(2,1)} %fusion.6.side_ref), custom_call_target="tpu_custom_call" | custom-call | tf_op jit(solution)/shard_map/conv/pallas_call | solution.py:200
  193.3 2.4 %pad_maximum_fusion = f32[32,32,2,2,128]{4,3,2,1,0:T(2,128)} fusion(f32[32,32,1,2,128]{4,3,2,1,0:T(2,128)S(1)} %get-tuple-element.24, f32[32,32,1,2,128]{4,3,2,1,0:T(2,128)S(1)} %get-tuple-element.23), kind=kLoop, calls=%fused_computation.4 | loop fusion | flops 524288 | bytes 4194304 | tf_op jit(solution)/shard_map/stack | solution.py:285
  195.7 1.7 fusion.2
  (89 shorter events, 12.4 us)
Async XLA Ops:
  0.6 47.2 %copy-start.3 = (bf16[32,32,2,2,128]{4,3,2,1,0:T(2,128)(2,1)S(1)}, bf16[32,32,2,2,128]{4,3,2,1,0:T(2,128)(2,1)}, u32[]{:S(2)}) copy-start(bf16[32,32,2,2,128]{4,3,2,1,0:T(2,128)(2,1)} %param.16) | copy-start | bytes 3145732
  23.7 31.5 %copy-start.4 = (bf16[1,32,64,256]{3,2,1,0:T(8,128)(2,1)S(1)}, bf16[1,32,64,256]{3,2,1,0:T(8,128)(2,1)}, u32[]{:S(2)}) copy-start(bf16[1,32,64,256]{3,2,1,0:T(8,128)(2,1)} %param.15) | copy-start | bytes 3145732
  47.8 13.5 %copy-start.8 = (bf16[9,32,32]{2,1,0:T(8,128)(2,1)S(1)}, bf16[9,32,32]{2,1,0:T(8,128)(2,1)}, u32[]{:S(2)}) copy-start(bf16[9,32,32]{2,1,0:T(8,128)(2,1)} %param.17) | copy-start | bytes 55300
  50.7 15.8 %all-to-all-start.2 = ((bf16[64,8,128]{2,1,0:T(8,128)(2,1)}), bf16[64,8,128]{2,1,0:T(8,128)(2,1)S(1)}, u32[]{:S(2)}, u32[]{:S(2)}) async-start(bf16[64,8,128]{2,1,0:T(8,128)(2,1)} %bitcast.39), calls=%async_computation.2 | async-start | bytes 262144 | tf_op jit(solution)/shard_map/all_to_all | solution.py:259
  55.8 19.0 %collective-permute-start = (bf16[32,256]{1,0:T(8,128)(2,1)S(1)}, bf16[32,256]{1,0:T(8,128)(2,1)S(1)}, u32[]{:S(2)}, u32[]{:S(2)}) collective-permute-start(bf16[32,256]{1,0:T(8,128)(2,1)S(1)} %get-tuple-element.19), channel_id=1, source_target_pairs={{0,4},{4,8},{8,12},{12,16},{16,20},{20,24},{24,28},{28,32},{32,36}... | collective-permute-start | bytes 49160 | tf_op jit(solution)/shard_map/ppermute | solution.py:219
  59.4 15.4 %collective-permute-start.1 = (bf16[32,256]{1,0:T(8,128)(2,1)S(1)}, bf16[32,256]{1,0:T(8,128)(2,1)S(1)}, u32[]{:S(2)}, u32[]{:S(2)}) collective-permute-start(bf16[32,256]{1,0:T(8,128)(2,1)S(1)} %get-tuple-element.20), channel_id=1, source_target_pairs={{4,0},{8,4},{12,8},{16,12},{20,16},{24,20},{28,24},{32,28},{36,32}... | collective-permute-start | bytes 49160 | tf_op jit(solution)/shard_map/ppermute | solution.py:219
  66.5 0.7 copy-start.6
  70.1 4.9 %copy-start.9 = (bf16[2,256]{1,0:T(2,128)(2,1)S(1)}, bf16[2,256]{1,0:T(2,128)(2,1)}, u32[]{:S(2)}) copy-start(bf16[2,256]{1,0:T(2,128)(2,1)} %constant.22.clone) | copy-start | bytes 3076
  70.1 24.7 %all-to-all-start.3 = ((bf16[16,2,64,256]{3,2,1,0:T(8,128)(2,1)}), bf16[16,2,64,256]{3,2,1,0:T(8,128)(2,1)}, u32[]{:S(2)}, u32[]{:S(2)}) async-start(bf16[16,2,64,256]{3,2,1,0:T(8,128)(2,1)} %to_field.2), calls=%async_computation.3 | async-start | bytes 2097152 | tf_op jit(solution)/shard_map/all_to_all | solution.py:259
  74.8 12.0 %copy-start.10 = (f32[128]{0:T(128)S(1)}, f32[128]{0:T(128)}, u32[]{:S(2)}) copy-start(f32[128]{0:T(128)} %constant.50) | copy-start | bytes 1540
  74.8 12.0 %copy-start.11 = (f32[128]{0:T(128)S(1)}, f32[128]{0:T(128)}, u32[]{:S(2)}) copy-start(f32[128]{0:T(128)} %constant.47) | copy-start | bytes 1540
  75.0 13.2 %copy-start.1 = (bf16[66,32,256]{2,1,0:T(8,128)(2,1)}, bf16[66,32,256]{2,1,0:T(8,128)(2,1)S(1)}, u32[]{:S(2)}) copy-start(bf16[66,32,256]{2,1,0:T(8,128)(2,1)S(1)} %pad_maximum_fusion.2) | copy-start | bytes 3244036
  75.4 7.0 %collective-permute-start.2 = (bf16[1,2112]{1,0:T(2,128)(2,1)S(1)}, bf16[1,2112]{1,0:T(2,128)(2,1)S(1)}, u32[]{:S(2)}, u32[]{:S(2)}) collective-permute-start(bf16[1,2112]{1,0:T(2,128)(2,1)S(1)} %get-tuple-element.39), channel_id=1, source_target_pairs={{1,0},{2,1},{3,2},{5,4},{6,5},{7,6},{9,8},{10,9},{11,10},{13,12},{... | collective-permute-start | bytes 12680 | tf_op jit(solution)/shard_map/ppermute | solution.py:219
  77.5 9.2 %collective-permute-start.3 = (bf16[1,2112]{1,0:T(2,128)(2,1)S(1)}, bf16[1,2112]{1,0:T(2,128)(2,1)S(1)}, u32[]{:S(2)}, u32[]{:S(2)}) collective-permute-start(bf16[1,2112]{1,0:T(2,128)(2,1)S(1)} %get-tuple-element.40), channel_id=1, source_target_pairs={{0,1},{1,2},{2,3},{4,5},{5,6},{6,7},{8,9},{9,10},{10,11},{12,13},{... | collective-permute-start | bytes 12680 | tf_op jit(solution)/shard_map/ppermute | solution.py:219
  88.2 6.7 %copy-start.5 = (bf16[1,32,64,256]{3,2,1,0:T(8,128)(2,1)S(1)}, bf16[1,32,64,256]{3,2,1,0:T(8,128)(2,1)}, u32[]{:S(2)}) copy-start(bf16[1,32,64,256]{3,2,1,0:T(8,128)(2,1)} %param.19) | copy-start | bytes 3145732
  88.2 6.7 %copy-start.12 = (f32[32]{0:T(128)S(1)}, f32[32]{0:T(128)}, u32[]{:S(2)}) copy-start(f32[32]{0:T(128)} %param.18) | copy-start | bytes 388
  125.0 17.2 %all-to-all-start.5 = ((bf16[64,8,128]{2,1,0:T(8,128)(2,1)}), bf16[64,8,128]{2,1,0:T(8,128)(2,1)S(1)}, u32[]{:S(2)}, u32[]{:S(2)}) async-start(bf16[64,8,128]{2,1,0:T(8,128)(2,1)} %to_modes.3), calls=%async_computation.5 | async-start | bytes 262144 | tf_op jit(solution)/shard_map/all_to_all | solution.py:259
  131.0 6.0 %collective-permute-start.5 = (bf16[32,256]{1,0:T(8,128)(2,1)S(1)}, bf16[32,256]{1,0:T(8,128)(2,1)S(1)}, u32[]{:S(2)}, u32[]{:S(2)}) collective-permute-start(bf16[32,256]{1,0:T(8,128)(2,1)S(1)} %bitcast.180), channel_id=1, source_target_pairs={{4,0},{8,4},{12,8},{16,12},{20,16},{24,20},{28,24},{32,28},{36,32}... | collective-permute-start | bytes 49160 | tf_op jit(solution)/shard_map/ppermute | solution.py:219
  133.4 4.1 %collective-permute-start.4 = (bf16[32,256]{1,0:T(8,128)(2,1)S(1)}, bf16[32,256]{1,0:T(8,128)(2,1)S(1)}, u32[]{:S(2)}, u32[]{:S(2)}) collective-permute-start(bf16[32,256]{1,0:T(8,128)(2,1)S(1)} %bitcast.182), channel_id=1, source_target_pairs={{0,4},{4,8},{8,12},{12,16},{16,20},{20,24},{24,28},{28,32},{32,36}... | collective-permute-start | bytes 49160 | tf_op jit(solution)/shard_map/ppermute | solution.py:219
  145.8 18.7 %all-to-all-start.6 = ((bf16[64,8,128]{2,1,0:T(8,128)(2,1)}), bf16[64,8,128]{2,1,0:T(8,128)(2,1)S(1)}, u32[]{:S(2)}, u32[]{:S(2)}) async-start(bf16[64,8,128]{2,1,0:T(8,128)(2,1)} %bitcast.74), calls=%async_computation.6 | async-start | bytes 262144 | tf_op jit(solution)/shard_map/all_to_all | solution.py:259
  154.3 13.9 %copy-start = (bf16[66,32,256]{2,1,0:T(8,128)(2,1)}, bf16[66,32,256]{2,1,0:T(8,128)(2,1)S(1)}, u32[]{:S(2)}) copy-start(bf16[66,32,256]{2,1,0:T(8,128)(2,1)S(1)} %copy.68) | copy-start | bytes 3244036
  164.5 0.7 copy-start.7
  168.2 27.6 %all-to-all-start.7 = ((bf16[16,2,64,256]{3,2,1,0:T(8,128)(2,1)}), bf16[16,2,64,256]{3,2,1,0:T(8,128)(2,1)S(1)}, u32[]{:S(2)}, u32[]{:S(2)}) async-start(bf16[16,2,64,256]{3,2,1,0:T(8,128)(2,1)} %to_field.3), calls=%async_computation.7 | async-start | bytes 2097152 | tf_op jit(solution)/shard_map/all_to_all | solution.py:259
  172.1 7.0 %collective-permute-start.6 = (bf16[1,2112]{1,0:T(2,128)(2,1)S(1)}, bf16[1,2112]{1,0:T(2,128)(2,1)S(1)}, u32[]{:S(2)}, u32[]{:S(2)}) collective-permute-start(bf16[1,2112]{1,0:T(2,128)(2,1)S(1)} %get-tuple-element.37), channel_id=1, source_target_pairs={{1,0},{2,1},{3,2},{5,4},{6,5},{7,6},{9,8},{10,9},{11,10},{13,12},{... | collective-permute-start | bytes 12680 | tf_op jit(solution)/shard_map/ppermute | solution.py:219
  174.2 9.8 %collective-permute-start.7 = (bf16[1,2112]{1,0:T(2,128)(2,1)S(1)}, bf16[1,2112]{1,0:T(2,128)(2,1)S(1)}, u32[]{:S(2)}, u32[]{:S(2)}) collective-permute-start(bf16[1,2112]{1,0:T(2,128)(2,1)S(1)} %get-tuple-element.38), channel_id=1, source_target_pairs={{0,1},{1,2},{2,3},{4,5},{5,6},{6,7},{8,9},{9,10},{10,11},{12,13},{... | collective-permute-start | bytes 12680 | tf_op jit(solution)/shard_map/ppermute | solution.py:219
  193.3 2.4 %copy-start.2 = (f32[32,64,256]{2,1,0:T(8,128)S(1)}, f32[32,64,256]{2,1,0:T(8,128)}, u32[]{:S(2)}) copy-start(f32[32,64,256]{2,1,0:T(8,128)} %conv.3) | copy-start | bytes 6291460

commit v2 on v1

v2 whole, which is shorter than its diff:
```python
import functools
import math

import jax
import jax.numpy as jnp
import numpy as np
from jax import lax
from jax.experimental import pallas as pl
from jax.experimental.pallas import tpu as pltpu
from jax.sharding import PartitionSpec as P

M1 = 128
M2 = 128
BF = jnp.bfloat16
F32 = jnp.float32


def dot(left, right):
    return jnp.dot(left, right, preferred_element_type=F32)


@functools.lru_cache(maxsize=None)
def x_table(length, owners):
    slots = M1 // owners
    order = np.arange(M1).reshape(owners, slots).T.reshape(-1)
    modes = np.where(order < M1 // 2, order, order + length - M1)
    angle = (modes[:, None] * np.arange(length)[None, :] % length) * (2.0 * math.pi / length)
    table = np.concatenate([np.cos(angle), -np.sin(angle)], axis=0)
    return table.astype(np.float32).astype(jnp.bfloat16)


@functools.lru_cache(maxsize=None)
def y_table(length, width):
    angle = (np.arange(width)[:, None] * np.arange(M2)[None, :] % length) * (2.0 * math.pi / length)
    cosine, sine = np.cos(angle), np.sin(angle)
    table = np.concatenate(
        [np.concatenate([cosine, -sine], axis=1), np.concatenate([sine, cosine], axis=1)], axis=0
    )
    return table.astype(np.float32).astype(jnp.bfloat16)


def turn(values, quarter, sign):
    half = values.shape[1] // 2
    lane = lax.broadcasted_iota(jnp.int32, (1, 2 * half), 1)
    second = lane >= half
    q = jnp.where(second, lane - half, lane)
    step = lax.rem(q * quarter, 4)
    one = jnp.where(step == 0, 1.0, jnp.where(step == 2, -1.0, 0.0))
    imag = jnp.where(step == 1, 1.0, jnp.where(step == 3, -1.0, 0.0)) * sign
    swap = jnp.concatenate([values[:, half:], values[:, :half]], axis=1)
    return values * one + swap * jnp.where(second, imag, -imag)


def column_weight(half):
    lane = lax.broadcasted_iota(jnp.int32, (1, 2 * half), 1)
    return jnp.where((lane == 0) | (lane == half), 1.0, 2.0)


def resident(value):
    return pltpu.with_memory_space_constraint(value, pltpu.VMEM)


def on_chip(kernel, outs, scratch, name, *values):
    spec = pl.BlockSpec(memory_space=pltpu.VMEM)
    many = isinstance(outs, list)
    return pl.pallas_call(
        kernel,
        in_specs=[spec] * len(values),
        out_specs=[spec] * len(outs) if many else spec,
        out_shape=[pltpu.VMEM(*out) for out in outs] if many else pltpu.VMEM(*outs),
        scratch_shapes=scratch,
        compiler_params=pltpu.CompilerParams(vmem_limit_bytes=48 << 20),
        name=name,
    )(*[resident(value) for value in values])


def forward_kernel(weighted, factor, block_ref, x_ref, y_ref, out_ref, rows_ref):
    owners, rows, _ = out_ref.shape
    _, channels, _, width = block_ref.shape
    slots = M1 // owners
    for channel in range(channels):
        block = block_ref[:, channel].reshape(-1, width)
        spec_x = dot(x_ref[...], block)
        if factor != 1.0:
            spec_x = spec_x * factor
        spec_x = spec_x.astype(BF)
        spec = dot(spec_x[:M1], y_ref[:width]) + dot(spec_x[M1:], y_ref[width:])
        spec = turn(spec, lax.axis_index("gy"), -1.0)
        if weighted:
            spec = spec * column_weight(M2)
        for slot in range(slots):
            for part in range(2):
                rows_ref[(channel * slots + slot) * 2 + part] = spec[
                    slot * owners : (slot + 1) * owners, part * M2 : (part + 1) * M2
                ]
    out_ref[...] = jnp.transpose(rows_ref[...], (1, 0, 2)).astype(BF)


def to_modes(block, weighted, factor, tables, owners):
    rows = block.shape[1] * (M1 // owners) * 2
    return on_chip(
        functools.partial(forward_kernel, weighted, factor),
        ((owners, rows, M2), BF),
        [pltpu.VMEM((rows, owners, M2), F32)],
        "to_modes",
        block,
        tables[0],
        tables[1],
    )


def inverse_kernel(weighted, factor, spec_ref, x_ref, y_ref, out_ref, rows_ref):
    owners = spec_ref.shape[0]
    strips, channels, rows, width = out_ref.shape
    slots = M1 // owners
    rows_ref[...] = jnp.transpose(spec_ref[...].astype(F32), (1, 0, 2))
    for channel in range(channels):
        spec = jnp.concatenate(
            [
                jnp.concatenate(
                    [rows_ref[(channel * slots + slot) * 2 + part] for part in range(2)], axis=1
                )
                for slot in range(slots)
            ],
            axis=0,
        )
        spec = turn(spec, lax.axis_index("gy"), 1.0)
        if weighted:
            spec = spec * column_weight(M2)
        over_y = dot(spec.astype(BF), y_ref[...]).astype(BF)
        over_y = jnp.concatenate([over_y[:, :width], over_y[:, width:]], axis=0)
        total = dot(x_ref[...], over_y)
        if factor != 1.0:
            total = total * factor
        out_ref[:, channel] = total.astype(BF).reshape(strips, rows, width)


def to_field(spec, weighted, factor, tables, shape):
    owners, rows, _ = spec.shape
    return on_chip(
        functools.partial(inverse_kernel, weighted, factor),
        (shape, BF),
        [pltpu.VMEM((rows, owners, M2), F32)],
        "to_field",
        spec,
        tables[2],
        tables[3],
    )


def mix_kernel(sign, parts_ref, weight_ref, out_ref, spec_ref, sum_ref, mixed_ref, place_ref):
    strips, rows, kept = spec_ref.shape
    pieces = parts_ref.shape[0] // strips
    slots, _, ins, outs, _ = weight_ref.shape
    share = ins // strips
    total = jnp.sum(parts_ref[...].reshape(strips, pieces, rows, kept).astype(F32), axis=1).astype(BF)
    spec_ref[...] = total
    sum_ref[...] = total.astype(F32)
    for slot in range(slots):
        real = jnp.zeros((outs, kept), F32)
        imag = jnp.zeros((outs, kept), F32)
        for channel in range(ins):
            strip, row = channel // share, (channel % share * slots + slot) * 2
            real_s = sum_ref[strip, row : row + 1, :]
            imag_s = sum_ref[strip, row + 1 : row + 2, :]
            real_w = weight_ref[slot, 0, channel].astype(F32)
            imag_w = weight_ref[slot, 1, channel].astype(F32)
            if sign > 0:
                real = real + (real_s * real_w - imag_s * imag_w)
                imag = imag + (real_s * imag_w + imag_s * real_w)
            else:
                real = real + (real_s * real_w + imag_s * imag_w)
                imag = imag + (imag_s * real_w - real_s * imag_w)
        mixed_ref[slot * 2] = real
        mixed_ref[slot * 2 + 1] = imag
    share = outs // strips
    for channel in range(share):
        for row in range(2 * slots):
            place_ref[:, channel * 2 * slots + row, :] = mixed_ref[
                row, pl.ds(channel, strips, stride=share), :
            ]
    placed = place_ref[...].astype(BF)
    out_ref[...] = jnp.broadcast_to(placed[:, None], (strips, pieces, rows, kept)).reshape(
        strips * pieces, rows, kept
    )


def mix(parts, weight, sign, strips):
    owners, rows, kept = parts.shape
    slots, _, _, outs, _ = weight.shape
    return on_chip(
        functools.partial(mix_kernel, sign),
        [((owners, rows, kept), BF), ((strips, rows, kept), BF)],
        [
            pltpu.VMEM((strips, rows, kept), F32),
            pltpu.VMEM((2 * slots, outs, kept), F32),
            pltpu.VMEM((strips, rows, kept), F32),
        ],
        "mix",
        parts,
        weight,
    )


def by_mode(rows, slots):
    strips, count, kept = rows.shape
    split = rows.reshape(strips, count // slots // 2, slots, 2, kept)
    return jnp.transpose(split, (2, 3, 0, 1, 4)).reshape(slots, 2, -1, kept)


CONV_ROWS = 4


def conv_matrix(weight):
    outs, ins = weight.shape[1:]
    band = jnp.transpose(weight.reshape(3, 3, outs, ins), (1, 2, 0, 3)).reshape(3 * outs, 3 * ins)
    return jnp.concatenate(
        [
            jnp.pad(band, ((0, 0), (row * ins, (CONV_ROWS - 1 - row) * ins)))
            for row in range(CONV_ROWS)
        ],
        axis=0,
    )


def conv_kernel(matrix_ref, main_ref, side_ref, out_ref):
    ins = matrix_ref.shape[1] // (CONV_ROWS + 2)
    outs, rows, width = out_ref.shape
    window = (CONV_ROWS + 2) * ins
    tall = 2 * CONV_ROWS

    @pl.loop(0, rows // tall)
    def _(step):
        pieces = []
        for part in range(tall // CONV_ROWS):
            start = pl.multiple_of((step * tall + part * CONV_ROWS) * ins, ins)
            main = dot(matrix_ref[...], main_ref[pl.ds(start, window), :])
            side = dot(matrix_ref[...], side_ref[pl.ds(start, window), :])
            taps = jnp.concatenate([main, side], axis=1)
            full = taps.shape[1]
            for row in range(CONV_ROWS):
                base = row * 3 * outs
                low = pltpu.roll(taps[base : base + outs], 1, 1)[:, :width]
                mid = taps[base + outs : base + 2 * outs, :width]
                high = pltpu.roll(taps[base + 2 * outs : base + 3 * outs], full - 1, 1)[:, :width]
                pieces.append(low + mid + high)
        first = pl.multiple_of(step * tall, tall)
        out_ref[:, pl.ds(first, tall), :] = jnp.transpose(jnp.stack(pieces, axis=0), (1, 0, 2))


def conv(matrix, main, side, rows):
    outs = matrix.shape[0] // (3 * CONV_ROWS)
    return on_chip(
        conv_kernel, ((outs, rows, main.shape[1]), F32), [], "conv", matrix, main, side
    )


def swap(value, axis, back=False):
    count = lax.axis_size(axis)
    pairs = [(i, i + 1) for i in range(count - 1)]
    if back:
        pairs = [(b, a) for a, b in pairs]
    return lax.ppermute(value, axis, pairs)


def rows_halo(field):
    channels, rows, width = field.shape
    top = swap(field[:, rows - 1], "gx")
    bottom = swap(field[:, 0], "gx", back=True)
    main = jnp.concatenate([top[None], jnp.transpose(field, (1, 0, 2)), bottom[None]], axis=0)
    main = main.reshape((rows + 2) * channels, width)
    pick = np.zeros((2, width), np.float32)
    pick[0, 0] = pick[1, width - 1] = 1.0
    ends = jnp.einsum("ry,ny->rn", pick.astype(BF), main, preferred_element_type=F32).astype(BF)
    return main, ends


def columns_halo(ends):
    right = swap(ends[:1], "gy", back=True)
    left = swap(ends[1:], "gy")
    place = np.zeros((2, 128), np.float32)
    place[0, 0] = place[1, 127] = 1.0
    return jnp.einsum(
        "rn,rk->nk", jnp.concatenate([right, left]), place.astype(BF), preferred_element_type=F32
    ).astype(BF)


def exchange(value, axes):
    return lax.all_to_all(value, axes, split_axis=0, concat_axis=0, tiled=True)


def pdot(form, left, right):
    return jnp.einsum(form, left, right, preferred_element_type=F32)


def weight_grads(spec, dmixed):
    real_s, imag_s = (spec[:, 0], spec[:, 1])
    real_d, imag_d = (dmixed[:, 0], dmixed[:, 1])
    form_w = "mcq,mdq->cdmq"
    grad_real = pdot(form_w, real_s, real_d) + pdot(form_w, imag_s, imag_d)
    grad_imag = pdot(form_w, real_s, imag_d) - pdot(form_w, imag_s, real_d)
    return jnp.stack([grad_real, grad_imag], axis=2)


def body(field_in, spectral_weight, conv_weight, conv_bias, upstream):
    strips, pieces = lax.axis_size("gx"), lax.axis_size("gy")
    owners = strips * pieces
    _, channels, width_x, width_y = field_in.shape
    length_x, length_y = width_x * strips, width_y * pieces
    scale = 1.0 / (length_x * length_y)
    both = ("gx", "gy")
    share = (strips, channels // strips, width_x, width_y)
    whole = (channels, width_x, width_y)

    table_x, table_y = x_table(length_x, owners), y_table(length_y, width_y)
    tables = [
        jnp.asarray(np.ascontiguousarray(table))
        for table in (table_x, table_y, table_x.T, table_y.T)
    ]
    hold = lax.optimization_barrier

    field = field_in[0]
    matrix = conv_matrix(conv_weight)
    dmatrix = conv_matrix(jnp.transpose(conv_weight[::-1], (0, 2, 1)))
    weight = jnp.transpose(spectral_weight, (3, 2, 0, 1, 4))
    dweight = jnp.transpose(spectral_weight, (3, 2, 1, 0, 4))
    block = exchange(field.reshape(share), "gx")
    main, ends = rows_halo(field)
    block, ends, matrix, dmatrix, weight, dweight = hold(
        (block, ends, matrix, dmatrix, weight, dweight)
    )
    parts = exchange(to_modes(block, False, 1.0, tables, owners), both)
    side = columns_halo(ends)
    parts, side = hold((parts, side))
    mixed, spec = mix(parts, weight, 1, strips)
    arrived = exchange(mixed, both)
    local = conv(matrix, main, side, width_x)
    arrived, local = hold((arrived, local))
    back = to_field(arrived, True, scale, tables, share)
    spectral = exchange(back, "gx").reshape(whole)

    pre = spectral.astype(F32) + local + conv_bias[:, None, None]
    gate = jax.nn.sigmoid(pre)
    activation = pre * gate
    dpre = (upstream[0].astype(F32) * gate * (1.0 + pre * (1.0 - gate))).astype(BF)

    dblock = exchange(dpre.reshape(share), "gx")
    dmain, dends = rows_halo(dpre)
    dblock, dends = hold((dblock, dends))
    dparts = exchange(to_modes(dblock, True, scale, tables, owners), both)
    dside = columns_halo(dends)
    dparts, dside = hold((dparts, dside))
    dmixed, dspec = mix(dparts, dweight, -1, strips)
    darrived = exchange(dmixed, both)
    back_local = conv(dmatrix, dmain, dside, width_x)
    darrived, back_local = hold((darrived, back_local))
    dback = to_field(darrived, False, 1.0, tables, share)
    dfield = exchange(dback, "gx").reshape(whole)
    slots = M1 // owners
    weight_grad = weight_grads(by_mode(spec, slots), by_mode(dspec, slots))
    dfield, weight_grad = hold((dfield, weight_grad))
    field_grad = dfield.astype(F32) + back_local
    return (activation[None], field_grad[None], weight_grad)


def solution(mesh):
    return jax.shard_map(
        body,
        mesh=mesh,
        in_specs=(
            P("dp", None, "gx", "gy"),
            P(None, None, None, ("gx", "gy"), None),
            P(),
            P(),
            P("dp", None, "gx", "gy"),
        ),
        out_specs=(
            P("dp", None, "gx", "gy"),
            P("dp", None, "gx", "gy"),
            P("dp", None, None, ("gx", "gy"), None),
        ),
        check_vma=False,
    )
```

time: 199 us -> 190 us (0.955)
  blocking collectives: 66.6 us -> 18.4 us
  starting transfers between devices: 50.1 us -> 76.3 us
  waiting for transfers between devices: 29 us -> 45.1 us
  local copies, waits for them, and re-layouts: 4.47 us -> 16 us
  Pallas kernels: 25.2 us -> 15.8 us
  other arithmetic: 20.1 us -> 15.3 us
    all_to_all x3 -> x1, blocking collectives: 66.6 us -> 18.4 us  [exchange(): return lax.all_to_all(value, axes, split_axis=0, concat_axis=0, tiled=True)]
    all_to_all x5 -> x7, starting transfers between devices: 26.6 us -> 54.4 us  [exchange(): return lax.all_to_all(value, axes, split_axis=0, concat_axis=0, tiled=True)]
    all_to_all x5 -> x7, waiting for transfers between devices: 19.5 us -> 32.5 us  [exchange(): return lax.all_to_all(value, axes, split_axis=0, concat_axis=0, tiled=True)]
    unnamed x33 -> x51, local copies, waits for them, and re-layouts: 2.07 us -> 14.1 us
    pallas_call x6 -> x8, Pallas kernels: 25.2 us -> 15.8 us  [on_chip(): pl.pallas_call(kernel, in_specs=[spec] * len(values), out_specs=[spec] *...]
    unnamed x6 -> x4, other arithmetic: 4.75 us -> 0.11 us
    ppermute x8, waiting for transfers between devices: 9.47 us -> 12.6 us  [swap(): return lax.ppermute(value, axis, pairs)]
    concatenate x2, other arithmetic: 0.85 us -> 3.34 us  [rows_halo(): jnp.concatenate([top[None], jnp.transpose(field, (1, 0, 2)), bottom[None]...]
  transfers between devices with their start and end apart: 13 -> 15, of which waited for: 6 -> 10; matrix products, arithmetic and copies ran while one was open for 6% -> 9% of each run, Pallas kernels for 8% -> 5%
where the time goes in v2:
time: 190 us; the launch traced here: 189 us
  starting transfers between devices  76.3 us (40%)
  waiting for transfers between devices  45.1 us (24%)
  blocking collectives  18.4 us (10%)
  local copies, waits for them, and re-layouts  16 us (8%)
  Pallas kernels  15.8 us (8%)
  other arithmetic  15.3 us (8%)
    all_to_all x7, starting transfers between devices, exchange(): return lax.all_to_all(value, axes, split_axis=0, concat_axis=0, tiled=True)  54.4 us
    all_to_all x7, waiting for transfers between devices, exchange(): return lax.all_to_all(value, axes, split_axis=0, concat_axis=0, tiled=True)  32.5 us
    ppermute x8, starting transfers between devices, swap(): return lax.ppermute(value, axis, pairs)  22 us
    all_to_all x1, blocking collectives, exchange(): return lax.all_to_all(value, axes, split_axis=0, concat_axis=0, tiled=True)  18.4 us
    pallas_call x8, Pallas kernels, on_chip(): pl.pallas_call(kernel, in_specs=[spec] * len(values), out_specs=[spec] *...  15.8 us
    unnamed x51, local copies, waits for them, and re-layouts  14.1 us
    ppermute x8, waiting for transfers between devices, swap(): return lax.ppermute(value, axis, pairs)  12.6 us
  transfers between devices with their start and end apart: 15, of which 10 were waited for; matrix products, arithmetic and copies ran while one was open for 9% of the time, Pallas kernels for 5%

profile of v2, /device:TPU:1, one launch (start us, length us, event | category | flops | bytes accessed | tf_op | source)
XLA Modules:
  0.0 188.8 jit_solution(15682841871457583651)
XLA Ops:
  0.6 7.5 %all-to-all-start = ((bf16[16,2,64,256]{3,2,1,0:T(8,128)(2,1)}), bf16[16,2,64,256]{3,2,1,0:T(8,128)(2,1)S(1)}, u32[]{:S(2)}, u32[]{:S(2)}) async-start(bf16[16,2,64,256]{3,2,1,0:T(8,128)(2,1)} %bitcast.118), calls=%async_computation | async-start | bytes 2097152 | tf_op jit(solution)/shard_map/all_to_all | solution.py:289
  8.1 1.9 %copy.83 = bf16[1,32,64,256]{3,1,2,0:T(8,128)(2,1)S(1)} copy(bf16[1,32,64,256]{3,2,1,0:T(8,128)(2,1)} %param.13) | data formatting | bytes 2097152 | tf_op args[0]
  10.1 3.5 %collective-permute-start = (bf16[32,256]{1,0:T(8,128)(2,1)S(1)}, bf16[32,256]{1,0:T(8,128)(2,1)S(1)}, u32[]{:S(2)}, u32[]{:S(2)}) collective-permute-start(bf16[32,256]{1,0:T(8,128)(2,1)S(1)} %get-tuple-element.51), channel_id=1, source_target_pairs={{0,4},{4,8},{8,12},{12,16},{16,20},{20,24},{24,28},{28,32},{32,36}... | collective-permute-start | bytes 49160 | tf_op jit(solution)/shard_map/ppermute | solution.py:263
  13.6 1.9 %collective-permute-start.1 = (bf16[32,256]{1,0:T(8,128)(2,1)S(1)}, bf16[32,256]{1,0:T(8,128)(2,1)S(1)}, u32[]{:S(2)}, u32[]{:S(2)}) collective-permute-start(bf16[32,256]{1,0:T(8,128)(2,1)S(1)} %get-tuple-element.52), channel_id=1, source_target_pairs={{4,0},{8,4},{12,8},{16,12},{20,16},{24,20},{28,24},{32,28},{36,32}... | collective-permute-start | bytes 49160 | tf_op jit(solution)/shard_map/ppermute | solution.py:263
  16.9 1.6 copy.81
  18.7 1.9 %collective-permute-done = bf16[32,256]{1,0:T(8,128)(2,1)S(1)} collective-permute-done((bf16[32,256]{1,0:T(8,128)(2,1)S(1)}, bf16[32,256]{1,0:T(8,128)(2,1)S(1)}, u32[]{:S(2)}, u32[]{:S(2)}) %collective-permute-start) | collective-permute-done | bytes 16416 | tf_op jit(solution)/shard_map/ppermute | solution.py:263
  20.6 1.7 collective-permute-done.1
  28.2 12.0 %all-to-all-start.1 = ((bf16[64,8,128]{2,1,0:T(8,128)(2,1)}), bf16[64,8,128]{2,1,0:T(8,128)(2,1)S(1)}, u32[]{:S(2)}, u32[]{:S(2)}) async-start(bf16[64,8,128]{2,1,0:T(8,128)(2,1)} %copy-done.13), calls=%async_computation.1 | async-start | bytes 262144 | tf_op jit(solution)/shard_map/all_to_all | solution.py:289
  40.2 4.2 %collective-permute-start.3 = (bf16[1,2112]{1,0:T(2,128)(2,1)S(1)}, bf16[1,2112]{1,0:T(2,128)(2,1)S(1)}, u32[]{:S(2)}, u32[]{:S(2)}) collective-permute-start(bf16[1,2112]{1,0:T(2,128)(2,1)S(1)} %get-tuple-element.64), channel_id=1, source_target_pairs={{0,1},{1,2},{2,3},{4,5},{5,6},{6,7},{8,9},{9,10},{10,11},{12,13},{... | collective-permute-start | bytes 12680 | tf_op jit(solution)/shard_map/ppermute | solution.py:263
  46.6 4.8 %all-to-all-done.1.parts_ref = bf16[64,8,128]{2,1,0:T(8,128)(2,1)S(1)} async-done(((bf16[64,8,128]{2,1,0:T(8,128)(2,1)}), bf16[64,8,128]{2,1,0:T(8,128)(2,1)S(1)}, u32[]{:S(2)}, u32[]{:S(2)}) %all-to-all-start.1) | async-done | bytes 131104 | tf_op jit(solution)/shard_map/all_to_all | solution.py:289
  52.4 8.5 %all-to-all-start.2 = ((bf16[64,8,128]{2,1,0:T(8,128)(2,1)}), bf16[64,8,128]{2,1,0:T(8,128)(2,1)}, u32[]{:S(2)}, u32[]{:S(2)}) async-start(bf16[64,8,128]{2,1,0:T(8,128)(2,1)} %get-tuple-element.29), calls=%async_computation.2 | async-start | bytes 262144 | tf_op jit(solution)/shard_map/all_to_all | solution.py:289
  63.0 3.7 %conv.2 = f32[32,64,256]{2,1,0:T(8,128)S(1)} custom-call(bf16[384,192]{1,0:T(8,128)(2,1)S(1)} %copy-done.11, bf16[2112,256]{1,0:T(8,128)(2,1)S(1)} %bitcast.110, bf16[2112,128]{1,0:T(8,128)(2,1)S(1)} %copy-done.2), custom_call_target="tpu_custom_call" | custom-call | tf_op jit(solution)/shard_map/conv/pallas_call | solution.py:66
  66.7 5.4 %all-to-all-done.2.spec_ref = bf16[64,8,128]{2,1,0:T(8,128)(2,1)} async-done(((bf16[64,8,128]{2,1,0:T(8,128)(2,1)}), bf16[64,8,128]{2,1,0:T(8,128)(2,1)}, u32[]{:S(2)}, u32[]{:S(2)}) %all-to-all-start.2) | async-done | bytes 131104 | tf_op jit(solution)/shard_map/all_to_all | solution.py:289
  73.1 1.7 to_field.2
  74.8 18.4 %all_to_all.40 = bf16[16,2,64,256]{3,2,1,0:T(8,128)(2,1)S(1)} all-to-all(bf16[16,2,64,256]{3,2,1,0:T(8,128)(2,1)S(1)} %to_field.2), channel_id=1, replica_groups=mesh['dp'=4,'gx'=16,'gy'=4] {'gx'}, dimensions={0} | all-to-all | bytes 2097152 | tf_op jit(solution)/shard_map/all_to_all | solution.py:289
  93.2 2.8 %fusion.3 = (bf16[32,64,256]{2,1,0:T(8,128)(2,1)}, f32[1,32,64,256]{3,2,1,0:T(8,128)}) fusion(f32[32,64,256]{2,1,0:T(8,128)S(1)} %conv.2, bf16[1,32,64,256]{3,2,1,0:T(8,128)(2,1)S(1)} %copy-done.17, bf16[16,2,64,256]{3,2,1,0:T(8,128)(2,1)S(1)} %all_to_all.40, f32[32]{0:T(128)S(1)} %copy-done.22), kind=kLoop, calls=%fused_computation.7 | loop fusion | flops 7340032 | bytes 7340160 | tf_op jit(solution)/shard_map/convert_element_type | solution.py:345
  96.0 4.6 %all-to-all-start.4 = ((bf16[16,2,64,256]{3,2,1,0:T(8,128)(2,1)}), bf16[16,2,64,256]{3,2,1,0:T(8,128)(2,1)S(1)}, u32[]{:S(2)}, u32[]{:S(2)}) async-start(bf16[16,2,64,256]{3,2,1,0:T(8,128)(2,1)} %bitcast.19), calls=%async_computation.4 | async-start | bytes 2097152 | tf_op jit(solution)/shard_map/all_to_all | solution.py:289
  101.7 2.1 %collective-permute-start.5 = (bf16[32,256]{1,0:T(8,128)(2,1)S(1)}, bf16[32,256]{1,0:T(8,128)(2,1)S(1)}, u32[]{:S(2)}, u32[]{:S(2)}) collective-permute-start(bf16[32,256]{1,0:T(8,128)(2,1)S(1)} %bitcast.125), channel_id=1, source_target_pairs={{4,0},{8,4},{12,8},{16,12},{20,16},{24,20},{28,24},{32,28},{36,32}... | collective-permute-start | bytes 49160 | tf_op jit(solution)/shard_map/ppermute | solution.py:263
  103.8 3.4 %collective-permute-start.4 = (bf16[32,256]{1,0:T(8,128)(2,1)S(1)}, bf16[32,256]{1,0:T(8,128)(2,1)S(1)}, u32[]{:S(2)}, u32[]{:S(2)}) collective-permute-start(bf16[32,256]{1,0:T(8,128)(2,1)S(1)} %bitcast.127), channel_id=1, source_target_pairs={{0,4},{4,8},{8,12},{12,16},{16,20},{20,24},{24,28},{28,32},{32,36}... | collective-permute-start | bytes 49160 | tf_op jit(solution)/shard_map/ppermute | solution.py:263
  107.3 7.5 %collective-permute-done.5 = bf16[32,256]{1,0:T(8,128)(2,1)S(1)} collective-permute-done((bf16[32,256]{1,0:T(8,128)(2,1)S(1)}, bf16[32,256]{1,0:T(8,128)(2,1)S(1)}, u32[]{:S(2)}, u32[]{:S(2)}) %collective-permute-start.5) | collective-permute-done | bytes 16416 | tf_op jit(solution)/shard_map/ppermute | solution.py:263
  114.9 2.0 %pad_maximum_fusion.1 = bf16[66,32,256]{2,0,1:T(8,128)(2,1)S(1)} fusion(bf16[1,32,256]{2,0,1:T(2,128)(2,1)S(1)} %copy.49, bf16[64,32,256]{2,0,1:T(8,128)(2,1)} %bitcast.21, bf16[1,32,256]{2,0,1:T(2,128)(2,1)S(1)} %copy.48), kind=kLoop, calls=%fused_computation.13 | loop fusion | flops 3244032 | bytes 2162688 | tf_op jit(solution)/shard_map/concatenate | solution.py:270
  122.5 9.5 %all-to-all-start.5 = ((bf16[64,8,128]{2,1,0:T(8,128)(2,1)}), bf16[64,8,128]{2,1,0:T(8,128)(2,1)S(1)}, u32[]{:S(2)}, u32[]{:S(2)}) async-start(bf16[64,8,128]{2,1,0:T(8,128)(2,1)} %copy-done.12), calls=%async_computation.5 | async-start | bytes 262144 | tf_op jit(solution)/shard_map/all_to_all | solution.py:289
  132.0 4.2 %collective-permute-start.7 = (bf16[1,2112]{1,0:T(2,128)(2,1)S(1)}, bf16[1,2112]{1,0:T(2,128)(2,1)S(1)}, u32[]{:S(2)}, u32[]{:S(2)}) collective-permute-start(bf16[1,2112]{1,0:T(2,128)(2,1)S(1)} %get-tuple-element.62), channel_id=1, source_target_pairs={{0,1},{1,2},{2,3},{4,5},{5,6},{6,7},{8,9},{9,10},{10,11},{12,13},{... | collective-permute-start | bytes 12680 | tf_op jit(solution)/shard_map/ppermute | solution.py:263
  138.5 4.8 %all-to-all-done.5.parts_ref = bf16[64,8,128]{2,1,0:T(8,128)(2,1)S(1)} async-done(((bf16[64,8,128]{2,1,0:T(8,128)(2,1)}), bf16[64,8,128]{2,1,0:T(8,128)(2,1)S(1)}, u32[]{:S(2)}, u32[]{:S(2)}) %all-to-all-start.5) | async-done | bytes 131104 | tf_op jit(solution)/shard_map/all_to_all | solution.py:289
  144.3 8.4 %all-to-all-start.6 = ((bf16[64,8,128]{2,1,0:T(8,128)(2,1)}), bf16[64,8,128]{2,1,0:T(8,128)(2,1)}, u32[]{:S(2)}, u32[]{:S(2)}) async-start(bf16[64,8,128]{2,1,0:T(8,128)(2,1)} %get-tuple-element.38), calls=%async_computation.6 | async-start | bytes 262144 | tf_op jit(solution)/shard_map/all_to_all | solution.py:289
  154.7 3.7 %conv.3 = f32[32,64,256]{2,1,0:T(8,128)S(1)} custom-call(bf16[384,192]{1,0:T(8,128)(2,1)S(1)} %copy-done.10, bf16[2112,256]{1,0:T(8,128)(2,1)S(1)} %bitcast.108, bf16[2112,128]{1,0:T(8,128)(2,1)S(1)} %copy-done.1), custom_call_target="tpu_custom_call" | custom-call | tf_op jit(solution)/shard_map/conv/pallas_call | solution.py:66
  158.4 5.4 %all-to-all-done.6.spec_ref = bf16[64,8,128]{2,1,0:T(8,128)(2,1)} async-done(((bf16[64,8,128]{2,1,0:T(8,128)(2,1)}), bf16[64,8,128]{2,1,0:T(8,128)(2,1)}, u32[]{:S(2)}, u32[]{:S(2)}) %all-to-all-start.6) | async-done | bytes 131104 | tf_op jit(solution)/shard_map/all_to_all | solution.py:289
  164.9 2.5 %to_field.3 = bf16[16,2,64,256]{3,2,1,0:T(8,128)(2,1)} custom-call(bf16[64,8,128]{2,1,0:T(8,128)(2,1)} %all-to-all-done.6.spec_ref, bf16[1024,256]{1,0:T(8,128)(2,1)S(1)} %copy-done.4, bf16[256,512]{1,0:T(8,128)(2,1)S(1)} %copy-done.7), custom_call_target="tpu_custom_call" | custom-call | tf_op jit(solution)/shard_map/to_field/pallas_call | solution.py:66
  167.4 3.9 %all-to-all-start.7 = ((bf16[16,2,64,256]{3,2,1,0:T(8,128)(2,1)}), bf16[16,2,64,256]{3,2,1,0:T(8,128)(2,1)S(1)}, u32[]{:S(2)}, u32[]{:S(2)}) async-start(bf16[16,2,64,256]{3,2,1,0:T(8,128)(2,1)} %to_field.3), calls=%async_computation.7 | async-start | bytes 2097152 | tf_op jit(solution)/shard_map/all_to_all | solution.py:289
  172.7 2.4 %pad_maximum_fusion = f32[32,32,2,2,128]{4,3,2,1,0:T(2,128)} fusion(f32[32,32,1,2,128]{4,3,2,1,0:T(2,128)S(1)} %get-tuple-element.56, f32[32,32,1,2,128]{4,3,2,1,0:T(2,128)S(1)} %get-tuple-element.55), kind=kLoop, calls=%fused_computation.4 | loop fusion | flops 524288 | bytes 4194304 | tf_op jit(solution)/shard_map/stack | solution.py:302
  175.1 12.1 %all-to-all-done.7 = bf16[16,2,64,256]{3,2,1,0:T(8,128)(2,1)S(1)} async-done(((bf16[16,2,64,256]{3,2,1,0:T(8,128)(2,1)}), bf16[16,2,64,256]{3,2,1,0:T(8,128)(2,1)S(1)}, u32[]{:S(2)}, u32[]{:S(2)}) %all-to-all-start.7) | async-done | bytes 1048608 | tf_op jit(solution)/shard_map/all_to_all | solution.py:289
  187.2 1.6 add_bitcast_fusion
  (91 shorter events, 28.0 us)
Async XLA Ops:
  0.6 14.9 %copy-start.18 = (bf16[9,32,32]{2,1,0:T(8,128)(2,1)S(1)}, bf16[9,32,32]{2,1,0:T(8,128)(2,1)}, u32[]{:S(2)}) copy-start(bf16[9,32,32]{2,1,0:T(8,128)(2,1)} %param.15) | copy-start | bytes 55300
  0.6 23.5 %all-to-all-start = ((bf16[16,2,64,256]{3,2,1,0:T(8,128)(2,1)}), bf16[16,2,64,256]{3,2,1,0:T(8,128)(2,1)S(1)}, u32[]{:S(2)}, u32[]{:S(2)}) async-start(bf16[16,2,64,256]{3,2,1,0:T(8,128)(2,1)} %bitcast.118), calls=%async_computation | async-start | bytes 2097152 | tf_op jit(solution)/shard_map/all_to_all | solution.py:289
  8.1 8.8 %copy-start.15 = (bf16[32,32,2,2,128]{4,3,2,1,0:T(2,128)(2,1)S(1)}, bf16[32,32,2,2,128]{4,3,2,1,0:T(2,128)(2,1)}, u32[]{:S(2)}) copy-start(bf16[32,32,2,2,128]{4,3,2,1,0:T(2,128)(2,1)} %param.14) | copy-start | bytes 3145732
  10.0 12.3 %copy-start.14 = (bf16[1,32,64,256]{3,1,2,0:T(8,128)(2,1)}, bf16[1,32,64,256]{3,1,2,0:T(8,128)(2,1)S(1)}, u32[]{:S(2)}) copy-start(bf16[1,32,64,256]{3,1,2,0:T(8,128)(2,1)S(1)} %copy.83) | copy-start | bytes 3145732
  10.1 10.6 %collective-permute-start = (bf16[32,256]{1,0:T(8,128)(2,1)S(1)}, bf16[32,256]{1,0:T(8,128)(2,1)S(1)}, u32[]{:S(2)}, u32[]{:S(2)}) collective-permute-start(bf16[32,256]{1,0:T(8,128)(2,1)S(1)} %get-tuple-element.51), channel_id=1, source_target_pairs={{0,4},{4,8},{8,12},{12,16},{16,20},{20,24},{24,28},{28,32},{32,36}... | collective-permute-start | bytes 49160 | tf_op jit(solution)/shard_map/ppermute | solution.py:263
  13.6 8.7 %collective-permute-start.1 = (bf16[32,256]{1,0:T(8,128)(2,1)S(1)}, bf16[32,256]{1,0:T(8,128)(2,1)S(1)}, u32[]{:S(2)}, u32[]{:S(2)}) collective-permute-start(bf16[32,256]{1,0:T(8,128)(2,1)S(1)} %get-tuple-element.52), channel_id=1, source_target_pairs={{4,0},{8,4},{12,8},{16,12},{20,16},{24,20},{28,24},{32,28},{36,32}... | collective-permute-start | bytes 49160 | tf_op jit(solution)/shard_map/ppermute | solution.py:263
  16.0 2.6 %copy-start.16 = (bf16[32,32,2,2,128]{4,3,2,1,0:T(2,128)(2,1)S(1)}, bf16[32,32,2,2,128]{4,3,2,1,0:T(2,128)(2,1)}, u32[]{:S(2)}) copy-start(bf16[32,32,2,2,128]{4,3,2,1,0:T(2,128)(2,1)} %param.14) | copy-start | bytes 3145732
  18.5 5.2 %copy-start.19 = (bf16[2,256]{1,0:T(2,128)(2,1)S(1)}, bf16[2,256]{1,0:T(2,128)(2,1)}, u32[]{:S(2)}) copy-start(bf16[2,256]{1,0:T(2,128)(2,1)} %constant.21.clone) | copy-start | bytes 3076
  18.7 6.7 %copy-start.8 = (bf16[512,256]{1,0:T(8,128)(2,1)S(1)}, bf16[512,256]{1,0:T(8,128)(2,1)}, u32[]{:S(2)}) copy-start(bf16[512,256]{1,0:T(8,128)(2,1)} %constant.18.clone.y_ref) | copy-start | bytes 786436
  23.7 21.5 %copy-start.20 = (f32[128]{0:T(128)S(1)}, f32[128]{0:T(128)}, u32[]{:S(2)}) copy-start(f32[128]{0:T(128)} %constant.47) | copy-start | bytes 1540
  23.7 21.5 %copy-start.21 = (f32[128]{0:T(128)S(1)}, f32[128]{0:T(128)}, u32[]{:S(2)}) copy-start(f32[128]{0:T(128)} %constant.44) | copy-start | bytes 1540
  24.1 20.2 %collective-permute-start.2 = (bf16[1,2112]{1,0:T(2,128)(2,1)S(1)}, bf16[1,2112]{1,0:T(2,128)(2,1)S(1)}, u32[]{:S(2)}, u32[]{:S(2)}) collective-permute-start(bf16[1,2112]{1,0:T(2,128)(2,1)S(1)} %get-tuple-element.63), channel_id=1, source_target_pairs={{1,0},{2,1},{3,2},{5,4},{6,5},{7,6},{9,8},{10,9},{11,10},{13,12},{... | collective-permute-start | bytes 12680 | tf_op jit(solution)/shard_map/ppermute | solution.py:263
  25.4 1.0 copy-start.5
  28.2 23.2 %all-to-all-start.1 = ((bf16[64,8,128]{2,1,0:T(8,128)(2,1)}), bf16[64,8,128]{2,1,0:T(8,128)(2,1)S(1)}, u32[]{:S(2)}, u32[]{:S(2)}) async-start(bf16[64,8,128]{2,1,0:T(8,128)(2,1)} %copy-done.13), calls=%async_computation.1 | async-start | bytes 262144 | tf_op jit(solution)/shard_map/all_to_all | solution.py:289
  40.2 5.0 %collective-permute-start.3 = (bf16[1,2112]{1,0:T(2,128)(2,1)S(1)}, bf16[1,2112]{1,0:T(2,128)(2,1)S(1)}, u32[]{:S(2)}, u32[]{:S(2)}) collective-permute-start(bf16[1,2112]{1,0:T(2,128)(2,1)S(1)} %get-tuple-element.64), channel_id=1, source_target_pairs={{0,1},{1,2},{2,3},{4,5},{5,6},{6,7},{8,9},{9,10},{10,11},{12,13},{... | collective-permute-start | bytes 12680 | tf_op jit(solution)/shard_map/ppermute | solution.py:263
  52.4 19.7 %copy-start.7 = (bf16[256,512]{1,0:T(8,128)(2,1)S(1)}, bf16[256,512]{1,0:T(8,128)(2,1)}, u32[]{:S(2)}) copy-start(bf16[256,512]{1,0:T(8,128)(2,1)} %constant.20.clone.y_ref) | copy-start | bytes 786436
  52.4 19.7 %all-to-all-start.2 = ((bf16[64,8,128]{2,1,0:T(8,128)(2,1)}), bf16[64,8,128]{2,1,0:T(8,128)(2,1)}, u32[]{:S(2)}, u32[]{:S(2)}) async-start(bf16[64,8,128]{2,1,0:T(8,128)(2,1)} %get-tuple-element.29), calls=%async_computation.2 | async-start | bytes 262144 | tf_op jit(solution)/shard_map/all_to_all | solution.py:289
  61.0 1.1 copy-start.2
  72.1 1.0 copy-start.3
  73.1 20.1 %copy-start.17 = (bf16[1,32,64,256]{3,2,1,0:T(8,128)(2,1)S(1)}, bf16[1,32,64,256]{3,2,1,0:T(8,128)(2,1)}, u32[]{:S(2)}) copy-start(bf16[1,32,64,256]{3,2,1,0:T(8,128)(2,1)} %param.17) | copy-start | bytes 3145732
  73.1 20.1 %copy-start.22 = (f32[32]{0:T(128)S(1)}, f32[32]{0:T(128)}, u32[]{:S(2)}) copy-start(f32[32]{0:T(128)} %param.16) | copy-start | bytes 388
  96.0 21.5 %all-to-all-start.4 = ((bf16[16,2,64,256]{3,2,1,0:T(8,128)(2,1)}), bf16[16,2,64,256]{3,2,1,0:T(8,128)(2,1)S(1)}, u32[]{:S(2)}, u32[]{:S(2)}) async-start(bf16[16,2,64,256]{3,2,1,0:T(8,128)(2,1)} %bitcast.19), calls=%async_computation.4 | async-start | bytes 2097152 | tf_op jit(solution)/shard_map/all_to_all | solution.py:289
  101.7 13.1 %collective-permute-start.5 = (bf16[32,256]{1,0:T(8,128)(2,1)S(1)}, bf16[32,256]{1,0:T(8,128)(2,1)S(1)}, u32[]{:S(2)}, u32[]{:S(2)}) collective-permute-start(bf16[32,256]{1,0:T(8,128)(2,1)S(1)} %bitcast.125), channel_id=1, source_target_pairs={{4,0},{8,4},{12,8},{16,12},{20,16},{24,20},{28,24},{32,28},{36,32}... | collective-permute-start | bytes 49160 | tf_op jit(solution)/shard_map/ppermute | solution.py:263
  103.8 11.0 %collective-permute-start.4 = (bf16[32,256]{1,0:T(8,128)(2,1)S(1)}, bf16[32,256]{1,0:T(8,128)(2,1)S(1)}, u32[]{:S(2)}, u32[]{:S(2)}) collective-permute-start(bf16[32,256]{1,0:T(8,128)(2,1)S(1)} %bitcast.127), channel_id=1, source_target_pairs={{0,4},{4,8},{8,12},{12,16},{16,20},{20,24},{24,28},{28,32},{32,36}... | collective-permute-start | bytes 49160 | tf_op jit(solution)/shard_map/ppermute | solution.py:263
  117.1 26.1 %copy-start = (bf16[32,32,2,2,128]{4,0,1,2,3:T(8,128)(2,1)S(1)}, bf16[32,32,2,2,128]{4,0,1,2,3:T(8,128)(2,1)}, u32[]{:S(2)}) copy-start(bf16[32,32,2,2,128]{4,0,1,2,3:T(8,128)(2,1)} %copy.81) | copy-start | bytes 3145732
  117.6 18.7 %collective-permute-start.6 = (bf16[1,2112]{1,0:T(2,128)(2,1)S(1)}, bf16[1,2112]{1,0:T(2,128)(2,1)S(1)}, u32[]{:S(2)}, u32[]{:S(2)}) collective-permute-start(bf16[1,2112]{1,0:T(2,128)(2,1)S(1)} %get-tuple-element.61), channel_id=1, source_target_pairs={{1,0},{2,1},{3,2},{5,4},{6,5},{7,6},{9,8},{10,9},{11,10},{13,12},{... | collective-permute-start | bytes 12680 | tf_op jit(solution)/shard_map/ppermute | solution.py:263
  118.9 1.0 copy-start.6
  122.5 20.7 %all-to-all-start.5 = ((bf16[64,8,128]{2,1,0:T(8,128)(2,1)}), bf16[64,8,128]{2,1,0:T(8,128)(2,1)S(1)}, u32[]{:S(2)}, u32[]{:S(2)}) async-start(bf16[64,8,128]{2,1,0:T(8,128)(2,1)} %copy-done.12), calls=%async_computation.5 | async-start | bytes 262144 | tf_op jit(solution)/shard_map/all_to_all | solution.py:289
  132.0 5.0 %collective-permute-start.7 = (bf16[1,2112]{1,0:T(2,128)(2,1)S(1)}, bf16[1,2112]{1,0:T(2,128)(2,1)S(1)}, u32[]{:S(2)}, u32[]{:S(2)}) collective-permute-start(bf16[1,2112]{1,0:T(2,128)(2,1)S(1)} %get-tuple-element.62), channel_id=1, source_target_pairs={{0,1},{1,2},{2,3},{4,5},{5,6},{6,7},{8,9},{9,10},{10,11},{12,13},{... | collective-permute-start | bytes 12680 | tf_op jit(solution)/shard_map/ppermute | solution.py:263
  144.3 19.5 %all-to-all-start.6 = ((bf16[64,8,128]{2,1,0:T(8,128)(2,1)}), bf16[64,8,128]{2,1,0:T(8,128)(2,1)}, u32[]{:S(2)}, u32[]{:S(2)}) async-start(bf16[64,8,128]{2,1,0:T(8,128)(2,1)} %get-tuple-element.38), calls=%async_computation.6 | async-start | bytes 262144 | tf_op jit(solution)/shard_map/all_to_all | solution.py:289
  152.7 1.1 copy-start.1
  167.4 19.8 %all-to-all-start.7 = ((bf16[16,2,64,256]{3,2,1,0:T(8,128)(2,1)}), bf16[16,2,64,256]{3,2,1,0:T(8,128)(2,1)S(1)}, u32[]{:S(2)}, u32[]{:S(2)}) async-start(bf16[16,2,64,256]{3,2,1,0:T(8,128)(2,1)} %to_field.3), calls=%async_computation.7 | async-start | bytes 2097152 | tf_op jit(solution)/shard_map/all_to_all | solution.py:289
  (6 other events, 5.2 us)

commit v3 on v2

--- a/solution.py
+++ b/solution.py
@@ -60,14 +60,14 @@
     return pltpu.with_memory_space_constraint(value, pltpu.VMEM)
 
 
-def on_chip(kernel, outs, scratch, name, *values):
+def on_chip(kernel, outs, scratch, name, *values, place=pltpu.VMEM):
     spec = pl.BlockSpec(memory_space=pltpu.VMEM)
     many = isinstance(outs, list)
     return pl.pallas_call(
         kernel,
         in_specs=[spec] * len(values),
         out_specs=[spec] * len(outs) if many else spec,
-        out_shape=[pltpu.VMEM(*out) for out in outs] if many else pltpu.VMEM(*outs),
+        out_shape=[place(*out) for out in outs] if many else place(*outs),
         scratch_shapes=scratch,
         compiler_params=pltpu.CompilerParams(vmem_limit_bytes=48 << 20),
         name=name,
@@ -106,6 +106,7 @@
         block,
         tables[0],
         tables[1],
+        place=jax.ShapeDtypeStruct,
     )
 
 
@@ -263,11 +264,13 @@
     return lax.ppermute(value, axis, pairs)
 
 
-def rows_halo(field):
+def across_rows(field):
+    return swap(field[:, -1], "gx"), swap(field[:, 0], "gx", back=True)
+
+
+def stack_rows(field, above, below):
     channels, rows, width = field.shape
-    top = swap(field[:, rows - 1], "gx")
-    bottom = swap(field[:, 0], "gx", back=True)
-    main = jnp.concatenate([top[None], jnp.transpose(field, (1, 0, 2)), bottom[None]], axis=0)
+    main = jnp.concatenate([above[None], jnp.transpose(field, (1, 0, 2)), below[None]], axis=0)
     main = main.reshape((rows + 2) * channels, width)
     pick = np.zeros((2, width), np.float32)
     pick[0, 0] = pick[1, width - 1] = 1.0
@@ -275,9 +278,11 @@
     return main, ends
 
 
-def columns_halo(ends):
-    right = swap(ends[:1], "gy", back=True)
-    left = swap(ends[1:], "gy")
+def across_columns(ends):
+    return swap(ends[:1], "gy", back=True), swap(ends[1:], "gy")
+
+
+def place_columns(right, left):
     place = np.zeros((2, 128), np.float32)
     place[0, 0] = place[1, 127] = 1.0
     return jnp.einsum(
@@ -313,31 +318,31 @@
     whole = (channels, width_x, width_y)
 
     table_x, table_y = x_table(length_x, owners), y_table(length_y, width_y)
+    live = lax.axis_index("gx") < strips
     tables = [
-        jnp.asarray(np.ascontiguousarray(table))
+        jnp.where(live, np.ascontiguousarray(table), jnp.zeros((), BF))
         for table in (table_x, table_y, table_x.T, table_y.T)
     ]
     hold = lax.optimization_barrier
 
     field = field_in[0]
-    matrix = conv_matrix(conv_weight)
-    dmatrix = conv_matrix(jnp.transpose(conv_weight[::-1], (0, 2, 1)))
+    block = exchange(field.reshape(share), "gx")
+    above, below = across_rows(field)
+    main, ends = stack_rows(field, above, below)
     weight = jnp.transpose(spectral_weight, (3, 2, 0, 1, 4))
-    dweight = jnp.transpose(spectral_weight, (3, 2, 1, 0, 4))
-    block = exchange(field.reshape(share), "gx")
-    main, ends = rows_halo(field)
-    block, ends, matrix, dmatrix, weight, dweight = hold(
-        (block, ends, matrix, dmatrix, weight, dweight)
-    )
+    block, main, ends, weight, tables = hold((block, main, ends, weight, tables))
     parts = exchange(to_modes(block, False, 1.0, tables, owners), both)
-    side = columns_halo(ends)
-    parts, side = hold((parts, side))
+    parts, ends = hold((parts, ends))
     mixed, spec = mix(parts, weight, 1, strips)
     arrived = exchange(mixed, both)
-    local = conv(matrix, main, side, width_x)
-    arrived, local = hold((arrived, local))
+    right, left = across_columns(ends)
     back = to_field(arrived, True, scale, tables, share)
+    back, right, left, raw, dweight = hold((back, right, left, conv_weight, spectral_weight))
     spectral = exchange(back, "gx").reshape(whole)
+    local = conv(conv_matrix(raw), main, place_columns(right, left), width_x)
+    dmatrix = conv_matrix(jnp.transpose(raw[::-1], (0, 2, 1)))
+    dweight = jnp.transpose(dweight, (3, 2, 1, 0, 4))
+    spectral, local, dmatrix, dweight = hold((spectral, local, dmatrix, dweight))
 
     pre = spectral.astype(F32) + local + conv_bias[:, None, None]
     gate = jax.nn.sigmoid(pre)
@@ -345,20 +350,22 @@
     dpre = (upstream[0].astype(F32) * gate * (1.0 + pre * (1.0 - gate))).astype(BF)
 
     dblock = exchange(dpre.reshape(share), "gx")
-    dmain, dends = rows_halo(dpre)
-    dblock, dends = hold((dblock, dends))
-    dparts = exchange(to_modes(dblock, True, scale, tables, owners), both)
-    dside = columns_halo(dends)
-    dparts, dside = hold((dparts, dside))
+    dabove, dbelow = across_rows(dpre)
+    dparts = to_modes(dblock, True, scale, tables, owners)
+    dparts, dhere, dabove, dbelow = hold((dparts, dpre, dabove, dbelow))
+    dparts = exchange(dparts, both)
+    dmain, dends = stack_rows(dhere, dabove, dbelow)
+    dparts, dends, dmain = hold((dparts, dends, dmain))
     dmixed, dspec = mix(dparts, dweight, -1, strips)
     darrived = exchange(dmixed, both)
-    back_local = conv(dmatrix, dmain, dside, width_x)
-    darrived, back_local = hold((darrived, back_local))
+    dright, dleft = across_columns(dends)
     dback = to_field(darrived, False, 1.0, tables, share)
+    dback, dright, dleft, spec, dspec = hold((dback, dright, dleft, spec, dspec))
     dfield = exchange(dback, "gx").reshape(whole)
+    back_local = conv(dmatrix, dmain, place_columns(dright, dleft), width_x)
     slots = M1 // owners
     weight_grad = weight_grads(by_mode(spec, slots), by_mode(dspec, slots))
-    dfield, weight_grad = hold((dfield, weight_grad))
+    dfield, back_local, weight_grad = hold((dfield, back_local, weight_grad))
     field_grad = dfield.astype(F32) + back_local
     return (activation[None], field_grad[None], weight_grad)
 

time: 190 us -> 175 us (0.921)
  starting transfers between devices: 76.3 us -> 58.4 us
  local copies, waits for them, and re-layouts: 16 us -> 6.48 us
  waiting for transfers between devices: 45.1 us -> 51.6 us
  blocking collectives: 18.4 us -> 21.9 us
    all_to_all x7, starting transfers between devices: 54.4 us -> 36.4 us  [exchange(): return lax.all_to_all(value, axes, split_axis=0, concat_axis=0, tiled=True)]
    all_to_all x7, waiting for transfers between devices: 32.5 us -> 47 us  [exchange(): return lax.all_to_all(value, axes, split_axis=0, concat_axis=0, tiled=True)]
    unnamed x51 -> x44, local copies, waits for them, and re-layouts: 14.1 us -> 3.94 us
    ppermute x8, waiting for transfers between devices: 12.6 us -> 4.62 us  [swap(): return lax.ppermute(value, axis, pairs)]
    all_to_all x1, blocking collectives: 18.4 us -> 21.9 us  [exchange(): return lax.all_to_all(value, axes, split_axis=0, concat_axis=0, tiled=True)]
    select_n x0 -> x4, other arithmetic: none -> 1.99 us  [body(): jnp.where(live, np.ascontiguousarray(table), jnp.zeros((), BF))]
  transfers between devices with their start and end apart: 15 -> 15, of which waited for: 10 -> 9; matrix products, arithmetic and copies ran while one was open for 9% -> 9% of each run, Pallas kernels for 5% -> 7%
where the time goes in v3:
time: 175 us; the launch traced here: 174 us
  starting transfers between devices  58.4 us (33%)
  waiting for transfers between devices  51.6 us (29%)
  blocking collectives  21.9 us (13%)
  other arithmetic  17.1 us (10%)
  Pallas kernels  16.8 us (10%)
  local copies, waits for them, and re-layouts  6.48 us (4%)
    all_to_all x7, waiting for transfers between devices, exchange(): return lax.all_to_all(value, axes, split_axis=0, concat_axis=0, tiled=True)  47 us
    all_to_all x7, starting transfers between devices, exchange(): return lax.all_to_all(value, axes, split_axis=0, concat_axis=0, tiled=True)  36.4 us
    ppermute x8, starting transfers between devices, swap(): return lax.ppermute(value, axis, pairs)  22 us
    all_to_all x1, blocking collectives, exchange(): return lax.all_to_all(value, axes, split_axis=0, concat_axis=0, tiled=True)  21.9 us
    pallas_call x8, Pallas kernels, on_chip(): pl.pallas_call(kernel, in_specs=[spec] * len(values), out_specs=[spec] *...  16.8 us
    ppermute x8, waiting for transfers between devices, swap(): return lax.ppermute(value, axis, pairs)  4.62 us
    convert_element_type x1, other arithmetic, body(): (upstream[0].astype(F32) * gate * (1.0 + pre * (1.0 - gate))).astype(BF)  4.29 us
    unnamed x44, local copies, waits for them, and re-layouts  3.94 us
  transfers between devices with their start and end apart: 15, of which 9 were waited for; matrix products, arithmetic and copies ran while one was open for 9% of the time, Pallas kernels for 7%

profile of v3, /device:TPU:1, one launch (start us, length us, event | category | flops | bytes accessed | tf_op | source)
XLA Modules:
  0.0 174.2 jit_solution(8496643510984534492)
XLA Ops:
  0.7 7.5 %all-to-all-start = ((bf16[16,2,64,256]{3,2,1,0:T(8,128)(2,1)}), bf16[16,2,64,256]{3,2,1,0:T(8,128)(2,1)}, u32[]{:S(2)}, u32[]{:S(2)}) async-start(bf16[16,2,64,256]{3,2,1,0:T(8,128)(2,1)} %bitcast.116), calls=%async_computation | async-start | bytes 2097152 | tf_op jit(solution)/shard_map/all_to_all | solution.py:294
  8.8 3.5 %collective-permute-start = (bf16[32,256]{1,0:T(8,128)(2,1)S(1)}, bf16[32,256]{1,0:T(8,128)(2,1)S(1)}, u32[]{:S(2)}, u32[]{:S(2)}) collective-permute-start(bf16[32,256]{1,0:T(8,128)(2,1)S(1)} %get-tuple-element.83), channel_id=1, source_target_pairs={{0,4},{4,8},{8,12},{12,16},{16,20},{20,24},{24,28},{28,32},{32,36}... | collective-permute-start | bytes 49160 | tf_op jit(solution)/shard_map/ppermute | solution.py:264
  12.3 1.9 %collective-permute-start.1 = (bf16[32,256]{1,0:T(8,128)(2,1)S(1)}, bf16[32,256]{1,0:T(8,128)(2,1)S(1)}, u32[]{:S(2)}, u32[]{:S(2)}) collective-permute-start(bf16[32,256]{1,0:T(8,128)(2,1)S(1)} %get-tuple-element.84), channel_id=1, source_target_pairs={{4,0},{8,4},{12,8},{16,12},{20,16},{24,20},{28,24},{32,28},{36,32}... | collective-permute-start | bytes 49160 | tf_op jit(solution)/shard_map/ppermute | solution.py:264
  17.7 2.6 %collective-permute-done = bf16[32,256]{1,0:T(8,128)(2,1)S(1)} collective-permute-done((bf16[32,256]{1,0:T(8,128)(2,1)S(1)}, bf16[32,256]{1,0:T(8,128)(2,1)S(1)}, u32[]{:S(2)}, u32[]{:S(2)}) %collective-permute-start) | collective-permute-done | bytes 16416 | tf_op jit(solution)/shard_map/ppermute | solution.py:264
  20.3 2.0 %collective-permute-done.1 = bf16[32,256]{1,0:T(8,128)(2,1)S(1)} collective-permute-done((bf16[32,256]{1,0:T(8,128)(2,1)S(1)}, bf16[32,256]{1,0:T(8,128)(2,1)S(1)}, u32[]{:S(2)}, u32[]{:S(2)}) %collective-permute-start.1) | collective-permute-done | bytes 16416 | tf_op jit(solution)/shard_map/ppermute | solution.py:264
  25.1 2.2 %to_modes.2 = bf16[64,8,128]{2,1,0:T(8,128)(2,1)S(1)} custom-call(bf16[16,2,64,256]{3,2,1,0:T(8,128)(2,1)} %all-to-all-done.block_ref, bf16[256,1024]{1,0:T(8,128)(2,1)S(1)} %broadcast_select_fusion.1.x_ref, bf16[512,256]{1,0:T(8,128)(2,1)S(1)} %copy-done.5), custom_call_target="tpu_custom_call" | custom-call | tf_op jit(solution)/shard_map/to_modes/pallas_call | solution.py:66
  27.3 21.9 %all_to_all.40.parts_ref = bf16[64,8,128]{2,1,0:T(8,128)(2,1)S(1)} all-to-all(bf16[64,8,128]{2,1,0:T(8,128)(2,1)S(1)} %to_modes.2), channel_id=1, replica_groups=mesh['dp'=4,'gx'=16,'gy'=4] {'gx','gy'}, dimensions={0} | all-to-all | bytes 262144 | tf_op jit(solution)/shard_map/all_to_all | solution.py:294
  50.3 4.5 %all-to-all-start.2 = ((bf16[64,8,128]{2,1,0:T(8,128)(2,1)}), bf16[64,8,128]{2,1,0:T(8,128)(2,1)S(1)}, u32[]{:S(2)}, u32[]{:S(2)}) async-start(bf16[64,8,128]{2,1,0:T(8,128)(2,1)} %get-tuple-element.47), calls=%async_computation.2 | async-start | bytes 262144 | tf_op jit(solution)/shard_map/all_to_all | solution.py:294
  54.9 4.2 %collective-permute-start.3 = (bf16[1,2112]{1,0:T(2,128)(2,1)S(1)}, bf16[1,2112]{1,0:T(2,128)(2,1)S(1)}, u32[]{:S(2)}, u32[]{:S(2)}) collective-permute-start(bf16[1,2112]{1,0:T(2,128)(2,1)S(1)} %get-tuple-element.95), channel_id=1, source_target_pairs={{0,1},{1,2},{2,3},{4,5},{5,6},{6,7},{8,9},{9,10},{10,11},{12,13},{... | collective-permute-start | bytes 12680 | tf_op jit(solution)/shard_map/ppermute | solution.py:264
  60.5 5.6 %all-to-all-done.2.spec_ref = bf16[64,8,128]{2,1,0:T(8,128)(2,1)S(1)} async-done(((bf16[64,8,128]{2,1,0:T(8,128)(2,1)}), bf16[64,8,128]{2,1,0:T(8,128)(2,1)S(1)}, u32[]{:S(2)}, u32[]{:S(2)}) %all-to-all-start.2) | async-done | bytes 131104 | tf_op jit(solution)/shard_map/all_to_all | solution.py:294
  66.2 1.6 to_field.2
  67.8 4.7 %all-to-all-start.3 = ((bf16[16,2,64,256]{3,2,1,0:T(8,128)(2,1)}), bf16[16,2,64,256]{3,2,1,0:T(8,128)(2,1)}, u32[]{:S(2)}, u32[]{:S(2)}) async-start(bf16[16,2,64,256]{3,2,1,0:T(8,128)(2,1)} %to_field.2), calls=%async_computation.3 | async-start | bytes 2097152 | tf_op jit(solution)/shard_map/all_to_all | solution.py:294
  72.9 1.6 copy.82
  75.4 3.7 %conv.2 = f32[32,64,256]{2,1,0:T(8,128)S(1)} custom-call(bf16[384,192]{1,0:T(8,128)(2,1)S(1)} %fusion.18.matrix_ref, bf16[2112,256]{1,0:T(8,128)(2,1)S(1)} %bitcast.105, bf16[2112,128]{1,0:T(8,128)(2,1)S(1)} %fusion.5.side_ref), custom_call_target="tpu_custom_call" | custom-call | tf_op jit(solution)/shard_map/conv/pallas_call | solution.py:66
  79.9 8.6 %all-to-all-done.3 = bf16[16,2,64,256]{3,2,1,0:T(8,128)(2,1)} async-done(((bf16[16,2,64,256]{3,2,1,0:T(8,128)(2,1)}), bf16[16,2,64,256]{3,2,1,0:T(8,128)(2,1)}, u32[]{:S(2)}, u32[]{:S(2)}) %all-to-all-start.3) | async-done | bytes 1048608 | tf_op jit(solution)/shard_map/all_to_all | solution.py:294
  88.5 4.3 %fusion.3 = (bf16[32,64,256]{2,1,0:T(8,128)(2,1)}, f32[1,32,64,256]{3,2,1,0:T(8,128)}) fusion(f32[32,64,256]{2,1,0:T(8,128)S(1)} %conv.2, bf16[32,64,256]{2,1,0:T(8,128)(2,1)} %bitcast.10, bf16[1,32,64,256]{3,2,1,0:T(8,128)(2,1)} %param.17, f32[32]{0:T(128)S(1)} %copy-done.19), kind=kLoop, calls=%fused_computation.7 | loop fusion | flops 7340032 | bytes 7340160 | tf_op jit(solution)/shard_map/convert_element_type | solution.py:350
  92.8 4.5 %all-to-all-start.4 = ((bf16[16,2,64,256]{3,2,1,0:T(8,128)(2,1)}), bf16[16,2,64,256]{3,2,1,0:T(8,128)(2,1)S(1)}, u32[]{:S(2)}, u32[]{:S(2)}) async-start(bf16[16,2,64,256]{3,2,1,0:T(8,128)(2,1)} %bitcast.112), calls=%async_computation.4 | async-start | bytes 2097152 | tf_op jit(solution)/shard_map/all_to_all | solution.py:294
  97.4 3.5 %collective-permute-start.4 = (bf16[32,256]{1,0:T(8,128)(2,1)S(1)}, bf16[32,256]{1,0:T(8,128)(2,1)S(1)}, u32[]{:S(2)}, u32[]{:S(2)}) collective-permute-start(bf16[32,256]{1,0:T(8,128)(2,1)S(1)} %bitcast.126), channel_id=1, source_target_pairs={{0,4},{4,8},{8,12},{12,16},{16,20},{20,24},{24,28},{28,32},{32,36}... | collective-permute-start | bytes 49160 | tf_op jit(solution)/shard_map/ppermute | solution.py:264
  100.9 1.9 %collective-permute-start.5 = (bf16[32,256]{1,0:T(8,128)(2,1)S(1)}, bf16[32,256]{1,0:T(8,128)(2,1)S(1)}, u32[]{:S(2)}, u32[]{:S(2)}) collective-permute-start(bf16[32,256]{1,0:T(8,128)(2,1)S(1)} %bitcast.124), channel_id=1, source_target_pairs={{4,0},{8,4},{12,8},{16,12},{20,16},{24,20},{28,24},{32,28},{36,32}... | collective-permute-start | bytes 49160 | tf_op jit(solution)/shard_map/ppermute | solution.py:264
  102.9 10.3 %all-to-all-done.4.block_ref = bf16[16,2,64,256]{3,2,1,0:T(8,128)(2,1)S(1)} async-done(((bf16[16,2,64,256]{3,2,1,0:T(8,128)(2,1)}), bf16[16,2,64,256]{3,2,1,0:T(8,128)(2,1)S(1)}, u32[]{:S(2)}, u32[]{:S(2)}) %all-to-all-start.4) | async-done | bytes 1048608 | tf_op jit(solution)/shard_map/all_to_all | solution.py:294
  113.2 1.7 to_modes.3
  114.9 6.2 %all-to-all-start.5 = ((bf16[64,8,128]{2,1,0:T(8,128)(2,1)}), bf16[64,8,128]{2,1,0:T(8,128)(2,1)S(1)}, u32[]{:S(2)}, u32[]{:S(2)}) async-start(bf16[64,8,128]{2,1,0:T(8,128)(2,1)} %to_modes.3), calls=%async_computation.5 | async-start | bytes 262144 | tf_op jit(solution)/shard_map/all_to_all | solution.py:294
  122.5 9.8 %all-to-all-done.5.parts_ref = bf16[64,8,128]{2,1,0:T(8,128)(2,1)S(1)} async-done(((bf16[64,8,128]{2,1,0:T(8,128)(2,1)}), bf16[64,8,128]{2,1,0:T(8,128)(2,1)S(1)}, u32[]{:S(2)}, u32[]{:S(2)}) %all-to-all-start.5) | async-done | bytes 131104 | tf_op jit(solution)/shard_map/all_to_all | solution.py:294
  133.4 4.5 %all-to-all-start.6 = ((bf16[64,8,128]{2,1,0:T(8,128)(2,1)}), bf16[64,8,128]{2,1,0:T(8,128)(2,1)S(1)}, u32[]{:S(2)}, u32[]{:S(2)}) async-start(bf16[64,8,128]{2,1,0:T(8,128)(2,1)} %get-tuple-element.65), calls=%async_computation.6 | async-start | bytes 262144 | tf_op jit(solution)/shard_map/all_to_all | solution.py:294
  137.9 4.2 %collective-permute-start.7 = (bf16[1,2112]{1,0:T(2,128)(2,1)S(1)}, bf16[1,2112]{1,0:T(2,128)(2,1)S(1)}, u32[]{:S(2)}, u32[]{:S(2)}) collective-permute-start(bf16[1,2112]{1,0:T(2,128)(2,1)S(1)} %get-tuple-element.93), channel_id=1, source_target_pairs={{0,1},{1,2},{2,3},{4,5},{5,6},{6,7},{8,9},{9,10},{10,11},{12,13},{... | collective-permute-start | bytes 12680 | tf_op jit(solution)/shard_map/ppermute | solution.py:264
  143.4 5.8 %all-to-all-done.6.spec_ref = bf16[64,8,128]{2,1,0:T(8,128)(2,1)S(1)} async-done(((bf16[64,8,128]{2,1,0:T(8,128)(2,1)}), bf16[64,8,128]{2,1,0:T(8,128)(2,1)S(1)}, u32[]{:S(2)}, u32[]{:S(2)}) %all-to-all-start.6) | async-done | bytes 131104 | tf_op jit(solution)/shard_map/all_to_all | solution.py:294
  149.2 1.6 to_field.3
  150.8 4.5 %all-to-all-start.7 = ((bf16[16,2,64,256]{3,2,1,0:T(8,128)(2,1)}), bf16[16,2,64,256]{3,2,1,0:T(8,128)(2,1)}, u32[]{:S(2)}, u32[]{:S(2)}) async-start(bf16[16,2,64,256]{3,2,1,0:T(8,128)(2,1)} %to_field.3), calls=%async_computation.7 | async-start | bytes 2097152 | tf_op jit(solution)/shard_map/all_to_all | solution.py:294
  157.0 3.7 %conv.3 = f32[32,64,256]{2,1,0:T(8,128)S(1)} custom-call(bf16[384,192]{1,0:T(8,128)(2,1)S(1)} %copy-done.7, bf16[2112,256]{1,0:T(8,128)(2,1)S(1)} %bitcast.107, bf16[2112,128]{1,0:T(8,128)(2,1)S(1)} %fusion.4.side_ref), custom_call_target="tpu_custom_call" | custom-call | tf_op jit(solution)/shard_map/conv/pallas_call | solution.py:66
  162.2 2.4 %pad_maximum_fusion = f32[32,32,2,2,128]{4,3,2,1,0:T(2,128)} fusion(f32[32,32,1,2,128]{4,3,2,1,0:T(2,128)S(1)} %get-tuple-element.88, f32[32,32,1,2,128]{4,3,2,1,0:T(2,128)S(1)} %get-tuple-element.87), kind=kLoop, calls=%fused_computation.4 | loop fusion | flops 524288 | bytes 4194304 | tf_op jit(solution)/shard_map/stack | solution.py:307
  164.6 6.9 %all-to-all-done.7 = bf16[16,2,64,256]{3,2,1,0:T(8,128)(2,1)} async-done(((bf16[16,2,64,256]{3,2,1,0:T(8,128)(2,1)}), bf16[16,2,64,256]{3,2,1,0:T(8,128)(2,1)}, u32[]{:S(2)}, u32[]{:S(2)}) %all-to-all-start.7) | async-done | bytes 1048608 | tf_op jit(solution)/shard_map/all_to_all | solution.py:294
  171.4 2.8 %add_bitcast_fusion = f32[1,32,64,256]{3,2,1,0:T(8,128)} fusion(f32[32,64,256]{2,1,0:T(8,128)S(1)} %conv.3, bf16[32,64,256]{2,1,0:T(8,128)(2,1)} %bitcast.25), kind=kLoop, calls=%fused_computation.8 | loop fusion | flops 1048576 | bytes 5242880 | tf_op jit(solution)/shard_map/broadcast_in_dim | solution.py:370
  (89 shorter events, 18.1 us)
Async XLA Ops:
  0.6 7.5 %copy-start.10 = (bf16[1,32,64,256]{3,2,1,0:T(8,128)(2,1)S(1)}, bf16[1,32,64,256]{3,2,1,0:T(8,128)(2,1)}, u32[]{:S(2)}) copy-start(bf16[1,32,64,256]{3,2,1,0:T(8,128)(2,1)} %param.13) | copy-start | bytes 3145732
  0.6 13.6 %copy-start.15 = (bf16[512,256]{1,0:T(8,128)(2,1)S(1)}, bf16[512,256]{1,0:T(8,128)(2,1)}, u32[]{:S(2)}) copy-start(bf16[512,256]{1,0:T(8,128)(2,1)} %constant.27.clone) | copy-start | bytes 786436
  0.7 14.3 %copy-start.13 = (bf16[256,1024]{1,0:T(8,128)(2,1)S(1)}, bf16[256,1024]{1,0:T(8,128)(2,1)}, u32[]{:S(2)}) copy-start(bf16[256,1024]{1,0:T(8,128)(2,1)} %constant.26.clone) | copy-start | bytes 1572868
  0.7 23.5 %all-to-all-start = ((bf16[16,2,64,256]{3,2,1,0:T(8,128)(2,1)}), bf16[16,2,64,256]{3,2,1,0:T(8,128)(2,1)}, u32[]{:S(2)}, u32[]{:S(2)}) async-start(bf16[16,2,64,256]{3,2,1,0:T(8,128)(2,1)} %bitcast.116), calls=%async_computation | async-start | bytes 2097152 | tf_op jit(solution)/shard_map/all_to_all | solution.py:294
  8.2 6.9 %copy-start.12 = (bf16[1024,256]{1,0:T(8,128)(2,1)S(1)}, bf16[1024,256]{1,0:T(8,128)(2,1)}, u32[]{:S(2)}) copy-start(bf16[1024,256]{1,0:T(8,128)(2,1)} %constant.28.clone) | copy-start | bytes 1572868
  8.8 8.9 %copy-start.9 = (bf16[1,32,64,256]{3,1,2,0:T(8,128)(2,1)}, bf16[1,32,64,256]{3,1,2,0:T(8,128)(2,1)S(1)}, u32[]{:S(2)}) copy-start(bf16[1,32,64,256]{3,1,2,0:T(8,128)(2,1)S(1)} %copy.84) | copy-start | bytes 3145732
  8.8 11.5 %collective-permute-start = (bf16[32,256]{1,0:T(8,128)(2,1)S(1)}, bf16[32,256]{1,0:T(8,128)(2,1)S(1)}, u32[]{:S(2)}, u32[]{:S(2)}) collective-permute-start(bf16[32,256]{1,0:T(8,128)(2,1)S(1)} %get-tuple-element.83), channel_id=1, source_target_pairs={{0,4},{4,8},{8,12},{12,16},{16,20},{20,24},{24,28},{28,32},{32,36}... | collective-permute-start | bytes 49160 | tf_op jit(solution)/shard_map/ppermute | solution.py:264
  12.3 10.0 %collective-permute-start.1 = (bf16[32,256]{1,0:T(8,128)(2,1)S(1)}, bf16[32,256]{1,0:T(8,128)(2,1)S(1)}, u32[]{:S(2)}, u32[]{:S(2)}) collective-permute-start(bf16[32,256]{1,0:T(8,128)(2,1)S(1)} %get-tuple-element.84), channel_id=1, source_target_pairs={{4,0},{8,4},{12,8},{16,12},{20,16},{24,20},{28,24},{32,28},{36,32}... | collective-permute-start | bytes 49160 | tf_op jit(solution)/shard_map/ppermute | solution.py:264
  15.1 9.1 %copy-start.2 = (bf16[256,1024]{1,0:T(8,128)(2,1)}, bf16[256,1024]{1,0:T(8,128)(2,1)S(1)}, u32[]{:S(2)}) copy-start(bf16[256,1024]{1,0:T(8,128)(2,1)S(1)} %broadcast_select_fusion.1.x_ref) | copy-start | bytes 1572868
  15.1 51.0 %copy-start = (bf16[1024,256]{1,0:T(8,128)(2,1)}, bf16[1024,256]{1,0:T(8,128)(2,1)S(1)}, u32[]{:S(2)}) copy-start(bf16[1024,256]{1,0:T(8,128)(2,1)S(1)} %broadcast_select_fusion.x_ref) | copy-start | bytes 1572868
  16.3 7.4 %copy-start.16 = (bf16[2,256]{1,0:T(2,128)(2,1)S(1)}, bf16[2,256]{1,0:T(2,128)(2,1)}, u32[]{:S(2)}) copy-start(bf16[2,256]{1,0:T(2,128)(2,1)} %constant.30.clone) | copy-start | bytes 3076
  50.3 15.8 %all-to-all-start.2 = ((bf16[64,8,128]{2,1,0:T(8,128)(2,1)}), bf16[64,8,128]{2,1,0:T(8,128)(2,1)S(1)}, u32[]{:S(2)}, u32[]{:S(2)}) async-start(bf16[64,8,128]{2,1,0:T(8,128)(2,1)} %get-tuple-element.47), calls=%async_computation.2 | async-start | bytes 262144 | tf_op jit(solution)/shard_map/all_to_all | solution.py:294
  54.9 17.6 %copy-start.14 = (bf16[9,32,32]{2,1,0:T(8,128)(2,1)S(1)}, bf16[9,32,32]{2,1,0:T(8,128)(2,1)}, u32[]{:S(2)}) copy-start(bf16[9,32,32]{2,1,0:T(8,128)(2,1)} %param.15) | copy-start | bytes 55300
  54.9 12.9 %collective-permute-start.3 = (bf16[1,2112]{1,0:T(2,128)(2,1)S(1)}, bf16[1,2112]{1,0:T(2,128)(2,1)S(1)}, u32[]{:S(2)}, u32[]{:S(2)}) collective-permute-start(bf16[1,2112]{1,0:T(2,128)(2,1)S(1)} %get-tuple-element.95), channel_id=1, source_target_pairs={{0,1},{1,2},{2,3},{4,5},{5,6},{6,7},{8,9},{9,10},{10,11},{12,13},{... | collective-permute-start | bytes 12680 | tf_op jit(solution)/shard_map/ppermute | solution.py:264
  59.1 13.8 %copy-start.11 = (bf16[32,32,2,2,128]{4,3,2,1,0:T(2,128)(2,1)S(1)}, bf16[32,32,2,2,128]{4,3,2,1,0:T(2,128)(2,1)}, u32[]{:S(2)}) copy-start(bf16[32,32,2,2,128]{4,3,2,1,0:T(2,128)(2,1)} %param.14) | copy-start | bytes 3145732
  59.1 8.7 %collective-permute-start.2 = (bf16[1,2112]{1,0:T(2,128)(2,1)S(1)}, bf16[1,2112]{1,0:T(2,128)(2,1)S(1)}, u32[]{:S(2)}, u32[]{:S(2)}) collective-permute-start(bf16[1,2112]{1,0:T(2,128)(2,1)S(1)} %get-tuple-element.96), channel_id=1, source_target_pairs={{1,0},{2,1},{3,2},{5,4},{6,5},{7,6},{9,8},{10,9},{11,10},{13,12},{... | collective-permute-start | bytes 12680 | tf_op jit(solution)/shard_map/ppermute | solution.py:264
  67.8 7.0 %copy-start.17 = (f32[128]{0:T(128)S(1)}, f32[128]{0:T(128)}, u32[]{:S(2)}) copy-start(f32[128]{0:T(128)} %constant.56) | copy-start | bytes 1540
  67.8 7.0 %copy-start.18 = (f32[128]{0:T(128)S(1)}, f32[128]{0:T(128)}, u32[]{:S(2)}) copy-start(f32[128]{0:T(128)} %constant.53) | copy-start | bytes 1540
  67.8 20.7 %all-to-all-start.3 = ((bf16[16,2,64,256]{3,2,1,0:T(8,128)(2,1)}), bf16[16,2,64,256]{3,2,1,0:T(8,128)(2,1)}, u32[]{:S(2)}, u32[]{:S(2)}) async-start(bf16[16,2,64,256]{3,2,1,0:T(8,128)(2,1)} %to_field.2), calls=%async_computation.3 | async-start | bytes 2097152 | tf_op jit(solution)/shard_map/all_to_all | solution.py:294
  75.4 13.1 %copy-start.19 = (f32[32]{0:T(128)S(1)}, f32[32]{0:T(128)}, u32[]{:S(2)}) copy-start(f32[32]{0:T(128)} %param.16) | copy-start | bytes 388
  92.8 20.4 %copy-start.3 = (bf16[256,1024]{1,0:T(8,128)(2,1)S(1)}, bf16[256,1024]{1,0:T(8,128)(2,1)}, u32[]{:S(2)}) copy-start(bf16[256,1024]{1,0:T(8,128)(2,1)} %copy-done.2) | copy-start | bytes 1572868
  92.8 20.4 %copy-start.6 = (bf16[512,256]{1,0:T(8,128)(2,1)S(1)}, bf16[512,256]{1,0:T(8,128)(2,1)}, u32[]{:S(2)}) copy-start(bf16[512,256]{1,0:T(8,128)(2,1)} %broadcast_select_fusion.3.y_ref) | copy-start | bytes 786436
  92.8 20.4 %all-to-all-start.4 = ((bf16[16,2,64,256]{3,2,1,0:T(8,128)(2,1)}), bf16[16,2,64,256]{3,2,1,0:T(8,128)(2,1)S(1)}, u32[]{:S(2)}, u32[]{:S(2)}) async-start(bf16[16,2,64,256]{3,2,1,0:T(8,128)(2,1)} %bitcast.112), calls=%async_computation.4 | async-start | bytes 2097152 | tf_op jit(solution)/shard_map/all_to_all | solution.py:294
  97.4 17.5 %collective-permute-start.4 = (bf16[32,256]{1,0:T(8,128)(2,1)S(1)}, bf16[32,256]{1,0:T(8,128)(2,1)S(1)}, u32[]{:S(2)}, u32[]{:S(2)}) collective-permute-start(bf16[32,256]{1,0:T(8,128)(2,1)S(1)} %bitcast.126), channel_id=1, source_target_pairs={{0,4},{4,8},{8,12},{12,16},{16,20},{20,24},{24,28},{28,32},{32,36}... | collective-permute-start | bytes 49160 | tf_op jit(solution)/shard_map/ppermute | solution.py:264
  100.9 14.0 %collective-permute-start.5 = (bf16[32,256]{1,0:T(8,128)(2,1)S(1)}, bf16[32,256]{1,0:T(8,128)(2,1)S(1)}, u32[]{:S(2)}, u32[]{:S(2)}) collective-permute-start(bf16[32,256]{1,0:T(8,128)(2,1)S(1)} %bitcast.124), channel_id=1, source_target_pairs={{4,0},{8,4},{12,8},{16,12},{20,16},{24,20},{28,24},{32,28},{36,32}... | collective-permute-start | bytes 49160 | tf_op jit(solution)/shard_map/ppermute | solution.py:264
  114.9 17.4 %all-to-all-start.5 = ((bf16[64,8,128]{2,1,0:T(8,128)(2,1)}), bf16[64,8,128]{2,1,0:T(8,128)(2,1)S(1)}, u32[]{:S(2)}, u32[]{:S(2)}) async-start(bf16[64,8,128]{2,1,0:T(8,128)(2,1)} %to_modes.3), calls=%async_computation.5 | async-start | bytes 262144 | tf_op jit(solution)/shard_map/all_to_all | solution.py:294
  121.9 10.4 %copy-start.4 = (bf16[32,32,2,2,128]{4,0,1,2,3:T(8,128)(2,1)S(1)}, bf16[32,32,2,2,128]{4,0,1,2,3:T(8,128)(2,1)}, u32[]{:S(2)}) copy-start(bf16[32,32,2,2,128]{4,0,1,2,3:T(8,128)(2,1)} %copy.82) | copy-start | bytes 3145732
  121.9 27.3 %copy-start.1 = (bf16[1024,256]{1,0:T(8,128)(2,1)S(1)}, bf16[1024,256]{1,0:T(8,128)(2,1)}, u32[]{:S(2)}) copy-start(bf16[1024,256]{1,0:T(8,128)(2,1)} %copy-done) | copy-start | bytes 1572868
  133.4 15.8 %all-to-all-start.6 = ((bf16[64,8,128]{2,1,0:T(8,128)(2,1)}), bf16[64,8,128]{2,1,0:T(8,128)(2,1)S(1)}, u32[]{:S(2)}, u32[]{:S(2)}) async-start(bf16[64,8,128]{2,1,0:T(8,128)(2,1)} %get-tuple-element.65), calls=%async_computation.6 | async-start | bytes 262144 | tf_op jit(solution)/shard_map/all_to_all | solution.py:294
  137.9 12.9 %collective-permute-start.7 = (bf16[1,2112]{1,0:T(2,128)(2,1)S(1)}, bf16[1,2112]{1,0:T(2,128)(2,1)S(1)}, u32[]{:S(2)}, u32[]{:S(2)}) collective-permute-start(bf16[1,2112]{1,0:T(2,128)(2,1)S(1)} %get-tuple-element.93), channel_id=1, source_target_pairs={{0,1},{1,2},{2,3},{4,5},{5,6},{6,7},{8,9},{9,10},{10,11},{12,13},{... | collective-permute-start | bytes 12680 | tf_op jit(solution)/shard_map/ppermute | solution.py:264
  142.1 8.7 %collective-permute-start.6 = (bf16[1,2112]{1,0:T(2,128)(2,1)S(1)}, bf16[1,2112]{1,0:T(2,128)(2,1)S(1)}, u32[]{:S(2)}, u32[]{:S(2)}) collective-permute-start(bf16[1,2112]{1,0:T(2,128)(2,1)S(1)} %get-tuple-element.94), channel_id=1, source_target_pairs={{1,0},{2,1},{3,2},{5,4},{6,5},{7,6},{9,8},{10,9},{11,10},{13,12},{... | collective-permute-start | bytes 12680 | tf_op jit(solution)/shard_map/ppermute | solution.py:264
  150.8 20.6 %all-to-all-start.7 = ((bf16[16,2,64,256]{3,2,1,0:T(8,128)(2,1)}), bf16[16,2,64,256]{3,2,1,0:T(8,128)(2,1)}, u32[]{:S(2)}, u32[]{:S(2)}) async-start(bf16[16,2,64,256]{3,2,1,0:T(8,128)(2,1)} %to_field.3), calls=%async_computation.7 | async-start | bytes 2097152 | tf_op jit(solution)/shard_map/all_to_all | solution.py:294
  (3 other events, 6.3 us)

commit v4 on v3

--- a/solution.py
+++ b/solution.py
@@ -69,17 +69,24 @@
         out_specs=[spec] * len(outs) if many else spec,
         out_shape=[place(*out) for out in outs] if many else place(*outs),
         scratch_shapes=scratch,
-        compiler_params=pltpu.CompilerParams(vmem_limit_bytes=48 << 20),
+        compiler_params=pltpu.CompilerParams(vmem_limit_bytes=24 << 20),
         name=name,
     )(*[resident(value) for value in values])
 
 
-def forward_kernel(weighted, factor, block_ref, x_ref, y_ref, out_ref, rows_ref):
+def forward_kernel(weighted, factor, block_hbm, x_ref, y_ref, out_ref, rows_ref, block_ref, sems):
     owners, rows, _ = out_ref.shape
-    _, channels, _, width = block_ref.shape
+    channels, _, _, width = block_ref.shape
     slots = M1 // owners
+    copies = [
+        pltpu.make_async_copy(block_hbm.at[:, channel], block_ref.at[channel], sems.at[channel])
+        for channel in range(channels)
+    ]
+    for copy in copies:
+        copy.start()
     for channel in range(channels):
-        block = block_ref[:, channel].reshape(-1, width)
+        copies[channel].wait()
+        block = block_ref[channel].reshape(-1, width)
         spec_x = dot(x_ref[...], block)
         if factor != 1.0:
             spec_x = spec_x * factor
@@ -97,17 +104,82 @@
 
 
 def to_modes(block, weighted, factor, tables, owners):
-    rows = block.shape[1] * (M1 // owners) * 2
-    return on_chip(
+    strips, channels, width_x, width_y = block.shape
+    rows = channels * (M1 // owners) * 2
+    vmem = pl.BlockSpec(memory_space=pltpu.VMEM)
+    return pl.pallas_call(
         functools.partial(forward_kernel, weighted, factor),
-        ((owners, rows, M2), BF),
-        [pltpu.VMEM((rows, owners, M2), F32)],
-        "to_modes",
-        block,
-        tables[0],
-        tables[1],
-        place=jax.ShapeDtypeStruct,
-    )
+        in_specs=[pl.BlockSpec(memory_space=pltpu.HBM), vmem, vmem],
+        out_specs=vmem,
+        out_shape=jax.ShapeDtypeStruct((owners, rows, M2), BF),
+        scratch_shapes=[
+            pltpu.VMEM((rows, owners, M2), F32),
+            pltpu.VMEM((channels, strips, width_x, width_y), BF),
+            pltpu.SemaphoreType.DMA((channels,)),
+        ],
+        compiler_params=pltpu.CompilerParams(vmem_limit_bytes=24 << 20),
+        name="to_modes",
+    )(block, resident(tables[0]), resident(tables[1]))
+
+
+CHUNK = 4
+
+
+def stream_kernel(step, count, *refs):
+    ins, held, out = refs[:count], refs[count], refs[count + 1]
+    bufs, out_buf, in_sems, out_sems = refs[count + 2 : -3], refs[-3], refs[-2], refs[-1]
+    pieces = [pl.ds(first, CHUNK) for first in range(0, out_buf.shape[0], CHUNK)]
+    loads = [
+        [
+            pltpu.make_async_copy(ref.at[piece], buf.at[piece], in_sems.at[index, place])
+            for index, (ref, buf) in enumerate(zip(ins, bufs))
+        ]
+        for place, piece in enumerate(pieces)
+    ]
+    stores = [
+        pltpu.make_async_copy(out_buf.at[piece], out.at[piece], out_sems.at[place])
+        for place, piece in enumerate(pieces)
+    ]
+    for load in loads:
+        for copy in load:
+            copy.start()
+    for piece, load, store in zip(pieces, loads, stores):
+        for copy in load:
+            copy.wait()
+        out_buf[piece] = step(held[piece], *[buf[piece] for buf in bufs])
+        store.start()
+    for store in stores:
+        store.wait()
+
+
+def stream(step, held, values, dtype, name):
+    shape = held.shape
+    pieces = shape[0] // CHUNK
+    hbm = pl.BlockSpec(memory_space=pltpu.HBM)
+    return pl.pallas_call(
+        functools.partial(stream_kernel, step, len(values)),
+        in_specs=[hbm] * len(values) + [pl.BlockSpec(memory_space=pltpu.VMEM)],
+        out_specs=hbm,
+        out_shape=jax.ShapeDtypeStruct(shape, dtype),
+        scratch_shapes=[pltpu.VMEM(shape, value.dtype) for value in values]
+        + [
+            pltpu.VMEM(shape, dtype),
+            pltpu.SemaphoreType.DMA((len(values), pieces)),
+            pltpu.SemaphoreType.DMA((pieces,)),
+        ],
+        compiler_params=pltpu.CompilerParams(vmem_limit_bytes=24 << 20),
+        name=name,
+    )(*[pltpu.with_memory_space_constraint(value, pltpu.HBM) for value in values], resident(held))
+
+
+def gate_grad(local, spectral, upstream):
+    pre = spectral.astype(F32) + local
+    gate = 0.5 + 0.5 * jnp.tanh(0.5 * pre)
+    return (upstream.astype(F32) * gate * (1.0 + pre * (1.0 - gate))).astype(BF)
+
+
+def add_field(local, field):
+    return field.astype(F32) + local
 
 
 def inverse_kernel(weighted, factor, spec_ref, x_ref, y_ref, out_ref, rows_ref):
@@ -224,7 +296,7 @@
     )
 
 
-def conv_kernel(matrix_ref, main_ref, side_ref, out_ref):
+def conv_kernel(matrix_ref, main_ref, side_ref, bias_ref, out_ref):
     ins = matrix_ref.shape[1] // (CONV_ROWS + 2)
     outs, rows, width = out_ref.shape
     window = (CONV_ROWS + 2) * ins
@@ -244,15 +316,15 @@
                 low = pltpu.roll(taps[base : base + outs], 1, 1)[:, :width]
                 mid = taps[base + outs : base + 2 * outs, :width]
                 high = pltpu.roll(taps[base + 2 * outs : base + 3 * outs], full - 1, 1)[:, :width]
-                pieces.append(low + mid + high)
+                pieces.append(low + mid + high + bias_ref[:, :1])
         first = pl.multiple_of(step * tall, tall)
         out_ref[:, pl.ds(first, tall), :] = jnp.transpose(jnp.stack(pieces, axis=0), (1, 0, 2))
 
 
-def conv(matrix, main, side, rows):
+def conv(matrix, main, side, bias, rows):
     outs = matrix.shape[0] // (3 * CONV_ROWS)
     return on_chip(
-        conv_kernel, ((outs, rows, main.shape[1]), F32), [], "conv", matrix, main, side
+        conv_kernel, ((outs, rows, main.shape[1]), F32), [], "conv", matrix, main, side, bias
     )
 
 
@@ -282,11 +354,15 @@
     return swap(ends[:1], "gy", back=True), swap(ends[1:], "gy")
 
 
-def place_columns(right, left):
+def side_slots():
     place = np.zeros((2, 128), np.float32)
     place[0, 0] = place[1, 127] = 1.0
+    return place.astype(BF)
+
+
+def place_columns(right, left, slots):
     return jnp.einsum(
-        "rn,rk->nk", jnp.concatenate([right, left]), place.astype(BF), preferred_element_type=F32
+        "rn,rk->nk", jnp.concatenate([right, left]), slots, preferred_element_type=F32
     ).astype(BF)
 
 
@@ -323,6 +399,7 @@
         jnp.where(live, np.ascontiguousarray(table), jnp.zeros((), BF))
         for table in (table_x, table_y, table_x.T, table_y.T)
     ]
+    bias = jnp.broadcast_to(conv_bias[:, None], (channels, 128))
     hold = lax.optimization_barrier
 
     field = field_in[0]
@@ -330,43 +407,45 @@
     above, below = across_rows(field)
     main, ends = stack_rows(field, above, below)
     weight = jnp.transpose(spectral_weight, (3, 2, 0, 1, 4))
-    block, main, ends, weight, tables = hold((block, main, ends, weight, tables))
+    block, ends, weight = hold((block, ends, weight))
     parts = exchange(to_modes(block, False, 1.0, tables, owners), both)
     parts, ends = hold((parts, ends))
     mixed, spec = mix(parts, weight, 1, strips)
     arrived = exchange(mixed, both)
     right, left = across_columns(ends)
     back = to_field(arrived, True, scale, tables, share)
-    back, right, left, raw, dweight = hold((back, right, left, conv_weight, spectral_weight))
+    back, right, places, taps = hold((back, right, side_slots(), conv_weight))
     spectral = exchange(back, "gx").reshape(whole)
-    local = conv(conv_matrix(raw), main, place_columns(right, left), width_x)
-    dmatrix = conv_matrix(jnp.transpose(raw[::-1], (0, 2, 1)))
-    dweight = jnp.transpose(dweight, (3, 2, 1, 0, 4))
-    spectral, local, dmatrix, dweight = hold((spectral, local, dmatrix, dweight))
-
-    pre = spectral.astype(F32) + local + conv_bias[:, None, None]
-    gate = jax.nn.sigmoid(pre)
-    activation = pre * gate
-    dpre = (upstream[0].astype(F32) * gate * (1.0 + pre * (1.0 - gate))).astype(BF)
+    local = conv(conv_matrix(taps), main, place_columns(right, left, places), bias, width_x)
+    spectral, local = hold((spectral, local))
+
+    dpre = stream(gate_grad, local, [spectral, upstream[0]], BF, "gate_grad")
+    dpre, spectral, local, taps, dweight = hold((dpre, spectral, local, conv_weight, spectral_weight))
 
     dblock = exchange(dpre.reshape(share), "gx")
     dabove, dbelow = across_rows(dpre)
+    pre = spectral.astype(F32) + local
+    activation = pre * jax.nn.sigmoid(pre)
+    dblock, activation, dweight, taps = hold((dblock, activation, dweight, taps))
     dparts = to_modes(dblock, True, scale, tables, owners)
     dparts, dhere, dabove, dbelow = hold((dparts, dpre, dabove, dbelow))
     dparts = exchange(dparts, both)
+    dmatrix = conv_matrix(jnp.transpose(taps[::-1], (0, 2, 1)))
+    dweight = jnp.transpose(dweight, (3, 2, 1, 0, 4))
     dmain, dends = stack_rows(dhere, dabove, dbelow)
-    dparts, dends, dmain = hold((dparts, dends, dmain))
+    dparts, dends, dmain, dmatrix, dweight = hold((dparts, dends, dmain, dmatrix, dweight))
     dmixed, dspec = mix(dparts, dweight, -1, strips)
     darrived = exchange(dmixed, both)
     dright, dleft = across_columns(dends)
     dback = to_field(darrived, False, 1.0, tables, share)
-    dback, dright, dleft, spec, dspec = hold((dback, dright, dleft, spec, dspec))
+    dback, dright, places, spec, dspec = hold((dback, dright, places, spec, dspec))
     dfield = exchange(dback, "gx").reshape(whole)
-    back_local = conv(dmatrix, dmain, place_columns(dright, dleft), width_x)
+    dside = place_columns(dright, dleft, places)
+    back_local = conv(dmatrix, dmain, dside, jnp.zeros_like(bias), width_x)
     slots = M1 // owners
     weight_grad = weight_grads(by_mode(spec, slots), by_mode(dspec, slots))
     dfield, back_local, weight_grad = hold((dfield, back_local, weight_grad))
-    field_grad = dfield.astype(F32) + back_local
+    field_grad = stream(add_field, back_local, [dfield], F32, "add_field")
     return (activation[None], field_grad[None], weight_grad)
 
 

time: 175 us -> 182 us (1.040)
  blocking collectives: 21.9 us -> 0 us
  waiting for transfers between devices: 51.6 us -> 67.5 us
  starting transfers between devices: 58.4 us -> 68.8 us
  Pallas kernels: 16.8 us -> 23.9 us
  other arithmetic: 17.1 us -> 12.3 us
    all_to_all x1 -> x0, blocking collectives: 21.9 us -> none  [exchange(): return lax.all_to_all(value, axes, split_axis=0, concat_axis=0, tiled=True)]
    ppermute x8, waiting for transfers between devices: 4.62 us -> 24.7 us  [swap(): return lax.ppermute(value, axis, pairs)]
    all_to_all x7 -> x8, starting transfers between devices: 36.4 us -> 50.1 us  [exchange(): return lax.all_to_all(value, axes, split_axis=0, concat_axis=0, tiled=True)]
    pallas_call x0 -> x4, Pallas kernels: none -> 11 us  [the longest x2 5.83 us: to_modes(): pl.pallas_call(functools.partial(forward_kernel, weighted, factor), in_sp...]
    convert_element_type x3 -> x0, other arithmetic: 5.53 us -> none  [the longest x1 4.29 us: body(): (upstream[0].astype(F32) * gate * (1.0 + pre * (1.0 - gate))).astype(BF)]
    all_to_all x7 -> x8, waiting for transfers between devices: 47 us -> 42.8 us  [exchange(): return lax.all_to_all(value, axes, split_axis=0, concat_axis=0, tiled=True)]
    pallas_call x8 -> x6, Pallas kernels: 16.8 us -> 12.9 us  [on_chip(): pl.pallas_call(kernel, in_specs=[spec] * len(values), out_specs=[spec] *...]
    ppermute x8, starting transfers between devices: 22 us -> 18.8 us  [swap(): return lax.ppermute(value, axis, pairs)]
  transfers between devices with their start and end apart: 15 -> 16, of which waited for: 9 -> 9; matrix products, arithmetic and copies ran while one was open for 9% -> 10% of each run, Pallas kernels for 7% -> 8%
where the time goes in v4:
time: 182 us; the launch traced here: 181 us
  starting transfers between devices  68.8 us (38%)
  waiting for transfers between devices  67.5 us (37%)
  Pallas kernels  23.9 us (13%)
  other arithmetic  12.3 us (7%)
  local copies, waits for them, and re-layouts  5.85 us (3%)
    all_to_all x8, starting transfers between devices, exchange(): return lax.all_to_all(value, axes, split_axis=0, concat_axis=0, tiled=True)  50.1 us
    all_to_all x8, waiting for transfers between devices, exchange(): return lax.all_to_all(value, axes, split_axis=0, concat_axis=0, tiled=True)  42.8 us
    ppermute x8, waiting for transfers between devices, swap(): return lax.ppermute(value, axis, pairs)  24.7 us
    ppermute x8, starting transfers between devices, swap(): return lax.ppermute(value, axis, pairs)  18.8 us
    pallas_call x6, Pallas kernels, on_chip(): pl.pallas_call(kernel, in_specs=[spec] * len(values), out_specs=[spec] *...  12.9 us
    pallas_call x2, Pallas kernels, to_modes(): pl.pallas_call(functools.partial(forward_kernel, weighted, factor), in_sp...  5.83 us
    pallas_call x2, Pallas kernels, stream(): pl.pallas_call(functools.partial(stream_kernel, step, len(values)), in_sp...  5.13 us
  transfers between devices with their start and end apart: 16, of which 9 were waited for; matrix products, arithmetic and copies ran while one was open for 10% of the time, Pallas kernels for 8%

profile of v4, /device:TPU:1, one launch (start us, length us, event | category | flops | bytes accessed | tf_op | source)
XLA Modules:
  0.0 181.3 jit_solution(8325403526161133726)
XLA Ops:
  0.7 7.5 %all-to-all-start = ((bf16[16,2,64,256]{3,2,1,0:T(8,128)(2,1)}), bf16[16,2,64,256]{3,2,1,0:T(8,128)(2,1)}, u32[]{:S(2)}, u32[]{:S(2)}) async-start(bf16[16,2,64,256]{3,2,1,0:T(8,128)(2,1)} %bitcast.112), calls=%async_computation | async-start | bytes 2097152 | tf_op jit(solution)/shard_map/all_to_all | solution.py:370
  8.8 3.5 %collective-permute-start = (bf16[32,256]{1,0:T(8,128)(2,1)S(1)}, bf16[32,256]{1,0:T(8,128)(2,1)S(1)}, u32[]{:S(2)}, u32[]{:S(2)}) collective-permute-start(bf16[32,256]{1,0:T(8,128)(2,1)S(1)} %get-tuple-element.87), channel_id=1, source_target_pairs={{0,4},{4,8},{8,12},{12,16},{16,20},{20,24},{24,28},{28,32},{32,36}... | collective-permute-start | bytes 49160 | tf_op jit(solution)/shard_map/ppermute | solution.py:336
  12.3 1.9 %collective-permute-start.1 = (bf16[32,256]{1,0:T(8,128)(2,1)S(1)}, bf16[32,256]{1,0:T(8,128)(2,1)S(1)}, u32[]{:S(2)}, u32[]{:S(2)}) collective-permute-start(bf16[32,256]{1,0:T(8,128)(2,1)S(1)} %get-tuple-element.88), channel_id=1, source_target_pairs={{4,0},{8,4},{12,8},{16,12},{20,16},{24,20},{28,24},{32,28},{36,32}... | collective-permute-start | bytes 49160 | tf_op jit(solution)/shard_map/ppermute | solution.py:336
  16.0 4.3 %collective-permute-done = bf16[32,256]{1,0:T(8,128)(2,1)S(1)} collective-permute-done((bf16[32,256]{1,0:T(8,128)(2,1)S(1)}, bf16[32,256]{1,0:T(8,128)(2,1)S(1)}, u32[]{:S(2)}, u32[]{:S(2)}) %collective-permute-start) | collective-permute-done | bytes 16416 | tf_op jit(solution)/shard_map/ppermute | solution.py:336
  20.4 2.0 %collective-permute-done.1 = bf16[32,256]{1,0:T(8,128)(2,1)S(1)} collective-permute-done((bf16[32,256]{1,0:T(8,128)(2,1)S(1)}, bf16[32,256]{1,0:T(8,128)(2,1)S(1)}, u32[]{:S(2)}, u32[]{:S(2)}) %collective-permute-start.1) | collective-permute-done | bytes 16416 | tf_op jit(solution)/shard_map/ppermute | solution.py:336
  24.1 2.9 %to_modes.2 = bf16[64,8,128]{2,1,0:T(8,128)(2,1)} custom-call(bf16[16,2,64,256]{3,2,1,0:T(8,128)(2,1)} %all-to-all-done.block_hbm, bf16[256,1024]{1,0:T(8,128)(2,1)S(1)} %broadcast_select_fusion.1.x_ref, bf16[512,256]{1,0:T(8,128)(2,1)S(1)} %broadcast_select_fusion.3.y_ref), custom_call_target="tpu_custom_call" | custom-call | tf_op jit(solution)/shard_map/to_modes/pallas_call | solution.py:110
  27.1 10.9 %all-to-all-start.1 = ((bf16[64,8,128]{2,1,0:T(8,128)(2,1)}), bf16[64,8,128]{2,1,0:T(8,128)(2,1)S(1)}, u32[]{:S(2)}, u32[]{:S(2)}) async-start(bf16[64,8,128]{2,1,0:T(8,128)(2,1)} %to_modes.2), calls=%async_computation.1 | async-start | bytes 262144 | tf_op jit(solution)/shard_map/all_to_all | solution.py:370
  39.1 10.1 %all-to-all-done.1.parts_ref = bf16[64,8,128]{2,1,0:T(8,128)(2,1)S(1)} async-done(((bf16[64,8,128]{2,1,0:T(8,128)(2,1)}), bf16[64,8,128]{2,1,0:T(8,128)(2,1)S(1)}, u32[]{:S(2)}, u32[]{:S(2)}) %all-to-all-start.1) | async-done | bytes 131104 | tf_op jit(solution)/shard_map/all_to_all | solution.py:370
  50.3 4.5 %all-to-all-start.2 = ((bf16[64,8,128]{2,1,0:T(8,128)(2,1)}), bf16[64,8,128]{2,1,0:T(8,128)(2,1)S(1)}, u32[]{:S(2)}, u32[]{:S(2)}) async-start(bf16[64,8,128]{2,1,0:T(8,128)(2,1)} %get-tuple-element.48), calls=%async_computation.2 | async-start | bytes 262144 | tf_op jit(solution)/shard_map/all_to_all | solution.py:370
  56.2 9.9 %all-to-all-done.2.spec_ref = bf16[64,8,128]{2,1,0:T(8,128)(2,1)S(1)} async-done(((bf16[64,8,128]{2,1,0:T(8,128)(2,1)}), bf16[64,8,128]{2,1,0:T(8,128)(2,1)S(1)}, u32[]{:S(2)}, u32[]{:S(2)}) %all-to-all-start.2) | async-done | bytes 131104 | tf_op jit(solution)/shard_map/all_to_all | solution.py:370
  67.8 4.5 %all-to-all-start.3 = ((bf16[16,2,64,256]{3,2,1,0:T(8,128)(2,1)}), bf16[16,2,64,256]{3,2,1,0:T(8,128)(2,1)}, u32[]{:S(2)}, u32[]{:S(2)}) async-start(bf16[16,2,64,256]{3,2,1,0:T(8,128)(2,1)} %to_field.2), calls=%async_computation.3 | async-start | bytes 2097152 | tf_op jit(solution)/shard_map/all_to_all | solution.py:370
  72.3 2.6 %collective-permute-start.3 = (bf16[1,2112]{1,0:T(2,128)(2,1)S(1)}, bf16[1,2112]{1,0:T(2,128)(2,1)S(1)}, u32[]{:S(2)}, u32[]{:S(2)}) collective-permute-start(bf16[1,2112]{1,0:T(2,128)(2,1)S(1)} %get-tuple-element.99), channel_id=1, source_target_pairs={{0,1},{1,2},{2,3},{4,5},{5,6},{6,7},{8,9},{9,10},{10,11},{12,13},{... | collective-permute-start | bytes 12680 | tf_op jit(solution)/shard_map/ppermute | solution.py:336
  75.2 9.1 %collective-permute-done.3 = bf16[1,2112]{1,0:T(2,128)(2,1)S(1)} collective-permute-done((bf16[1,2112]{1,0:T(2,128)(2,1)S(1)}, bf16[1,2112]{1,0:T(2,128)(2,1)S(1)}, u32[]{:S(2)}, u32[]{:S(2)}) %collective-permute-start.3) | collective-permute-done | bytes 4256 | tf_op jit(solution)/shard_map/ppermute | solution.py:336
  84.7 3.8 %conv.2.refs_2_ = f32[32,64,256]{2,1,0:T(8,128)S(1)} custom-call(bf16[384,192]{1,0:T(8,128)(2,1)S(1)} %fusion.14.matrix_ref, bf16[2112,256]{1,0:T(8,128)(2,1)S(1)} %bitcast.103, bf16[2112,128]{1,0:T(8,128)(2,1)S(1)} %convolution_convert_fusion.1.side_ref, f32[32,128]{1,0:T(8,128)S(1)} %broadcast_in_dim.49.bias_ref), custom_call_target="tpu_custom_call" | custom-call | tf_op jit(solution)/shard_map/conv/pallas_call | solution.py:66
  88.5 2.8 %gate_grad.1 = bf16[32,64,256]{2,1,0:T(8,128)(2,1)} custom-call(bf16[32,64,256]{2,1,0:T(8,128)(2,1)} %bitcast.10.refs_0_, bf16[32,64,256]{2,1,0:T(8,128)(2,1)} %bitcast.115, f32[32,64,256]{2,1,0:T(8,128)S(1)} %conv.2.refs_2_), custom_call_target="tpu_custom_call" | custom-call | tf_op jit(solution)/shard_map/gate_grad/pallas_call | solution.py:159
  91.2 5.2 %all-to-all-start.4 = ((bf16[16,2,64,256]{3,2,1,0:T(8,128)(2,1)}), bf16[16,2,64,256]{3,2,1,0:T(8,128)(2,1)}, u32[]{:S(2)}, u32[]{:S(2)}) async-start(bf16[16,2,64,256]{3,2,1,0:T(8,128)(2,1)} %bitcast.14), calls=%async_computation.4 | async-start | bytes 2097152 | tf_op jit(solution)/shard_map/all_to_all | solution.py:370
  97.5 3.5 %collective-permute-start.4 = (bf16[32,256]{1,0:T(8,128)(2,1)S(1)}, bf16[32,256]{1,0:T(8,128)(2,1)S(1)}, u32[]{:S(2)}, u32[]{:S(2)}) collective-permute-start(bf16[32,256]{1,0:T(8,128)(2,1)S(1)} %bitcast.125), channel_id=1, source_target_pairs={{0,4},{4,8},{8,12},{12,16},{16,20},{20,24},{24,28},{28,32},{32,36}... | collective-permute-start | bytes 49160 | tf_op jit(solution)/shard_map/ppermute | solution.py:336
  101.1 2.1 %collective-permute-start.5 = (bf16[32,256]{1,0:T(8,128)(2,1)S(1)}, bf16[32,256]{1,0:T(8,128)(2,1)S(1)}, u32[]{:S(2)}, u32[]{:S(2)}) collective-permute-start(bf16[32,256]{1,0:T(8,128)(2,1)S(1)} %bitcast.123), channel_id=1, source_target_pairs={{4,0},{8,4},{12,8},{16,12},{20,16},{24,20},{28,24},{32,28},{36,32}... | collective-permute-start | bytes 49160 | tf_op jit(solution)/shard_map/ppermute | solution.py:336
  103.1 3.1 %divide_multiply_fusion = f32[32,64,256]{2,1,0:T(8,128)} fusion(f32[32,64,256]{2,1,0:T(8,128)S(1)} %conv.2.refs_2_, bf16[32,64,256]{2,1,0:T(8,128)(2,1)} %bitcast.10.refs_0_), kind=kLoop, calls=%fused_computation.7 | loop fusion | flops 3145728 | bytes 5242880 | tf_op jit(solution)/shard_map/mul | solution.py:428
  106.2 6.1 %all-to-all-done.4.block_hbm = bf16[16,2,64,256]{3,2,1,0:T(8,128)(2,1)} async-done(((bf16[16,2,64,256]{3,2,1,0:T(8,128)(2,1)}), bf16[16,2,64,256]{3,2,1,0:T(8,128)(2,1)}, u32[]{:S(2)}, u32[]{:S(2)}) %all-to-all-start.4) | async-done | bytes 1048608 | tf_op jit(solution)/shard_map/all_to_all | solution.py:370
  112.4 2.9 %to_modes.3 = bf16[64,8,128]{2,1,0:T(8,128)(2,1)} custom-call(bf16[16,2,64,256]{3,2,1,0:T(8,128)(2,1)} %all-to-all-done.4.block_hbm, bf16[256,1024]{1,0:T(8,128)(2,1)S(1)} %copy-done.3, bf16[512,256]{1,0:T(8,128)(2,1)S(1)} %copy-done.5), custom_call_target="tpu_custom_call" | custom-call | tf_op jit(solution)/shard_map/to_modes/pallas_call | solution.py:110
  115.3 8.3 %all-to-all-start.5 = ((bf16[64,8,128]{2,1,0:T(8,128)(2,1)}), bf16[64,8,128]{2,1,0:T(8,128)(2,1)S(1)}, u32[]{:S(2)}, u32[]{:S(2)}) async-start(bf16[64,8,128]{2,1,0:T(8,128)(2,1)} %to_modes.3), calls=%async_computation.5 | async-start | bytes 262144 | tf_op jit(solution)/shard_map/all_to_all | solution.py:370
  124.0 2.1 %pad_maximum_fusion.1 = bf16[66,32,256]{2,0,1:T(8,128)(2,1)S(1)} fusion(bf16[1,32,256]{2,0,1:T(2,128)(2,1)S(1)} %copy.47, bf16[64,32,256]{2,0,1:T(8,128)(2,1)} %bitcast.17, bf16[1,32,256]{2,0,1:T(2,128)(2,1)S(1)} %copy.46), kind=kLoop, calls=%fused_computation.8 | loop fusion | flops 3244032 | bytes 2162688 | tf_op jit(solution)/shard_map/concatenate | solution.py:345
  128.2 6.7 %all-to-all-done.5.parts_ref = bf16[64,8,128]{2,1,0:T(8,128)(2,1)S(1)} async-done(((bf16[64,8,128]{2,1,0:T(8,128)(2,1)}), bf16[64,8,128]{2,1,0:T(8,128)(2,1)S(1)}, u32[]{:S(2)}, u32[]{:S(2)}) %all-to-all-start.5) | async-done | bytes 131104 | tf_op jit(solution)/shard_map/all_to_all | solution.py:370
  135.9 4.5 %all-to-all-start.6 = ((bf16[64,8,128]{2,1,0:T(8,128)(2,1)}), bf16[64,8,128]{2,1,0:T(8,128)(2,1)S(1)}, u32[]{:S(2)}, u32[]{:S(2)}) async-start(bf16[64,8,128]{2,1,0:T(8,128)(2,1)} %get-tuple-element.71), calls=%async_computation.6 | async-start | bytes 262144 | tf_op jit(solution)/shard_map/all_to_all | solution.py:370
  141.8 10.0 %all-to-all-done.6.spec_ref = bf16[64,8,128]{2,1,0:T(8,128)(2,1)S(1)} async-done(((bf16[64,8,128]{2,1,0:T(8,128)(2,1)}), bf16[64,8,128]{2,1,0:T(8,128)(2,1)S(1)}, u32[]{:S(2)}, u32[]{:S(2)}) %all-to-all-start.6) | async-done | bytes 131104 | tf_op jit(solution)/shard_map/all_to_all | solution.py:370
  153.4 4.5 %all-to-all-start.7 = ((bf16[16,2,64,256]{3,2,1,0:T(8,128)(2,1)}), bf16[16,2,64,256]{3,2,1,0:T(8,128)(2,1)}, u32[]{:S(2)}, u32[]{:S(2)}) async-start(bf16[16,2,64,256]{3,2,1,0:T(8,128)(2,1)} %to_field.3), calls=%async_computation.7 | async-start | bytes 2097152 | tf_op jit(solution)/shard_map/all_to_all | solution.py:370
  157.9 2.6 %collective-permute-start.7 = (bf16[1,2112]{1,0:T(2,128)(2,1)S(1)}, bf16[1,2112]{1,0:T(2,128)(2,1)S(1)}, u32[]{:S(2)}, u32[]{:S(2)}) collective-permute-start(bf16[1,2112]{1,0:T(2,128)(2,1)S(1)} %get-tuple-element.97), channel_id=1, source_target_pairs={{0,1},{1,2},{2,3},{4,5},{5,6},{6,7},{8,9},{9,10},{10,11},{12,13},{... | collective-permute-start | bytes 12680 | tf_op jit(solution)/shard_map/ppermute | solution.py:336
  160.5 9.4 %collective-permute-done.7 = bf16[1,2112]{1,0:T(2,128)(2,1)S(1)} collective-permute-done((bf16[1,2112]{1,0:T(2,128)(2,1)S(1)}, bf16[1,2112]{1,0:T(2,128)(2,1)S(1)}, u32[]{:S(2)}, u32[]{:S(2)}) %collective-permute-start.7) | collective-permute-done | bytes 4256 | tf_op jit(solution)/shard_map/ppermute | solution.py:336
  171.2 3.8 %conv.3.refs_1_ = f32[32,64,256]{2,1,0:T(8,128)S(1)} custom-call(bf16[384,192]{1,0:T(8,128)(2,1)S(1)} %copy-done.6, bf16[2112,256]{1,0:T(8,128)(2,1)S(1)} %bitcast.105, bf16[2112,128]{1,0:T(8,128)(2,1)S(1)} %convolution_convert_fusion.side_ref, f32[32,128]{1,0:T(8,128)S(1)} %broadcast_in_dim.53.bias_ref), custom_call_target="tpu_custom_call" | custom-call | tf_op jit(solution)/shard_map/conv/pallas_call | solution.py:66
  176.3 2.4 %pad_maximum_fusion = f32[32,32,2,2,128]{4,3,2,1,0:T(2,128)} fusion(f32[32,32,1,2,128]{4,3,2,1,0:T(2,128)S(1)} %get-tuple-element.92, f32[32,32,1,2,128]{4,3,2,1,0:T(2,128)S(1)} %get-tuple-element.91), kind=kLoop, calls=%fused_computation.6 | loop fusion | flops 524288 | bytes 4194304 | tf_op jit(solution)/shard_map/stack | solution.py:383
  178.7 2.4 %add_field.1 = f32[32,64,256]{2,1,0:T(8,128)} custom-call(bf16[32,64,256]{2,1,0:T(8,128)(2,1)} %bitcast.25.refs_0_, f32[32,64,256]{2,1,0:T(8,128)S(1)} %conv.3.refs_1_), custom_call_target="tpu_custom_call" | custom-call | tf_op jit(solution)/shard_map/add_field/pallas_call | solution.py:159
  (82 shorter events, 20.1 us)
Async XLA Ops:
  0.6 7.5 %copy-start.8 = (bf16[1,32,64,256]{3,2,1,0:T(8,128)(2,1)S(1)}, bf16[1,32,64,256]{3,2,1,0:T(8,128)(2,1)}, u32[]{:S(2)}) copy-start(bf16[1,32,64,256]{3,2,1,0:T(8,128)(2,1)} %param.12) | copy-start | bytes 3145732
  0.6 13.6 %copy-start.10 = (bf16[256,1024]{1,0:T(8,128)(2,1)S(1)}, bf16[256,1024]{1,0:T(8,128)(2,1)}, u32[]{:S(2)}) copy-start(bf16[256,1024]{1,0:T(8,128)(2,1)} %constant.28.clone) | copy-start | bytes 1572868
  0.7 23.5 %all-to-all-start = ((bf16[16,2,64,256]{3,2,1,0:T(8,128)(2,1)}), bf16[16,2,64,256]{3,2,1,0:T(8,128)(2,1)}, u32[]{:S(2)}, u32[]{:S(2)}) async-start(bf16[16,2,64,256]{3,2,1,0:T(8,128)(2,1)} %bitcast.112), calls=%async_computation | async-start | bytes 2097152 | tf_op jit(solution)/shard_map/all_to_all | solution.py:370
  8.1 6.2 %copy-start.13 = (bf16[512,256]{1,0:T(8,128)(2,1)S(1)}, bf16[512,256]{1,0:T(8,128)(2,1)}, u32[]{:S(2)}) copy-start(bf16[512,256]{1,0:T(8,128)(2,1)} %constant.29.clone) | copy-start | bytes 786436
  8.7 13.6 %copy-start.7 = (bf16[1,32,64,256]{3,1,2,0:T(8,128)(2,1)}, bf16[1,32,64,256]{3,1,2,0:T(8,128)(2,1)S(1)}, u32[]{:S(2)}) copy-start(bf16[1,32,64,256]{3,1,2,0:T(8,128)(2,1)S(1)} %copy.83) | copy-start | bytes 3145732
  8.8 11.6 %collective-permute-start = (bf16[32,256]{1,0:T(8,128)(2,1)S(1)}, bf16[32,256]{1,0:T(8,128)(2,1)S(1)}, u32[]{:S(2)}, u32[]{:S(2)}) collective-permute-start(bf16[32,256]{1,0:T(8,128)(2,1)S(1)} %get-tuple-element.87), channel_id=1, source_target_pairs={{0,4},{4,8},{8,12},{12,16},{16,20},{20,24},{24,28},{28,32},{32,36}... | collective-permute-start | bytes 49160 | tf_op jit(solution)/shard_map/ppermute | solution.py:336
  12.3 10.0 %collective-permute-start.1 = (bf16[32,256]{1,0:T(8,128)(2,1)S(1)}, bf16[32,256]{1,0:T(8,128)(2,1)S(1)}, u32[]{:S(2)}, u32[]{:S(2)}) collective-permute-start(bf16[32,256]{1,0:T(8,128)(2,1)S(1)} %get-tuple-element.88), channel_id=1, source_target_pairs={{4,0},{8,4},{12,8},{16,12},{20,16},{24,20},{28,24},{32,28},{36,32}... | collective-permute-start | bytes 49160 | tf_op jit(solution)/shard_map/ppermute | solution.py:336
  14.3 9.8 %copy-start.2 = (bf16[256,1024]{1,0:T(8,128)(2,1)}, bf16[256,1024]{1,0:T(8,128)(2,1)S(1)}, u32[]{:S(2)}) copy-start(bf16[256,1024]{1,0:T(8,128)(2,1)S(1)} %broadcast_select_fusion.1.x_ref) | copy-start | bytes 1572868
  14.4 9.8 %copy-start.4 = (bf16[512,256]{1,0:T(8,128)(2,1)}, bf16[512,256]{1,0:T(8,128)(2,1)S(1)}, u32[]{:S(2)}) copy-start(bf16[512,256]{1,0:T(8,128)(2,1)S(1)} %broadcast_select_fusion.3.y_ref) | copy-start | bytes 786436
  14.4 9.3 %copy-start.14 = (bf16[2,256]{1,0:T(2,128)(2,1)S(1)}, bf16[2,256]{1,0:T(2,128)(2,1)}, u32[]{:S(2)}) copy-start(bf16[2,256]{1,0:T(2,128)(2,1)} %constant.32.clone) | copy-start | bytes 3076
  24.1 32.0 %copy-start.12 = (bf16[256,512]{1,0:T(8,128)(2,1)S(1)}, bf16[256,512]{1,0:T(8,128)(2,1)}, u32[]{:S(2)}) copy-start(bf16[256,512]{1,0:T(8,128)(2,1)} %constant.31.clone) | copy-start | bytes 786436
  27.1 22.1 %all-to-all-start.1 = ((bf16[64,8,128]{2,1,0:T(8,128)(2,1)}), bf16[64,8,128]{2,1,0:T(8,128)(2,1)S(1)}, u32[]{:S(2)}, u32[]{:S(2)}) async-start(bf16[64,8,128]{2,1,0:T(8,128)(2,1)} %to_modes.2), calls=%async_computation.1 | async-start | bytes 262144 | tf_op jit(solution)/shard_map/all_to_all | solution.py:370
  39.1 28.7 %copy-start = (bf16[1024,256]{1,0:T(8,128)(2,1)}, bf16[1024,256]{1,0:T(8,128)(2,1)S(1)}, u32[]{:S(2)}) copy-start(bf16[1024,256]{1,0:T(8,128)(2,1)S(1)} %broadcast_select_fusion.x_ref) | copy-start | bytes 1572868
  50.3 15.8 %all-to-all-start.2 = ((bf16[64,8,128]{2,1,0:T(8,128)(2,1)}), bf16[64,8,128]{2,1,0:T(8,128)(2,1)S(1)}, u32[]{:S(2)}, u32[]{:S(2)}) async-start(bf16[64,8,128]{2,1,0:T(8,128)(2,1)} %get-tuple-element.48), calls=%async_computation.2 | async-start | bytes 262144 | tf_op jit(solution)/shard_map/all_to_all | solution.py:370
  54.8 12.9 %collective-permute-start.2 = (bf16[1,2112]{1,0:T(2,128)(2,1)S(1)}, bf16[1,2112]{1,0:T(2,128)(2,1)S(1)}, u32[]{:S(2)}, u32[]{:S(2)}) collective-permute-start(bf16[1,2112]{1,0:T(2,128)(2,1)S(1)} %get-tuple-element.100), channel_id=1, source_target_pairs={{1,0},{2,1},{3,2},{5,4},{6,5},{7,6},{9,8},{10,9},{11,10},{13,12},{... | collective-permute-start | bytes 12680 | tf_op jit(solution)/shard_map/ppermute | solution.py:336
  56.2 18.7 %copy-start.11 = (bf16[9,32,32]{2,1,0:T(8,128)(2,1)S(1)}, bf16[9,32,32]{2,1,0:T(8,128)(2,1)}, u32[]{:S(2)}) copy-start(bf16[9,32,32]{2,1,0:T(8,128)(2,1)} %param.14) | copy-start | bytes 55300
  56.2 28.0 %copy-start.15 = (bf16[2,128]{1,0:T(2,128)(2,1)S(1)}, bf16[2,128]{1,0:T(2,128)(2,1)}, u32[]{:S(2)}) copy-start(bf16[2,128]{1,0:T(2,128)(2,1)} %constant.33.clone) | copy-start | bytes 1540
  56.2 28.4 %copy-start.16 = (f32[32]{0:T(128)S(1)}, f32[32]{0:T(128)}, u32[]{:S(2)}) copy-start(f32[32]{0:T(128)} %param.15) | copy-start | bytes 388
  67.8 20.7 %all-to-all-start.3 = ((bf16[16,2,64,256]{3,2,1,0:T(8,128)(2,1)}), bf16[16,2,64,256]{3,2,1,0:T(8,128)(2,1)}, u32[]{:S(2)}, u32[]{:S(2)}) async-start(bf16[16,2,64,256]{3,2,1,0:T(8,128)(2,1)} %to_field.2), calls=%async_computation.3 | async-start | bytes 2097152 | tf_op jit(solution)/shard_map/all_to_all | solution.py:370
  72.3 11.9 %collective-permute-start.3 = (bf16[1,2112]{1,0:T(2,128)(2,1)S(1)}, bf16[1,2112]{1,0:T(2,128)(2,1)S(1)}, u32[]{:S(2)}, u32[]{:S(2)}) collective-permute-start(bf16[1,2112]{1,0:T(2,128)(2,1)S(1)} %get-tuple-element.99), channel_id=1, source_target_pairs={{0,1},{1,2},{2,3},{4,5},{5,6},{6,7},{8,9},{9,10},{10,11},{12,13},{... | collective-permute-start | bytes 12680 | tf_op jit(solution)/shard_map/ppermute | solution.py:336
  91.2 21.2 %all-to-all-start.4 = ((bf16[16,2,64,256]{3,2,1,0:T(8,128)(2,1)}), bf16[16,2,64,256]{3,2,1,0:T(8,128)(2,1)}, u32[]{:S(2)}, u32[]{:S(2)}) async-start(bf16[16,2,64,256]{3,2,1,0:T(8,128)(2,1)} %bitcast.14), calls=%async_computation.4 | async-start | bytes 2097152 | tf_op jit(solution)/shard_map/all_to_all | solution.py:370
  97.5 17.8 %collective-permute-start.4 = (bf16[32,256]{1,0:T(8,128)(2,1)S(1)}, bf16[32,256]{1,0:T(8,128)(2,1)S(1)}, u32[]{:S(2)}, u32[]{:S(2)}) collective-permute-start(bf16[32,256]{1,0:T(8,128)(2,1)S(1)} %bitcast.125), channel_id=1, source_target_pairs={{0,4},{4,8},{8,12},{12,16},{16,20},{20,24},{24,28},{28,32},{32,36}... | collective-permute-start | bytes 49160 | tf_op jit(solution)/shard_map/ppermute | solution.py:336
  101.1 11.3 %copy-start.3 = (bf16[256,1024]{1,0:T(8,128)(2,1)S(1)}, bf16[256,1024]{1,0:T(8,128)(2,1)}, u32[]{:S(2)}) copy-start(bf16[256,1024]{1,0:T(8,128)(2,1)} %copy-done.2) | copy-start | bytes 1572868
  101.1 11.3 %copy-start.5 = (bf16[512,256]{1,0:T(8,128)(2,1)S(1)}, bf16[512,256]{1,0:T(8,128)(2,1)}, u32[]{:S(2)}) copy-start(bf16[512,256]{1,0:T(8,128)(2,1)} %copy-done.4) | copy-start | bytes 786436
  101.1 14.2 %collective-permute-start.5 = (bf16[32,256]{1,0:T(8,128)(2,1)S(1)}, bf16[32,256]{1,0:T(8,128)(2,1)S(1)}, u32[]{:S(2)}, u32[]{:S(2)}) collective-permute-start(bf16[32,256]{1,0:T(8,128)(2,1)S(1)} %bitcast.123), channel_id=1, source_target_pairs={{4,0},{8,4},{12,8},{16,12},{20,16},{24,20},{28,24},{32,28},{36,32}... | collective-permute-start | bytes 49160 | tf_op jit(solution)/shard_map/ppermute | solution.py:336
  115.3 19.5 %all-to-all-start.5 = ((bf16[64,8,128]{2,1,0:T(8,128)(2,1)}), bf16[64,8,128]{2,1,0:T(8,128)(2,1)S(1)}, u32[]{:S(2)}, u32[]{:S(2)}) async-start(bf16[64,8,128]{2,1,0:T(8,128)(2,1)} %to_modes.3), calls=%async_computation.5 | async-start | bytes 262144 | tf_op jit(solution)/shard_map/all_to_all | solution.py:370
  124.0 3.1 %copy-start.9 = (bf16[32,32,2,2,128]{4,3,2,1,0:T(2,128)(2,1)S(1)}, bf16[32,32,2,2,128]{4,3,2,1,0:T(2,128)(2,1)}, u32[]{:S(2)}) copy-start(bf16[32,32,2,2,128]{4,3,2,1,0:T(2,128)(2,1)} %param.13) | copy-start | bytes 3145732
  127.1 24.6 %copy-start.1 = (bf16[1024,256]{1,0:T(8,128)(2,1)S(1)}, bf16[1024,256]{1,0:T(8,128)(2,1)}, u32[]{:S(2)}) copy-start(bf16[1024,256]{1,0:T(8,128)(2,1)} %copy-done) | copy-start | bytes 1572868
  135.9 15.8 %all-to-all-start.6 = ((bf16[64,8,128]{2,1,0:T(8,128)(2,1)}), bf16[64,8,128]{2,1,0:T(8,128)(2,1)S(1)}, u32[]{:S(2)}, u32[]{:S(2)}) async-start(bf16[64,8,128]{2,1,0:T(8,128)(2,1)} %get-tuple-element.71), calls=%async_computation.6 | async-start | bytes 262144 | tf_op jit(solution)/shard_map/all_to_all | solution.py:370
  140.5 12.9 %collective-permute-start.6 = (bf16[1,2112]{1,0:T(2,128)(2,1)S(1)}, bf16[1,2112]{1,0:T(2,128)(2,1)S(1)}, u32[]{:S(2)}, u32[]{:S(2)}) collective-permute-start(bf16[1,2112]{1,0:T(2,128)(2,1)S(1)} %get-tuple-element.98), channel_id=1, source_target_pairs={{1,0},{2,1},{3,2},{5,4},{6,5},{7,6},{9,8},{10,9},{11,10},{13,12},{... | collective-permute-start | bytes 12680 | tf_op jit(solution)/shard_map/ppermute | solution.py:336
  153.4 25.3 %all-to-all-start.7 = ((bf16[16,2,64,256]{3,2,1,0:T(8,128)(2,1)}), bf16[16,2,64,256]{3,2,1,0:T(8,128)(2,1)}, u32[]{:S(2)}, u32[]{:S(2)}) async-start(bf16[16,2,64,256]{3,2,1,0:T(8,128)(2,1)} %to_field.3), calls=%async_computation.7 | async-start | bytes 2097152 | tf_op jit(solution)/shard_map/all_to_all | solution.py:370
  157.9 11.9 %collective-permute-start.7 = (bf16[1,2112]{1,0:T(2,128)(2,1)S(1)}, bf16[1,2112]{1,0:T(2,128)(2,1)S(1)}, u32[]{:S(2)}, u32[]{:S(2)}) collective-permute-start(bf16[1,2112]{1,0:T(2,128)(2,1)S(1)} %get-tuple-element.97), channel_id=1, source_target_pairs={{0,1},{1,2},{2,3},{4,5},{5,6},{6,7},{8,9},{9,10},{10,11},{12,13},{... | collective-permute-start | bytes 12680 | tf_op jit(solution)/shard_map/ppermute | solution.py:336
  (1 other events, 0.9 us)

commit v5 on v3

--- a/solution.py
+++ b/solution.py
@@ -69,22 +69,24 @@
         out_specs=[spec] * len(outs) if many else spec,
         out_shape=[place(*out) for out in outs] if many else place(*outs),
         scratch_shapes=scratch,
-        compiler_params=pltpu.CompilerParams(vmem_limit_bytes=48 << 20),
+        compiler_params=pltpu.CompilerParams(vmem_limit_bytes=24 << 20),
         name=name,
     )(*[resident(value) for value in values])
 
 
-def forward_kernel(weighted, factor, block_ref, x_ref, y_ref, out_ref, rows_ref):
+def forward_kernel(weighted, factor, block_ref, table_ref, out_ref, rows_ref):
+    length = block_ref.shape[0] * block_ref.shape[2]
     owners, rows, _ = out_ref.shape
     _, channels, _, width = block_ref.shape
     slots = M1 // owners
     for channel in range(channels):
         block = block_ref[:, channel].reshape(-1, width)
-        spec_x = dot(x_ref[...], block)
+        spec_x = dot(table_ref[:, :length], block)
         if factor != 1.0:
             spec_x = spec_x * factor
         spec_x = spec_x.astype(BF)
-        spec = dot(spec_x[:M1], y_ref[:width]) + dot(spec_x[M1:], y_ref[width:])
+        spec = dot(spec_x[:M1], table_ref[:, length : length + 2 * M2])
+        spec = spec + dot(spec_x[M1:], table_ref[:, length + 2 * M2 :])
         spec = turn(spec, lax.axis_index("gy"), -1.0)
         if weighted:
             spec = spec * column_weight(M2)
@@ -105,14 +107,14 @@
         "to_modes",
         block,
         tables[0],
-        tables[1],
         place=jax.ShapeDtypeStruct,
     )
 
 
-def inverse_kernel(weighted, factor, spec_ref, x_ref, y_ref, out_ref, rows_ref):
+def inverse_kernel(weighted, factor, spec_ref, table_ref, out_ref, rows_ref):
     owners = spec_ref.shape[0]
     strips, channels, rows, width = out_ref.shape
+    length = strips * rows
     slots = M1 // owners
     rows_ref[...] = jnp.transpose(spec_ref[...].astype(F32), (1, 0, 2))
     for channel in range(channels):
@@ -128,9 +130,14 @@
         spec = turn(spec, lax.axis_index("gy"), 1.0)
         if weighted:
             spec = spec * column_weight(M2)
-        over_y = dot(spec.astype(BF), y_ref[...]).astype(BF)
-        over_y = jnp.concatenate([over_y[:, :width], over_y[:, width:]], axis=0)
-        total = dot(x_ref[...], over_y)
+        spec = spec.astype(BF)
+        over_y = [
+            lax.dot_general(
+                spec, table_ref[first : first + width], (((1,), (1,)), ((), ())), preferred_element_type=F32
+            ).astype(BF)
+            for first in (length, length + width)
+        ]
+        total = dot(table_ref[:length], jnp.concatenate(over_y, axis=0))
         if factor != 1.0:
             total = total * factor
         out_ref[:, channel] = total.astype(BF).reshape(strips, rows, width)
@@ -144,8 +151,7 @@
         [pltpu.VMEM((rows, owners, M2), F32)],
         "to_field",
         spec,
-        tables[2],
-        tables[3],
+        tables[1],
     )
 
 
@@ -282,11 +288,15 @@
     return swap(ends[:1], "gy", back=True), swap(ends[1:], "gy")
 
 
-def place_columns(right, left):
+def side_slots():
     place = np.zeros((2, 128), np.float32)
     place[0, 0] = place[1, 127] = 1.0
+    return place.astype(BF)
+
+
+def place_columns(right, left, slots):
     return jnp.einsum(
-        "rn,rk->nk", jnp.concatenate([right, left]), place.astype(BF), preferred_element_type=F32
+        "rn,rk->nk", jnp.concatenate([right, left]), slots, preferred_element_type=F32
     ).astype(BF)
 
 
@@ -318,31 +328,30 @@
     whole = (channels, width_x, width_y)
 
     table_x, table_y = x_table(length_x, owners), y_table(length_y, width_y)
-    live = lax.axis_index("gx") < strips
+    hold = lax.optimization_barrier
     tables = [
-        jnp.where(live, np.ascontiguousarray(table), jnp.zeros((), BF))
-        for table in (table_x, table_y, table_x.T, table_y.T)
+        jnp.asarray(np.concatenate([table_x, table_y[:width_y], table_y[width_y:]], axis=1)),
+        jnp.asarray(np.concatenate([table_x.T, table_y], axis=0)),
     ]
-    hold = lax.optimization_barrier
 
     field = field_in[0]
     block = exchange(field.reshape(share), "gx")
     above, below = across_rows(field)
     main, ends = stack_rows(field, above, below)
     weight = jnp.transpose(spectral_weight, (3, 2, 0, 1, 4))
-    block, main, ends, weight, tables = hold((block, main, ends, weight, tables))
-    parts = exchange(to_modes(block, False, 1.0, tables, owners), both)
-    parts, ends = hold((parts, ends))
+    block, ends, weight = hold((block, ends, weight))
+    parts = to_modes(block, False, 1.0, tables, owners)
+    parts, ends, taps = hold((parts, ends, conv_weight))
+    parts = exchange(parts, both)
+    right, left = across_columns(ends)
+    matrix = conv_matrix(taps)
+    parts, right, left, matrix, places = hold((parts, right, left, matrix, side_slots()))
     mixed, spec = mix(parts, weight, 1, strips)
     arrived = exchange(mixed, both)
-    right, left = across_columns(ends)
+    local = conv(matrix, main, place_columns(right, left, places), width_x)
+    arrived, local = hold((arrived, local))
     back = to_field(arrived, True, scale, tables, share)
-    back, right, left, raw, dweight = hold((back, right, left, conv_weight, spectral_weight))
     spectral = exchange(back, "gx").reshape(whole)
-    local = conv(conv_matrix(raw), main, place_columns(right, left), width_x)
-    dmatrix = conv_matrix(jnp.transpose(raw[::-1], (0, 2, 1)))
-    dweight = jnp.transpose(dweight, (3, 2, 1, 0, 4))
-    spectral, local, dmatrix, dweight = hold((spectral, local, dmatrix, dweight))
 
     pre = spectral.astype(F32) + local + conv_bias[:, None, None]
     gate = jax.nn.sigmoid(pre)
@@ -352,17 +361,21 @@
     dblock = exchange(dpre.reshape(share), "gx")
     dabove, dbelow = across_rows(dpre)
     dparts = to_modes(dblock, True, scale, tables, owners)
-    dparts, dhere, dabove, dbelow = hold((dparts, dpre, dabove, dbelow))
+    dparts, dhere, dabove, dbelow, taps, dweight = hold(
+        (dparts, dpre, dabove, dbelow, taps, spectral_weight)
+    )
     dparts = exchange(dparts, both)
+    dmatrix = conv_matrix(jnp.transpose(taps[::-1], (0, 2, 1)))
+    dweight = jnp.transpose(dweight, (3, 2, 1, 0, 4))
     dmain, dends = stack_rows(dhere, dabove, dbelow)
-    dparts, dends, dmain = hold((dparts, dends, dmain))
+    dparts, dends, dmain, dmatrix, dweight = hold((dparts, dends, dmain, dmatrix, dweight))
     dmixed, dspec = mix(dparts, dweight, -1, strips)
     darrived = exchange(dmixed, both)
     dright, dleft = across_columns(dends)
     dback = to_field(darrived, False, 1.0, tables, share)
-    dback, dright, dleft, spec, dspec = hold((dback, dright, dleft, spec, dspec))
+    dback, dright, dleft, places, spec, dspec = hold((dback, dright, dleft, places, spec, dspec))
     dfield = exchange(dback, "gx").reshape(whole)
-    back_local = conv(dmatrix, dmain, place_columns(dright, dleft), width_x)
+    back_local = conv(dmatrix, dmain, place_columns(dright, dleft, places), width_x)
     slots = M1 // owners
     weight_grad = weight_grads(by_mode(spec, slots), by_mode(dspec, slots))
     dfield, back_local, weight_grad = hold((dfield, back_local, weight_grad))

time: 175 us -> 174 us (level)
  starting transfers between devices: 58.4 us -> 67.2 us
  other arithmetic: 17.1 us -> 10.4 us
  blocking collectives: 21.9 us -> 18.4 us
  waiting for transfers between devices: 51.6 us -> 54.3 us
    all_to_all x7, starting transfers between devices: 36.4 us -> 45.3 us  [exchange(): return lax.all_to_all(value, axes, split_axis=0, concat_axis=0, tiled=True)]
    ppermute x8, waiting for transfers between devices: 4.62 us -> 12.8 us  [swap(): return lax.ppermute(value, axis, pairs)]
    all_to_all x7, waiting for transfers between devices: 47 us -> 41.5 us  [exchange(): return lax.all_to_all(value, axes, split_axis=0, concat_axis=0, tiled=True)]
    all_to_all x1, blocking collectives: 21.9 us -> 18.4 us  [exchange(): return lax.all_to_all(value, axes, split_axis=0, concat_axis=0, tiled=True)]
    select_n x4 -> x0, other arithmetic: 1.99 us -> none  [body(): jnp.where(live, np.ascontiguousarray(table), jnp.zeros((), BF))]
    unnamed x44 -> x32, local copies, waits for them, and re-layouts: 3.94 us -> 3.22 us
  transfers between devices with their start and end apart: 15 -> 15, of which waited for: 9 -> 10; matrix products, arithmetic and copies ran while one was open for 9% -> 5% of each run, Pallas kernels for 7% -> 6%
where the time goes in v5:
time: 174 us; the launch traced here: 173 us
  starting transfers between devices  67.2 us (39%)
  waiting for transfers between devices  54.3 us (31%)
  blocking collectives  18.4 us (11%)
  Pallas kernels  15.3 us (9%)
  other arithmetic  10.4 us (6%)
  local copies, waits for them, and re-layouts  4.79 us (3%)
    all_to_all x7, starting transfers between devices, exchange(): return lax.all_to_all(value, axes, split_axis=0, concat_axis=0, tiled=True)  45.3 us
    all_to_all x7, waiting for transfers between devices, exchange(): return lax.all_to_all(value, axes, split_axis=0, concat_axis=0, tiled=True)  41.5 us
    ppermute x8, starting transfers between devices, swap(): return lax.ppermute(value, axis, pairs)  21.9 us
    all_to_all x1, blocking collectives, exchange(): return lax.all_to_all(value, axes, split_axis=0, concat_axis=0, tiled=True)  18.4 us
    pallas_call x8, Pallas kernels, on_chip(): pl.pallas_call(kernel, in_specs=[spec] * len(values), out_specs=[spec] *...  15.3 us
    ppermute x8, waiting for transfers between devices, swap(): return lax.ppermute(value, axis, pairs)  12.8 us
    another operation x2, other arithmetic, weight_grads(): return jnp.stack([grad_real, grad_imag], axis=2)  3.62 us
  transfers between devices with their start and end apart: 15, of which 10 were waited for; matrix products, arithmetic and copies ran while one was open for 5% of the time, Pallas kernels for 6%

profile of v5, /device:TPU:1, one launch (start us, length us, event | category | flops | bytes accessed | tf_op | source)
XLA Modules:
  0.0 173.0 jit_solution(10449041722408961537)
XLA Ops:
  0.6 7.5 %all-to-all-start = ((bf16[16,2,64,256]{3,2,1,0:T(8,128)(2,1)}), bf16[16,2,64,256]{3,2,1,0:T(8,128)(2,1)S(1)}, u32[]{:S(2)}, u32[]{:S(2)}) async-start(bf16[16,2,64,256]{3,2,1,0:T(8,128)(2,1)} %bitcast.121), calls=%async_computation | async-start | bytes 2097152 | tf_op jit(solution)/shard_map/all_to_all | solution.py:304
  8.7 3.5 %collective-permute-start = (bf16[32,256]{1,0:T(8,128)(2,1)S(1)}, bf16[32,256]{1,0:T(8,128)(2,1)S(1)}, u32[]{:S(2)}, u32[]{:S(2)}) collective-permute-start(bf16[32,256]{1,0:T(8,128)(2,1)S(1)} %get-tuple-element.81), channel_id=1, source_target_pairs={{0,4},{4,8},{8,12},{12,16},{16,20},{20,24},{24,28},{28,32},{32,36}... | collective-permute-start | bytes 49160 | tf_op jit(solution)/shard_map/ppermute | solution.py:270
  12.3 1.9 %collective-permute-start.1 = (bf16[32,256]{1,0:T(8,128)(2,1)S(1)}, bf16[32,256]{1,0:T(8,128)(2,1)S(1)}, u32[]{:S(2)}, u32[]{:S(2)}) collective-permute-start(bf16[32,256]{1,0:T(8,128)(2,1)S(1)} %get-tuple-element.82), channel_id=1, source_target_pairs={{4,0},{8,4},{12,8},{16,12},{20,16},{24,20},{28,24},{32,28},{36,32}... | collective-permute-start | bytes 49160 | tf_op jit(solution)/shard_map/ppermute | solution.py:270
  14.4 6.2 %collective-permute-done = bf16[32,256]{1,0:T(8,128)(2,1)S(1)} collective-permute-done((bf16[32,256]{1,0:T(8,128)(2,1)S(1)}, bf16[32,256]{1,0:T(8,128)(2,1)S(1)}, u32[]{:S(2)}, u32[]{:S(2)}) %collective-permute-start) | collective-permute-done | bytes 16416 | tf_op jit(solution)/shard_map/ppermute | solution.py:270
  20.6 1.7 collective-permute-done.1
  25.1 1.7 to_modes.2
  26.8 9.8 %all-to-all-start.1 = ((bf16[64,8,128]{2,1,0:T(8,128)(2,1)}), bf16[64,8,128]{2,1,0:T(8,128)(2,1)S(1)}, u32[]{:S(2)}, u32[]{:S(2)}) async-start(bf16[64,8,128]{2,1,0:T(8,128)(2,1)} %to_modes.2), calls=%async_computation.1 | async-start | bytes 262144 | tf_op jit(solution)/shard_map/all_to_all | solution.py:304
  36.6 4.2 %collective-permute-start.3 = (bf16[1,2112]{1,0:T(2,128)(2,1)S(1)}, bf16[1,2112]{1,0:T(2,128)(2,1)S(1)}, u32[]{:S(2)}, u32[]{:S(2)}) collective-permute-start(bf16[1,2112]{1,0:T(2,128)(2,1)S(1)} %get-tuple-element.93), channel_id=1, source_target_pairs={{0,1},{1,2},{2,3},{4,5},{5,6},{6,7},{8,9},{9,10},{10,11},{12,13},{... | collective-permute-start | bytes 12680 | tf_op jit(solution)/shard_map/ppermute | solution.py:270
  40.8 1.3 collective-permute-start.2
  42.4 4.9 %collective-permute-done.2 = bf16[1,2112]{1,0:T(2,128)(2,1)S(1)} collective-permute-done((bf16[1,2112]{1,0:T(2,128)(2,1)S(1)}, bf16[1,2112]{1,0:T(2,128)(2,1)S(1)}, u32[]{:S(2)}, u32[]{:S(2)}) %collective-permute-start.2) | collective-permute-done | bytes 4256 | tf_op jit(solution)/shard_map/ppermute | solution.py:270
  48.8 9.3 %all-to-all-start.2 = ((bf16[64,8,128]{2,1,0:T(8,128)(2,1)}), bf16[64,8,128]{2,1,0:T(8,128)(2,1)S(1)}, u32[]{:S(2)}, u32[]{:S(2)}) async-start(bf16[64,8,128]{2,1,0:T(8,128)(2,1)} %get-tuple-element.47), calls=%async_computation.2 | async-start | bytes 262144 | tf_op jit(solution)/shard_map/all_to_all | solution.py:304
  58.5 3.7 %conv.2 = f32[32,64,256]{2,1,0:T(8,128)S(1)} custom-call(bf16[384,192]{1,0:T(8,128)(2,1)S(1)} %fusion.17.matrix_ref, bf16[2112,256]{1,0:T(8,128)(2,1)S(1)} %bitcast.112, bf16[2112,128]{1,0:T(8,128)(2,1)S(1)} %convolution_convert_fusion.1.side_ref), custom_call_target="tpu_custom_call" | custom-call | tf_op jit(solution)/shard_map/conv/pallas_call | solution.py:66
  62.3 7.1 %all-to-all-done.2.spec_ref = bf16[64,8,128]{2,1,0:T(8,128)(2,1)S(1)} async-done(((bf16[64,8,128]{2,1,0:T(8,128)(2,1)}), bf16[64,8,128]{2,1,0:T(8,128)(2,1)S(1)}, u32[]{:S(2)}, u32[]{:S(2)}) %all-to-all-start.2) | async-done | bytes 131104 | tf_op jit(solution)/shard_map/all_to_all | solution.py:304
  71.2 18.4 %all_to_all.40 = bf16[16,2,64,256]{3,2,1,0:T(8,128)(2,1)S(1)} all-to-all(bf16[16,2,64,256]{3,2,1,0:T(8,128)(2,1)S(1)} %to_field.2), channel_id=1, replica_groups=mesh['dp'=4,'gx'=16,'gy'=4] {'gx'}, dimensions={0} | all-to-all | bytes 2097152 | tf_op jit(solution)/shard_map/all_to_all | solution.py:304
  89.6 2.8 %fusion.3 = (bf16[32,64,256]{2,1,0:T(8,128)(2,1)}, f32[1,32,64,256]{3,2,1,0:T(8,128)}) fusion(f32[32,64,256]{2,1,0:T(8,128)S(1)} %conv.2, bf16[1,32,64,256]{3,2,1,0:T(8,128)(2,1)S(1)} %copy-done.8, bf16[16,2,64,256]{3,2,1,0:T(8,128)(2,1)S(1)} %all_to_all.40, f32[32]{0:T(128)S(1)} %copy-done.13), kind=kLoop, calls=%fused_computation.9 | loop fusion | flops 7340032 | bytes 7340160 | tf_op jit(solution)/shard_map/convert_element_type | solution.py:359
  92.4 4.7 %all-to-all-start.4 = ((bf16[16,2,64,256]{3,2,1,0:T(8,128)(2,1)}), bf16[16,2,64,256]{3,2,1,0:T(8,128)(2,1)S(1)}, u32[]{:S(2)}, u32[]{:S(2)}) async-start(bf16[16,2,64,256]{3,2,1,0:T(8,128)(2,1)} %bitcast.117), calls=%async_computation.4 | async-start | bytes 2097152 | tf_op jit(solution)/shard_map/all_to_all | solution.py:304
  97.3 3.5 %collective-permute-start.4 = (bf16[32,256]{1,0:T(8,128)(2,1)S(1)}, bf16[32,256]{1,0:T(8,128)(2,1)S(1)}, u32[]{:S(2)}, u32[]{:S(2)}) collective-permute-start(bf16[32,256]{1,0:T(8,128)(2,1)S(1)} %bitcast.131), channel_id=1, source_target_pairs={{0,4},{4,8},{8,12},{12,16},{16,20},{20,24},{24,28},{28,32},{32,36}... | collective-permute-start | bytes 49160 | tf_op jit(solution)/shard_map/ppermute | solution.py:270
  100.8 1.9 %collective-permute-start.5 = (bf16[32,256]{1,0:T(8,128)(2,1)S(1)}, bf16[32,256]{1,0:T(8,128)(2,1)S(1)}, u32[]{:S(2)}, u32[]{:S(2)}) collective-permute-start(bf16[32,256]{1,0:T(8,128)(2,1)S(1)} %bitcast.129), channel_id=1, source_target_pairs={{4,0},{8,4},{12,8},{16,12},{20,16},{24,20},{28,24},{32,28},{36,32}... | collective-permute-start | bytes 49160 | tf_op jit(solution)/shard_map/ppermute | solution.py:270
  102.7 10.3 %all-to-all-done.4.block_ref = bf16[16,2,64,256]{3,2,1,0:T(8,128)(2,1)S(1)} async-done(((bf16[16,2,64,256]{3,2,1,0:T(8,128)(2,1)}), bf16[16,2,64,256]{3,2,1,0:T(8,128)(2,1)S(1)}, u32[]{:S(2)}, u32[]{:S(2)}) %all-to-all-start.4) | async-done | bytes 1048608 | tf_op jit(solution)/shard_map/all_to_all | solution.py:304
  113.1 1.7 to_modes.3
  114.8 5.0 %all-to-all-start.5 = ((bf16[64,8,128]{2,1,0:T(8,128)(2,1)}), bf16[64,8,128]{2,1,0:T(8,128)(2,1)S(1)}, u32[]{:S(2)}, u32[]{:S(2)}) async-start(bf16[64,8,128]{2,1,0:T(8,128)(2,1)} %to_modes.3), calls=%async_computation.5 | async-start | bytes 262144 | tf_op jit(solution)/shard_map/all_to_all | solution.py:304
  122.4 8.7 %all-to-all-done.5.parts_ref = bf16[64,8,128]{2,1,0:T(8,128)(2,1)S(1)} async-done(((bf16[64,8,128]{2,1,0:T(8,128)(2,1)}), bf16[64,8,128]{2,1,0:T(8,128)(2,1)S(1)}, u32[]{:S(2)}, u32[]{:S(2)}) %all-to-all-start.5) | async-done | bytes 131104 | tf_op jit(solution)/shard_map/all_to_all | solution.py:304
  132.1 4.5 %all-to-all-start.6 = ((bf16[64,8,128]{2,1,0:T(8,128)(2,1)}), bf16[64,8,128]{2,1,0:T(8,128)(2,1)S(1)}, u32[]{:S(2)}, u32[]{:S(2)}) async-start(bf16[64,8,128]{2,1,0:T(8,128)(2,1)} %get-tuple-element.62), calls=%async_computation.6 | async-start | bytes 262144 | tf_op jit(solution)/shard_map/all_to_all | solution.py:304
  136.7 4.2 %collective-permute-start.7 = (bf16[1,2112]{1,0:T(2,128)(2,1)S(1)}, bf16[1,2112]{1,0:T(2,128)(2,1)S(1)}, u32[]{:S(2)}, u32[]{:S(2)}) collective-permute-start(bf16[1,2112]{1,0:T(2,128)(2,1)S(1)} %get-tuple-element.91), channel_id=1, source_target_pairs={{0,1},{1,2},{2,3},{4,5},{5,6},{6,7},{8,9},{9,10},{10,11},{12,13},{... | collective-permute-start | bytes 12680 | tf_op jit(solution)/shard_map/ppermute | solution.py:270
  140.8 1.3 collective-permute-start.6
  142.1 5.8 %all-to-all-done.6.spec_ref = bf16[64,8,128]{2,1,0:T(8,128)(2,1)S(1)} async-done(((bf16[64,8,128]{2,1,0:T(8,128)(2,1)}), bf16[64,8,128]{2,1,0:T(8,128)(2,1)S(1)}, u32[]{:S(2)}, u32[]{:S(2)}) %all-to-all-start.6) | async-done | bytes 131104 | tf_op jit(solution)/shard_map/all_to_all | solution.py:304
  147.9 1.7 to_field.3
  149.6 4.5 %all-to-all-start.7 = ((bf16[16,2,64,256]{3,2,1,0:T(8,128)(2,1)}), bf16[16,2,64,256]{3,2,1,0:T(8,128)(2,1)}, u32[]{:S(2)}, u32[]{:S(2)}) async-start(bf16[16,2,64,256]{3,2,1,0:T(8,128)(2,1)} %to_field.3), calls=%async_computation.7 | async-start | bytes 2097152 | tf_op jit(solution)/shard_map/all_to_all | solution.py:304
  154.5 3.7 %conv.3 = f32[32,64,256]{2,1,0:T(8,128)S(1)} custom-call(bf16[384,192]{1,0:T(8,128)(2,1)S(1)} %fusion.20.matrix_ref, bf16[2112,256]{1,0:T(8,128)(2,1)S(1)} %bitcast.110, bf16[2112,128]{1,0:T(8,128)(2,1)S(1)} %convolution_convert_fusion.side_ref), custom_call_target="tpu_custom_call" | custom-call | tf_op jit(solution)/shard_map/conv/pallas_call | solution.py:66
  159.7 2.4 %pad_maximum_fusion = f32[32,32,2,2,128]{4,3,2,1,0:T(2,128)} fusion(f32[32,32,1,2,128]{4,3,2,1,0:T(2,128)S(1)} %get-tuple-element.86, f32[32,32,1,2,128]{4,3,2,1,0:T(2,128)S(1)} %get-tuple-element.85), kind=kLoop, calls=%fused_computation.6 | loop fusion | flops 524288 | bytes 4194304 | tf_op jit(solution)/shard_map/stack | solution.py:317
  162.1 8.1 %all-to-all-done.7 = bf16[16,2,64,256]{3,2,1,0:T(8,128)(2,1)} async-done(((bf16[16,2,64,256]{3,2,1,0:T(8,128)(2,1)}), bf16[16,2,64,256]{3,2,1,0:T(8,128)(2,1)}, u32[]{:S(2)}, u32[]{:S(2)}) %all-to-all-start.7) | async-done | bytes 1048608 | tf_op jit(solution)/shard_map/all_to_all | solution.py:304
  170.2 2.8 %add_bitcast_fusion = f32[1,32,64,256]{3,2,1,0:T(8,128)} fusion(f32[32,64,256]{2,1,0:T(8,128)S(1)} %conv.3, bf16[32,64,256]{2,1,0:T(8,128)(2,1)} %bitcast.25), kind=kLoop, calls=%fused_computation.12 | loop fusion | flops 1048576 | bytes 5242880 | tf_op jit(solution)/shard_map/broadcast_in_dim | solution.py:383
  (68 shorter events, 13.0 us)
Async XLA Ops:
  0.6 7.5 %copy-start.5 = (bf16[1,32,64,256]{3,2,1,0:T(8,128)(2,1)S(1)}, bf16[1,32,64,256]{3,2,1,0:T(8,128)(2,1)}, u32[]{:S(2)}) copy-start(bf16[1,32,64,256]{3,2,1,0:T(8,128)(2,1)} %param.10) | copy-start | bytes 3145732
  0.6 23.3 %all-to-all-start = ((bf16[16,2,64,256]{3,2,1,0:T(8,128)(2,1)}), bf16[16,2,64,256]{3,2,1,0:T(8,128)(2,1)S(1)}, u32[]{:S(2)}, u32[]{:S(2)}) async-start(bf16[16,2,64,256]{3,2,1,0:T(8,128)(2,1)} %bitcast.121), calls=%async_computation | async-start | bytes 2097152 | tf_op jit(solution)/shard_map/all_to_all | solution.py:304
  8.1 6.1 %copy-start.6 = (bf16[32,32,2,2,128]{4,3,2,1,0:T(2,128)(2,1)S(1)}, bf16[32,32,2,2,128]{4,3,2,1,0:T(2,128)(2,1)}, u32[]{:S(2)}) copy-start(bf16[32,32,2,2,128]{4,3,2,1,0:T(2,128)(2,1)} %param.11) | copy-start | bytes 3145732
  8.7 11.9 %collective-permute-start = (bf16[32,256]{1,0:T(8,128)(2,1)S(1)}, bf16[32,256]{1,0:T(8,128)(2,1)S(1)}, u32[]{:S(2)}, u32[]{:S(2)}) collective-permute-start(bf16[32,256]{1,0:T(8,128)(2,1)S(1)} %get-tuple-element.81), channel_id=1, source_target_pairs={{0,4},{4,8},{8,12},{12,16},{16,20},{20,24},{24,28},{28,32},{32,36}... | collective-permute-start | bytes 49160 | tf_op jit(solution)/shard_map/ppermute | solution.py:270
  12.3 10.2 %copy-start.11 = (bf16[2,256]{1,0:T(2,128)(2,1)S(1)}, bf16[2,256]{1,0:T(2,128)(2,1)}, u32[]{:S(2)}) copy-start(bf16[2,256]{1,0:T(2,128)(2,1)} %constant.15.clone) | copy-start | bytes 3076
  12.3 10.0 %collective-permute-start.1 = (bf16[32,256]{1,0:T(8,128)(2,1)S(1)}, bf16[32,256]{1,0:T(8,128)(2,1)S(1)}, u32[]{:S(2)}, u32[]{:S(2)}) collective-permute-start(bf16[32,256]{1,0:T(8,128)(2,1)S(1)} %get-tuple-element.82), channel_id=1, source_target_pairs={{4,0},{8,4},{12,8},{16,12},{20,16},{24,20},{28,24},{32,28},{36,32}... | collective-permute-start | bytes 49160 | tf_op jit(solution)/shard_map/ppermute | solution.py:270
  22.4 19.6 %copy-start.9 = (bf16[9,32,32]{2,1,0:T(8,128)(2,1)S(1)}, bf16[9,32,32]{2,1,0:T(8,128)(2,1)}, u32[]{:S(2)}) copy-start(bf16[9,32,32]{2,1,0:T(8,128)(2,1)} %param.12) | copy-start | bytes 55300
  24.0 1.1 copy-start.2
  25.1 33.1 %copy-start.12 = (bf16[2,128]{1,0:T(2,128)(2,1)S(1)}, bf16[2,128]{1,0:T(2,128)(2,1)}, u32[]{:S(2)}) copy-start(bf16[2,128]{1,0:T(2,128)(2,1)} %constant.16.clone) | copy-start | bytes 1540
  26.8 21.0 %all-to-all-start.1 = ((bf16[64,8,128]{2,1,0:T(8,128)(2,1)}), bf16[64,8,128]{2,1,0:T(8,128)(2,1)S(1)}, u32[]{:S(2)}, u32[]{:S(2)}) async-start(bf16[64,8,128]{2,1,0:T(8,128)(2,1)} %to_modes.2), calls=%async_computation.1 | async-start | bytes 262144 | tf_op jit(solution)/shard_map/all_to_all | solution.py:304
  36.6 5.8 %collective-permute-start.3 = (bf16[1,2112]{1,0:T(2,128)(2,1)S(1)}, bf16[1,2112]{1,0:T(2,128)(2,1)S(1)}, u32[]{:S(2)}, u32[]{:S(2)}) collective-permute-start(bf16[1,2112]{1,0:T(2,128)(2,1)S(1)} %get-tuple-element.93), channel_id=1, source_target_pairs={{0,1},{1,2},{2,3},{4,5},{5,6},{6,7},{8,9},{9,10},{10,11},{12,13},{... | collective-permute-start | bytes 12680 | tf_op jit(solution)/shard_map/ppermute | solution.py:270
  40.8 6.5 %collective-permute-start.2 = (bf16[1,2112]{1,0:T(2,128)(2,1)S(1)}, bf16[1,2112]{1,0:T(2,128)(2,1)S(1)}, u32[]{:S(2)}, u32[]{:S(2)}) collective-permute-start(bf16[1,2112]{1,0:T(2,128)(2,1)S(1)} %get-tuple-element.94), channel_id=1, source_target_pairs={{1,0},{2,1},{3,2},{5,4},{6,5},{7,6},{9,8},{10,9},{11,10},{13,12},{... | collective-permute-start | bytes 12680 | tf_op jit(solution)/shard_map/ppermute | solution.py:270
  48.8 20.5 %all-to-all-start.2 = ((bf16[64,8,128]{2,1,0:T(8,128)(2,1)}), bf16[64,8,128]{2,1,0:T(8,128)(2,1)S(1)}, u32[]{:S(2)}, u32[]{:S(2)}) async-start(bf16[64,8,128]{2,1,0:T(8,128)(2,1)} %get-tuple-element.47), calls=%async_computation.2 | async-start | bytes 262144 | tf_op jit(solution)/shard_map/all_to_all | solution.py:304
  69.4 1.1 copy-start
  70.5 19.1 %copy-start.8 = (bf16[1,32,64,256]{3,2,1,0:T(8,128)(2,1)S(1)}, bf16[1,32,64,256]{3,2,1,0:T(8,128)(2,1)}, u32[]{:S(2)}) copy-start(bf16[1,32,64,256]{3,2,1,0:T(8,128)(2,1)} %param.14) | copy-start | bytes 3145732
  70.5 19.1 %copy-start.13 = (f32[32]{0:T(128)S(1)}, f32[32]{0:T(128)}, u32[]{:S(2)}) copy-start(f32[32]{0:T(128)} %param.13) | copy-start | bytes 388
  92.4 4.8 %copy-start.4 = (bf16[32,64,256]{2,1,0:T(8,128)(2,1)S(1)}, bf16[32,64,256]{2,1,0:T(8,128)(2,1)}, u32[]{:S(2)}) copy-start(bf16[32,64,256]{2,1,0:T(8,128)(2,1)} %get-tuple-element.56) | copy-start | bytes 3145732
  92.4 20.7 %copy-start.3 = (bf16[256,1536]{1,0:T(8,128)(2,1)S(1)}, bf16[256,1536]{1,0:T(8,128)(2,1)}, u32[]{:S(2)}) copy-start(bf16[256,1536]{1,0:T(8,128)(2,1)} %constant.13.clone.table_ref) | copy-start | bytes 2359300
  92.4 27.4 %copy-start.10 = (bf16[9,32,32]{2,1,0:T(8,128)(2,1)S(1)}, bf16[9,32,32]{2,1,0:T(8,128)(2,1)}, u32[]{:S(2)}) copy-start(bf16[9,32,32]{2,1,0:T(8,128)(2,1)} %param.12) | copy-start | bytes 55300
  92.4 20.7 %all-to-all-start.4 = ((bf16[16,2,64,256]{3,2,1,0:T(8,128)(2,1)}), bf16[16,2,64,256]{3,2,1,0:T(8,128)(2,1)S(1)}, u32[]{:S(2)}, u32[]{:S(2)}) async-start(bf16[16,2,64,256]{3,2,1,0:T(8,128)(2,1)} %bitcast.117), calls=%async_computation.4 | async-start | bytes 2097152 | tf_op jit(solution)/shard_map/all_to_all | solution.py:304
  97.3 17.5 %collective-permute-start.4 = (bf16[32,256]{1,0:T(8,128)(2,1)S(1)}, bf16[32,256]{1,0:T(8,128)(2,1)S(1)}, u32[]{:S(2)}, u32[]{:S(2)}) collective-permute-start(bf16[32,256]{1,0:T(8,128)(2,1)S(1)} %bitcast.131), channel_id=1, source_target_pairs={{0,4},{4,8},{8,12},{12,16},{16,20},{20,24},{24,28},{28,32},{32,36}... | collective-permute-start | bytes 49160 | tf_op jit(solution)/shard_map/ppermute | solution.py:270
  100.8 14.0 %collective-permute-start.5 = (bf16[32,256]{1,0:T(8,128)(2,1)S(1)}, bf16[32,256]{1,0:T(8,128)(2,1)S(1)}, u32[]{:S(2)}, u32[]{:S(2)}) collective-permute-start(bf16[32,256]{1,0:T(8,128)(2,1)S(1)} %bitcast.129), channel_id=1, source_target_pairs={{4,0},{8,4},{12,8},{16,12},{20,16},{24,20},{28,24},{32,28},{36,32}... | collective-permute-start | bytes 49160 | tf_op jit(solution)/shard_map/ppermute | solution.py:270
  114.8 16.2 %all-to-all-start.5 = ((bf16[64,8,128]{2,1,0:T(8,128)(2,1)}), bf16[64,8,128]{2,1,0:T(8,128)(2,1)S(1)}, u32[]{:S(2)}, u32[]{:S(2)}) async-start(bf16[64,8,128]{2,1,0:T(8,128)(2,1)} %to_modes.3), calls=%async_computation.5 | async-start | bytes 262144 | tf_op jit(solution)/shard_map/all_to_all | solution.py:304
  120.1 1.2 copy-start.7
  121.3 26.6 %copy-start.1 = (bf16[1536,256]{1,0:T(8,128)(2,1)S(1)}, bf16[1536,256]{1,0:T(8,128)(2,1)}, u32[]{:S(2)}) copy-start(bf16[1536,256]{1,0:T(8,128)(2,1)} %constant.14.clone.table_ref) | copy-start | bytes 2359300
  132.1 15.8 %all-to-all-start.6 = ((bf16[64,8,128]{2,1,0:T(8,128)(2,1)}), bf16[64,8,128]{2,1,0:T(8,128)(2,1)S(1)}, u32[]{:S(2)}, u32[]{:S(2)}) async-start(bf16[64,8,128]{2,1,0:T(8,128)(2,1)} %get-tuple-element.62), calls=%async_computation.6 | async-start | bytes 262144 | tf_op jit(solution)/shard_map/all_to_all | solution.py:304
  136.7 13.0 %collective-permute-start.7 = (bf16[1,2112]{1,0:T(2,128)(2,1)S(1)}, bf16[1,2112]{1,0:T(2,128)(2,1)S(1)}, u32[]{:S(2)}, u32[]{:S(2)}) collective-permute-start(bf16[1,2112]{1,0:T(2,128)(2,1)S(1)} %get-tuple-element.91), channel_id=1, source_target_pairs={{0,1},{1,2},{2,3},{4,5},{5,6},{6,7},{8,9},{9,10},{10,11},{12,13},{... | collective-permute-start | bytes 12680 | tf_op jit(solution)/shard_map/ppermute | solution.py:270
  140.8 8.8 %collective-permute-start.6 = (bf16[1,2112]{1,0:T(2,128)(2,1)S(1)}, bf16[1,2112]{1,0:T(2,128)(2,1)S(1)}, u32[]{:S(2)}, u32[]{:S(2)}) collective-permute-start(bf16[1,2112]{1,0:T(2,128)(2,1)S(1)} %get-tuple-element.92), channel_id=1, source_target_pairs={{1,0},{2,1},{3,2},{5,4},{6,5},{7,6},{9,8},{10,9},{11,10},{13,12},{... | collective-permute-start | bytes 12680 | tf_op jit(solution)/shard_map/ppermute | solution.py:270
  149.6 20.5 %all-to-all-start.7 = ((bf16[16,2,64,256]{3,2,1,0:T(8,128)(2,1)}), bf16[16,2,64,256]{3,2,1,0:T(8,128)(2,1)}, u32[]{:S(2)}, u32[]{:S(2)}) async-start(bf16[16,2,64,256]{3,2,1,0:T(8,128)(2,1)} %to_field.3), calls=%async_computation.7 | async-start | bytes 2097152 | tf_op jit(solution)/shard_map/all_to_all | solution.py:304

commit v6 on v5

--- a/solution.py
+++ b/solution.py
@@ -60,7 +60,7 @@
     return pltpu.with_memory_space_constraint(value, pltpu.VMEM)
 
 
-def on_chip(kernel, outs, scratch, name, *values, place=pltpu.VMEM):
+def on_chip(kernel, outs, scratch, name, *values, place=pltpu.VMEM, apart=()):
     spec = pl.BlockSpec(memory_space=pltpu.VMEM)
     many = isinstance(outs, list)
     return pl.pallas_call(
@@ -71,7 +71,7 @@
         scratch_shapes=scratch,
         compiler_params=pltpu.CompilerParams(vmem_limit_bytes=24 << 20),
         name=name,
-    )(*[resident(value) for value in values])
+    )(*[value if index in apart else resident(value) for index, value in enumerate(values)])
 
 
 def forward_kernel(weighted, factor, block_ref, table_ref, out_ref, rows_ref):
@@ -215,6 +215,81 @@
     return jnp.transpose(split, (2, 3, 0, 1, 4)).reshape(slots, 2, -1, kept)
 
 
+CHUNK = 4
+
+
+def gate_kernel(local_ref, field_ref, up_ref, grad_out, act_out, grad_ref, act_ref, sems):
+    copies = []
+    for place, first in enumerate(range(0, local_ref.shape[0], CHUNK)):
+        piece = pl.ds(first, CHUNK)
+        pre = field_ref[piece].astype(F32) + local_ref[piece]
+        gate = 0.5 + 0.5 * jnp.tanh(0.5 * pre)
+        grad_ref[piece] = (up_ref[piece].astype(F32) * gate * (1.0 + pre * (1.0 - gate))).astype(BF)
+        act_ref[piece] = pre * gate
+        for index, (ref, out) in enumerate(((grad_ref, grad_out), (act_ref, act_out))):
+            copies.append(pltpu.make_async_copy(ref.at[piece], out.at[piece], sems.at[index, place]))
+            copies[-1].start()
+    for copy in copies:
+        copy.wait()
+
+
+def gate_both(local, field, upstream):
+    shape = local.shape
+    vmem, hbm = pl.BlockSpec(memory_space=pltpu.VMEM), pl.BlockSpec(memory_space=pltpu.HBM)
+    return pl.pallas_call(
+        gate_kernel,
+        in_specs=[vmem] * 3,
+        out_specs=[hbm] * 2,
+        out_shape=[jax.ShapeDtypeStruct(shape, BF), jax.ShapeDtypeStruct(shape, F32)],
+        scratch_shapes=[
+            pltpu.VMEM(shape, BF),
+            pltpu.VMEM(shape, F32),
+            pltpu.SemaphoreType.DMA((2, shape[0] // CHUNK)),
+        ],
+        compiler_params=pltpu.CompilerParams(vmem_limit_bytes=24 << 20),
+        name="gate_both",
+    )(resident(local), resident(field), resident(upstream))
+
+
+def add_kernel(local_ref, field_hbm, out, field_ref, out_ref, in_sems, out_sems):
+    pieces = [pl.ds(first, CHUNK) for first in range(0, local_ref.shape[0], CHUNK)]
+    loads = [
+        pltpu.make_async_copy(field_hbm.at[piece], field_ref.at[piece], in_sems.at[place])
+        for place, piece in enumerate(pieces)
+    ]
+    stores = [
+        pltpu.make_async_copy(out_ref.at[piece], out.at[piece], out_sems.at[place])
+        for place, piece in enumerate(pieces)
+    ]
+    for load in loads:
+        load.start()
+    for piece, load, store in zip(pieces, loads, stores):
+        load.wait()
+        out_ref[piece] = field_ref[piece].astype(F32) + local_ref[piece]
+        store.start()
+    for store in stores:
+        store.wait()
+
+
+def add_field(local, field):
+    shape = local.shape
+    vmem, hbm = pl.BlockSpec(memory_space=pltpu.VMEM), pl.BlockSpec(memory_space=pltpu.HBM)
+    return pl.pallas_call(
+        add_kernel,
+        in_specs=[vmem, hbm],
+        out_specs=hbm,
+        out_shape=jax.ShapeDtypeStruct(shape, F32),
+        scratch_shapes=[
+            pltpu.VMEM(shape, BF),
+            pltpu.VMEM(shape, F32),
+            pltpu.SemaphoreType.DMA((shape[0] // CHUNK,)),
+            pltpu.SemaphoreType.DMA((shape[0] // CHUNK,)),
+        ],
+        compiler_params=pltpu.CompilerParams(vmem_limit_bytes=24 << 20),
+        name="add_field",
+    )(resident(local), pltpu.with_memory_space_constraint(field, pltpu.HBM))
+
+
 CONV_ROWS = 4
 
 
@@ -230,7 +305,7 @@
     )
 
 
-def conv_kernel(matrix_ref, main_ref, side_ref, out_ref):
+def conv_kernel(matrix_ref, main_ref, side_ref, bias_ref, out_ref):
     ins = matrix_ref.shape[1] // (CONV_ROWS + 2)
     outs, rows, width = out_ref.shape
     window = (CONV_ROWS + 2) * ins
@@ -250,15 +325,23 @@
                 low = pltpu.roll(taps[base : base + outs], 1, 1)[:, :width]
                 mid = taps[base + outs : base + 2 * outs, :width]
                 high = pltpu.roll(taps[base + 2 * outs : base + 3 * outs], full - 1, 1)[:, :width]
-                pieces.append(low + mid + high)
+                pieces.append(low + mid + high + bias_ref[:, :1])
         first = pl.multiple_of(step * tall, tall)
         out_ref[:, pl.ds(first, tall), :] = jnp.transpose(jnp.stack(pieces, axis=0), (1, 0, 2))
 
 
-def conv(matrix, main, side, rows):
+def conv(matrix, main, side, bias, rows):
     outs = matrix.shape[0] // (3 * CONV_ROWS)
     return on_chip(
-        conv_kernel, ((outs, rows, main.shape[1]), F32), [], "conv", matrix, main, side
+        conv_kernel,
+        ((outs, rows, main.shape[1]), F32),
+        [],
+        "conv",
+        matrix,
+        pltpu.with_memory_space_constraint(main, pltpu.HBM),
+        side,
+        bias,
+        apart=(1,),
     )
 
 
@@ -335,6 +418,7 @@
     ]
 
     field = field_in[0]
+    bias = jnp.broadcast_to(conv_bias[:, None], (channels, 128))
     block = exchange(field.reshape(share), "gx")
     above, below = across_rows(field)
     main, ends = stack_rows(field, above, below)
@@ -345,18 +429,16 @@
     parts = exchange(parts, both)
     right, left = across_columns(ends)
     matrix = conv_matrix(taps)
-    parts, right, left, matrix, places = hold((parts, right, left, matrix, side_slots()))
+    parts, matrix, places = hold((parts, matrix, side_slots()))
     mixed, spec = mix(parts, weight, 1, strips)
+    mixed, right, left = hold((mixed, right, left))
     arrived = exchange(mixed, both)
-    local = conv(matrix, main, place_columns(right, left, places), width_x)
+    local = conv(matrix, main, place_columns(right, left, places), bias, width_x)
     arrived, local = hold((arrived, local))
     back = to_field(arrived, True, scale, tables, share)
     spectral = exchange(back, "gx").reshape(whole)
 
-    pre = spectral.astype(F32) + local + conv_bias[:, None, None]
-    gate = jax.nn.sigmoid(pre)
-    activation = pre * gate
-    dpre = (upstream[0].astype(F32) * gate * (1.0 + pre * (1.0 - gate))).astype(BF)
+    dpre, activation = gate_both(local, spectral, upstream[0])
 
     dblock = exchange(dpre.reshape(share), "gx")
     dabove, dbelow = across_rows(dpre)
@@ -375,11 +457,11 @@
     dback = to_field(darrived, False, 1.0, tables, share)
     dback, dright, dleft, places, spec, dspec = hold((dback, dright, dleft, places, spec, dspec))
     dfield = exchange(dback, "gx").reshape(whole)
-    back_local = conv(dmatrix, dmain, place_columns(dright, dleft, places), width_x)
+    back_local = conv(dmatrix, dmain, place_columns(dright, dleft, places), jnp.zeros_like(bias), width_x)
     slots = M1 // owners
     weight_grad = weight_grads(by_mode(spec, slots), by_mode(dspec, slots))
     dfield, back_local, weight_grad = hold((dfield, back_local, weight_grad))
-    field_grad = dfield.astype(F32) + back_local
+    field_grad = add_field(back_local, dfield)
     return (activation[None], field_grad[None], weight_grad)
 
 

time: 174 us -> 171 us (0.983)
  waiting for transfers between devices: 54.3 us -> 47.1 us
  Pallas kernels: 15.3 us -> 22.2 us
  other arithmetic: 10.4 us -> 6.01 us
    ppermute x8, waiting for transfers between devices: 12.8 us -> 7.89 us  [swap(): return lax.ppermute(value, axis, pairs)]
    pallas_call x0 -> x2, Pallas kernels: none -> 4.27 us  [the longest x1 2.37 us: add_field(): pl.pallas_call(add_kernel, in_specs=[vmem, hbm], out_specs=hbm, out_shape...]
    broadcast_in_dim x1 -> x0, other arithmetic: 2.83 us -> none  [body(): return (activation[None], field_grad[None], weight_grad)]
    convert_element_type x1 -> x0, other arithmetic: 2.79 us -> none  [body(): (upstream[0].astype(F32) * gate * (1.0 + pre * (1.0 - gate))).astype(BF)]
    pallas_call x8, Pallas kernels: 15.3 us -> 18 us  [on_chip(): pl.pallas_call(kernel, in_specs=[spec] * len(values), out_specs=[spec] *...]
    all_to_all x7, waiting for transfers between devices: 41.5 us -> 39.2 us  [exchange(): return lax.all_to_all(value, axes, split_axis=0, concat_axis=0, tiled=True)]
  transfers between devices with their start and end apart: 15 -> 15, of which waited for: 10 -> 9; matrix products, arithmetic and copies ran while one was open for 5% -> 6% of each run, Pallas kernels for 6% -> 9%
where the time goes in v6:
time: 171 us; the launch traced here: 170 us
  starting transfers between devices  67.4 us (39%)
  waiting for transfers between devices  47.1 us (28%)
  Pallas kernels  22.2 us (13%)
  blocking collectives  18.5 us (11%)
  other arithmetic  6.01 us (4%)
  local copies, waits for them, and re-layouts  5.69 us (3%)
    all_to_all x7, starting transfers between devices, exchange(): return lax.all_to_all(value, axes, split_axis=0, concat_axis=0, tiled=True)  45.4 us
    all_to_all x7, waiting for transfers between devices, exchange(): return lax.all_to_all(value, axes, split_axis=0, concat_axis=0, tiled=True)  39.2 us
    ppermute x8, starting transfers between devices, swap(): return lax.ppermute(value, axis, pairs)  22 us
    all_to_all x1, blocking collectives, exchange(): return lax.all_to_all(value, axes, split_axis=0, concat_axis=0, tiled=True)  18.5 us
    pallas_call x8, Pallas kernels, on_chip(): pl.pallas_call(kernel, in_specs=[spec] * len(values), out_specs=[spec] *...  18 us
    ppermute x8, waiting for transfers between devices, swap(): return lax.ppermute(value, axis, pairs)  7.89 us
    another operation x2, other arithmetic, weight_grads(): return jnp.stack([grad_real, grad_imag], axis=2)  3.62 us
  transfers between devices with their start and end apart: 15, of which 9 were waited for; matrix products, arithmetic and copies ran while one was open for 6% of the time, Pallas kernels for 9%

profile of v6, /device:TPU:1, one launch (start us, length us, event | category | flops | bytes accessed | tf_op | source)
XLA Modules:
  0.0 169.7 jit_solution(2472900617903772509)
XLA Ops:
  0.6 7.5 %all-to-all-start = ((bf16[16,2,64,256]{3,2,1,0:T(8,128)(2,1)}), bf16[16,2,64,256]{3,2,1,0:T(8,128)(2,1)S(1)}, u32[]{:S(2)}, u32[]{:S(2)}) async-start(bf16[16,2,64,256]{3,2,1,0:T(8,128)(2,1)} %bitcast.114), calls=%async_computation | async-start | bytes 2097152 | tf_op jit(solution)/shard_map/all_to_all | solution.py:387
  8.7 3.5 %collective-permute-start = (bf16[32,256]{1,0:T(8,128)(2,1)S(1)}, bf16[32,256]{1,0:T(8,128)(2,1)S(1)}, u32[]{:S(2)}, u32[]{:S(2)}) collective-permute-start(bf16[32,256]{1,0:T(8,128)(2,1)S(1)} %get-tuple-element.85), channel_id=1, source_target_pairs={{0,4},{4,8},{8,12},{12,16},{16,20},{20,24},{24,28},{28,32},{32,36}... | collective-permute-start | bytes 49160 | tf_op jit(solution)/shard_map/ppermute | solution.py:353
  12.3 1.9 %collective-permute-start.1 = (bf16[32,256]{1,0:T(8,128)(2,1)S(1)}, bf16[32,256]{1,0:T(8,128)(2,1)S(1)}, u32[]{:S(2)}, u32[]{:S(2)}) collective-permute-start(bf16[32,256]{1,0:T(8,128)(2,1)S(1)} %get-tuple-element.86), channel_id=1, source_target_pairs={{4,0},{8,4},{12,8},{16,12},{20,16},{24,20},{28,24},{32,28},{36,32}... | collective-permute-start | bytes 49160 | tf_op jit(solution)/shard_map/ppermute | solution.py:353
  14.4 6.2 %collective-permute-done = bf16[32,256]{1,0:T(8,128)(2,1)S(1)} collective-permute-done((bf16[32,256]{1,0:T(8,128)(2,1)S(1)}, bf16[32,256]{1,0:T(8,128)(2,1)S(1)}, u32[]{:S(2)}, u32[]{:S(2)}) %collective-permute-start) | collective-permute-done | bytes 16416 | tf_op jit(solution)/shard_map/ppermute | solution.py:353
  20.6 1.7 collective-permute-done.1
  24.0 1.7 to_modes.2
  25.6 10.9 %all-to-all-start.1 = ((bf16[64,8,128]{2,1,0:T(8,128)(2,1)}), bf16[64,8,128]{2,1,0:T(8,128)(2,1)S(1)}, u32[]{:S(2)}, u32[]{:S(2)}) async-start(bf16[64,8,128]{2,1,0:T(8,128)(2,1)} %to_modes.2), calls=%async_computation.1 | async-start | bytes 262144 | tf_op jit(solution)/shard_map/all_to_all | solution.py:387
  36.5 4.2 %collective-permute-start.3 = (bf16[1,2112]{1,0:T(2,128)(2,1)S(1)}, bf16[1,2112]{1,0:T(2,128)(2,1)S(1)}, u32[]{:S(2)}, u32[]{:S(2)}) collective-permute-start(bf16[1,2112]{1,0:T(2,128)(2,1)S(1)} %get-tuple-element.97), channel_id=1, source_target_pairs={{0,1},{1,2},{2,3},{4,5},{5,6},{6,7},{8,9},{9,10},{10,11},{12,13},{... | collective-permute-start | bytes 12680 | tf_op jit(solution)/shard_map/ppermute | solution.py:353
  40.7 1.3 collective-permute-start.2
  42.3 5.4 %all-to-all-done.1.parts_ref = bf16[64,8,128]{2,1,0:T(8,128)(2,1)S(1)} async-done(((bf16[64,8,128]{2,1,0:T(8,128)(2,1)}), bf16[64,8,128]{2,1,0:T(8,128)(2,1)S(1)}, u32[]{:S(2)}, u32[]{:S(2)}) %all-to-all-start.1) | async-done | bytes 131104 | tf_op jit(solution)/shard_map/all_to_all | solution.py:387
  48.8 8.3 %all-to-all-start.2 = ((bf16[64,8,128]{2,1,0:T(8,128)(2,1)}), bf16[64,8,128]{2,1,0:T(8,128)(2,1)S(1)}, u32[]{:S(2)}, u32[]{:S(2)}) async-start(bf16[64,8,128]{2,1,0:T(8,128)(2,1)} %get-tuple-element.51), calls=%async_computation.2 | async-start | bytes 262144 | tf_op jit(solution)/shard_map/all_to_all | solution.py:387
  57.5 5.1 %conv.2.local_ref = f32[32,64,256]{2,1,0:T(8,128)S(1)} custom-call(bf16[384,192]{1,0:T(8,128)(2,1)S(1)} %fusion.14.matrix_ref, bf16[2112,256]{1,0:T(8,128)(2,1)} %bitcast.111, bf16[2112,128]{1,0:T(8,128)(2,1)S(1)} %convolution_convert_fusion.1.side_ref, f32[32,128]{1,0:T(8,128)S(1)} %broadcast_in_dim.29.bias_ref), custom_call_target="tpu_custom_call" | custom-call | tf_op jit(solution)/shard_map/conv/pallas_call | solution.py:66
  62.6 5.6 %all-to-all-done.2.spec_ref = bf16[64,8,128]{2,1,0:T(8,128)(2,1)S(1)} async-done(((bf16[64,8,128]{2,1,0:T(8,128)(2,1)}), bf16[64,8,128]{2,1,0:T(8,128)(2,1)S(1)}, u32[]{:S(2)}, u32[]{:S(2)}) %all-to-all-start.2) | async-done | bytes 131104 | tf_op jit(solution)/shard_map/all_to_all | solution.py:387
  69.0 18.5 %all_to_all.40 = bf16[16,2,64,256]{3,2,1,0:T(8,128)(2,1)S(1)} all-to-all(bf16[16,2,64,256]{3,2,1,0:T(8,128)(2,1)S(1)} %to_field.2), channel_id=1, replica_groups=mesh['dp'=4,'gx'=16,'gy'=4] {'gx'}, dimensions={0} | all-to-all | bytes 2097152 | tf_op jit(solution)/shard_map/all_to_all | solution.py:387
  87.5 1.9 %gate_both.1 = (bf16[32,64,256]{2,1,0:T(8,128)(2,1)}, f32[32,64,256]{2,1,0:T(8,128)}) custom-call(f32[32,64,256]{2,1,0:T(8,128)S(1)} %conv.2.local_ref, bf16[32,64,256]{2,1,0:T(8,128)(2,1)S(1)} %bitcast.104, bf16[32,64,256]{2,1,0:T(8,128)(2,1)S(1)} %bitcast.105), custom_call_target="tpu_custom_call" | custom-call | tf_op jit(solution)/shard_map/gate_both/pallas_call | solution.py:239
  89.4 4.8 %all-to-all-start.4 = ((bf16[16,2,64,256]{3,2,1,0:T(8,128)(2,1)}), bf16[16,2,64,256]{3,2,1,0:T(8,128)(2,1)S(1)}, u32[]{:S(2)}, u32[]{:S(2)}) async-start(bf16[16,2,64,256]{3,2,1,0:T(8,128)(2,1)} %bitcast.15), calls=%async_computation.4 | async-start | bytes 2097152 | tf_op jit(solution)/shard_map/all_to_all | solution.py:387
  95.3 3.7 %collective-permute-start.4 = (bf16[32,256]{1,0:T(8,128)(2,1)S(1)}, bf16[32,256]{1,0:T(8,128)(2,1)S(1)}, u32[]{:S(2)}, u32[]{:S(2)}) collective-permute-start(bf16[32,256]{1,0:T(8,128)(2,1)S(1)} %bitcast.125), channel_id=1, source_target_pairs={{0,4},{4,8},{8,12},{12,16},{16,20},{20,24},{24,28},{28,32},{32,36}... | collective-permute-start | bytes 49160 | tf_op jit(solution)/shard_map/ppermute | solution.py:353
  99.0 1.9 %collective-permute-start.5 = (bf16[32,256]{1,0:T(8,128)(2,1)S(1)}, bf16[32,256]{1,0:T(8,128)(2,1)S(1)}, u32[]{:S(2)}, u32[]{:S(2)}) collective-permute-start(bf16[32,256]{1,0:T(8,128)(2,1)S(1)} %bitcast.123), channel_id=1, source_target_pairs={{4,0},{8,4},{12,8},{16,12},{20,16},{24,20},{28,24},{32,28},{36,32}... | collective-permute-start | bytes 49160 | tf_op jit(solution)/shard_map/ppermute | solution.py:353
  100.9 9.2 %all-to-all-done.4.block_ref = bf16[16,2,64,256]{3,2,1,0:T(8,128)(2,1)S(1)} async-done(((bf16[16,2,64,256]{3,2,1,0:T(8,128)(2,1)}), bf16[16,2,64,256]{3,2,1,0:T(8,128)(2,1)S(1)}, u32[]{:S(2)}, u32[]{:S(2)}) %all-to-all-start.4) | async-done | bytes 1048608 | tf_op jit(solution)/shard_map/all_to_all | solution.py:387
  110.1 1.7 to_modes.3
  111.8 5.0 %all-to-all-start.5 = ((bf16[64,8,128]{2,1,0:T(8,128)(2,1)}), bf16[64,8,128]{2,1,0:T(8,128)(2,1)S(1)}, u32[]{:S(2)}, u32[]{:S(2)}) async-start(bf16[64,8,128]{2,1,0:T(8,128)(2,1)} %to_modes.3), calls=%async_computation.5 | async-start | bytes 262144 | tf_op jit(solution)/shard_map/all_to_all | solution.py:387
  117.1 2.0 %pad_maximum_fusion.1 = bf16[66,32,256]{2,0,1:T(8,128)(2,1)S(1)} fusion(bf16[1,32,256]{2,0,1:T(2,128)(2,1)S(1)} %copy.45, bf16[64,32,256]{2,0,1:T(8,128)(2,1)} %bitcast.17, bf16[1,32,256]{2,0,1:T(2,128)(2,1)S(1)} %copy.44), kind=kLoop, calls=%fused_computation.7 | loop fusion | flops 3244032 | bytes 2162688 | tf_op jit(solution)/shard_map/concatenate | solution.py:362
  121.8 6.3 %all-to-all-done.5.parts_ref = bf16[64,8,128]{2,1,0:T(8,128)(2,1)S(1)} async-done(((bf16[64,8,128]{2,1,0:T(8,128)(2,1)}), bf16[64,8,128]{2,1,0:T(8,128)(2,1)S(1)}, u32[]{:S(2)}, u32[]{:S(2)}) %all-to-all-start.5) | async-done | bytes 131104 | tf_op jit(solution)/shard_map/all_to_all | solution.py:387
  129.1 4.5 %all-to-all-start.6 = ((bf16[64,8,128]{2,1,0:T(8,128)(2,1)}), bf16[64,8,128]{2,1,0:T(8,128)(2,1)S(1)}, u32[]{:S(2)}, u32[]{:S(2)}) async-start(bf16[64,8,128]{2,1,0:T(8,128)(2,1)} %get-tuple-element.68), calls=%async_computation.6 | async-start | bytes 262144 | tf_op jit(solution)/shard_map/all_to_all | solution.py:387
  133.7 4.2 %collective-permute-start.7 = (bf16[1,2112]{1,0:T(2,128)(2,1)S(1)}, bf16[1,2112]{1,0:T(2,128)(2,1)S(1)}, u32[]{:S(2)}, u32[]{:S(2)}) collective-permute-start(bf16[1,2112]{1,0:T(2,128)(2,1)S(1)} %get-tuple-element.95), channel_id=1, source_target_pairs={{0,1},{1,2},{2,3},{4,5},{5,6},{6,7},{8,9},{9,10},{10,11},{12,13},{... | collective-permute-start | bytes 12680 | tf_op jit(solution)/shard_map/ppermute | solution.py:353
  139.2 5.8 %all-to-all-done.6.spec_ref = bf16[64,8,128]{2,1,0:T(8,128)(2,1)S(1)} async-done(((bf16[64,8,128]{2,1,0:T(8,128)(2,1)}), bf16[64,8,128]{2,1,0:T(8,128)(2,1)S(1)}, u32[]{:S(2)}, u32[]{:S(2)}) %all-to-all-start.6) | async-done | bytes 131104 | tf_op jit(solution)/shard_map/all_to_all | solution.py:387
  145.0 1.7 to_field.3
  146.7 4.5 %all-to-all-start.7 = ((bf16[16,2,64,256]{3,2,1,0:T(8,128)(2,1)}), bf16[16,2,64,256]{3,2,1,0:T(8,128)(2,1)}, u32[]{:S(2)}, u32[]{:S(2)}) async-start(bf16[16,2,64,256]{3,2,1,0:T(8,128)(2,1)} %to_field.3), calls=%async_computation.7 | async-start | bytes 2097152 | tf_op jit(solution)/shard_map/all_to_all | solution.py:387
  151.6 5.0 %conv.3.local_ref = f32[32,64,256]{2,1,0:T(8,128)S(1)} custom-call(bf16[384,192]{1,0:T(8,128)(2,1)S(1)} %fusion.17.matrix_ref, bf16[2112,256]{1,0:T(8,128)(2,1)} %bitcast.109, bf16[2112,128]{1,0:T(8,128)(2,1)S(1)} %convolution_convert_fusion.side_ref, f32[32,128]{1,0:T(8,128)S(1)} %broadcast_in_dim.33.bias_ref), custom_call_target="tpu_custom_call" | custom-call | tf_op jit(solution)/shard_map/conv/pallas_call | solution.py:66
  158.0 2.4 %pad_maximum_fusion = f32[32,32,2,2,128]{4,3,2,1,0:T(2,128)} fusion(f32[32,32,1,2,128]{4,3,2,1,0:T(2,128)S(1)} %get-tuple-element.90, f32[32,32,1,2,128]{4,3,2,1,0:T(2,128)S(1)} %get-tuple-element.89), kind=kLoop, calls=%fused_computation.6 | loop fusion | flops 524288 | bytes 4194304 | tf_op jit(solution)/shard_map/stack | solution.py:400
  160.4 6.8 %all-to-all-done.7 = bf16[16,2,64,256]{3,2,1,0:T(8,128)(2,1)} async-done(((bf16[16,2,64,256]{3,2,1,0:T(8,128)(2,1)}), bf16[16,2,64,256]{3,2,1,0:T(8,128)(2,1)}, u32[]{:S(2)}, u32[]{:S(2)}) %all-to-all-start.7) | async-done | bytes 1048608 | tf_op jit(solution)/shard_map/all_to_all | solution.py:387
  167.2 2.4 %add_field.1 = f32[32,64,256]{2,1,0:T(8,128)} custom-call(f32[32,64,256]{2,1,0:T(8,128)S(1)} %conv.3.local_ref, bf16[32,64,256]{2,1,0:T(8,128)(2,1)} %bitcast.25.field_hbm), custom_call_target="tpu_custom_call" | custom-call | tf_op jit(solution)/shard_map/add_field/pallas_call | solution.py:277
  (70 shorter events, 13.1 us)
Async XLA Ops:
  0.6 7.5 %copy-start.6 = (bf16[1,32,64,256]{3,2,1,0:T(8,128)(2,1)S(1)}, bf16[1,32,64,256]{3,2,1,0:T(8,128)(2,1)}, u32[]{:S(2)}) copy-start(bf16[1,32,64,256]{3,2,1,0:T(8,128)(2,1)} %param.10) | copy-start | bytes 3145732
  0.6 23.3 %all-to-all-start = ((bf16[16,2,64,256]{3,2,1,0:T(8,128)(2,1)}), bf16[16,2,64,256]{3,2,1,0:T(8,128)(2,1)S(1)}, u32[]{:S(2)}, u32[]{:S(2)}) async-start(bf16[16,2,64,256]{3,2,1,0:T(8,128)(2,1)} %bitcast.114), calls=%async_computation | async-start | bytes 2097152 | tf_op jit(solution)/shard_map/all_to_all | solution.py:387
  8.1 6.1 %copy-start.7 = (bf16[32,32,2,2,128]{4,3,2,1,0:T(2,128)(2,1)S(1)}, bf16[32,32,2,2,128]{4,3,2,1,0:T(2,128)(2,1)}, u32[]{:S(2)}) copy-start(bf16[32,32,2,2,128]{4,3,2,1,0:T(2,128)(2,1)} %param.11) | copy-start | bytes 3145732
  8.7 11.9 %collective-permute-start = (bf16[32,256]{1,0:T(8,128)(2,1)S(1)}, bf16[32,256]{1,0:T(8,128)(2,1)S(1)}, u32[]{:S(2)}, u32[]{:S(2)}) collective-permute-start(bf16[32,256]{1,0:T(8,128)(2,1)S(1)} %get-tuple-element.85), channel_id=1, source_target_pairs={{0,4},{4,8},{8,12},{12,16},{16,20},{20,24},{24,28},{28,32},{32,36}... | collective-permute-start | bytes 49160 | tf_op jit(solution)/shard_map/ppermute | solution.py:353
  12.3 10.0 %collective-permute-start.1 = (bf16[32,256]{1,0:T(8,128)(2,1)S(1)}, bf16[32,256]{1,0:T(8,128)(2,1)S(1)}, u32[]{:S(2)}, u32[]{:S(2)}) collective-permute-start(bf16[32,256]{1,0:T(8,128)(2,1)S(1)} %get-tuple-element.86), channel_id=1, source_target_pairs={{4,0},{8,4},{12,8},{16,12},{20,16},{24,20},{28,24},{32,28},{36,32}... | collective-permute-start | bytes 49160 | tf_op jit(solution)/shard_map/ppermute | solution.py:353
  14.4 9.0 %copy-start.11 = (bf16[2,256]{1,0:T(2,128)(2,1)S(1)}, bf16[2,256]{1,0:T(2,128)(2,1)}, u32[]{:S(2)}) copy-start(bf16[2,256]{1,0:T(2,128)(2,1)} %constant.15.clone) | copy-start | bytes 3076
  22.3 1.7 copy-start.1
  22.4 1.0 copy-start.5
  23.8 18.2 %copy-start.9 = (bf16[9,32,32]{2,1,0:T(8,128)(2,1)S(1)}, bf16[9,32,32]{2,1,0:T(8,128)(2,1)}, u32[]{:S(2)}) copy-start(bf16[9,32,32]{2,1,0:T(8,128)(2,1)} %param.12) | copy-start | bytes 55300
  25.6 31.4 %copy-start.12 = (bf16[2,128]{1,0:T(2,128)(2,1)S(1)}, bf16[2,128]{1,0:T(2,128)(2,1)}, u32[]{:S(2)}) copy-start(bf16[2,128]{1,0:T(2,128)(2,1)} %constant.16.clone) | copy-start | bytes 1540
  25.6 22.1 %all-to-all-start.1 = ((bf16[64,8,128]{2,1,0:T(8,128)(2,1)}), bf16[64,8,128]{2,1,0:T(8,128)(2,1)S(1)}, u32[]{:S(2)}, u32[]{:S(2)}) async-start(bf16[64,8,128]{2,1,0:T(8,128)(2,1)} %to_modes.2), calls=%async_computation.1 | async-start | bytes 262144 | tf_op jit(solution)/shard_map/all_to_all | solution.py:387
  36.5 12.2 %collective-permute-start.3 = (bf16[1,2112]{1,0:T(2,128)(2,1)S(1)}, bf16[1,2112]{1,0:T(2,128)(2,1)S(1)}, u32[]{:S(2)}, u32[]{:S(2)}) collective-permute-start(bf16[1,2112]{1,0:T(2,128)(2,1)S(1)} %get-tuple-element.97), channel_id=1, source_target_pairs={{0,1},{1,2},{2,3},{4,5},{5,6},{6,7},{8,9},{9,10},{10,11},{12,13},{... | collective-permute-start | bytes 12680 | tf_op jit(solution)/shard_map/ppermute | solution.py:353
  40.7 8.1 %collective-permute-start.2 = (bf16[1,2112]{1,0:T(2,128)(2,1)S(1)}, bf16[1,2112]{1,0:T(2,128)(2,1)S(1)}, u32[]{:S(2)}, u32[]{:S(2)}) collective-permute-start(bf16[1,2112]{1,0:T(2,128)(2,1)S(1)} %get-tuple-element.98), channel_id=1, source_target_pairs={{1,0},{2,1},{3,2},{5,4},{6,5},{7,6},{9,8},{10,9},{11,10},{13,12},{... | collective-permute-start | bytes 12680 | tf_op jit(solution)/shard_map/ppermute | solution.py:353
  42.1 15.3 %copy-start.13 = (f32[32]{0:T(128)S(1)}, f32[32]{0:T(128)}, u32[]{:S(2)}) copy-start(f32[32]{0:T(128)} %param.13) | copy-start | bytes 388
  48.8 19.5 %all-to-all-start.2 = ((bf16[64,8,128]{2,1,0:T(8,128)(2,1)}), bf16[64,8,128]{2,1,0:T(8,128)(2,1)S(1)}, u32[]{:S(2)}, u32[]{:S(2)}) async-start(bf16[64,8,128]{2,1,0:T(8,128)(2,1)} %get-tuple-element.51), calls=%async_computation.2 | async-start | bytes 262144 | tf_op jit(solution)/shard_map/all_to_all | solution.py:387
  57.5 10.7 %copy-start = (bf16[1536,256]{1,0:T(8,128)(2,1)S(1)}, bf16[1536,256]{1,0:T(8,128)(2,1)}, u32[]{:S(2)}) copy-start(bf16[1536,256]{1,0:T(8,128)(2,1)} %constant.14.clone.table_ref) | copy-start | bytes 2359300
  69.0 18.6 %copy-start.3 = (bf16[1,32,64,256]{3,2,1,0:T(8,128)(2,1)S(1)}, bf16[1,32,64,256]{3,2,1,0:T(8,128)(2,1)}, u32[]{:S(2)}) copy-start(bf16[1,32,64,256]{3,2,1,0:T(8,128)(2,1)} %param.14) | copy-start | bytes 3145732
  89.4 20.7 %copy-start.2 = (bf16[256,1536]{1,0:T(8,128)(2,1)S(1)}, bf16[256,1536]{1,0:T(8,128)(2,1)}, u32[]{:S(2)}) copy-start(bf16[256,1536]{1,0:T(8,128)(2,1)} %constant.13.clone.table_ref) | copy-start | bytes 2359300
  89.4 20.7 %all-to-all-start.4 = ((bf16[16,2,64,256]{3,2,1,0:T(8,128)(2,1)}), bf16[16,2,64,256]{3,2,1,0:T(8,128)(2,1)S(1)}, u32[]{:S(2)}, u32[]{:S(2)}) async-start(bf16[16,2,64,256]{3,2,1,0:T(8,128)(2,1)} %bitcast.15), calls=%async_computation.4 | async-start | bytes 2097152 | tf_op jit(solution)/shard_map/all_to_all | solution.py:387
  95.2 21.6 %copy-start.10 = (bf16[9,32,32]{2,1,0:T(8,128)(2,1)S(1)}, bf16[9,32,32]{2,1,0:T(8,128)(2,1)}, u32[]{:S(2)}) copy-start(bf16[9,32,32]{2,1,0:T(8,128)(2,1)} %param.12) | copy-start | bytes 55300
  95.3 16.5 %collective-permute-start.4 = (bf16[32,256]{1,0:T(8,128)(2,1)S(1)}, bf16[32,256]{1,0:T(8,128)(2,1)S(1)}, u32[]{:S(2)}, u32[]{:S(2)}) collective-permute-start(bf16[32,256]{1,0:T(8,128)(2,1)S(1)} %bitcast.125), channel_id=1, source_target_pairs={{0,4},{4,8},{8,12},{12,16},{16,20},{20,24},{24,28},{28,32},{32,36}... | collective-permute-start | bytes 49160 | tf_op jit(solution)/shard_map/ppermute | solution.py:353
  99.0 12.9 %collective-permute-start.5 = (bf16[32,256]{1,0:T(8,128)(2,1)S(1)}, bf16[32,256]{1,0:T(8,128)(2,1)S(1)}, u32[]{:S(2)}, u32[]{:S(2)}) collective-permute-start(bf16[32,256]{1,0:T(8,128)(2,1)S(1)} %bitcast.123), channel_id=1, source_target_pairs={{4,0},{8,4},{12,8},{16,12},{20,16},{24,20},{28,24},{32,28},{36,32}... | collective-permute-start | bytes 49160 | tf_op jit(solution)/shard_map/ppermute | solution.py:353
  111.8 16.3 %all-to-all-start.5 = ((bf16[64,8,128]{2,1,0:T(8,128)(2,1)}), bf16[64,8,128]{2,1,0:T(8,128)(2,1)S(1)}, u32[]{:S(2)}, u32[]{:S(2)}) async-start(bf16[64,8,128]{2,1,0:T(8,128)(2,1)} %to_modes.3), calls=%async_computation.5 | async-start | bytes 262144 | tf_op jit(solution)/shard_map/all_to_all | solution.py:387
  119.2 1.2 copy-start.8
  120.4 1.0 copy-start.4
  129.1 15.8 %all-to-all-start.6 = ((bf16[64,8,128]{2,1,0:T(8,128)(2,1)}), bf16[64,8,128]{2,1,0:T(8,128)(2,1)S(1)}, u32[]{:S(2)}, u32[]{:S(2)}) async-start(bf16[64,8,128]{2,1,0:T(8,128)(2,1)} %get-tuple-element.68), calls=%async_computation.6 | async-start | bytes 262144 | tf_op jit(solution)/shard_map/all_to_all | solution.py:387
  133.7 13.0 %collective-permute-start.7 = (bf16[1,2112]{1,0:T(2,128)(2,1)S(1)}, bf16[1,2112]{1,0:T(2,128)(2,1)S(1)}, u32[]{:S(2)}, u32[]{:S(2)}) collective-permute-start(bf16[1,2112]{1,0:T(2,128)(2,1)S(1)} %get-tuple-element.95), channel_id=1, source_target_pairs={{0,1},{1,2},{2,3},{4,5},{5,6},{6,7},{8,9},{9,10},{10,11},{12,13},{... | collective-permute-start | bytes 12680 | tf_op jit(solution)/shard_map/ppermute | solution.py:353
  137.9 8.8 %collective-permute-start.6 = (bf16[1,2112]{1,0:T(2,128)(2,1)S(1)}, bf16[1,2112]{1,0:T(2,128)(2,1)S(1)}, u32[]{:S(2)}, u32[]{:S(2)}) collective-permute-start(bf16[1,2112]{1,0:T(2,128)(2,1)S(1)} %get-tuple-element.96), channel_id=1, source_target_pairs={{1,0},{2,1},{3,2},{5,4},{6,5},{7,6},{9,8},{10,9},{11,10},{13,12},{... | collective-permute-start | bytes 12680 | tf_op jit(solution)/shard_map/ppermute | solution.py:353
  146.7 20.5 %all-to-all-start.7 = ((bf16[16,2,64,256]{3,2,1,0:T(8,128)(2,1)}), bf16[16,2,64,256]{3,2,1,0:T(8,128)(2,1)}, u32[]{:S(2)}, u32[]{:S(2)}) async-start(bf16[16,2,64,256]{3,2,1,0:T(8,128)(2,1)} %to_field.3), calls=%async_computation.7 | async-start | bytes 2097152 | tf_op jit(solution)/shard_map/all_to_all | solution.py:387

commit v7 on v6

--- a/solution.py
+++ b/solution.py
@@ -251,24 +251,15 @@
     )(resident(local), resident(field), resident(upstream))
 
 
-def add_kernel(local_ref, field_hbm, out, field_ref, out_ref, in_sems, out_sems):
-    pieces = [pl.ds(first, CHUNK) for first in range(0, local_ref.shape[0], CHUNK)]
-    loads = [
-        pltpu.make_async_copy(field_hbm.at[piece], field_ref.at[piece], in_sems.at[place])
-        for place, piece in enumerate(pieces)
-    ]
-    stores = [
-        pltpu.make_async_copy(out_ref.at[piece], out.at[piece], out_sems.at[place])
-        for place, piece in enumerate(pieces)
-    ]
-    for load in loads:
-        load.start()
-    for piece, load, store in zip(pieces, loads, stores):
-        load.wait()
+def add_kernel(local_ref, field_ref, out, out_ref, sems):
+    copies = []
+    for place, first in enumerate(range(0, local_ref.shape[0], CHUNK)):
+        piece = pl.ds(first, CHUNK)
         out_ref[piece] = field_ref[piece].astype(F32) + local_ref[piece]
-        store.start()
-    for store in stores:
-        store.wait()
+        copies.append(pltpu.make_async_copy(out_ref.at[piece], out.at[piece], sems.at[place]))
+        copies[-1].start()
+    for copy in copies:
+        copy.wait()
 
 
 def add_field(local, field):
@@ -276,18 +267,16 @@
     vmem, hbm = pl.BlockSpec(memory_space=pltpu.VMEM), pl.BlockSpec(memory_space=pltpu.HBM)
     return pl.pallas_call(
         add_kernel,
-        in_specs=[vmem, hbm],
+        in_specs=[vmem, vmem],
         out_specs=hbm,
         out_shape=jax.ShapeDtypeStruct(shape, F32),
         scratch_shapes=[
-            pltpu.VMEM(shape, BF),
             pltpu.VMEM(shape, F32),
-            pltpu.SemaphoreType.DMA((shape[0] // CHUNK,)),
             pltpu.SemaphoreType.DMA((shape[0] // CHUNK,)),
         ],
         compiler_params=pltpu.CompilerParams(vmem_limit_bytes=24 << 20),
         name="add_field",
-    )(resident(local), pltpu.with_memory_space_constraint(field, pltpu.HBM))
+    )(resident(local), resident(field))
 
 
 CONV_ROWS = 4
@@ -423,13 +412,13 @@
     above, below = across_rows(field)
     main, ends = stack_rows(field, above, below)
     weight = jnp.transpose(spectral_weight, (3, 2, 0, 1, 4))
-    block, ends, weight = hold((block, ends, weight))
+    matrix = conv_matrix(conv_weight)
+    block, ends, weight, matrix = hold((block, ends, weight, matrix))
     parts = to_modes(block, False, 1.0, tables, owners)
     parts, ends, taps = hold((parts, ends, conv_weight))
     parts = exchange(parts, both)
     right, left = across_columns(ends)
-    matrix = conv_matrix(taps)
-    parts, matrix, places = hold((parts, matrix, side_slots()))
+    parts, places = hold((parts, side_slots()))
     mixed, spec = mix(parts, weight, 1, strips)
     mixed, right, left = hold((mixed, right, left))
     arrived = exchange(mixed, both)

time: 171 us -> 169 us (0.988)
  local copies, waits for them, and re-layouts: 5.69 us -> 7.91 us
  waiting for transfers between devices: 47.1 us -> 45 us
    ppermute x8, waiting for transfers between devices: 7.89 us -> 5.37 us  [swap(): return lax.ppermute(value, axis, pairs)]
    unnamed x32, local copies, waits for them, and re-layouts: 3.07 us -> 5.3 us
  transfers between devices with their start and end apart: 15 -> 15, of which waited for: 9 -> 9; matrix products, arithmetic and copies ran while one was open for 6% -> 7% of each run, Pallas kernels for 9% -> 9%
where the time goes in v7:
time: 169 us; the launch traced here: 168 us
  starting transfers between devices  66.6 us (39%)
  waiting for transfers between devices  45 us (27%)
  Pallas kernels  21.3 us (13%)
  blocking collectives  18.5 us (11%)
  local copies, waits for them, and re-layouts  7.91 us (5%)
  other arithmetic  6.01 us (4%)
    all_to_all x7, starting transfers between devices, exchange(): return lax.all_to_all(value, axes, split_axis=0, concat_axis=0, tiled=True)  44.8 us
    all_to_all x7, waiting for transfers between devices, exchange(): return lax.all_to_all(value, axes, split_axis=0, concat_axis=0, tiled=True)  39.6 us
    ppermute x8, starting transfers between devices, swap(): return lax.ppermute(value, axis, pairs)  21.9 us
    all_to_all x1, blocking collectives, exchange(): return lax.all_to_all(value, axes, split_axis=0, concat_axis=0, tiled=True)  18.5 us
    pallas_call x8, Pallas kernels, on_chip(): pl.pallas_call(kernel, in_specs=[spec] * len(values), out_specs=[spec] *...  18 us
    ppermute x8, waiting for transfers between devices, swap(): return lax.ppermute(value, axis, pairs)  5.37 us
    unnamed x32, local copies, waits for them, and re-layouts  5.3 us
    another operation x2, other arithmetic, weight_grads(): return jnp.stack([grad_real, grad_imag], axis=2)  3.62 us
  transfers between devices with their start and end apart: 15, of which 9 were waited for; matrix products, arithmetic and copies ran while one was open for 7% of the time, Pallas kernels for 9%

profile of v7, /device:TPU:1, one launch (start us, length us, event | category | flops | bytes accessed | tf_op | source)
XLA Modules:
  0.0 168.0 jit_solution(1890873355960576093)
XLA Ops:
  0.6 7.5 %all-to-all-start = ((bf16[16,2,64,256]{3,2,1,0:T(8,128)(2,1)}), bf16[16,2,64,256]{3,2,1,0:T(8,128)(2,1)S(1)}, u32[]{:S(2)}, u32[]{:S(2)}) async-start(bf16[16,2,64,256]{3,2,1,0:T(8,128)(2,1)} %bitcast.115), calls=%async_computation | async-start | bytes 2097152 | tf_op jit(solution)/shard_map/all_to_all | solution.py:376
  9.7 3.5 %collective-permute-start = (bf16[32,256]{1,0:T(8,128)(2,1)S(1)}, bf16[32,256]{1,0:T(8,128)(2,1)S(1)}, u32[]{:S(2)}, u32[]{:S(2)}) collective-permute-start(bf16[32,256]{1,0:T(8,128)(2,1)S(1)} %get-tuple-element.85), channel_id=1, source_target_pairs={{0,4},{4,8},{8,12},{12,16},{16,20},{20,24},{24,28},{28,32},{32,36}... | collective-permute-start | bytes 49160 | tf_op jit(solution)/shard_map/ppermute | solution.py:342
  13.2 1.9 %collective-permute-start.1 = (bf16[32,256]{1,0:T(8,128)(2,1)S(1)}, bf16[32,256]{1,0:T(8,128)(2,1)S(1)}, u32[]{:S(2)}, u32[]{:S(2)}) collective-permute-start(bf16[32,256]{1,0:T(8,128)(2,1)S(1)} %get-tuple-element.86), channel_id=1, source_target_pairs={{4,0},{8,4},{12,8},{16,12},{20,16},{24,20},{28,24},{32,28},{36,32}... | collective-permute-start | bytes 49160 | tf_op jit(solution)/shard_map/ppermute | solution.py:342
  15.5 1.4 copy.80
  16.9 3.7 %collective-permute-done = bf16[32,256]{1,0:T(8,128)(2,1)S(1)} collective-permute-done((bf16[32,256]{1,0:T(8,128)(2,1)S(1)}, bf16[32,256]{1,0:T(8,128)(2,1)S(1)}, u32[]{:S(2)}, u32[]{:S(2)}) %collective-permute-start) | collective-permute-done | bytes 16416 | tf_op jit(solution)/shard_map/ppermute | solution.py:342
  20.6 1.7 collective-permute-done.1
  24.0 1.7 %to_modes.2 = bf16[64,8,128]{2,1,0:T(8,128)(2,1)} custom-call(bf16[16,2,64,256]{3,2,1,0:T(8,128)(2,1)S(1)} %all-to-all-done.block_ref, bf16[256,1536]{1,0:T(8,128)(2,1)S(1)} %copy-done.1), custom_call_target="tpu_custom_call" | custom-call | tf_op jit(solution)/shard_map/to_modes/pallas_call | solution.py:66
  25.6 10.9 %all-to-all-start.1 = ((bf16[64,8,128]{2,1,0:T(8,128)(2,1)}), bf16[64,8,128]{2,1,0:T(8,128)(2,1)S(1)}, u32[]{:S(2)}, u32[]{:S(2)}) async-start(bf16[64,8,128]{2,1,0:T(8,128)(2,1)} %to_modes.2), calls=%async_computation.1 | async-start | bytes 262144 | tf_op jit(solution)/shard_map/all_to_all | solution.py:376
  36.5 4.2 %collective-permute-start.3 = (bf16[1,2112]{1,0:T(2,128)(2,1)S(1)}, bf16[1,2112]{1,0:T(2,128)(2,1)S(1)}, u32[]{:S(2)}, u32[]{:S(2)}) collective-permute-start(bf16[1,2112]{1,0:T(2,128)(2,1)S(1)} %get-tuple-element.97), channel_id=1, source_target_pairs={{0,1},{1,2},{2,3},{4,5},{5,6},{6,7},{8,9},{9,10},{10,11},{12,13},{... | collective-permute-start | bytes 12680 | tf_op jit(solution)/shard_map/ppermute | solution.py:342
  42.0 5.7 %all-to-all-done.1.parts_ref = bf16[64,8,128]{2,1,0:T(8,128)(2,1)S(1)} async-done(((bf16[64,8,128]{2,1,0:T(8,128)(2,1)}), bf16[64,8,128]{2,1,0:T(8,128)(2,1)S(1)}, u32[]{:S(2)}, u32[]{:S(2)}) %all-to-all-start.1) | async-done | bytes 131104 | tf_op jit(solution)/shard_map/all_to_all | solution.py:376
  48.8 8.3 %all-to-all-start.2 = ((bf16[64,8,128]{2,1,0:T(8,128)(2,1)}), bf16[64,8,128]{2,1,0:T(8,128)(2,1)S(1)}, u32[]{:S(2)}, u32[]{:S(2)}) async-start(bf16[64,8,128]{2,1,0:T(8,128)(2,1)} %get-tuple-element.50), calls=%async_computation.2 | async-start | bytes 262144 | tf_op jit(solution)/shard_map/all_to_all | solution.py:376
  57.5 5.1 %conv.2.local_ref = f32[32,64,256]{2,1,0:T(8,128)S(1)} custom-call(bf16[384,192]{1,0:T(8,128)(2,1)S(1)} %fusion.14.matrix_ref, bf16[2112,256]{1,0:T(8,128)(2,1)} %bitcast.112, bf16[2112,128]{1,0:T(8,128)(2,1)S(1)} %convolution_convert_fusion.1.side_ref, f32[32,128]{1,0:T(8,128)S(1)} %broadcast_in_dim.29.bias_ref), custom_call_target="tpu_custom_call" | custom-call | tf_op jit(solution)/shard_map/conv/pallas_call | solution.py:66
  62.6 5.6 %all-to-all-done.2.spec_ref = bf16[64,8,128]{2,1,0:T(8,128)(2,1)S(1)} async-done(((bf16[64,8,128]{2,1,0:T(8,128)(2,1)}), bf16[64,8,128]{2,1,0:T(8,128)(2,1)S(1)}, u32[]{:S(2)}, u32[]{:S(2)}) %all-to-all-start.2) | async-done | bytes 131104 | tf_op jit(solution)/shard_map/all_to_all | solution.py:376
  69.0 18.5 %all_to_all.40 = bf16[16,2,64,256]{3,2,1,0:T(8,128)(2,1)S(1)} all-to-all(bf16[16,2,64,256]{3,2,1,0:T(8,128)(2,1)S(1)} %to_field.2), channel_id=1, replica_groups=mesh['dp'=4,'gx'=16,'gy'=4] {'gx'}, dimensions={0} | all-to-all | bytes 2097152 | tf_op jit(solution)/shard_map/all_to_all | solution.py:376
  87.5 1.9 %gate_both.1 = (bf16[32,64,256]{2,1,0:T(8,128)(2,1)}, f32[32,64,256]{2,1,0:T(8,128)}) custom-call(f32[32,64,256]{2,1,0:T(8,128)S(1)} %conv.2.local_ref, bf16[32,64,256]{2,1,0:T(8,128)(2,1)S(1)} %bitcast.105, bf16[32,64,256]{2,1,0:T(8,128)(2,1)S(1)} %bitcast.106), custom_call_target="tpu_custom_call" | custom-call | tf_op jit(solution)/shard_map/gate_both/pallas_call | solution.py:239
  89.4 4.8 %all-to-all-start.4 = ((bf16[16,2,64,256]{3,2,1,0:T(8,128)(2,1)}), bf16[16,2,64,256]{3,2,1,0:T(8,128)(2,1)S(1)}, u32[]{:S(2)}, u32[]{:S(2)}) async-start(bf16[16,2,64,256]{3,2,1,0:T(8,128)(2,1)} %bitcast.15), calls=%async_computation.4 | async-start | bytes 2097152 | tf_op jit(solution)/shard_map/all_to_all | solution.py:376
  95.3 3.5 %collective-permute-start.4 = (bf16[32,256]{1,0:T(8,128)(2,1)S(1)}, bf16[32,256]{1,0:T(8,128)(2,1)S(1)}, u32[]{:S(2)}, u32[]{:S(2)}) collective-permute-start(bf16[32,256]{1,0:T(8,128)(2,1)S(1)} %bitcast.126), channel_id=1, source_target_pairs={{0,4},{4,8},{8,12},{12,16},{16,20},{20,24},{24,28},{28,32},{32,36}... | collective-permute-start | bytes 49160 | tf_op jit(solution)/shard_map/ppermute | solution.py:342
  98.8 1.9 %collective-permute-start.5 = (bf16[32,256]{1,0:T(8,128)(2,1)S(1)}, bf16[32,256]{1,0:T(8,128)(2,1)S(1)}, u32[]{:S(2)}, u32[]{:S(2)}) collective-permute-start(bf16[32,256]{1,0:T(8,128)(2,1)S(1)} %bitcast.124), channel_id=1, source_target_pairs={{4,0},{8,4},{12,8},{16,12},{20,16},{24,20},{28,24},{32,28},{36,32}... | collective-permute-start | bytes 49160 | tf_op jit(solution)/shard_map/ppermute | solution.py:342
  100.7 9.4 %all-to-all-done.4.block_ref = bf16[16,2,64,256]{3,2,1,0:T(8,128)(2,1)S(1)} async-done(((bf16[16,2,64,256]{3,2,1,0:T(8,128)(2,1)}), bf16[16,2,64,256]{3,2,1,0:T(8,128)(2,1)S(1)}, u32[]{:S(2)}, u32[]{:S(2)}) %all-to-all-start.4) | async-done | bytes 1048608 | tf_op jit(solution)/shard_map/all_to_all | solution.py:376
  110.1 1.7 %to_modes.3 = bf16[64,8,128]{2,1,0:T(8,128)(2,1)} custom-call(bf16[16,2,64,256]{3,2,1,0:T(8,128)(2,1)S(1)} %all-to-all-done.4.block_ref, bf16[256,1536]{1,0:T(8,128)(2,1)S(1)} %copy-done.2), custom_call_target="tpu_custom_call" | custom-call | tf_op jit(solution)/shard_map/to_modes/pallas_call | solution.py:66
  111.8 5.0 %all-to-all-start.5 = ((bf16[64,8,128]{2,1,0:T(8,128)(2,1)}), bf16[64,8,128]{2,1,0:T(8,128)(2,1)S(1)}, u32[]{:S(2)}, u32[]{:S(2)}) async-start(bf16[64,8,128]{2,1,0:T(8,128)(2,1)} %to_modes.3), calls=%async_computation.5 | async-start | bytes 262144 | tf_op jit(solution)/shard_map/all_to_all | solution.py:376
  117.1 2.0 %pad_maximum_fusion.1 = bf16[66,32,256]{2,0,1:T(8,128)(2,1)S(1)} fusion(bf16[1,32,256]{2,0,1:T(2,128)(2,1)S(1)} %copy.45, bf16[64,32,256]{2,0,1:T(8,128)(2,1)} %bitcast.17, bf16[1,32,256]{2,0,1:T(2,128)(2,1)S(1)} %copy.44), kind=kLoop, calls=%fused_computation.7 | loop fusion | flops 3244032 | bytes 2162688 | tf_op jit(solution)/shard_map/concatenate | solution.py:351
  121.8 6.3 %all-to-all-done.5.parts_ref = bf16[64,8,128]{2,1,0:T(8,128)(2,1)S(1)} async-done(((bf16[64,8,128]{2,1,0:T(8,128)(2,1)}), bf16[64,8,128]{2,1,0:T(8,128)(2,1)S(1)}, u32[]{:S(2)}, u32[]{:S(2)}) %all-to-all-start.5) | async-done | bytes 131104 | tf_op jit(solution)/shard_map/all_to_all | solution.py:376
  129.1 4.5 %all-to-all-start.6 = ((bf16[64,8,128]{2,1,0:T(8,128)(2,1)}), bf16[64,8,128]{2,1,0:T(8,128)(2,1)S(1)}, u32[]{:S(2)}, u32[]{:S(2)}) async-start(bf16[64,8,128]{2,1,0:T(8,128)(2,1)} %get-tuple-element.68), calls=%async_computation.6 | async-start | bytes 262144 | tf_op jit(solution)/shard_map/all_to_all | solution.py:376
  133.7 4.2 %collective-permute-start.7 = (bf16[1,2112]{1,0:T(2,128)(2,1)S(1)}, bf16[1,2112]{1,0:T(2,128)(2,1)S(1)}, u32[]{:S(2)}, u32[]{:S(2)}) collective-permute-start(bf16[1,2112]{1,0:T(2,128)(2,1)S(1)} %get-tuple-element.95), channel_id=1, source_target_pairs={{0,1},{1,2},{2,3},{4,5},{5,6},{6,7},{8,9},{9,10},{10,11},{12,13},{... | collective-permute-start | bytes 12680 | tf_op jit(solution)/shard_map/ppermute | solution.py:342
  139.2 5.8 %all-to-all-done.6.spec_ref = bf16[64,8,128]{2,1,0:T(8,128)(2,1)S(1)} async-done(((bf16[64,8,128]{2,1,0:T(8,128)(2,1)}), bf16[64,8,128]{2,1,0:T(8,128)(2,1)S(1)}, u32[]{:S(2)}, u32[]{:S(2)}) %all-to-all-start.6) | async-done | bytes 131104 | tf_op jit(solution)/shard_map/all_to_all | solution.py:376
  145.0 1.7 %to_field.3 = bf16[16,2,64,256]{3,2,1,0:T(8,128)(2,1)} custom-call(bf16[64,8,128]{2,1,0:T(8,128)(2,1)S(1)} %all-to-all-done.6.spec_ref, bf16[1536,256]{1,0:T(8,128)(2,1)S(1)} %copy-done), custom_call_target="tpu_custom_call" | custom-call | tf_op jit(solution)/shard_map/to_field/pallas_call | solution.py:66
  146.7 3.9 %all-to-all-start.7 = ((bf16[16,2,64,256]{3,2,1,0:T(8,128)(2,1)}), bf16[16,2,64,256]{3,2,1,0:T(8,128)(2,1)S(1)}, u32[]{:S(2)}, u32[]{:S(2)}) async-start(bf16[16,2,64,256]{3,2,1,0:T(8,128)(2,1)} %to_field.3), calls=%async_computation.7 | async-start | bytes 2097152 | tf_op jit(solution)/shard_map/all_to_all | solution.py:376
  151.0 5.0 %conv.3.local_ref = f32[32,64,256]{2,1,0:T(8,128)S(1)} custom-call(bf16[384,192]{1,0:T(8,128)(2,1)S(1)} %fusion.17.matrix_ref, bf16[2112,256]{1,0:T(8,128)(2,1)} %bitcast.110, bf16[2112,128]{1,0:T(8,128)(2,1)S(1)} %convolution_convert_fusion.side_ref, f32[32,128]{1,0:T(8,128)S(1)} %broadcast_in_dim.33.bias_ref), custom_call_target="tpu_custom_call" | custom-call | tf_op jit(solution)/shard_map/conv/pallas_call | solution.py:66
  157.4 2.4 %pad_maximum_fusion = f32[32,32,2,2,128]{4,3,2,1,0:T(2,128)} fusion(f32[32,32,1,2,128]{4,3,2,1,0:T(2,128)S(1)} %get-tuple-element.90, f32[32,32,1,2,128]{4,3,2,1,0:T(2,128)S(1)} %get-tuple-element.89), kind=kLoop, calls=%fused_computation.6 | loop fusion | flops 524288 | bytes 4194304 | tf_op jit(solution)/shard_map/stack | solution.py:389
  159.8 6.7 %all-to-all-done.7 = bf16[16,2,64,256]{3,2,1,0:T(8,128)(2,1)S(1)} async-done(((bf16[16,2,64,256]{3,2,1,0:T(8,128)(2,1)}), bf16[16,2,64,256]{3,2,1,0:T(8,128)(2,1)S(1)}, u32[]{:S(2)}, u32[]{:S(2)}) %all-to-all-start.7) | async-done | bytes 1048608 | tf_op jit(solution)/shard_map/all_to_all | solution.py:376
  166.5 1.4 add_field.1
  (70 shorter events, 15.2 us)
Async XLA Ops:
  0.6 7.5 %copy-start.8 = (bf16[1,32,64,256]{3,2,1,0:T(8,128)(2,1)S(1)}, bf16[1,32,64,256]{3,2,1,0:T(8,128)(2,1)}, u32[]{:S(2)}) copy-start(bf16[1,32,64,256]{3,2,1,0:T(8,128)(2,1)} %param.10) | copy-start | bytes 3145732
  0.6 23.3 %all-to-all-start = ((bf16[16,2,64,256]{3,2,1,0:T(8,128)(2,1)}), bf16[16,2,64,256]{3,2,1,0:T(8,128)(2,1)S(1)}, u32[]{:S(2)}, u32[]{:S(2)}) async-start(bf16[16,2,64,256]{3,2,1,0:T(8,128)(2,1)} %bitcast.115), calls=%async_computation | async-start | bytes 2097152 | tf_op jit(solution)/shard_map/all_to_all | solution.py:376
  8.1 7.0 %copy-start.10 = (bf16[9,32,32]{2,1,0:T(8,128)(2,1)S(1)}, bf16[9,32,32]{2,1,0:T(8,128)(2,1)}, u32[]{:S(2)}) copy-start(bf16[9,32,32]{2,1,0:T(8,128)(2,1)} %param.12) | copy-start | bytes 55300
  8.7 1.0 copy-start.6
  9.7 10.9 %collective-permute-start = (bf16[32,256]{1,0:T(8,128)(2,1)S(1)}, bf16[32,256]{1,0:T(8,128)(2,1)S(1)}, u32[]{:S(2)}, u32[]{:S(2)}) collective-permute-start(bf16[32,256]{1,0:T(8,128)(2,1)S(1)} %get-tuple-element.85), channel_id=1, source_target_pairs={{0,4},{4,8},{8,12},{12,16},{16,20},{20,24},{24,28},{28,32},{32,36}... | collective-permute-start | bytes 49160 | tf_op jit(solution)/shard_map/ppermute | solution.py:342
  13.2 9.1 %collective-permute-start.1 = (bf16[32,256]{1,0:T(8,128)(2,1)S(1)}, bf16[32,256]{1,0:T(8,128)(2,1)S(1)}, u32[]{:S(2)}, u32[]{:S(2)}) collective-permute-start(bf16[32,256]{1,0:T(8,128)(2,1)S(1)} %get-tuple-element.86), channel_id=1, source_target_pairs={{4,0},{8,4},{12,8},{16,12},{20,16},{24,20},{28,24},{32,28},{36,32}... | collective-permute-start | bytes 49160 | tf_op jit(solution)/shard_map/ppermute | solution.py:342
  15.4 6.9 %copy-start.7 = (bf16[1,32,64,256]{3,1,2,0:T(8,128)(2,1)S(1)}, bf16[1,32,64,256]{3,1,2,0:T(8,128)(2,1)}, u32[]{:S(2)}) copy-start(bf16[1,32,64,256]{3,1,2,0:T(8,128)(2,1)} %copy-done.6) | copy-start | bytes 3145732
  16.9 6.5 %copy-start.11 = (bf16[2,256]{1,0:T(2,128)(2,1)S(1)}, bf16[2,256]{1,0:T(2,128)(2,1)}, u32[]{:S(2)}) copy-start(bf16[2,256]{1,0:T(2,128)(2,1)} %constant.15.clone) | copy-start | bytes 3076
  22.3 1.6 copy-start.1
  22.5 1.0 copy-start.5
  25.6 31.4 %copy-start.12 = (bf16[2,128]{1,0:T(2,128)(2,1)S(1)}, bf16[2,128]{1,0:T(2,128)(2,1)}, u32[]{:S(2)}) copy-start(bf16[2,128]{1,0:T(2,128)(2,1)} %constant.16.clone) | copy-start | bytes 1540
  25.6 31.8 %copy-start.13 = (f32[32]{0:T(128)S(1)}, f32[32]{0:T(128)}, u32[]{:S(2)}) copy-start(f32[32]{0:T(128)} %param.13) | copy-start | bytes 388
  25.6 22.1 %all-to-all-start.1 = ((bf16[64,8,128]{2,1,0:T(8,128)(2,1)}), bf16[64,8,128]{2,1,0:T(8,128)(2,1)S(1)}, u32[]{:S(2)}, u32[]{:S(2)}) async-start(bf16[64,8,128]{2,1,0:T(8,128)(2,1)} %to_modes.2), calls=%async_computation.1 | async-start | bytes 262144 | tf_op jit(solution)/shard_map/all_to_all | solution.py:376
  36.5 12.2 %collective-permute-start.3 = (bf16[1,2112]{1,0:T(2,128)(2,1)S(1)}, bf16[1,2112]{1,0:T(2,128)(2,1)S(1)}, u32[]{:S(2)}, u32[]{:S(2)}) collective-permute-start(bf16[1,2112]{1,0:T(2,128)(2,1)S(1)} %get-tuple-element.97), channel_id=1, source_target_pairs={{0,1},{1,2},{2,3},{4,5},{5,6},{6,7},{8,9},{9,10},{10,11},{12,13},{... | collective-permute-start | bytes 12680 | tf_op jit(solution)/shard_map/ppermute | solution.py:342
  40.7 8.1 %collective-permute-start.2 = (bf16[1,2112]{1,0:T(2,128)(2,1)S(1)}, bf16[1,2112]{1,0:T(2,128)(2,1)S(1)}, u32[]{:S(2)}, u32[]{:S(2)}) collective-permute-start(bf16[1,2112]{1,0:T(2,128)(2,1)S(1)} %get-tuple-element.98), channel_id=1, source_target_pairs={{1,0},{2,1},{3,2},{5,4},{6,5},{7,6},{9,8},{10,9},{11,10},{13,12},{... | collective-permute-start | bytes 12680 | tf_op jit(solution)/shard_map/ppermute | solution.py:342
  48.8 19.5 %all-to-all-start.2 = ((bf16[64,8,128]{2,1,0:T(8,128)(2,1)}), bf16[64,8,128]{2,1,0:T(8,128)(2,1)S(1)}, u32[]{:S(2)}, u32[]{:S(2)}) async-start(bf16[64,8,128]{2,1,0:T(8,128)(2,1)} %get-tuple-element.50), calls=%async_computation.2 | async-start | bytes 262144 | tf_op jit(solution)/shard_map/all_to_all | solution.py:376
  57.5 10.7 %copy-start = (bf16[1536,256]{1,0:T(8,128)(2,1)S(1)}, bf16[1536,256]{1,0:T(8,128)(2,1)}, u32[]{:S(2)}) copy-start(bf16[1536,256]{1,0:T(8,128)(2,1)} %constant.14.clone.table_ref) | copy-start | bytes 2359300
  69.0 18.6 %copy-start.3 = (bf16[1,32,64,256]{3,2,1,0:T(8,128)(2,1)S(1)}, bf16[1,32,64,256]{3,2,1,0:T(8,128)(2,1)}, u32[]{:S(2)}) copy-start(bf16[1,32,64,256]{3,2,1,0:T(8,128)(2,1)} %param.14) | copy-start | bytes 3145732
  89.4 20.7 %copy-start.2 = (bf16[256,1536]{1,0:T(8,128)(2,1)S(1)}, bf16[256,1536]{1,0:T(8,128)(2,1)}, u32[]{:S(2)}) copy-start(bf16[256,1536]{1,0:T(8,128)(2,1)} %constant.13.clone.table_ref) | copy-start | bytes 2359300
  89.4 20.7 %all-to-all-start.4 = ((bf16[16,2,64,256]{3,2,1,0:T(8,128)(2,1)}), bf16[16,2,64,256]{3,2,1,0:T(8,128)(2,1)S(1)}, u32[]{:S(2)}, u32[]{:S(2)}) async-start(bf16[16,2,64,256]{3,2,1,0:T(8,128)(2,1)} %bitcast.15), calls=%async_computation.4 | async-start | bytes 2097152 | tf_op jit(solution)/shard_map/all_to_all | solution.py:376
  95.3 16.5 %collective-permute-start.4 = (bf16[32,256]{1,0:T(8,128)(2,1)S(1)}, bf16[32,256]{1,0:T(8,128)(2,1)S(1)}, u32[]{:S(2)}, u32[]{:S(2)}) collective-permute-start(bf16[32,256]{1,0:T(8,128)(2,1)S(1)} %bitcast.126), channel_id=1, source_target_pairs={{0,4},{4,8},{8,12},{12,16},{16,20},{20,24},{24,28},{28,32},{32,36}... | collective-permute-start | bytes 49160 | tf_op jit(solution)/shard_map/ppermute | solution.py:342
  98.8 13.0 %collective-permute-start.5 = (bf16[32,256]{1,0:T(8,128)(2,1)S(1)}, bf16[32,256]{1,0:T(8,128)(2,1)S(1)}, u32[]{:S(2)}, u32[]{:S(2)}) collective-permute-start(bf16[32,256]{1,0:T(8,128)(2,1)S(1)} %bitcast.124), channel_id=1, source_target_pairs={{4,0},{8,4},{12,8},{16,12},{20,16},{24,20},{28,24},{32,28},{36,32}... | collective-permute-start | bytes 49160 | tf_op jit(solution)/shard_map/ppermute | solution.py:342
  111.8 16.3 %all-to-all-start.5 = ((bf16[64,8,128]{2,1,0:T(8,128)(2,1)}), bf16[64,8,128]{2,1,0:T(8,128)(2,1)S(1)}, u32[]{:S(2)}, u32[]{:S(2)}) async-start(bf16[64,8,128]{2,1,0:T(8,128)(2,1)} %to_modes.3), calls=%async_computation.5 | async-start | bytes 262144 | tf_op jit(solution)/shard_map/all_to_all | solution.py:376
  119.2 1.2 copy-start.9
  120.4 1.0 copy-start.4
  129.1 15.8 %all-to-all-start.6 = ((bf16[64,8,128]{2,1,0:T(8,128)(2,1)}), bf16[64,8,128]{2,1,0:T(8,128)(2,1)S(1)}, u32[]{:S(2)}, u32[]{:S(2)}) async-start(bf16[64,8,128]{2,1,0:T(8,128)(2,1)} %get-tuple-element.68), calls=%async_computation.6 | async-start | bytes 262144 | tf_op jit(solution)/shard_map/all_to_all | solution.py:376
  133.7 13.0 %collective-permute-start.7 = (bf16[1,2112]{1,0:T(2,128)(2,1)S(1)}, bf16[1,2112]{1,0:T(2,128)(2,1)S(1)}, u32[]{:S(2)}, u32[]{:S(2)}) collective-permute-start(bf16[1,2112]{1,0:T(2,128)(2,1)S(1)} %get-tuple-element.95), channel_id=1, source_target_pairs={{0,1},{1,2},{2,3},{4,5},{5,6},{6,7},{8,9},{9,10},{10,11},{12,13},{... | collective-permute-start | bytes 12680 | tf_op jit(solution)/shard_map/ppermute | solution.py:342
  137.9 8.8 %collective-permute-start.6 = (bf16[1,2112]{1,0:T(2,128)(2,1)S(1)}, bf16[1,2112]{1,0:T(2,128)(2,1)S(1)}, u32[]{:S(2)}, u32[]{:S(2)}) collective-permute-start(bf16[1,2112]{1,0:T(2,128)(2,1)S(1)} %get-tuple-element.96), channel_id=1, source_target_pairs={{1,0},{2,1},{3,2},{5,4},{6,5},{7,6},{9,8},{10,9},{11,10},{13,12},{... | collective-permute-start | bytes 12680 | tf_op jit(solution)/shard_map/ppermute | solution.py:342
  146.7 19.8 %all-to-all-start.7 = ((bf16[16,2,64,256]{3,2,1,0:T(8,128)(2,1)}), bf16[16,2,64,256]{3,2,1,0:T(8,128)(2,1)S(1)}, u32[]{:S(2)}, u32[]{:S(2)}) async-start(bf16[16,2,64,256]{3,2,1,0:T(8,128)(2,1)} %to_field.3), calls=%async_computation.7 | async-start | bytes 2097152 | tf_op jit(solution)/shard_map/all_to_all | solution.py:376

commit v8 on v7

--- a/solution.py
+++ b/solution.py
@@ -294,21 +294,32 @@
     )
 
 
-def conv_kernel(matrix_ref, main_ref, side_ref, bias_ref, out_ref):
+def conv_kernel(
+    matrix_ref, main_hbm, side_hbm, above_ref, below_ref, bias_ref, out_ref, all_ref, sems
+):
     ins = matrix_ref.shape[1] // (CONV_ROWS + 2)
     outs, rows, width = out_ref.shape
+    full = all_ref.shape[1]
     window = (CONV_ROWS + 2) * ins
     tall = 2 * CONV_ROWS
+    inner = pl.ds(ins, rows * ins)
+    copies = [
+        pltpu.make_async_copy(main_hbm, all_ref.at[inner, pl.ds(0, width)], sems.at[0]),
+        pltpu.make_async_copy(side_hbm, all_ref.at[inner, pl.ds(width, full - width)], sems.at[1]),
+    ]
+    for copy in copies:
+        copy.start()
+    all_ref[:ins, :] = above_ref[...]
+    all_ref[(rows + 1) * ins :, :] = below_ref[...]
+    for copy in copies:
+        copy.wait()
 
     @pl.loop(0, rows // tall)
     def _(step):
         pieces = []
         for part in range(tall // CONV_ROWS):
             start = pl.multiple_of((step * tall + part * CONV_ROWS) * ins, ins)
-            main = dot(matrix_ref[...], main_ref[pl.ds(start, window), :])
-            side = dot(matrix_ref[...], side_ref[pl.ds(start, window), :])
-            taps = jnp.concatenate([main, side], axis=1)
-            full = taps.shape[1]
+            taps = dot(matrix_ref[...], all_ref[pl.ds(start, window), :])
             for row in range(CONV_ROWS):
                 base = row * 3 * outs
                 low = pltpu.roll(taps[base : base + outs], 1, 1)[:, :width]
@@ -319,18 +330,29 @@
         out_ref[:, pl.ds(first, tall), :] = jnp.transpose(jnp.stack(pieces, axis=0), (1, 0, 2))
 
 
-def conv(matrix, main, side, bias, rows):
+def conv(matrix, main, side, above, below, bias):
     outs = matrix.shape[0] // (3 * CONV_ROWS)
-    return on_chip(
+    ins = above.shape[0]
+    rows, width = main.shape[0] // ins, main.shape[1]
+    vmem, hbm = pl.BlockSpec(memory_space=pltpu.VMEM), pl.BlockSpec(memory_space=pltpu.HBM)
+    return pl.pallas_call(
         conv_kernel,
-        ((outs, rows, main.shape[1]), F32),
-        [],
-        "conv",
-        matrix,
+        in_specs=[vmem, hbm, hbm, vmem, vmem, vmem],
+        out_specs=vmem,
+        out_shape=pltpu.VMEM((outs, rows, width), F32),
+        scratch_shapes=[
+            pltpu.VMEM(((rows + 2) * ins, above.shape[1]), BF),
+            pltpu.SemaphoreType.DMA((2,)),
+        ],
+        compiler_params=pltpu.CompilerParams(vmem_limit_bytes=24 << 20),
+        name="conv",
+    )(
+        resident(matrix),
         pltpu.with_memory_space_constraint(main, pltpu.HBM),
-        side,
-        bias,
-        apart=(1,),
+        pltpu.with_memory_space_constraint(side, pltpu.HBM),
+        resident(above),
+        resident(below),
+        resident(bias),
     )
 
 
@@ -342,18 +364,24 @@
     return lax.ppermute(value, axis, pairs)
 
 
-def across_rows(field):
-    return swap(field[:, -1], "gx"), swap(field[:, 0], "gx", back=True)
-
-
-def stack_rows(field, above, below):
+def by_rows(field):
     channels, rows, width = field.shape
-    main = jnp.concatenate([above[None], jnp.transpose(field, (1, 0, 2)), below[None]], axis=0)
-    main = main.reshape((rows + 2) * channels, width)
+    main = jnp.transpose(field, (1, 0, 2)).reshape(rows * channels, width)
     pick = np.zeros((2, width), np.float32)
     pick[0, 0] = pick[1, width - 1] = 1.0
     ends = jnp.einsum("ry,ny->rn", pick.astype(BF), main, preferred_element_type=F32).astype(BF)
     return main, ends
+
+
+def edge_rows(main, side, channels):
+    return (
+        jnp.concatenate([main[:channels], side[:channels]], axis=1),
+        jnp.concatenate([main[-channels:], side[-channels:]], axis=1),
+    )
+
+
+def across_rows(first, last):
+    return swap(last, "gx"), swap(first, "gx", back=True)
 
 
 def across_columns(ends):
@@ -409,47 +437,49 @@
     field = field_in[0]
     bias = jnp.broadcast_to(conv_bias[:, None], (channels, 128))
     block = exchange(field.reshape(share), "gx")
-    above, below = across_rows(field)
-    main, ends = stack_rows(field, above, below)
+    main, ends = by_rows(field)
+    right, left = across_columns(ends)
     weight = jnp.transpose(spectral_weight, (3, 2, 0, 1, 4))
     matrix = conv_matrix(conv_weight)
-    block, ends, weight, matrix = hold((block, ends, weight, matrix))
+    side = place_columns(right, left, side_slots())
+    first, last = edge_rows(main, side, channels)
+    block, first, last, weight, matrix = hold((block, first, last, weight, matrix))
     parts = to_modes(block, False, 1.0, tables, owners)
-    parts, ends, taps = hold((parts, ends, conv_weight))
+    parts, first, last = hold((parts, first, last))
     parts = exchange(parts, both)
-    right, left = across_columns(ends)
-    parts, places = hold((parts, side_slots()))
+    above, below = across_rows(first, last)
     mixed, spec = mix(parts, weight, 1, strips)
-    mixed, right, left = hold((mixed, right, left))
+    mixed, above, below = hold((mixed, above, below))
     arrived = exchange(mixed, both)
-    local = conv(matrix, main, place_columns(right, left, places), bias, width_x)
+    local = conv(matrix, main, side, above, below, bias)
     arrived, local = hold((arrived, local))
     back = to_field(arrived, True, scale, tables, share)
     spectral = exchange(back, "gx").reshape(whole)
 
     dpre, activation = gate_both(local, spectral, upstream[0])
+    dpre, taps, dweight = hold((dpre, conv_weight, spectral_weight))
 
     dblock = exchange(dpre.reshape(share), "gx")
-    dabove, dbelow = across_rows(dpre)
+    dmain, dends = by_rows(dpre)
+    dright, dleft = across_columns(dends)
+    dmatrix = conv_matrix(jnp.transpose(taps[::-1], (0, 2, 1)))
+    dblock, dmatrix, dmain = hold((dblock, dmatrix, dmain))
     dparts = to_modes(dblock, True, scale, tables, owners)
-    dparts, dhere, dabove, dbelow, taps, dweight = hold(
-        (dparts, dpre, dabove, dbelow, taps, spectral_weight)
-    )
+    dparts, dright, dleft, dweight, places = hold((dparts, dright, dleft, dweight, side_slots()))
     dparts = exchange(dparts, both)
-    dmatrix = conv_matrix(jnp.transpose(taps[::-1], (0, 2, 1)))
     dweight = jnp.transpose(dweight, (3, 2, 1, 0, 4))
-    dmain, dends = stack_rows(dhere, dabove, dbelow)
-    dparts, dends, dmain, dmatrix, dweight = hold((dparts, dends, dmain, dmatrix, dweight))
+    dside = place_columns(dright, dleft, places)
+    dabove, dbelow = across_rows(*edge_rows(dmain, dside, channels))
+    dparts, dweight = hold((dparts, dweight))
     dmixed, dspec = mix(dparts, dweight, -1, strips)
+    dmixed, dabove, dbelow = hold((dmixed, dabove, dbelow))
     darrived = exchange(dmixed, both)
-    dright, dleft = across_columns(dends)
-    dback = to_field(darrived, False, 1.0, tables, share)
-    dback, dright, dleft, places, spec, dspec = hold((dback, dright, dleft, places, spec, dspec))
-    dfield = exchange(dback, "gx").reshape(whole)
-    back_local = conv(dmatrix, dmain, place_columns(dright, dleft, places), jnp.zeros_like(bias), width_x)
+    back_local = conv(dmatrix, dmain, dside, dabove, dbelow, jnp.zeros_like(bias))
     slots = M1 // owners
     weight_grad = weight_grads(by_mode(spec, slots), by_mode(dspec, slots))
-    dfield, back_local, weight_grad = hold((dfield, back_local, weight_grad))
+    darrived, back_local, weight_grad = hold((darrived, back_local, weight_grad))
+    dback = to_field(darrived, False, 1.0, tables, share)
+    dfield = exchange(dback, "gx").reshape(whole)
     field_grad = add_field(back_local, dfield)
     return (activation[None], field_grad[None], weight_grad)
 

time: 169 us -> 170 us (level)
  blocking collectives: 18.5 us -> 37.2 us
  waiting for transfers between devices: 45 us -> 30.9 us
    all_to_all x1 -> x2, blocking collectives: 18.5 us -> 37.2 us  [exchange(): return lax.all_to_all(value, axes, split_axis=0, concat_axis=0, tiled=True)]
    all_to_all x7 -> x6, waiting for transfers between devices: 39.6 us -> 28.4 us  [exchange(): return lax.all_to_all(value, axes, split_axis=0, concat_axis=0, tiled=True)]
    pallas_call x8 -> x6, Pallas kernels: 18 us -> 6.9 us  [on_chip(): pl.pallas_call(kernel, in_specs=[spec] * len(values), out_specs=[spec] *...]
    pallas_call x0 -> x2, Pallas kernels: none -> 10.3 us  [conv(): pl.pallas_call(conv_kernel, in_specs=[vmem, hbm, hbm, vmem, vmem, vmem],...]
    ppermute x8, waiting for transfers between devices: 5.37 us -> 2.56 us  [swap(): return lax.ppermute(value, axis, pairs)]
    unnamed x32, local copies, waits for them, and re-layouts: 5.3 us -> 2.82 us
    concatenate x2 -> x3, other arithmetic: 2.12 us -> 0.02 us  [the longest x2 0.01 us: edge_rows(): jnp.concatenate([main[:channels], side[:channels]], axis=1)]
    transpose x0 -> x1, local copies, waits for them, and re-layouts: none -> 1.81 us  [by_rows(): main = jnp.transpose(field, (1, 0, 2)).reshape(rows * channels, width)]
  transfers between devices with their start and end apart: 15 -> 14, of which waited for: 9 -> 7; matrix products, arithmetic and copies ran while one was open for 7% -> 8% of each run, Pallas kernels for 9% -> 8%
where the time goes in v8:
time: 170 us; the launch traced here: 169 us
  starting transfers between devices  65.7 us (39%)
  blocking collectives  37.2 us (22%)
  waiting for transfers between devices  30.9 us (18%)
  Pallas kernels  20.5 us (12%)
  local copies, waits for them, and re-layouts  7.92 us (5%)
  other arithmetic  4.52 us (3%)
    all_to_all x6, starting transfers between devices, exchange(): return lax.all_to_all(value, axes, split_axis=0, concat_axis=0, tiled=True)  43.8 us
    all_to_all x2, blocking collectives, exchange(): return lax.all_to_all(value, axes, split_axis=0, concat_axis=0, tiled=True)  37.2 us
    all_to_all x6, waiting for transfers between devices, exchange(): return lax.all_to_all(value, axes, split_axis=0, concat_axis=0, tiled=True)  28.4 us
    ppermute x8, starting transfers between devices, swap(): return lax.ppermute(value, axis, pairs)  21.8 us
    pallas_call x2, Pallas kernels, conv(): pl.pallas_call(conv_kernel, in_specs=[vmem, hbm, hbm, vmem, vmem, vmem],...  10.3 us
    pallas_call x6, Pallas kernels, on_chip(): pl.pallas_call(kernel, in_specs=[spec] * len(values), out_specs=[spec] *...  6.9 us
    another operation x2, other arithmetic, weight_grads(): return jnp.stack([grad_real, grad_imag], axis=2)  3.61 us
  transfers between devices with their start and end apart: 14, of which 7 were waited for; matrix products, arithmetic and copies ran while one was open for 8% of the time, Pallas kernels for 8%

profile of v8, /device:TPU:1, one launch (start us, length us, event | category | flops | bytes accessed | tf_op | source)
XLA Modules:
  0.0 169.1 jit_solution(11054467387230939737)
XLA Ops:
  0.7 7.5 %all-to-all-start = ((bf16[16,2,64,256]{3,2,1,0:T(8,128)(2,1)}), bf16[16,2,64,256]{3,2,1,0:T(8,128)(2,1)S(1)}, u32[]{:S(2)}, u32[]{:S(2)}) async-start(bf16[16,2,64,256]{3,2,1,0:T(8,128)(2,1)} %bitcast.104), calls=%async_computation | async-start | bytes 2097152 | tf_op jit(solution)/shard_map/all_to_all | solution.py:404
  9.2 1.4 collective-permute-start
  10.6 5.5 %collective-permute-start.1 = (bf16[1,2048]{1,0:T(2,128)(2,1)S(1)}, bf16[1,2048]{1,0:T(2,128)(2,1)S(1)}, u32[]{:S(2)}, u32[]{:S(2)}) collective-permute-start(bf16[1,2048]{1,0:T(2,128)(2,1)S(1)} %get-tuple-element.98), channel_id=1, source_target_pairs={{0,1},{1,2},{2,3},{4,5},{5,6},{6,7},{8,9},{9,10},{10,11},{12,13},{... | collective-permute-start | bytes 12296 | tf_op jit(solution)/shard_map/ppermute | solution.py:364
  16.5 1.4 copy.58
  17.9 2.5 %collective-permute-done.1 = bf16[1,2048]{1,0:T(2,128)(2,1)S(1)} collective-permute-done((bf16[1,2048]{1,0:T(2,128)(2,1)S(1)}, bf16[1,2048]{1,0:T(2,128)(2,1)S(1)}, u32[]{:S(2)}, u32[]{:S(2)}) %collective-permute-start.1) | collective-permute-done | bytes 4128 | tf_op jit(solution)/shard_map/ppermute | solution.py:364
  21.9 2.2 %all-to-all-done.block_ref = bf16[16,2,64,256]{3,2,1,0:T(8,128)(2,1)S(1)} async-done(((bf16[16,2,64,256]{3,2,1,0:T(8,128)(2,1)}), bf16[16,2,64,256]{3,2,1,0:T(8,128)(2,1)S(1)}, u32[]{:S(2)}, u32[]{:S(2)}) %all-to-all-start) | async-done | bytes 1048608 | tf_op jit(solution)/shard_map/all_to_all | solution.py:404
  24.1 1.7 to_modes.2
  25.8 10.9 %all-to-all-start.1 = ((bf16[64,8,128]{2,1,0:T(8,128)(2,1)}), bf16[64,8,128]{2,1,0:T(8,128)(2,1)S(1)}, u32[]{:S(2)}, u32[]{:S(2)}) async-start(bf16[64,8,128]{2,1,0:T(8,128)(2,1)} %to_modes.2), calls=%async_computation.1 | async-start | bytes 262144 | tf_op jit(solution)/shard_map/all_to_all | solution.py:404
  36.7 3.5 %collective-permute-start.2 = (bf16[32,384]{1,0:T(8,128)(2,1)S(1)}, bf16[32,384]{1,0:T(8,128)(2,1)S(1)}, u32[]{:S(2)}, u32[]{:S(2)}) collective-permute-start(bf16[32,384]{1,0:T(8,128)(2,1)S(1)} %get-tuple-element.47), channel_id=1, source_target_pairs={{0,4},{4,8},{8,12},{12,16},{16,20},{20,24},{24,28},{28,32},{32,36}... | collective-permute-start | bytes 73736 | tf_op jit(solution)/shard_map/ppermute | solution.py:364
  40.2 1.9 %collective-permute-start.3 = (bf16[32,384]{1,0:T(8,128)(2,1)S(1)}, bf16[32,384]{1,0:T(8,128)(2,1)S(1)}, u32[]{:S(2)}, u32[]{:S(2)}) collective-permute-start(bf16[32,384]{1,0:T(8,128)(2,1)S(1)} %get-tuple-element.48), channel_id=1, source_target_pairs={{4,0},{8,4},{12,8},{16,12},{20,16},{24,20},{28,24},{32,28},{36,32}... | collective-permute-start | bytes 73736 | tf_op jit(solution)/shard_map/ppermute | solution.py:364
  42.2 5.7 %all-to-all-done.1.parts_ref = bf16[64,8,128]{2,1,0:T(8,128)(2,1)S(1)} async-done(((bf16[64,8,128]{2,1,0:T(8,128)(2,1)}), bf16[64,8,128]{2,1,0:T(8,128)(2,1)S(1)}, u32[]{:S(2)}, u32[]{:S(2)}) %all-to-all-start.1) | async-done | bytes 131104 | tf_op jit(solution)/shard_map/all_to_all | solution.py:404
  49.0 7.1 %all-to-all-start.2 = ((bf16[64,8,128]{2,1,0:T(8,128)(2,1)}), bf16[64,8,128]{2,1,0:T(8,128)(2,1)S(1)}, u32[]{:S(2)}, u32[]{:S(2)}) async-start(bf16[64,8,128]{2,1,0:T(8,128)(2,1)} %get-tuple-element.49), calls=%async_computation.2 | async-start | bytes 262144 | tf_op jit(solution)/shard_map/all_to_all | solution.py:404
  56.1 5.1 %conv.2.local_ref = f32[32,64,256]{2,1,0:T(8,128)S(1)} custom-call(bf16[384,192]{1,0:T(8,128)(2,1)S(1)} %fusion.14.matrix_ref, bf16[2048,256]{1,0:T(8,128)(2,1)} %bitcast.103, bf16[2048,128]{1,0:T(8,128)(2,1)} %copy-done.8, bf16[32,384]{1,0:T(8,128)(2,1)S(1)} %collective-permute-done.2.above_ref, bf16[32,384]{1,0:T(8,128)(2,1)S(1)} %collective-permute-done.3.below_ref, ...), custom_call_target="tpu_custom_call" | custom-call | tf_op jit(solution)/shard_map/conv/pallas_call | solution.py:338
  61.3 6.0 %all-to-all-done.2.spec_ref = bf16[64,8,128]{2,1,0:T(8,128)(2,1)S(1)} async-done(((bf16[64,8,128]{2,1,0:T(8,128)(2,1)}), bf16[64,8,128]{2,1,0:T(8,128)(2,1)S(1)}, u32[]{:S(2)}, u32[]{:S(2)}) %all-to-all-start.2) | async-done | bytes 131104 | tf_op jit(solution)/shard_map/all_to_all | solution.py:404
  68.0 18.4 %all_to_all.40 = bf16[16,2,64,256]{3,2,1,0:T(8,128)(2,1)S(1)} all-to-all(bf16[16,2,64,256]{3,2,1,0:T(8,128)(2,1)S(1)} %to_field.2), channel_id=1, replica_groups=mesh['dp'=4,'gx'=16,'gy'=4] {'gx'}, dimensions={0} | all-to-all | bytes 2097152 | tf_op jit(solution)/shard_map/all_to_all | solution.py:404
  86.4 1.9 %gate_both.1 = (bf16[32,64,256]{2,1,0:T(8,128)(2,1)}, f32[32,64,256]{2,1,0:T(8,128)}) custom-call(f32[32,64,256]{2,1,0:T(8,128)S(1)} %conv.2.local_ref, bf16[32,64,256]{2,1,0:T(8,128)(2,1)S(1)} %bitcast.94, bf16[32,64,256]{2,1,0:T(8,128)(2,1)S(1)} %bitcast.95), custom_call_target="tpu_custom_call" | custom-call | tf_op jit(solution)/shard_map/gate_both/pallas_call | solution.py:239
  88.3 4.6 %all-to-all-start.4 = ((bf16[16,2,64,256]{3,2,1,0:T(8,128)(2,1)}), bf16[16,2,64,256]{3,2,1,0:T(8,128)(2,1)S(1)}, u32[]{:S(2)}, u32[]{:S(2)}) async-start(bf16[16,2,64,256]{3,2,1,0:T(8,128)(2,1)} %bitcast.16), calls=%async_computation.4 | async-start | bytes 2097152 | tf_op jit(solution)/shard_map/all_to_all | solution.py:404
  93.3 1.8 %copy.29 = bf16[64,32,256]{2,1,0:T(8,128)(2,1)S(1)} copy(bf16[64,32,256]{2,0,1:T(8,128)(2,1)} %bitcast.20) | data formatting | bytes 2097152 | tf_op jit(solution)/shard_map/transpose | solution.py:369
  95.5 2.4 %collective-permute-start.5 = (bf16[1,2048]{1,0:T(2,128)(2,1)S(1)}, bf16[1,2048]{1,0:T(2,128)(2,1)S(1)}, u32[]{:S(2)}, u32[]{:S(2)}) collective-permute-start(bf16[1,2048]{1,0:T(2,128)(2,1)S(1)} %get-tuple-element.95), channel_id=1, source_target_pairs={{0,1},{1,2},{2,3},{4,5},{5,6},{6,7},{8,9},{9,10},{10,11},{12,13},{... | collective-permute-start | bytes 12296 | tf_op jit(solution)/shard_map/ppermute | solution.py:364
  99.4 9.6 %all-to-all-done.4.block_ref = bf16[16,2,64,256]{3,2,1,0:T(8,128)(2,1)S(1)} async-done(((bf16[16,2,64,256]{3,2,1,0:T(8,128)(2,1)}), bf16[16,2,64,256]{3,2,1,0:T(8,128)(2,1)S(1)}, u32[]{:S(2)}, u32[]{:S(2)}) %all-to-all-start.4) | async-done | bytes 1048608 | tf_op jit(solution)/shard_map/all_to_all | solution.py:404
  109.0 1.7 to_modes.3
  110.7 4.9 %all-to-all-start.5 = ((bf16[64,8,128]{2,1,0:T(8,128)(2,1)}), bf16[64,8,128]{2,1,0:T(8,128)(2,1)S(1)}, u32[]{:S(2)}, u32[]{:S(2)}) async-start(bf16[64,8,128]{2,1,0:T(8,128)(2,1)} %to_modes.3), calls=%async_computation.5 | async-start | bytes 262144 | tf_op jit(solution)/shard_map/all_to_all | solution.py:404
  116.8 3.6 %collective-permute-start.6 = (bf16[32,384]{1,0:T(8,128)(2,1)S(1)}, bf16[32,384]{1,0:T(8,128)(2,1)S(1)}, u32[]{:S(2)}, u32[]{:S(2)}) collective-permute-start(bf16[32,384]{1,0:T(8,128)(2,1)S(1)} %pad_maximum_fusion.3), channel_id=1, source_target_pairs={{0,4},{4,8},{8,12},{12,16},{16,20},{20,24},{24,28},{28,32},{32,36}... | collective-permute-start | bytes 73736 | tf_op jit(solution)/shard_map/ppermute | solution.py:364
  120.4 2.1 %collective-permute-start.7 = (bf16[32,384]{1,0:T(8,128)(2,1)S(1)}, bf16[32,384]{1,0:T(8,128)(2,1)S(1)}, u32[]{:S(2)}, u32[]{:S(2)}) collective-permute-start(bf16[32,384]{1,0:T(8,128)(2,1)S(1)} %pad_maximum_fusion.4), channel_id=1, source_target_pairs={{4,0},{8,4},{12,8},{16,12},{20,16},{24,20},{28,24},{32,28},{36,32}... | collective-permute-start | bytes 73736 | tf_op jit(solution)/shard_map/ppermute | solution.py:364
  122.5 1.9 %copy.57 = bf16[32,32,2,2,128]{4,0,1,2,3:T(8,128)(2,1)S(1)} copy(bf16[32,32,2,2,128]{4,3,2,1,0:T(2,128)(2,1)} %param.12) | data formatting | bytes 2097152 | tf_op jit(solution)/shard_map/optimization_barrier | solution.py:468
  124.4 2.5 %all-to-all-done.5.parts_ref = bf16[64,8,128]{2,1,0:T(8,128)(2,1)S(1)} async-done(((bf16[64,8,128]{2,1,0:T(8,128)(2,1)}), bf16[64,8,128]{2,1,0:T(8,128)(2,1)S(1)}, u32[]{:S(2)}, u32[]{:S(2)}) %all-to-all-start.5) | async-done | bytes 131104 | tf_op jit(solution)/shard_map/all_to_all | solution.py:404
  128.0 8.8 %all-to-all-start.6 = ((bf16[64,8,128]{2,1,0:T(8,128)(2,1)}), bf16[64,8,128]{2,1,0:T(8,128)(2,1)S(1)}, u32[]{:S(2)}, u32[]{:S(2)}) async-start(bf16[64,8,128]{2,1,0:T(8,128)(2,1)} %get-tuple-element.70), calls=%async_computation.6 | async-start | bytes 262144 | tf_op jit(solution)/shard_map/all_to_all | solution.py:404
  138.2 5.1 %conv.3.local_ref = f32[32,64,256]{2,1,0:T(8,128)S(1)} custom-call(bf16[384,192]{1,0:T(8,128)(2,1)S(1)} %fusion.17.matrix_ref, bf16[2048,256]{1,0:T(8,128)(2,1)} %bitcast.100, bf16[2048,128]{1,0:T(8,128)(2,1)} %copy-done.7, bf16[32,384]{1,0:T(8,128)(2,1)S(1)} %collective-permute-done.6.above_ref, bf16[32,384]{1,0:T(8,128)(2,1)S(1)} %collective-permute-done.7.below_ref, ...), custom_call_target="tpu_custom_call" | custom-call | tf_op jit(solution)/shard_map/conv/pallas_call | solution.py:338
  143.4 2.4 %pad_maximum_fusion = f32[32,32,2,2,128]{4,3,2,1,0:T(2,128)} fusion(f32[32,32,1,2,128]{4,3,2,1,0:T(2,128)S(1)} %get-tuple-element.90, f32[32,32,1,2,128]{4,3,2,1,0:T(2,128)S(1)} %get-tuple-element.89), kind=kLoop, calls=%fused_computation.4 | loop fusion | flops 524288 | bytes 4194304 | tf_op jit(solution)/shard_map/stack | solution.py:417
  145.8 2.3 %all-to-all-done.6.spec_ref = bf16[64,8,128]{2,1,0:T(8,128)(2,1)S(1)} async-done(((bf16[64,8,128]{2,1,0:T(8,128)(2,1)}), bf16[64,8,128]{2,1,0:T(8,128)(2,1)S(1)}, u32[]{:S(2)}, u32[]{:S(2)}) %all-to-all-start.6) | async-done | bytes 131104 | tf_op jit(solution)/shard_map/all_to_all | solution.py:404
  148.8 18.8 %all_to_all.41 = bf16[16,2,64,256]{3,2,1,0:T(8,128)(2,1)S(1)} all-to-all(bf16[16,2,64,256]{3,2,1,0:T(8,128)(2,1)S(1)} %to_field.3), channel_id=1, replica_groups=mesh['dp'=4,'gx'=16,'gy'=4] {'gx'}, dimensions={0} | all-to-all | bytes 2097152 | tf_op jit(solution)/shard_map/all_to_all | solution.py:404
  167.6 1.4 add_field.1
  (74 shorter events, 10.9 us)
Async XLA Ops:
  0.6 7.5 %copy-start.6 = (bf16[1,32,64,256]{3,2,1,0:T(8,128)(2,1)S(1)}, bf16[1,32,64,256]{3,2,1,0:T(8,128)(2,1)}, u32[]{:S(2)}) copy-start(bf16[1,32,64,256]{3,2,1,0:T(8,128)(2,1)} %param.11) | copy-start | bytes 3145732
  0.6 8.1 %copy-start.10 = (bf16[2,256]{1,0:T(2,128)(2,1)S(1)}, bf16[2,256]{1,0:T(2,128)(2,1)}, u32[]{:S(2)}) copy-start(bf16[2,256]{1,0:T(2,128)(2,1)} %constant.15.clone) | copy-start | bytes 3076
  0.7 23.5 %all-to-all-start = ((bf16[16,2,64,256]{3,2,1,0:T(8,128)(2,1)}), bf16[16,2,64,256]{3,2,1,0:T(8,128)(2,1)S(1)}, u32[]{:S(2)}, u32[]{:S(2)}) async-start(bf16[16,2,64,256]{3,2,1,0:T(8,128)(2,1)} %bitcast.104), calls=%async_computation | async-start | bytes 2097152 | tf_op jit(solution)/shard_map/all_to_all | solution.py:404
  8.1 8.1 %copy-start.9 = (bf16[9,32,32]{2,1,0:T(8,128)(2,1)S(1)}, bf16[9,32,32]{2,1,0:T(8,128)(2,1)}, u32[]{:S(2)}) copy-start(bf16[9,32,32]{2,1,0:T(8,128)(2,1)} %param.13) | copy-start | bytes 55300
  8.7 7.6 %copy-start.5 = (bf16[1,32,64,256]{3,1,2,0:T(8,128)(2,1)}, bf16[1,32,64,256]{3,1,2,0:T(8,128)(2,1)S(1)}, u32[]{:S(2)}) copy-start(bf16[1,32,64,256]{3,1,2,0:T(8,128)(2,1)S(1)} %copy.60) | copy-start | bytes 3145732
  8.8 11.7 %copy-start.13 = (f32[128]{0:T(128)S(1)}, f32[128]{0:T(128)}, u32[]{:S(2)}) copy-start(f32[128]{0:T(128)} %constant.41) | copy-start | bytes 1540
  8.8 11.7 %copy-start.14 = (f32[128]{0:T(128)S(1)}, f32[128]{0:T(128)}, u32[]{:S(2)}) copy-start(f32[128]{0:T(128)} %constant.38) | copy-start | bytes 1540
  8.8 15.3 %copy-start.1 = (bf16[256,1536]{1,0:T(8,128)(2,1)S(1)}, bf16[256,1536]{1,0:T(8,128)(2,1)}, u32[]{:S(2)}) copy-start(bf16[256,1536]{1,0:T(8,128)(2,1)} %constant.13.clone.table_ref) | copy-start | bytes 2359300
  9.2 8.7 %collective-permute-start = (bf16[1,2048]{1,0:T(2,128)(2,1)S(1)}, bf16[1,2048]{1,0:T(2,128)(2,1)S(1)}, u32[]{:S(2)}, u32[]{:S(2)}) collective-permute-start(bf16[1,2048]{1,0:T(2,128)(2,1)S(1)} %get-tuple-element.97), channel_id=1, source_target_pairs={{1,0},{2,1},{3,2},{5,4},{6,5},{7,6},{9,8},{10,9},{11,10},{13,12},{... | collective-permute-start | bytes 12296 | tf_op jit(solution)/shard_map/ppermute | solution.py:364
  10.6 9.8 %collective-permute-start.1 = (bf16[1,2048]{1,0:T(2,128)(2,1)S(1)}, bf16[1,2048]{1,0:T(2,128)(2,1)S(1)}, u32[]{:S(2)}, u32[]{:S(2)}) collective-permute-start(bf16[1,2048]{1,0:T(2,128)(2,1)S(1)} %get-tuple-element.98), channel_id=1, source_target_pairs={{0,1},{1,2},{2,3},{4,5},{5,6},{6,7},{8,9},{9,10},{10,11},{12,13},{... | collective-permute-start | bytes 12296 | tf_op jit(solution)/shard_map/ppermute | solution.py:364
  20.5 35.6 %copy-start.12 = (f32[32]{0:T(128)S(1)}, f32[32]{0:T(128)}, u32[]{:S(2)}) copy-start(f32[32]{0:T(128)} %param.14) | copy-start | bytes 388
  21.1 0.8 copy-start.8
  25.8 22.1 %all-to-all-start.1 = ((bf16[64,8,128]{2,1,0:T(8,128)(2,1)}), bf16[64,8,128]{2,1,0:T(8,128)(2,1)S(1)}, u32[]{:S(2)}, u32[]{:S(2)}) async-start(bf16[64,8,128]{2,1,0:T(8,128)(2,1)} %to_modes.2), calls=%async_computation.1 | async-start | bytes 262144 | tf_op jit(solution)/shard_map/all_to_all | solution.py:404
  36.7 12.3 %collective-permute-start.2 = (bf16[32,384]{1,0:T(8,128)(2,1)S(1)}, bf16[32,384]{1,0:T(8,128)(2,1)S(1)}, u32[]{:S(2)}, u32[]{:S(2)}) collective-permute-start(bf16[32,384]{1,0:T(8,128)(2,1)S(1)} %get-tuple-element.47), channel_id=1, source_target_pairs={{0,4},{4,8},{8,12},{12,16},{16,20},{20,24},{24,28},{28,32},{32,36}... | collective-permute-start | bytes 73736 | tf_op jit(solution)/shard_map/ppermute | solution.py:364
  40.2 8.7 %collective-permute-start.3 = (bf16[32,384]{1,0:T(8,128)(2,1)S(1)}, bf16[32,384]{1,0:T(8,128)(2,1)S(1)}, u32[]{:S(2)}, u32[]{:S(2)}) collective-permute-start(bf16[32,384]{1,0:T(8,128)(2,1)S(1)} %get-tuple-element.48), channel_id=1, source_target_pairs={{4,0},{8,4},{12,8},{16,12},{20,16},{24,20},{28,24},{32,28},{36,32}... | collective-permute-start | bytes 73736 | tf_op jit(solution)/shard_map/ppermute | solution.py:364
  49.0 18.3 %copy-start = (bf16[1536,256]{1,0:T(8,128)(2,1)S(1)}, bf16[1536,256]{1,0:T(8,128)(2,1)}, u32[]{:S(2)}) copy-start(bf16[1536,256]{1,0:T(8,128)(2,1)} %constant.14.clone.table_ref) | copy-start | bytes 2359300
  49.0 18.3 %all-to-all-start.2 = ((bf16[64,8,128]{2,1,0:T(8,128)(2,1)}), bf16[64,8,128]{2,1,0:T(8,128)(2,1)S(1)}, u32[]{:S(2)}, u32[]{:S(2)}) async-start(bf16[64,8,128]{2,1,0:T(8,128)(2,1)} %get-tuple-element.49), calls=%async_computation.2 | async-start | bytes 262144 | tf_op jit(solution)/shard_map/all_to_all | solution.py:404
  67.3 19.1 %copy-start.3 = (bf16[1,32,64,256]{3,2,1,0:T(8,128)(2,1)S(1)}, bf16[1,32,64,256]{3,2,1,0:T(8,128)(2,1)}, u32[]{:S(2)}) copy-start(bf16[1,32,64,256]{3,2,1,0:T(8,128)(2,1)} %param.15) | copy-start | bytes 3145732
  88.3 20.7 %all-to-all-start.4 = ((bf16[16,2,64,256]{3,2,1,0:T(8,128)(2,1)}), bf16[16,2,64,256]{3,2,1,0:T(8,128)(2,1)S(1)}, u32[]{:S(2)}, u32[]{:S(2)}) async-start(bf16[16,2,64,256]{3,2,1,0:T(8,128)(2,1)} %bitcast.16), calls=%async_computation.4 | async-start | bytes 2097152 | tf_op jit(solution)/shard_map/all_to_all | solution.py:404
  92.9 16.1 %copy-start.2 = (bf16[256,1536]{1,0:T(8,128)(2,1)S(1)}, bf16[256,1536]{1,0:T(8,128)(2,1)}, u32[]{:S(2)}) copy-start(bf16[256,1536]{1,0:T(8,128)(2,1)} %constant.13.clone.table_ref) | copy-start | bytes 2359300
  95.1 4.2 %copy-start.4 = (bf16[64,32,256]{2,1,0:T(8,128)(2,1)}, bf16[64,32,256]{2,1,0:T(8,128)(2,1)S(1)}, u32[]{:S(2)}) copy-start(bf16[64,32,256]{2,1,0:T(8,128)(2,1)S(1)} %copy.29) | copy-start | bytes 3145732
  95.1 21.3 %copy-start.11 = (bf16[2,128]{1,0:T(2,128)(2,1)S(1)}, bf16[2,128]{1,0:T(2,128)(2,1)}, u32[]{:S(2)}) copy-start(bf16[2,128]{1,0:T(2,128)(2,1)} %constant.16.clone) | copy-start | bytes 1540
  95.5 15.2 %collective-permute-start.5 = (bf16[1,2048]{1,0:T(2,128)(2,1)S(1)}, bf16[1,2048]{1,0:T(2,128)(2,1)S(1)}, u32[]{:S(2)}, u32[]{:S(2)}) collective-permute-start(bf16[1,2048]{1,0:T(2,128)(2,1)S(1)} %get-tuple-element.95), channel_id=1, source_target_pairs={{0,1},{1,2},{2,3},{4,5},{5,6},{6,7},{8,9},{9,10},{10,11},{12,13},{... | collective-permute-start | bytes 12296 | tf_op jit(solution)/shard_map/ppermute | solution.py:364
  97.9 12.8 %collective-permute-start.4 = (bf16[1,2048]{1,0:T(2,128)(2,1)S(1)}, bf16[1,2048]{1,0:T(2,128)(2,1)S(1)}, u32[]{:S(2)}, u32[]{:S(2)}) collective-permute-start(bf16[1,2048]{1,0:T(2,128)(2,1)S(1)} %get-tuple-element.96), channel_id=1, source_target_pairs={{1,0},{2,1},{3,2},{5,4},{6,5},{7,6},{9,8},{10,9},{11,10},{13,12},{... | collective-permute-start | bytes 12296 | tf_op jit(solution)/shard_map/ppermute | solution.py:364
  110.7 16.2 %all-to-all-start.5 = ((bf16[64,8,128]{2,1,0:T(8,128)(2,1)}), bf16[64,8,128]{2,1,0:T(8,128)(2,1)S(1)}, u32[]{:S(2)}, u32[]{:S(2)}) async-start(bf16[64,8,128]{2,1,0:T(8,128)(2,1)} %to_modes.3), calls=%async_computation.5 | async-start | bytes 262144 | tf_op jit(solution)/shard_map/all_to_all | solution.py:404
  116.8 10.2 %copy-start.7 = (bf16[2048,128]{1,0:T(8,128)(2,1)}, bf16[2048,128]{1,0:T(8,128)(2,1)S(1)}, u32[]{:S(2)}) copy-start(bf16[2048,128]{1,0:T(8,128)(2,1)S(1)} %convolution_convert_fusion.side_hbm) | copy-start | bytes 1572868
  116.8 11.2 %collective-permute-start.6 = (bf16[32,384]{1,0:T(8,128)(2,1)S(1)}, bf16[32,384]{1,0:T(8,128)(2,1)S(1)}, u32[]{:S(2)}, u32[]{:S(2)}) collective-permute-start(bf16[32,384]{1,0:T(8,128)(2,1)S(1)} %pad_maximum_fusion.3), channel_id=1, source_target_pairs={{0,4},{4,8},{8,12},{12,16},{16,20},{20,24},{24,28},{28,32},{32,36}... | collective-permute-start | bytes 73736 | tf_op jit(solution)/shard_map/ppermute | solution.py:364
  120.4 7.6 %collective-permute-start.7 = (bf16[32,384]{1,0:T(8,128)(2,1)S(1)}, bf16[32,384]{1,0:T(8,128)(2,1)S(1)}, u32[]{:S(2)}, u32[]{:S(2)}) collective-permute-start(bf16[32,384]{1,0:T(8,128)(2,1)S(1)} %pad_maximum_fusion.4), channel_id=1, source_target_pairs={{4,0},{8,4},{12,8},{16,12},{20,16},{24,20},{28,24},{32,28},{36,32}... | collective-permute-start | bytes 73736 | tf_op jit(solution)/shard_map/ppermute | solution.py:364
  128.0 20.1 %all-to-all-start.6 = ((bf16[64,8,128]{2,1,0:T(8,128)(2,1)}), bf16[64,8,128]{2,1,0:T(8,128)(2,1)S(1)}, u32[]{:S(2)}, u32[]{:S(2)}) async-start(bf16[64,8,128]{2,1,0:T(8,128)(2,1)} %get-tuple-element.70), calls=%async_computation.6 | async-start | bytes 262144 | tf_op jit(solution)/shard_map/all_to_all | solution.py:404

commit v9 on v8

--- a/solution.py
+++ b/solution.py
@@ -463,23 +463,25 @@
     dmain, dends = by_rows(dpre)
     dright, dleft = across_columns(dends)
     dmatrix = conv_matrix(jnp.transpose(taps[::-1], (0, 2, 1)))
-    dblock, dmatrix, dmain = hold((dblock, dmatrix, dmain))
+    dside = place_columns(dright, dleft, side_slots())
+    dfirst, dlast = edge_rows(dmain, dside, channels)
+    dblock, dmatrix, dfirst, dlast = hold((dblock, dmatrix, dfirst, dlast))
     dparts = to_modes(dblock, True, scale, tables, owners)
-    dparts, dright, dleft, dweight, places = hold((dparts, dright, dleft, dweight, side_slots()))
+    dparts, dfirst, dlast, dweight = hold((dparts, dfirst, dlast, dweight))
     dparts = exchange(dparts, both)
     dweight = jnp.transpose(dweight, (3, 2, 1, 0, 4))
-    dside = place_columns(dright, dleft, places)
-    dabove, dbelow = across_rows(*edge_rows(dmain, dside, channels))
+    dabove, dbelow = across_rows(dfirst, dlast)
     dparts, dweight = hold((dparts, dweight))
     dmixed, dspec = mix(dparts, dweight, -1, strips)
     dmixed, dabove, dbelow = hold((dmixed, dabove, dbelow))
     darrived = exchange(dmixed, both)
+    dback = to_field(darrived, False, 1.0, tables, share)
+    dback, dabove, dbelow, spec, dspec = hold((dback, dabove, dbelow, spec, dspec))
+    dfield = exchange(dback, "gx").reshape(whole)
     back_local = conv(dmatrix, dmain, dside, dabove, dbelow, jnp.zeros_like(bias))
     slots = M1 // owners
     weight_grad = weight_grads(by_mode(spec, slots), by_mode(dspec, slots))
-    darrived, back_local, weight_grad = hold((darrived, back_local, weight_grad))
-    dback = to_field(darrived, False, 1.0, tables, share)
-    dfield = exchange(dback, "gx").reshape(whole)
+    dfield, back_local, weight_grad = hold((dfield, back_local, weight_grad))
     field_grad = add_field(back_local, dfield)
     return (activation[None], field_grad[None], weight_grad)
 

time: 170 us -> 174 us (1.024)
  local copies, waits for them, and re-layouts: 7.92 us -> 9.71 us
    optimization_barrier x1 -> x2, local copies, waits for them, and re-layouts: 1.91 us -> 4.76 us  [the longest x1 2.85 us: body(): dpre, taps, dweight = hold((dpre, conv_weight, spectral_weight))]
    ppermute x8, starting transfers between devices: 21.8 us -> 24.3 us  [swap(): return lax.ppermute(value, axis, pairs)]
    transpose x1 -> x0, local copies, waits for them, and re-layouts: 1.81 us -> none  [by_rows(): main = jnp.transpose(field, (1, 0, 2)).reshape(rows * channels, width)]
    unnamed x32 -> x28, local copies, waits for them, and re-layouts: 2.82 us -> 3.57 us
  transfers between devices with their start and end apart: 14 -> 14, of which waited for: 7 -> 8; matrix products, arithmetic and copies ran while one was open for 8% -> 9% of each run, Pallas kernels for 8% -> 7%
where the time goes in v9:
time: 174 us; the launch traced here: 173 us
  starting transfers between devices  67.2 us (39%)
  blocking collectives  37.1 us (21%)
  waiting for transfers between devices  29.8 us (17%)
  Pallas kernels  20.9 us (12%)
  local copies, waits for them, and re-layouts  9.71 us (6%)
  other arithmetic  5.15 us (3%)
  matrix products  1.97 us (1%)
    all_to_all x6, starting transfers between devices, exchange(): return lax.all_to_all(value, axes, split_axis=0, concat_axis=0, tiled=True)  42.9 us
    all_to_all x2, blocking collectives, exchange(): return lax.all_to_all(value, axes, split_axis=0, concat_axis=0, tiled=True)  37.1 us
    all_to_all x6, waiting for transfers between devices, exchange(): return lax.all_to_all(value, axes, split_axis=0, concat_axis=0, tiled=True)  27.2 us
    ppermute x8, starting transfers between devices, swap(): return lax.ppermute(value, axis, pairs)  24.3 us
    pallas_call x2, Pallas kernels, conv(): pl.pallas_call(conv_kernel, in_specs=[vmem, hbm, hbm, vmem, vmem, vmem],...  10.3 us
    pallas_call x6, Pallas kernels, on_chip(): pl.pallas_call(kernel, in_specs=[spec] * len(values), out_specs=[spec] *...  7.27 us
    another operation x2, other arithmetic, weight_grads(): return jnp.stack([grad_real, grad_imag], axis=2)  3.62 us
    unnamed x28, local copies, waits for them, and re-layouts  3.57 us
  transfers between devices with their start and end apart: 14, of which 8 were waited for; matrix products, arithmetic and copies ran while one was open for 9% of the time, Pallas kernels for 7%

profile of v9, /device:TPU:1, one launch (start us, length us, event | category | flops | bytes accessed | tf_op | source)
XLA Modules:
  0.0 173.1 jit_solution(5818658961083291624)
XLA Ops:
  0.7 7.5 %all-to-all-start = ((bf16[16,2,64,256]{3,2,1,0:T(8,128)(2,1)}), bf16[16,2,64,256]{3,2,1,0:T(8,128)(2,1)S(1)}, u32[]{:S(2)}, u32[]{:S(2)}) async-start(bf16[16,2,64,256]{3,2,1,0:T(8,128)(2,1)} %bitcast.112), calls=%async_computation | async-start | bytes 2097152 | tf_op jit(solution)/shard_map/all_to_all | solution.py:404
  9.2 1.4 collective-permute-start
  10.6 5.5 %collective-permute-start.1 = (bf16[1,2048]{1,0:T(2,128)(2,1)S(1)}, bf16[1,2048]{1,0:T(2,128)(2,1)S(1)}, u32[]{:S(2)}, u32[]{:S(2)}) collective-permute-start(bf16[1,2048]{1,0:T(2,128)(2,1)S(1)} %get-tuple-element.110), channel_id=1, source_target_pairs={{0,1},{1,2},{2,3},{4,5},{5,6},{6,7},{8,9},{9,10},{10,11},{12,13},{... | collective-permute-start | bytes 12296 | tf_op jit(solution)/shard_map/ppermute | solution.py:364
  17.9 2.5 %collective-permute-done.1 = bf16[1,2048]{1,0:T(2,128)(2,1)S(1)} collective-permute-done((bf16[1,2048]{1,0:T(2,128)(2,1)S(1)}, bf16[1,2048]{1,0:T(2,128)(2,1)S(1)}, u32[]{:S(2)}, u32[]{:S(2)}) %collective-permute-start.1) | collective-permute-done | bytes 4128 | tf_op jit(solution)/shard_map/ppermute | solution.py:364
  21.9 2.2 %all-to-all-done.block_ref = bf16[16,2,64,256]{3,2,1,0:T(8,128)(2,1)S(1)} async-done(((bf16[16,2,64,256]{3,2,1,0:T(8,128)(2,1)}), bf16[16,2,64,256]{3,2,1,0:T(8,128)(2,1)S(1)}, u32[]{:S(2)}, u32[]{:S(2)}) %all-to-all-start) | async-done | bytes 1048608 | tf_op jit(solution)/shard_map/all_to_all | solution.py:404
  24.1 1.7 to_modes.2
  25.8 10.9 %all-to-all-start.1 = ((bf16[64,8,128]{2,1,0:T(8,128)(2,1)}), bf16[64,8,128]{2,1,0:T(8,128)(2,1)S(1)}, u32[]{:S(2)}, u32[]{:S(2)}) async-start(bf16[64,8,128]{2,1,0:T(8,128)(2,1)} %to_modes.2), calls=%async_computation.1 | async-start | bytes 262144 | tf_op jit(solution)/shard_map/all_to_all | solution.py:404
  36.7 3.5 %collective-permute-start.2 = (bf16[32,384]{1,0:T(8,128)(2,1)S(1)}, bf16[32,384]{1,0:T(8,128)(2,1)S(1)}, u32[]{:S(2)}, u32[]{:S(2)}) collective-permute-start(bf16[32,384]{1,0:T(8,128)(2,1)S(1)} %get-tuple-element.52), channel_id=1, source_target_pairs={{0,4},{4,8},{8,12},{12,16},{16,20},{20,24},{24,28},{28,32},{32,36}... | collective-permute-start | bytes 73736 | tf_op jit(solution)/shard_map/ppermute | solution.py:364
  40.2 1.9 %collective-permute-start.3 = (bf16[32,384]{1,0:T(8,128)(2,1)S(1)}, bf16[32,384]{1,0:T(8,128)(2,1)S(1)}, u32[]{:S(2)}, u32[]{:S(2)}) collective-permute-start(bf16[32,384]{1,0:T(8,128)(2,1)S(1)} %get-tuple-element.53), channel_id=1, source_target_pairs={{4,0},{8,4},{12,8},{16,12},{20,16},{24,20},{28,24},{32,28},{36,32}... | collective-permute-start | bytes 73736 | tf_op jit(solution)/shard_map/ppermute | solution.py:364
  42.2 5.7 %all-to-all-done.1.parts_ref = bf16[64,8,128]{2,1,0:T(8,128)(2,1)S(1)} async-done(((bf16[64,8,128]{2,1,0:T(8,128)(2,1)}), bf16[64,8,128]{2,1,0:T(8,128)(2,1)S(1)}, u32[]{:S(2)}, u32[]{:S(2)}) %all-to-all-start.1) | async-done | bytes 131104 | tf_op jit(solution)/shard_map/all_to_all | solution.py:404
  49.0 7.1 %all-to-all-start.2 = ((bf16[64,8,128]{2,1,0:T(8,128)(2,1)}), bf16[64,8,128]{2,1,0:T(8,128)(2,1)S(1)}, u32[]{:S(2)}, u32[]{:S(2)}) async-start(bf16[64,8,128]{2,1,0:T(8,128)(2,1)} %get-tuple-element.54), calls=%async_computation.2 | async-start | bytes 262144 | tf_op jit(solution)/shard_map/all_to_all | solution.py:404
  56.1 5.1 %conv.2.local_ref = f32[32,64,256]{2,1,0:T(8,128)S(1)} custom-call(bf16[384,192]{1,0:T(8,128)(2,1)S(1)} %fusion.15.matrix_ref, bf16[2048,256]{1,0:T(8,128)(2,1)} %bitcast.111, bf16[2048,128]{1,0:T(8,128)(2,1)} %copy-done.7, bf16[32,384]{1,0:T(8,128)(2,1)S(1)} %collective-permute-done.2.above_ref, bf16[32,384]{1,0:T(8,128)(2,1)S(1)} %collective-permute-done.3.below_ref, ...), custom_call_target="tpu_custom_call" | custom-call | tf_op jit(solution)/shard_map/conv/pallas_call | solution.py:338
  61.3 6.0 %all-to-all-done.2.spec_ref = bf16[64,8,128]{2,1,0:T(8,128)(2,1)S(1)} async-done(((bf16[64,8,128]{2,1,0:T(8,128)(2,1)}), bf16[64,8,128]{2,1,0:T(8,128)(2,1)S(1)}, u32[]{:S(2)}, u32[]{:S(2)}) %all-to-all-start.2) | async-done | bytes 131104 | tf_op jit(solution)/shard_map/all_to_all | solution.py:404
  68.0 18.4 %all_to_all.40 = bf16[16,2,64,256]{3,2,1,0:T(8,128)(2,1)S(1)} all-to-all(bf16[16,2,64,256]{3,2,1,0:T(8,128)(2,1)S(1)} %to_field.2), channel_id=1, replica_groups=mesh['dp'=4,'gx'=16,'gy'=4] {'gx'}, dimensions={0} | all-to-all | bytes 2097152 | tf_op jit(solution)/shard_map/all_to_all | solution.py:404
  86.4 1.9 %gate_both.1 = (bf16[32,64,256]{2,1,0:T(8,128)(2,1)}, f32[32,64,256]{2,1,0:T(8,128)}) custom-call(f32[32,64,256]{2,1,0:T(8,128)S(1)} %conv.2.local_ref, bf16[32,64,256]{2,1,0:T(8,128)(2,1)S(1)} %bitcast.102, bf16[32,64,256]{2,1,0:T(8,128)(2,1)S(1)} %bitcast.103), custom_call_target="tpu_custom_call" | custom-call | tf_op jit(solution)/shard_map/gate_both/pallas_call | solution.py:239
  88.3 4.6 %all-to-all-start.4 = ((bf16[16,2,64,256]{3,2,1,0:T(8,128)(2,1)}), bf16[16,2,64,256]{3,2,1,0:T(8,128)(2,1)S(1)}, u32[]{:S(2)}, u32[]{:S(2)}) async-start(bf16[16,2,64,256]{3,2,1,0:T(8,128)(2,1)} %bitcast.16), calls=%async_computation.4 | async-start | bytes 2097152 | tf_op jit(solution)/shard_map/all_to_all | solution.py:404
  92.9 2.9 %copy.62 = bf16[32,64,256]{2,0,1:T(8,128)(2,1)} copy(bf16[32,64,256]{2,1,0:T(8,128)(2,1)} %get-tuple-element.62) | data formatting | bytes 2097152 | tf_op jit(solution)/shard_map/optimization_barrier | solution.py:460
  96.0 1.6 fusion
  99.0 4.9 %collective-permute-start.5 = (bf16[1,2048]{1,0:T(2,128)(2,1)S(1)}, bf16[1,2048]{1,0:T(2,128)(2,1)S(1)}, u32[]{:S(2)}, u32[]{:S(2)}) collective-permute-start(bf16[1,2048]{1,0:T(2,128)(2,1)S(1)} %get-tuple-element.108), channel_id=1, source_target_pairs={{0,1},{1,2},{2,3},{4,5},{5,6},{6,7},{8,9},{9,10},{10,11},{12,13},{... | collective-permute-start | bytes 12296 | tf_op jit(solution)/shard_map/ppermute | solution.py:364
  106.3 2.7 %all-to-all-done.4.block_ref = bf16[16,2,64,256]{3,2,1,0:T(8,128)(2,1)S(1)} async-done(((bf16[16,2,64,256]{3,2,1,0:T(8,128)(2,1)}), bf16[16,2,64,256]{3,2,1,0:T(8,128)(2,1)S(1)}, u32[]{:S(2)}, u32[]{:S(2)}) %all-to-all-start.4) | async-done | bytes 1048608 | tf_op jit(solution)/shard_map/all_to_all | solution.py:404
  109.0 1.7 to_modes.3
  110.7 9.0 %all-to-all-start.5 = ((bf16[64,8,128]{2,1,0:T(8,128)(2,1)}), bf16[64,8,128]{2,1,0:T(8,128)(2,1)S(1)}, u32[]{:S(2)}, u32[]{:S(2)}) async-start(bf16[64,8,128]{2,1,0:T(8,128)(2,1)} %to_modes.3), calls=%async_computation.5 | async-start | bytes 262144 | tf_op jit(solution)/shard_map/all_to_all | solution.py:404
  119.7 3.5 %collective-permute-start.6 = (bf16[32,384]{1,0:T(8,128)(2,1)S(1)}, bf16[32,384]{1,0:T(8,128)(2,1)S(1)}, u32[]{:S(2)}, u32[]{:S(2)}) collective-permute-start(bf16[32,384]{1,0:T(8,128)(2,1)S(1)} %pad_maximum_fusion.4), channel_id=1, source_target_pairs={{0,4},{4,8},{8,12},{12,16},{16,20},{20,24},{24,28},{28,32},{32,36}... | collective-permute-start | bytes 73736 | tf_op jit(solution)/shard_map/ppermute | solution.py:364
  123.2 2.1 %collective-permute-start.7 = (bf16[32,384]{1,0:T(8,128)(2,1)S(1)}, bf16[32,384]{1,0:T(8,128)(2,1)S(1)}, u32[]{:S(2)}, u32[]{:S(2)}) collective-permute-start(bf16[32,384]{1,0:T(8,128)(2,1)S(1)} %pad_maximum_fusion.3), channel_id=1, source_target_pairs={{4,0},{8,4},{12,8},{16,12},{20,16},{24,20},{28,24},{32,28},{36,32}... | collective-permute-start | bytes 73736 | tf_op jit(solution)/shard_map/ppermute | solution.py:364
  125.3 1.9 %copy.59 = bf16[32,32,2,2,128]{4,0,1,2,3:T(8,128)(2,1)S(1)} copy(bf16[32,32,2,2,128]{4,3,2,1,0:T(2,128)(2,1)} %param.12) | data formatting | bytes 2097152 | tf_op jit(solution)/shard_map/optimization_barrier | solution.py:470
  127.2 3.6 %all-to-all-done.5.parts_ref = bf16[64,8,128]{2,1,0:T(8,128)(2,1)S(1)} async-done(((bf16[64,8,128]{2,1,0:T(8,128)(2,1)}), bf16[64,8,128]{2,1,0:T(8,128)(2,1)S(1)}, u32[]{:S(2)}, u32[]{:S(2)}) %all-to-all-start.5) | async-done | bytes 131104 | tf_op jit(solution)/shard_map/all_to_all | solution.py:404
  131.3 18.7 %all_to_all.41.spec_ref = bf16[64,8,128]{2,1,0:T(8,128)(2,1)S(1)} all-to-all(bf16[64,8,128]{2,1,0:T(8,128)(2,1)S(1)} %get-tuple-element.75), channel_id=1, replica_groups=mesh['dp'=4,'gx'=16,'gy'=4] {'gx','gy'}, dimensions={0} | all-to-all | bytes 262144 | tf_op jit(solution)/shard_map/all_to_all | solution.py:404
  150.0 1.7 to_field.3
  151.7 3.9 %all-to-all-start.7 = ((bf16[16,2,64,256]{3,2,1,0:T(8,128)(2,1)}), bf16[16,2,64,256]{3,2,1,0:T(8,128)(2,1)S(1)}, u32[]{:S(2)}, u32[]{:S(2)}) async-start(bf16[16,2,64,256]{3,2,1,0:T(8,128)(2,1)} %to_field.3), calls=%async_computation.7 | async-start | bytes 2097152 | tf_op jit(solution)/shard_map/all_to_all | solution.py:404
  155.6 5.1 %conv.3.local_ref = f32[32,64,256]{2,1,0:T(8,128)S(1)} custom-call(bf16[384,192]{1,0:T(8,128)(2,1)S(1)} %fusion.18.matrix_ref, bf16[2048,256]{1,0:T(8,128)(2,1)} %bitcast.108, bf16[2048,128]{1,0:T(8,128)(2,1)} %copy-done.6, bf16[32,384]{1,0:T(8,128)(2,1)S(1)} %collective-permute-done.6.above_ref, bf16[32,384]{1,0:T(8,128)(2,1)S(1)} %collective-permute-done.7.below_ref, ...), custom_call_target="tpu_custom_call" | custom-call | tf_op jit(solution)/shard_map/conv/pallas_call | solution.py:338
  162.2 2.4 %pad_maximum_fusion = f32[32,32,2,2,128]{4,3,2,1,0:T(2,128)} fusion(f32[32,32,1,2,128]{4,3,2,1,0:T(2,128)S(1)} %get-tuple-element.102, f32[32,32,1,2,128]{4,3,2,1,0:T(2,128)S(1)} %get-tuple-element.101), kind=kLoop, calls=%fused_computation.3 | loop fusion | flops 524288 | bytes 4194304 | tf_op jit(solution)/shard_map/stack | solution.py:417
  164.6 6.9 %all-to-all-done.7 = bf16[16,2,64,256]{3,2,1,0:T(8,128)(2,1)S(1)} async-done(((bf16[16,2,64,256]{3,2,1,0:T(8,128)(2,1)}), bf16[16,2,64,256]{3,2,1,0:T(8,128)(2,1)S(1)}, u32[]{:S(2)}, u32[]{:S(2)}) %all-to-all-start.7) | async-done | bytes 1048608 | tf_op jit(solution)/shard_map/all_to_all | solution.py:404
  (72 shorter events, 13.1 us)
Async XLA Ops:
  0.6 7.5 %copy-start.5 = (bf16[1,32,64,256]{3,2,1,0:T(8,128)(2,1)S(1)}, bf16[1,32,64,256]{3,2,1,0:T(8,128)(2,1)}, u32[]{:S(2)}) copy-start(bf16[1,32,64,256]{3,2,1,0:T(8,128)(2,1)} %param.11) | copy-start | bytes 3145732
  0.6 8.1 %copy-start.9 = (bf16[2,256]{1,0:T(2,128)(2,1)S(1)}, bf16[2,256]{1,0:T(2,128)(2,1)}, u32[]{:S(2)}) copy-start(bf16[2,256]{1,0:T(2,128)(2,1)} %constant.15.clone) | copy-start | bytes 3076
  0.7 23.5 %all-to-all-start = ((bf16[16,2,64,256]{3,2,1,0:T(8,128)(2,1)}), bf16[16,2,64,256]{3,2,1,0:T(8,128)(2,1)S(1)}, u32[]{:S(2)}, u32[]{:S(2)}) async-start(bf16[16,2,64,256]{3,2,1,0:T(8,128)(2,1)} %bitcast.112), calls=%async_computation | async-start | bytes 2097152 | tf_op jit(solution)/shard_map/all_to_all | solution.py:404
  8.1 8.1 %copy-start.8 = (bf16[9,32,32]{2,1,0:T(8,128)(2,1)S(1)}, bf16[9,32,32]{2,1,0:T(8,128)(2,1)}, u32[]{:S(2)}) copy-start(bf16[9,32,32]{2,1,0:T(8,128)(2,1)} %param.13) | copy-start | bytes 55300
  8.7 7.6 %copy-start.4 = (bf16[1,32,64,256]{3,1,2,0:T(8,128)(2,1)}, bf16[1,32,64,256]{3,1,2,0:T(8,128)(2,1)S(1)}, u32[]{:S(2)}) copy-start(bf16[1,32,64,256]{3,1,2,0:T(8,128)(2,1)S(1)} %copy.63) | copy-start | bytes 3145732
  8.8 11.7 %copy-start.10 = (f32[128]{0:T(128)S(1)}, f32[128]{0:T(128)}, u32[]{:S(2)}) copy-start(f32[128]{0:T(128)} %constant.41) | copy-start | bytes 1540
  8.8 11.7 %copy-start.11 = (f32[128]{0:T(128)S(1)}, f32[128]{0:T(128)}, u32[]{:S(2)}) copy-start(f32[128]{0:T(128)} %constant.38) | copy-start | bytes 1540
  8.8 15.3 %copy-start.1 = (bf16[256,1536]{1,0:T(8,128)(2,1)S(1)}, bf16[256,1536]{1,0:T(8,128)(2,1)}, u32[]{:S(2)}) copy-start(bf16[256,1536]{1,0:T(8,128)(2,1)} %constant.13.clone.table_ref) | copy-start | bytes 2359300
  9.2 8.7 %collective-permute-start = (bf16[1,2048]{1,0:T(2,128)(2,1)S(1)}, bf16[1,2048]{1,0:T(2,128)(2,1)S(1)}, u32[]{:S(2)}, u32[]{:S(2)}) collective-permute-start(bf16[1,2048]{1,0:T(2,128)(2,1)S(1)} %get-tuple-element.109), channel_id=1, source_target_pairs={{1,0},{2,1},{3,2},{5,4},{6,5},{7,6},{9,8},{10,9},{11,10},{13,12},{... | collective-permute-start | bytes 12296 | tf_op jit(solution)/shard_map/ppermute | solution.py:364
  10.6 9.8 %collective-permute-start.1 = (bf16[1,2048]{1,0:T(2,128)(2,1)S(1)}, bf16[1,2048]{1,0:T(2,128)(2,1)S(1)}, u32[]{:S(2)}, u32[]{:S(2)}) collective-permute-start(bf16[1,2048]{1,0:T(2,128)(2,1)S(1)} %get-tuple-element.110), channel_id=1, source_target_pairs={{0,1},{1,2},{2,3},{4,5},{5,6},{6,7},{8,9},{9,10},{10,11},{12,13},{... | collective-permute-start | bytes 12296 | tf_op jit(solution)/shard_map/ppermute | solution.py:364
  20.5 35.6 %copy-start.12 = (f32[32]{0:T(128)S(1)}, f32[32]{0:T(128)}, u32[]{:S(2)}) copy-start(f32[32]{0:T(128)} %param.14) | copy-start | bytes 388
  21.1 0.8 copy-start.7
  25.8 22.1 %all-to-all-start.1 = ((bf16[64,8,128]{2,1,0:T(8,128)(2,1)}), bf16[64,8,128]{2,1,0:T(8,128)(2,1)S(1)}, u32[]{:S(2)}, u32[]{:S(2)}) async-start(bf16[64,8,128]{2,1,0:T(8,128)(2,1)} %to_modes.2), calls=%async_computation.1 | async-start | bytes 262144 | tf_op jit(solution)/shard_map/all_to_all | solution.py:404
  36.7 12.3 %collective-permute-start.2 = (bf16[32,384]{1,0:T(8,128)(2,1)S(1)}, bf16[32,384]{1,0:T(8,128)(2,1)S(1)}, u32[]{:S(2)}, u32[]{:S(2)}) collective-permute-start(bf16[32,384]{1,0:T(8,128)(2,1)S(1)} %get-tuple-element.52), channel_id=1, source_target_pairs={{0,4},{4,8},{8,12},{12,16},{16,20},{20,24},{24,28},{28,32},{32,36}... | collective-permute-start | bytes 73736 | tf_op jit(solution)/shard_map/ppermute | solution.py:364
  40.2 8.7 %collective-permute-start.3 = (bf16[32,384]{1,0:T(8,128)(2,1)S(1)}, bf16[32,384]{1,0:T(8,128)(2,1)S(1)}, u32[]{:S(2)}, u32[]{:S(2)}) collective-permute-start(bf16[32,384]{1,0:T(8,128)(2,1)S(1)} %get-tuple-element.53), channel_id=1, source_target_pairs={{4,0},{8,4},{12,8},{16,12},{20,16},{24,20},{28,24},{32,28},{36,32}... | collective-permute-start | bytes 73736 | tf_op jit(solution)/shard_map/ppermute | solution.py:364
  49.0 18.3 %copy-start = (bf16[1536,256]{1,0:T(8,128)(2,1)S(1)}, bf16[1536,256]{1,0:T(8,128)(2,1)}, u32[]{:S(2)}) copy-start(bf16[1536,256]{1,0:T(8,128)(2,1)} %constant.14.clone.table_ref) | copy-start | bytes 2359300
  49.0 18.3 %all-to-all-start.2 = ((bf16[64,8,128]{2,1,0:T(8,128)(2,1)}), bf16[64,8,128]{2,1,0:T(8,128)(2,1)S(1)}, u32[]{:S(2)}, u32[]{:S(2)}) async-start(bf16[64,8,128]{2,1,0:T(8,128)(2,1)} %get-tuple-element.54), calls=%async_computation.2 | async-start | bytes 262144 | tf_op jit(solution)/shard_map/all_to_all | solution.py:404
  67.3 19.1 %copy-start.3 = (bf16[1,32,64,256]{3,2,1,0:T(8,128)(2,1)S(1)}, bf16[1,32,64,256]{3,2,1,0:T(8,128)(2,1)}, u32[]{:S(2)}) copy-start(bf16[1,32,64,256]{3,2,1,0:T(8,128)(2,1)} %param.15) | copy-start | bytes 3145732
  88.3 20.7 %all-to-all-start.4 = ((bf16[16,2,64,256]{3,2,1,0:T(8,128)(2,1)}), bf16[16,2,64,256]{3,2,1,0:T(8,128)(2,1)S(1)}, u32[]{:S(2)}, u32[]{:S(2)}) async-start(bf16[16,2,64,256]{3,2,1,0:T(8,128)(2,1)} %bitcast.16), calls=%async_computation.4 | async-start | bytes 2097152 | tf_op jit(solution)/shard_map/all_to_all | solution.py:404
  92.9 16.1 %copy-start.2 = (bf16[256,1536]{1,0:T(8,128)(2,1)S(1)}, bf16[256,1536]{1,0:T(8,128)(2,1)}, u32[]{:S(2)}) copy-start(bf16[256,1536]{1,0:T(8,128)(2,1)} %constant.13.clone.table_ref) | copy-start | bytes 2359300
  97.7 7.1 %collective-permute-start.4 = (bf16[1,2048]{1,0:T(2,128)(2,1)S(1)}, bf16[1,2048]{1,0:T(2,128)(2,1)S(1)}, u32[]{:S(2)}, u32[]{:S(2)}) collective-permute-start(bf16[1,2048]{1,0:T(2,128)(2,1)S(1)} %get-tuple-element.107), channel_id=1, source_target_pairs={{1,0},{2,1},{3,2},{5,4},{6,5},{7,6},{9,8},{10,9},{11,10},{13,12},{... | collective-permute-start | bytes 12296 | tf_op jit(solution)/shard_map/ppermute | solution.py:364
  99.0 5.9 %collective-permute-start.5 = (bf16[1,2048]{1,0:T(2,128)(2,1)S(1)}, bf16[1,2048]{1,0:T(2,128)(2,1)S(1)}, u32[]{:S(2)}, u32[]{:S(2)}) collective-permute-start(bf16[1,2048]{1,0:T(2,128)(2,1)S(1)} %get-tuple-element.108), channel_id=1, source_target_pairs={{0,1},{1,2},{2,3},{4,5},{5,6},{6,7},{8,9},{9,10},{10,11},{12,13},{... | collective-permute-start | bytes 12296 | tf_op jit(solution)/shard_map/ppermute | solution.py:364
  105.5 0.8 copy-start.6
  110.7 20.2 %all-to-all-start.5 = ((bf16[64,8,128]{2,1,0:T(8,128)(2,1)}), bf16[64,8,128]{2,1,0:T(8,128)(2,1)S(1)}, u32[]{:S(2)}, u32[]{:S(2)}) async-start(bf16[64,8,128]{2,1,0:T(8,128)(2,1)} %to_modes.3), calls=%async_computation.5 | async-start | bytes 262144 | tf_op jit(solution)/shard_map/all_to_all | solution.py:404
  119.7 11.6 %collective-permute-start.6 = (bf16[32,384]{1,0:T(8,128)(2,1)S(1)}, bf16[32,384]{1,0:T(8,128)(2,1)S(1)}, u32[]{:S(2)}, u32[]{:S(2)}) collective-permute-start(bf16[32,384]{1,0:T(8,128)(2,1)S(1)} %pad_maximum_fusion.4), channel_id=1, source_target_pairs={{0,4},{4,8},{8,12},{12,16},{16,20},{20,24},{24,28},{28,32},{32,36}... | collective-permute-start | bytes 73736 | tf_op jit(solution)/shard_map/ppermute | solution.py:364
  123.2 8.1 %collective-permute-start.7 = (bf16[32,384]{1,0:T(8,128)(2,1)S(1)}, bf16[32,384]{1,0:T(8,128)(2,1)S(1)}, u32[]{:S(2)}, u32[]{:S(2)}) collective-permute-start(bf16[32,384]{1,0:T(8,128)(2,1)S(1)} %pad_maximum_fusion.3), channel_id=1, source_target_pairs={{4,0},{8,4},{12,8},{16,12},{20,16},{24,20},{28,24},{32,28},{36,32}... | collective-permute-start | bytes 73736 | tf_op jit(solution)/shard_map/ppermute | solution.py:364
  151.7 19.8 %all-to-all-start.7 = ((bf16[16,2,64,256]{3,2,1,0:T(8,128)(2,1)}), bf16[16,2,64,256]{3,2,1,0:T(8,128)(2,1)S(1)}, u32[]{:S(2)}, u32[]{:S(2)}) async-start(bf16[16,2,64,256]{3,2,1,0:T(8,128)(2,1)} %to_field.3), calls=%async_computation.7 | async-start | bytes 2097152 | tf_op jit(solution)/shard_map/all_to_all | solution.py:404

commit v10 on v9

--- a/solution.py
+++ b/solution.py
@@ -356,12 +356,66 @@
     )
 
 
+def conv_stacked_kernel(matrix_ref, main_ref, side_ref, bias_ref, out_ref):
+    ins = matrix_ref.shape[1] // (CONV_ROWS + 2)
+    outs, rows, width = out_ref.shape
+    window = (CONV_ROWS + 2) * ins
+    tall = 2 * CONV_ROWS
+
+    @pl.loop(0, rows // tall)
+    def _(step):
+        pieces = []
+        for part in range(tall // CONV_ROWS):
+            start = pl.multiple_of((step * tall + part * CONV_ROWS) * ins, ins)
+            main = dot(matrix_ref[...], main_ref[pl.ds(start, window), :])
+            side = dot(matrix_ref[...], side_ref[pl.ds(start, window), :])
+            taps = jnp.concatenate([main, side], axis=1)
+            full = taps.shape[1]
+            for row in range(CONV_ROWS):
+                base = row * 3 * outs
+                low = pltpu.roll(taps[base : base + outs], 1, 1)[:, :width]
+                mid = taps[base + outs : base + 2 * outs, :width]
+                high = pltpu.roll(taps[base + 2 * outs : base + 3 * outs], full - 1, 1)[:, :width]
+                pieces.append(low + mid + high + bias_ref[:, :1])
+        first = pl.multiple_of(step * tall, tall)
+        out_ref[:, pl.ds(first, tall), :] = jnp.transpose(jnp.stack(pieces, axis=0), (1, 0, 2))
+
+
+def conv_stacked(matrix, main, side, bias, rows):
+    outs = matrix.shape[0] // (3 * CONV_ROWS)
+    return on_chip(
+        conv_stacked_kernel,
+        ((outs, rows, main.shape[1]), F32),
+        [],
+        "conv_stacked",
+        matrix,
+        pltpu.with_memory_space_constraint(main, pltpu.HBM),
+        side,
+        bias,
+        apart=(1,),
+    )
+
+
 def swap(value, axis, back=False):
     count = lax.axis_size(axis)
     pairs = [(i, i + 1) for i in range(count - 1)]
     if back:
         pairs = [(b, a) for a, b in pairs]
     return lax.ppermute(value, axis, pairs)
+
+
+def across_edges(field):
+    return swap(field[:, -1], "gx"), swap(field[:, 0], "gx", back=True)
+
+
+def stack_rows(field, above, below):
+    channels, rows, width = field.shape
+    main = jnp.concatenate([above[None], jnp.transpose(field, (1, 0, 2)), below[None]], axis=0)
+    main = main.reshape((rows + 2) * channels, width)
+    pick = np.zeros((2, width), np.float32)
+    pick[0, 0] = pick[1, width - 1] = 1.0
+    ends = jnp.einsum("ry,ny->rn", pick.astype(BF), main, preferred_element_type=F32).astype(BF)
+    return main, ends
 
 
 def by_rows(field):
@@ -441,13 +495,12 @@
     right, left = across_columns(ends)
     weight = jnp.transpose(spectral_weight, (3, 2, 0, 1, 4))
     matrix = conv_matrix(conv_weight)
-    side = place_columns(right, left, side_slots())
-    first, last = edge_rows(main, side, channels)
-    block, first, last, weight, matrix = hold((block, first, last, weight, matrix))
+    block, weight, matrix = hold((block, weight, matrix))
     parts = to_modes(block, False, 1.0, tables, owners)
-    parts, first, last = hold((parts, first, last))
+    parts, right, left, places = hold((parts, right, left, side_slots()))
     parts = exchange(parts, both)
-    above, below = across_rows(first, last)
+    side = place_columns(right, left, places)
+    above, below = across_rows(*edge_rows(main, side, channels))
     mixed, spec = mix(parts, weight, 1, strips)
     mixed, above, below = hold((mixed, above, below))
     arrived = exchange(mixed, both)
@@ -457,28 +510,25 @@
     spectral = exchange(back, "gx").reshape(whole)
 
     dpre, activation = gate_both(local, spectral, upstream[0])
-    dpre, taps, dweight = hold((dpre, conv_weight, spectral_weight))
 
     dblock = exchange(dpre.reshape(share), "gx")
-    dmain, dends = by_rows(dpre)
+    dabove, dbelow = across_edges(dpre)
+    dparts = to_modes(dblock, True, scale, tables, owners)
+    dparts, dhere, dabove, dbelow, taps, dweight = hold(
+        (dparts, dpre, dabove, dbelow, conv_weight, spectral_weight)
+    )
+    dparts = exchange(dparts, both)
+    dmatrix = conv_matrix(jnp.transpose(taps[::-1], (0, 2, 1)))
+    dweight = jnp.transpose(dweight, (3, 2, 1, 0, 4))
+    dmain, dends = stack_rows(dhere, dabove, dbelow)
+    dparts, dends, dmain, dmatrix, dweight = hold((dparts, dends, dmain, dmatrix, dweight))
+    dmixed, dspec = mix(dparts, dweight, -1, strips)
+    darrived = exchange(dmixed, both)
     dright, dleft = across_columns(dends)
-    dmatrix = conv_matrix(jnp.transpose(taps[::-1], (0, 2, 1)))
-    dside = place_columns(dright, dleft, side_slots())
-    dfirst, dlast = edge_rows(dmain, dside, channels)
-    dblock, dmatrix, dfirst, dlast = hold((dblock, dmatrix, dfirst, dlast))
-    dparts = to_modes(dblock, True, scale, tables, owners)
-    dparts, dfirst, dlast, dweight = hold((dparts, dfirst, dlast, dweight))
-    dparts = exchange(dparts, both)
-    dweight = jnp.transpose(dweight, (3, 2, 1, 0, 4))
-    dabove, dbelow = across_rows(dfirst, dlast)
-    dparts, dweight = hold((dparts, dweight))
-    dmixed, dspec = mix(dparts, dweight, -1, strips)
-    dmixed, dabove, dbelow = hold((dmixed, dabove, dbelow))
-    darrived = exchange(dmixed, both)
     dback = to_field(darrived, False, 1.0, tables, share)
-    dback, dabove, dbelow, spec, dspec = hold((dback, dabove, dbelow, spec, dspec))
+    dback, dright, dleft, places, spec, dspec = hold((dback, dright, dleft, places, spec, dspec))
     dfield = exchange(dback, "gx").reshape(whole)
-    back_local = conv(dmatrix, dmain, dside, dabove, dbelow, jnp.zeros_like(bias))
+    back_local = conv_stacked(dmatrix, dmain, place_columns(dright, dleft, places), jnp.zeros_like(bias), width_x)
     slots = M1 // owners
     weight_grad = weight_grads(by_mode(spec, slots), by_mode(dspec, slots))
     dfield, back_local, weight_grad = hold((dfield, back_local, weight_grad))

time: 174 us -> 167 us (0.960)
  blocking collectives: 37.1 us -> 18.4 us
  waiting for transfers between devices: 29.8 us -> 47.2 us
  local copies, waits for them, and re-layouts: 9.71 us -> 4.96 us
  starting transfers between devices: 67.2 us -> 65.4 us
    all_to_all x6 -> x7, waiting for transfers between devices: 27.2 us -> 47.1 us  [exchange(): return lax.all_to_all(value, axes, split_axis=0, concat_axis=0, tiled=True)]
    all_to_all x2 -> x1, blocking collectives: 37.1 us -> 18.4 us  [exchange(): return lax.all_to_all(value, axes, split_axis=0, concat_axis=0, tiled=True)]
    pallas_call x6 -> x7, Pallas kernels: 7.27 us -> 12.9 us  [on_chip(): pl.pallas_call(kernel, in_specs=[spec] * len(values), out_specs=[spec] *...]
    pallas_call x2 -> x1, Pallas kernels: 10.3 us -> 5.15 us  [conv(): pl.pallas_call(conv_kernel, in_specs=[vmem, hbm, hbm, vmem, vmem, vmem],...]
    optimization_barrier x2 -> x1, local copies, waits for them, and re-layouts: 4.76 us -> 0.68 us  [body(): hold((dparts, dpre, dabove, dbelow, conv_weight, spectral_weight))]
    ppermute x8, waiting for transfers between devices: 2.66 us -> 0.02 us  [swap(): return lax.ppermute(value, axis, pairs)]
    concatenate x0 -> x1, other arithmetic: none -> 2.07 us  [stack_rows(): jnp.concatenate([above[None], jnp.transpose(field, (1, 0, 2)), below[None...]
    unnamed x28 -> x30, local copies, waits for them, and re-layouts: 3.57 us -> 2.33 us
  transfers between devices with their start and end apart: 14 -> 15, of which waited for: 8 -> 7; matrix products, arithmetic and copies ran while one was open for 9% -> 7% of each run, Pallas kernels for 7% -> 10%
where the time goes in v10:
time: 167 us; the launch traced here: 166 us
  starting transfers between devices  65.4 us (39%)
  waiting for transfers between devices  47.2 us (28%)
  Pallas kernels  21.3 us (13%)
  blocking collectives  18.4 us (11%)
  other arithmetic  5.96 us (4%)
  local copies, waits for them, and re-layouts  4.96 us (3%)
    all_to_all x7, waiting for transfers between devices, exchange(): return lax.all_to_all(value, axes, split_axis=0, concat_axis=0, tiled=True)  47.1 us
    all_to_all x7, starting transfers between devices, exchange(): return lax.all_to_all(value, axes, split_axis=0, concat_axis=0, tiled=True)  42.7 us
    ppermute x8, starting transfers between devices, swap(): return lax.ppermute(value, axis, pairs)  22.7 us
    all_to_all x1, blocking collectives, exchange(): return lax.all_to_all(value, axes, split_axis=0, concat_axis=0, tiled=True)  18.4 us
    pallas_call x7, Pallas kernels, on_chip(): pl.pallas_call(kernel, in_specs=[spec] * len(values), out_specs=[spec] *...  12.9 us
    pallas_call x1, Pallas kernels, conv(): pl.pallas_call(conv_kernel, in_specs=[vmem, hbm, hbm, vmem, vmem, vmem],...  5.15 us
    another operation x2, other arithmetic, weight_grads(): return jnp.stack([grad_real, grad_imag], axis=2)  3.62 us
  transfers between devices with their start and end apart: 15, of which 7 were waited for; matrix products, arithmetic and copies ran while one was open for 7% of the time, Pallas kernels for 10%

profile of v10, /device:TPU:1, one launch (start us, length us, event | category | flops | bytes accessed | tf_op | source)
XLA Modules:
  0.0 166.0 jit_solution(13837832057033127602)
XLA Ops:
  0.7 7.5 %all-to-all-start = ((bf16[16,2,64,256]{3,2,1,0:T(8,128)(2,1)}), bf16[16,2,64,256]{3,2,1,0:T(8,128)(2,1)S(1)}, u32[]{:S(2)}, u32[]{:S(2)}) async-start(bf16[16,2,64,256]{3,2,1,0:T(8,128)(2,1)} %bitcast.110), calls=%async_computation | async-start | bytes 2097152 | tf_op jit(solution)/shard_map/all_to_all | solution.py:458
  9.2 5.1 %collective-permute-start.1 = (bf16[1,2048]{1,0:T(2,128)(2,1)S(1)}, bf16[1,2048]{1,0:T(2,128)(2,1)S(1)}, u32[]{:S(2)}, u32[]{:S(2)}) collective-permute-start(bf16[1,2048]{1,0:T(2,128)(2,1)S(1)} %get-tuple-element.95), channel_id=1, source_target_pairs={{0,1},{1,2},{2,3},{4,5},{5,6},{6,7},{8,9},{9,10},{10,11},{12,13},{... | collective-permute-start | bytes 12296 | tf_op jit(solution)/shard_map/ppermute | solution.py:404
  14.2 1.3 collective-permute-start
  15.9 1.4 copy.78
  17.3 6.9 %all-to-all-done.block_ref = bf16[16,2,64,256]{3,2,1,0:T(8,128)(2,1)S(1)} async-done(((bf16[16,2,64,256]{3,2,1,0:T(8,128)(2,1)}), bf16[16,2,64,256]{3,2,1,0:T(8,128)(2,1)S(1)}, u32[]{:S(2)}, u32[]{:S(2)}) %all-to-all-start) | async-done | bytes 1048608 | tf_op jit(solution)/shard_map/all_to_all | solution.py:458
  24.1 1.7 %to_modes.2 = bf16[64,8,128]{2,1,0:T(8,128)(2,1)} custom-call(bf16[16,2,64,256]{3,2,1,0:T(8,128)(2,1)S(1)} %all-to-all-done.block_ref, bf16[256,1536]{1,0:T(8,128)(2,1)S(1)} %copy-done.1), custom_call_target="tpu_custom_call" | custom-call | tf_op jit(solution)/shard_map/to_modes/pallas_call | solution.py:66
  25.8 9.4 %all-to-all-start.1 = ((bf16[64,8,128]{2,1,0:T(8,128)(2,1)}), bf16[64,8,128]{2,1,0:T(8,128)(2,1)S(1)}, u32[]{:S(2)}, u32[]{:S(2)}) async-start(bf16[64,8,128]{2,1,0:T(8,128)(2,1)} %to_modes.2), calls=%async_computation.1 | async-start | bytes 262144 | tf_op jit(solution)/shard_map/all_to_all | solution.py:458
  35.6 3.5 %collective-permute-start.2 = (bf16[32,384]{1,0:T(8,128)(2,1)S(1)}, bf16[32,384]{1,0:T(8,128)(2,1)S(1)}, u32[]{:S(2)}, u32[]{:S(2)}) collective-permute-start(bf16[32,384]{1,0:T(8,128)(2,1)S(1)} %pad_maximum_fusion.2), channel_id=1, source_target_pairs={{0,4},{4,8},{8,12},{12,16},{16,20},{20,24},{24,28},{28,32},{32,36}... | collective-permute-start | bytes 73736 | tf_op jit(solution)/shard_map/ppermute | solution.py:404
  39.2 1.9 %collective-permute-start.3 = (bf16[32,384]{1,0:T(8,128)(2,1)S(1)}, bf16[32,384]{1,0:T(8,128)(2,1)S(1)}, u32[]{:S(2)}, u32[]{:S(2)}) collective-permute-start(bf16[32,384]{1,0:T(8,128)(2,1)S(1)} %pad_maximum_fusion.3), channel_id=1, source_target_pairs={{4,0},{8,4},{12,8},{16,12},{20,16},{24,20},{28,24},{32,28},{36,32}... | collective-permute-start | bytes 73736 | tf_op jit(solution)/shard_map/ppermute | solution.py:404
  41.1 5.3 %all-to-all-done.1.parts_ref = bf16[64,8,128]{2,1,0:T(8,128)(2,1)S(1)} async-done(((bf16[64,8,128]{2,1,0:T(8,128)(2,1)}), bf16[64,8,128]{2,1,0:T(8,128)(2,1)S(1)}, u32[]{:S(2)}, u32[]{:S(2)}) %all-to-all-start.1) | async-done | bytes 131104 | tf_op jit(solution)/shard_map/all_to_all | solution.py:458
  47.5 7.5 %all-to-all-start.2 = ((bf16[64,8,128]{2,1,0:T(8,128)(2,1)}), bf16[64,8,128]{2,1,0:T(8,128)(2,1)S(1)}, u32[]{:S(2)}, u32[]{:S(2)}) async-start(bf16[64,8,128]{2,1,0:T(8,128)(2,1)} %get-tuple-element.48), calls=%async_computation.2 | async-start | bytes 262144 | tf_op jit(solution)/shard_map/all_to_all | solution.py:458
  55.1 5.1 %conv.1.local_ref = f32[32,64,256]{2,1,0:T(8,128)S(1)} custom-call(bf16[384,192]{1,0:T(8,128)(2,1)S(1)} %fusion.13.matrix_ref, bf16[2048,256]{1,0:T(8,128)(2,1)} %bitcast.109, bf16[2048,128]{1,0:T(8,128)(2,1)} %copy-done.8, bf16[32,384]{1,0:T(8,128)(2,1)S(1)} %collective-permute-done.2.above_ref, bf16[32,384]{1,0:T(8,128)(2,1)S(1)} %collective-permute-done.3.below_ref, ...), custom_call_target="tpu_custom_call" | custom-call | tf_op jit(solution)/shard_map/conv/pallas_call | solution.py:338
  60.3 6.0 %all-to-all-done.2.spec_ref = bf16[64,8,128]{2,1,0:T(8,128)(2,1)S(1)} async-done(((bf16[64,8,128]{2,1,0:T(8,128)(2,1)}), bf16[64,8,128]{2,1,0:T(8,128)(2,1)S(1)}, u32[]{:S(2)}, u32[]{:S(2)}) %all-to-all-start.2) | async-done | bytes 131104 | tf_op jit(solution)/shard_map/all_to_all | solution.py:458
  66.9 18.4 %all_to_all.40 = bf16[16,2,64,256]{3,2,1,0:T(8,128)(2,1)S(1)} all-to-all(bf16[16,2,64,256]{3,2,1,0:T(8,128)(2,1)S(1)} %to_field.2), channel_id=1, replica_groups=mesh['dp'=4,'gx'=16,'gy'=4] {'gx'}, dimensions={0} | all-to-all | bytes 2097152 | tf_op jit(solution)/shard_map/all_to_all | solution.py:458
  85.3 1.9 %gate_both.1 = (bf16[32,64,256]{2,1,0:T(8,128)(2,1)}, f32[32,64,256]{2,1,0:T(8,128)}) custom-call(f32[32,64,256]{2,1,0:T(8,128)S(1)} %conv.1.local_ref, bf16[32,64,256]{2,1,0:T(8,128)(2,1)S(1)} %bitcast.101, bf16[32,64,256]{2,1,0:T(8,128)(2,1)S(1)} %bitcast.102), custom_call_target="tpu_custom_call" | custom-call | tf_op jit(solution)/shard_map/gate_both/pallas_call | solution.py:239
  87.3 4.8 %all-to-all-start.4 = ((bf16[16,2,64,256]{3,2,1,0:T(8,128)(2,1)}), bf16[16,2,64,256]{3,2,1,0:T(8,128)(2,1)S(1)}, u32[]{:S(2)}, u32[]{:S(2)}) async-start(bf16[16,2,64,256]{3,2,1,0:T(8,128)(2,1)} %bitcast.14), calls=%async_computation.4 | async-start | bytes 2097152 | tf_op jit(solution)/shard_map/all_to_all | solution.py:458
  93.1 3.5 %collective-permute-start.4 = (bf16[32,256]{1,0:T(8,128)(2,1)S(1)}, bf16[32,256]{1,0:T(8,128)(2,1)S(1)}, u32[]{:S(2)}, u32[]{:S(2)}) collective-permute-start(bf16[32,256]{1,0:T(8,128)(2,1)S(1)} %bitcast.119), channel_id=1, source_target_pairs={{0,4},{4,8},{8,12},{12,16},{16,20},{20,24},{24,28},{28,32},{32,36}... | collective-permute-start | bytes 49160 | tf_op jit(solution)/shard_map/ppermute | solution.py:404
  96.6 1.9 %collective-permute-start.5 = (bf16[32,256]{1,0:T(8,128)(2,1)S(1)}, bf16[32,256]{1,0:T(8,128)(2,1)S(1)}, u32[]{:S(2)}, u32[]{:S(2)}) collective-permute-start(bf16[32,256]{1,0:T(8,128)(2,1)S(1)} %bitcast.117), channel_id=1, source_target_pairs={{4,0},{8,4},{12,8},{16,12},{20,16},{24,20},{28,24},{32,28},{36,32}... | collective-permute-start | bytes 49160 | tf_op jit(solution)/shard_map/ppermute | solution.py:404
  98.6 9.4 %all-to-all-done.4.block_ref = bf16[16,2,64,256]{3,2,1,0:T(8,128)(2,1)S(1)} async-done(((bf16[16,2,64,256]{3,2,1,0:T(8,128)(2,1)}), bf16[16,2,64,256]{3,2,1,0:T(8,128)(2,1)S(1)}, u32[]{:S(2)}, u32[]{:S(2)}) %all-to-all-start.4) | async-done | bytes 1048608 | tf_op jit(solution)/shard_map/all_to_all | solution.py:458
  107.9 1.7 %to_modes.3 = bf16[64,8,128]{2,1,0:T(8,128)(2,1)} custom-call(bf16[16,2,64,256]{3,2,1,0:T(8,128)(2,1)S(1)} %all-to-all-done.4.block_ref, bf16[256,1536]{1,0:T(8,128)(2,1)S(1)} %copy-done.2), custom_call_target="tpu_custom_call" | custom-call | tf_op jit(solution)/shard_map/to_modes/pallas_call | solution.py:66
  109.6 4.9 %all-to-all-start.5 = ((bf16[64,8,128]{2,1,0:T(8,128)(2,1)}), bf16[64,8,128]{2,1,0:T(8,128)(2,1)S(1)}, u32[]{:S(2)}, u32[]{:S(2)}) async-start(bf16[64,8,128]{2,1,0:T(8,128)(2,1)} %to_modes.3), calls=%async_computation.5 | async-start | bytes 262144 | tf_op jit(solution)/shard_map/all_to_all | solution.py:458
  114.9 2.1 %pad_maximum_fusion.1 = bf16[66,32,256]{2,0,1:T(8,128)(2,1)S(1)} fusion(bf16[1,32,256]{2,0,1:T(2,128)(2,1)S(1)} %copy.43, bf16[64,32,256]{2,0,1:T(8,128)(2,1)} %bitcast.16, bf16[1,32,256]{2,0,1:T(2,128)(2,1)S(1)} %copy.42), kind=kLoop, calls=%fused_computation.6 | loop fusion | flops 3244032 | bytes 2162688 | tf_op jit(solution)/shard_map/concatenate | solution.py:413
  118.7 7.1 %all-to-all-done.5.parts_ref = bf16[64,8,128]{2,1,0:T(8,128)(2,1)S(1)} async-done(((bf16[64,8,128]{2,1,0:T(8,128)(2,1)}), bf16[64,8,128]{2,1,0:T(8,128)(2,1)S(1)}, u32[]{:S(2)}, u32[]{:S(2)}) %all-to-all-start.5) | async-done | bytes 131104 | tf_op jit(solution)/shard_map/all_to_all | solution.py:458
  126.9 4.7 %all-to-all-start.6 = ((bf16[64,8,128]{2,1,0:T(8,128)(2,1)}), bf16[64,8,128]{2,1,0:T(8,128)(2,1)S(1)}, u32[]{:S(2)}, u32[]{:S(2)}) async-start(bf16[64,8,128]{2,1,0:T(8,128)(2,1)} %get-tuple-element.64), calls=%async_computation.6 | async-start | bytes 262144 | tf_op jit(solution)/shard_map/all_to_all | solution.py:458
  131.7 4.2 %collective-permute-start.7 = (bf16[1,2112]{1,0:T(2,128)(2,1)S(1)}, bf16[1,2112]{1,0:T(2,128)(2,1)S(1)}, u32[]{:S(2)}, u32[]{:S(2)}) collective-permute-start(bf16[1,2112]{1,0:T(2,128)(2,1)S(1)} %get-tuple-element.93), channel_id=1, source_target_pairs={{0,1},{1,2},{2,3},{4,5},{5,6},{6,7},{8,9},{9,10},{10,11},{12,13},{... | collective-permute-start | bytes 12680 | tf_op jit(solution)/shard_map/ppermute | solution.py:404
  137.2 5.8 %all-to-all-done.6.spec_ref = bf16[64,8,128]{2,1,0:T(8,128)(2,1)S(1)} async-done(((bf16[64,8,128]{2,1,0:T(8,128)(2,1)}), bf16[64,8,128]{2,1,0:T(8,128)(2,1)S(1)}, u32[]{:S(2)}, u32[]{:S(2)}) %all-to-all-start.6) | async-done | bytes 131104 | tf_op jit(solution)/shard_map/all_to_all | solution.py:458
  143.0 1.7 %to_field.3 = bf16[16,2,64,256]{3,2,1,0:T(8,128)(2,1)} custom-call(bf16[64,8,128]{2,1,0:T(8,128)(2,1)S(1)} %all-to-all-done.6.spec_ref, bf16[1536,256]{1,0:T(8,128)(2,1)S(1)} %copy-done), custom_call_target="tpu_custom_call" | custom-call | tf_op jit(solution)/shard_map/to_field/pallas_call | solution.py:66
  144.6 3.9 %all-to-all-start.7 = ((bf16[16,2,64,256]{3,2,1,0:T(8,128)(2,1)}), bf16[16,2,64,256]{3,2,1,0:T(8,128)(2,1)S(1)}, u32[]{:S(2)}, u32[]{:S(2)}) async-start(bf16[16,2,64,256]{3,2,1,0:T(8,128)(2,1)} %to_field.3), calls=%async_computation.7 | async-start | bytes 2097152 | tf_op jit(solution)/shard_map/all_to_all | solution.py:458
  148.9 5.0 %conv_stacked.1.local_ref = f32[32,64,256]{2,1,0:T(8,128)S(1)} custom-call(bf16[384,192]{1,0:T(8,128)(2,1)S(1)} %fusion.16.matrix_ref, bf16[2112,256]{1,0:T(8,128)(2,1)} %bitcast.106, bf16[2112,128]{1,0:T(8,128)(2,1)S(1)} %convolution_convert_fusion.side_ref, f32[32,128]{1,0:T(8,128)S(1)} %broadcast_in_dim.25.bias_ref), custom_call_target="tpu_custom_call" | custom-call | tf_op jit(solution)/shard_map/conv_stacked/pallas_call | solution.py:66
  155.4 2.4 %pad_maximum_fusion = f32[32,32,2,2,128]{4,3,2,1,0:T(2,128)} fusion(f32[32,32,1,2,128]{4,3,2,1,0:T(2,128)S(1)} %get-tuple-element.88, f32[32,32,1,2,128]{4,3,2,1,0:T(2,128)S(1)} %get-tuple-element.87), kind=kLoop, calls=%fused_computation.5 | loop fusion | flops 524288 | bytes 4194304 | tf_op jit(solution)/shard_map/stack | solution.py:471
  157.8 6.7 %all-to-all-done.7 = bf16[16,2,64,256]{3,2,1,0:T(8,128)(2,1)S(1)} async-done(((bf16[16,2,64,256]{3,2,1,0:T(8,128)(2,1)}), bf16[16,2,64,256]{3,2,1,0:T(8,128)(2,1)S(1)}, u32[]{:S(2)}, u32[]{:S(2)}) %all-to-all-start.7) | async-done | bytes 1048608 | tf_op jit(solution)/shard_map/all_to_all | solution.py:458
  164.5 1.4 add_field.1
  (70 shorter events, 10.7 us)
Async XLA Ops:
  0.6 7.5 %copy-start.6 = (bf16[1,32,64,256]{3,2,1,0:T(8,128)(2,1)S(1)}, bf16[1,32,64,256]{3,2,1,0:T(8,128)(2,1)}, u32[]{:S(2)}) copy-start(bf16[1,32,64,256]{3,2,1,0:T(8,128)(2,1)} %param.10) | copy-start | bytes 3145732
  0.6 8.1 %copy-start.10 = (bf16[2,256]{1,0:T(2,128)(2,1)S(1)}, bf16[2,256]{1,0:T(2,128)(2,1)}, u32[]{:S(2)}) copy-start(bf16[2,256]{1,0:T(2,128)(2,1)} %constant.15.clone) | copy-start | bytes 3076
  0.7 23.5 %all-to-all-start = ((bf16[16,2,64,256]{3,2,1,0:T(8,128)(2,1)}), bf16[16,2,64,256]{3,2,1,0:T(8,128)(2,1)S(1)}, u32[]{:S(2)}, u32[]{:S(2)}) async-start(bf16[16,2,64,256]{3,2,1,0:T(8,128)(2,1)} %bitcast.110), calls=%async_computation | async-start | bytes 2097152 | tf_op jit(solution)/shard_map/all_to_all | solution.py:458
  8.1 7.4 %copy-start.9 = (bf16[9,32,32]{2,1,0:T(8,128)(2,1)S(1)}, bf16[9,32,32]{2,1,0:T(8,128)(2,1)}, u32[]{:S(2)}) copy-start(bf16[9,32,32]{2,1,0:T(8,128)(2,1)} %param.12) | copy-start | bytes 55300
  8.7 7.0 %copy-start.5 = (bf16[1,32,64,256]{3,1,2,0:T(8,128)(2,1)}, bf16[1,32,64,256]{3,1,2,0:T(8,128)(2,1)S(1)}, u32[]{:S(2)}) copy-start(bf16[1,32,64,256]{3,1,2,0:T(8,128)(2,1)S(1)} %copy.82) | copy-start | bytes 3145732
  8.8 15.4 %copy-start.1 = (bf16[256,1536]{1,0:T(8,128)(2,1)S(1)}, bf16[256,1536]{1,0:T(8,128)(2,1)}, u32[]{:S(2)}) copy-start(bf16[256,1536]{1,0:T(8,128)(2,1)} %constant.13.clone.table_ref) | copy-start | bytes 2359300
  9.2 16.6 %collective-permute-start.1 = (bf16[1,2048]{1,0:T(2,128)(2,1)S(1)}, bf16[1,2048]{1,0:T(2,128)(2,1)S(1)}, u32[]{:S(2)}, u32[]{:S(2)}) collective-permute-start(bf16[1,2048]{1,0:T(2,128)(2,1)S(1)} %get-tuple-element.95), channel_id=1, source_target_pairs={{0,1},{1,2},{2,3},{4,5},{5,6},{6,7},{8,9},{9,10},{10,11},{12,13},{... | collective-permute-start | bytes 12296 | tf_op jit(solution)/shard_map/ppermute | solution.py:404
  14.2 11.6 %collective-permute-start = (bf16[1,2048]{1,0:T(2,128)(2,1)S(1)}, bf16[1,2048]{1,0:T(2,128)(2,1)S(1)}, u32[]{:S(2)}, u32[]{:S(2)}) collective-permute-start(bf16[1,2048]{1,0:T(2,128)(2,1)S(1)} %get-tuple-element.96), channel_id=1, source_target_pairs={{1,0},{2,1},{3,2},{5,4},{6,5},{7,6},{9,8},{10,9},{11,10},{13,12},{... | collective-permute-start | bytes 12296 | tf_op jit(solution)/shard_map/ppermute | solution.py:404
  15.9 19.3 %copy-start.11 = (bf16[2,128]{1,0:T(2,128)(2,1)S(1)}, bf16[2,128]{1,0:T(2,128)(2,1)}, u32[]{:S(2)}) copy-start(bf16[2,128]{1,0:T(2,128)(2,1)} %constant.16.clone) | copy-start | bytes 1540
  24.1 30.9 %copy-start.12 = (f32[32]{0:T(128)S(1)}, f32[32]{0:T(128)}, u32[]{:S(2)}) copy-start(f32[32]{0:T(128)} %param.13) | copy-start | bytes 388
  25.8 20.6 %all-to-all-start.1 = ((bf16[64,8,128]{2,1,0:T(8,128)(2,1)}), bf16[64,8,128]{2,1,0:T(8,128)(2,1)S(1)}, u32[]{:S(2)}, u32[]{:S(2)}) async-start(bf16[64,8,128]{2,1,0:T(8,128)(2,1)} %to_modes.2), calls=%async_computation.1 | async-start | bytes 262144 | tf_op jit(solution)/shard_map/all_to_all | solution.py:458
  35.6 19.4 %copy-start.8 = (bf16[2048,128]{1,0:T(8,128)(2,1)}, bf16[2048,128]{1,0:T(8,128)(2,1)S(1)}, u32[]{:S(2)}) copy-start(bf16[2048,128]{1,0:T(8,128)(2,1)S(1)} %convolution_convert_fusion.2.side_hbm) | copy-start | bytes 1572868
  35.6 11.9 %collective-permute-start.2 = (bf16[32,384]{1,0:T(8,128)(2,1)S(1)}, bf16[32,384]{1,0:T(8,128)(2,1)S(1)}, u32[]{:S(2)}, u32[]{:S(2)}) collective-permute-start(bf16[32,384]{1,0:T(8,128)(2,1)S(1)} %pad_maximum_fusion.2), channel_id=1, source_target_pairs={{0,4},{4,8},{8,12},{12,16},{16,20},{20,24},{24,28},{28,32},{32,36}... | collective-permute-start | bytes 73736 | tf_op jit(solution)/shard_map/ppermute | solution.py:404
  39.2 8.3 %collective-permute-start.3 = (bf16[32,384]{1,0:T(8,128)(2,1)S(1)}, bf16[32,384]{1,0:T(8,128)(2,1)S(1)}, u32[]{:S(2)}, u32[]{:S(2)}) collective-permute-start(bf16[32,384]{1,0:T(8,128)(2,1)S(1)} %pad_maximum_fusion.3), channel_id=1, source_target_pairs={{4,0},{8,4},{12,8},{16,12},{20,16},{24,20},{28,24},{32,28},{36,32}... | collective-permute-start | bytes 73736 | tf_op jit(solution)/shard_map/ppermute | solution.py:404
  47.5 18.7 %copy-start = (bf16[1536,256]{1,0:T(8,128)(2,1)S(1)}, bf16[1536,256]{1,0:T(8,128)(2,1)}, u32[]{:S(2)}) copy-start(bf16[1536,256]{1,0:T(8,128)(2,1)} %constant.14.clone.table_ref) | copy-start | bytes 2359300
  47.5 18.7 %all-to-all-start.2 = ((bf16[64,8,128]{2,1,0:T(8,128)(2,1)}), bf16[64,8,128]{2,1,0:T(8,128)(2,1)S(1)}, u32[]{:S(2)}, u32[]{:S(2)}) async-start(bf16[64,8,128]{2,1,0:T(8,128)(2,1)} %get-tuple-element.48), calls=%async_computation.2 | async-start | bytes 262144 | tf_op jit(solution)/shard_map/all_to_all | solution.py:458
  66.2 19.1 %copy-start.3 = (bf16[1,32,64,256]{3,2,1,0:T(8,128)(2,1)S(1)}, bf16[1,32,64,256]{3,2,1,0:T(8,128)(2,1)}, u32[]{:S(2)}) copy-start(bf16[1,32,64,256]{3,2,1,0:T(8,128)(2,1)} %param.14) | copy-start | bytes 3145732
  87.2 20.7 %copy-start.2 = (bf16[256,1536]{1,0:T(8,128)(2,1)S(1)}, bf16[256,1536]{1,0:T(8,128)(2,1)}, u32[]{:S(2)}) copy-start(bf16[256,1536]{1,0:T(8,128)(2,1)} %constant.13.clone.table_ref) | copy-start | bytes 2359300
  87.3 20.7 %all-to-all-start.4 = ((bf16[16,2,64,256]{3,2,1,0:T(8,128)(2,1)}), bf16[16,2,64,256]{3,2,1,0:T(8,128)(2,1)S(1)}, u32[]{:S(2)}, u32[]{:S(2)}) async-start(bf16[16,2,64,256]{3,2,1,0:T(8,128)(2,1)} %bitcast.14), calls=%async_computation.4 | async-start | bytes 2097152 | tf_op jit(solution)/shard_map/all_to_all | solution.py:458
  93.1 16.5 %collective-permute-start.4 = (bf16[32,256]{1,0:T(8,128)(2,1)S(1)}, bf16[32,256]{1,0:T(8,128)(2,1)S(1)}, u32[]{:S(2)}, u32[]{:S(2)}) collective-permute-start(bf16[32,256]{1,0:T(8,128)(2,1)S(1)} %bitcast.119), channel_id=1, source_target_pairs={{0,4},{4,8},{8,12},{12,16},{16,20},{20,24},{24,28},{28,32},{32,36}... | collective-permute-start | bytes 49160 | tf_op jit(solution)/shard_map/ppermute | solution.py:404
  96.6 13.0 %collective-permute-start.5 = (bf16[32,256]{1,0:T(8,128)(2,1)S(1)}, bf16[32,256]{1,0:T(8,128)(2,1)S(1)}, u32[]{:S(2)}, u32[]{:S(2)}) collective-permute-start(bf16[32,256]{1,0:T(8,128)(2,1)S(1)} %bitcast.117), channel_id=1, source_target_pairs={{4,0},{8,4},{12,8},{16,12},{20,16},{24,20},{28,24},{32,28},{36,32}... | collective-permute-start | bytes 49160 | tf_op jit(solution)/shard_map/ppermute | solution.py:404
  109.6 16.3 %all-to-all-start.5 = ((bf16[64,8,128]{2,1,0:T(8,128)(2,1)}), bf16[64,8,128]{2,1,0:T(8,128)(2,1)S(1)}, u32[]{:S(2)}, u32[]{:S(2)}) async-start(bf16[64,8,128]{2,1,0:T(8,128)(2,1)} %to_modes.3), calls=%async_computation.5 | async-start | bytes 262144 | tf_op jit(solution)/shard_map/all_to_all | solution.py:458
  114.9 2.5 %copy-start.7 = (bf16[32,32,2,2,128]{4,3,2,1,0:T(2,128)(2,1)S(1)}, bf16[32,32,2,2,128]{4,3,2,1,0:T(2,128)(2,1)}, u32[]{:S(2)}) copy-start(bf16[32,32,2,2,128]{4,3,2,1,0:T(2,128)(2,1)} %param.11) | copy-start | bytes 3145732
  117.4 1.0 copy-start.4
  126.9 16.0 %all-to-all-start.6 = ((bf16[64,8,128]{2,1,0:T(8,128)(2,1)}), bf16[64,8,128]{2,1,0:T(8,128)(2,1)S(1)}, u32[]{:S(2)}, u32[]{:S(2)}) async-start(bf16[64,8,128]{2,1,0:T(8,128)(2,1)} %get-tuple-element.64), calls=%async_computation.6 | async-start | bytes 262144 | tf_op jit(solution)/shard_map/all_to_all | solution.py:458
  131.7 13.0 %collective-permute-start.7 = (bf16[1,2112]{1,0:T(2,128)(2,1)S(1)}, bf16[1,2112]{1,0:T(2,128)(2,1)S(1)}, u32[]{:S(2)}, u32[]{:S(2)}) collective-permute-start(bf16[1,2112]{1,0:T(2,128)(2,1)S(1)} %get-tuple-element.93), channel_id=1, source_target_pairs={{0,1},{1,2},{2,3},{4,5},{5,6},{6,7},{8,9},{9,10},{10,11},{12,13},{... | collective-permute-start | bytes 12680 | tf_op jit(solution)/shard_map/ppermute | solution.py:404
  135.9 8.8 %collective-permute-start.6 = (bf16[1,2112]{1,0:T(2,128)(2,1)S(1)}, bf16[1,2112]{1,0:T(2,128)(2,1)S(1)}, u32[]{:S(2)}, u32[]{:S(2)}) collective-permute-start(bf16[1,2112]{1,0:T(2,128)(2,1)S(1)} %get-tuple-element.94), channel_id=1, source_target_pairs={{1,0},{2,1},{3,2},{5,4},{6,5},{7,6},{9,8},{10,9},{11,10},{13,12},{... | collective-permute-start | bytes 12680 | tf_op jit(solution)/shard_map/ppermute | solution.py:404
  144.6 19.8 %all-to-all-start.7 = ((bf16[16,2,64,256]{3,2,1,0:T(8,128)(2,1)}), bf16[16,2,64,256]{3,2,1,0:T(8,128)(2,1)S(1)}, u32[]{:S(2)}, u32[]{:S(2)}) async-start(bf16[16,2,64,256]{3,2,1,0:T(8,128)(2,1)} %to_field.3), calls=%async_computation.7 | async-start | bytes 2097152 | tf_op jit(solution)/shard_map/all_to_all | solution.py:458

commit v11 on v10

--- a/solution.py
+++ b/solution.py
@@ -500,10 +500,11 @@
     parts, right, left, places = hold((parts, right, left, side_slots()))
     parts = exchange(parts, both)
     side = place_columns(right, left, places)
-    above, below = across_rows(*edge_rows(main, side, channels))
+    first, last = edge_rows(main, side, channels)
+    parts, first, last = hold((parts, first, last))
     mixed, spec = mix(parts, weight, 1, strips)
-    mixed, above, below = hold((mixed, above, below))
     arrived = exchange(mixed, both)
+    above, below = across_rows(first, last)
     local = conv(matrix, main, side, above, below, bias)
     arrived, local = hold((arrived, local))
     back = to_field(arrived, True, scale, tables, share)

time: 167 us -> 173 us (1.036)
  waiting for transfers between devices: 47.2 us -> 50.1 us
  blocking collectives: 18.4 us -> 21.1 us
    ppermute x8, waiting for transfers between devices: 0.02 us -> 3.52 us  [swap(): return lax.ppermute(value, axis, pairs)]
    all_to_all x1, blocking collectives: 18.4 us -> 21.1 us  [exchange(): return lax.all_to_all(value, axes, split_axis=0, concat_axis=0, tiled=True)]
  transfers between devices with their start and end apart: 15 -> 15, of which waited for: 7 -> 7; matrix products, arithmetic and copies ran while one was open for 7% -> 7% of each run, Pallas kernels for 10% -> 9%
where the time goes in v11:
time: 173 us; the launch traced here: 172 us
  starting transfers between devices  66.1 us (38%)
  waiting for transfers between devices  50.1 us (29%)
  Pallas kernels  21.3 us (12%)
  blocking collectives  21.1 us (12%)
  other arithmetic  5.96 us (3%)
  local copies, waits for them, and re-layouts  4.97 us (3%)
    all_to_all x7, waiting for transfers between devices, exchange(): return lax.all_to_all(value, axes, split_axis=0, concat_axis=0, tiled=True)  46.6 us
    all_to_all x7, starting transfers between devices, exchange(): return lax.all_to_all(value, axes, split_axis=0, concat_axis=0, tiled=True)  43.4 us
    ppermute x8, starting transfers between devices, swap(): return lax.ppermute(value, axis, pairs)  22.8 us
    all_to_all x1, blocking collectives, exchange(): return lax.all_to_all(value, axes, split_axis=0, concat_axis=0, tiled=True)  21.1 us
    pallas_call x7, Pallas kernels, on_chip(): pl.pallas_call(kernel, in_specs=[spec] * len(values), out_specs=[spec] *...  12.9 us
    pallas_call x1, Pallas kernels, conv(): pl.pallas_call(conv_kernel, in_specs=[vmem, hbm, hbm, vmem, vmem, vmem],...  5.15 us
    another operation x2, other arithmetic, weight_grads(): return jnp.stack([grad_real, grad_imag], axis=2)  3.62 us
    ppermute x8, waiting for transfers between devices, swap(): return lax.ppermute(value, axis, pairs)  3.52 us
  transfers between devices with their start and end apart: 15, of which 7 were waited for; matrix products, arithmetic and copies ran while one was open for 7% of the time, Pallas kernels for 9%

profile of v11, /device:TPU:1, one launch (start us, length us, event | category | flops | bytes accessed | tf_op | source)
XLA Modules:
  0.0 172.4 jit_solution(4480153666807138889)
XLA Ops:
  0.7 7.5 %all-to-all-start = ((bf16[16,2,64,256]{3,2,1,0:T(8,128)(2,1)}), bf16[16,2,64,256]{3,2,1,0:T(8,128)(2,1)S(1)}, u32[]{:S(2)}, u32[]{:S(2)}) async-start(bf16[16,2,64,256]{3,2,1,0:T(8,128)(2,1)} %bitcast.110), calls=%async_computation | async-start | bytes 2097152 | tf_op jit(solution)/shard_map/all_to_all | solution.py:458
  9.2 5.1 %collective-permute-start.1 = (bf16[1,2048]{1,0:T(2,128)(2,1)S(1)}, bf16[1,2048]{1,0:T(2,128)(2,1)S(1)}, u32[]{:S(2)}, u32[]{:S(2)}) collective-permute-start(bf16[1,2048]{1,0:T(2,128)(2,1)S(1)} %get-tuple-element.95), channel_id=1, source_target_pairs={{0,1},{1,2},{2,3},{4,5},{5,6},{6,7},{8,9},{9,10},{10,11},{12,13},{... | collective-permute-start | bytes 12296 | tf_op jit(solution)/shard_map/ppermute | solution.py:404
  14.2 1.3 collective-permute-start
  15.9 1.4 copy.78
  17.3 6.9 %all-to-all-done.block_ref = bf16[16,2,64,256]{3,2,1,0:T(8,128)(2,1)S(1)} async-done(((bf16[16,2,64,256]{3,2,1,0:T(8,128)(2,1)}), bf16[16,2,64,256]{3,2,1,0:T(8,128)(2,1)S(1)}, u32[]{:S(2)}, u32[]{:S(2)}) %all-to-all-start) | async-done | bytes 1048608 | tf_op jit(solution)/shard_map/all_to_all | solution.py:458
  24.1 1.7 to_modes.2
  25.8 9.4 %all-to-all-start.1 = ((bf16[64,8,128]{2,1,0:T(8,128)(2,1)}), bf16[64,8,128]{2,1,0:T(8,128)(2,1)S(1)}, u32[]{:S(2)}, u32[]{:S(2)}) async-start(bf16[64,8,128]{2,1,0:T(8,128)(2,1)} %to_modes.2), calls=%async_computation.1 | async-start | bytes 262144 | tf_op jit(solution)/shard_map/all_to_all | solution.py:458
  35.6 10.8 %all-to-all-done.1.parts_ref = bf16[64,8,128]{2,1,0:T(8,128)(2,1)S(1)} async-done(((bf16[64,8,128]{2,1,0:T(8,128)(2,1)}), bf16[64,8,128]{2,1,0:T(8,128)(2,1)S(1)}, u32[]{:S(2)}, u32[]{:S(2)}) %all-to-all-start.1) | async-done | bytes 131104 | tf_op jit(solution)/shard_map/all_to_all | solution.py:458
  47.5 4.7 %all-to-all-start.2 = ((bf16[64,8,128]{2,1,0:T(8,128)(2,1)}), bf16[64,8,128]{2,1,0:T(8,128)(2,1)S(1)}, u32[]{:S(2)}, u32[]{:S(2)}) async-start(bf16[64,8,128]{2,1,0:T(8,128)(2,1)} %get-tuple-element.48), calls=%async_computation.2 | async-start | bytes 262144 | tf_op jit(solution)/shard_map/all_to_all | solution.py:458
  52.1 3.6 %collective-permute-start.2 = (bf16[32,384]{1,0:T(8,128)(2,1)S(1)}, bf16[32,384]{1,0:T(8,128)(2,1)S(1)}, u32[]{:S(2)}, u32[]{:S(2)}) collective-permute-start(bf16[32,384]{1,0:T(8,128)(2,1)S(1)} %get-tuple-element.50), channel_id=1, source_target_pairs={{0,4},{4,8},{8,12},{12,16},{16,20},{20,24},{24,28},{28,32},{32,36}... | collective-permute-start | bytes 73736 | tf_op jit(solution)/shard_map/ppermute | solution.py:404
  55.7 1.9 %collective-permute-start.3 = (bf16[32,384]{1,0:T(8,128)(2,1)S(1)}, bf16[32,384]{1,0:T(8,128)(2,1)S(1)}, u32[]{:S(2)}, u32[]{:S(2)}) collective-permute-start(bf16[32,384]{1,0:T(8,128)(2,1)S(1)} %get-tuple-element.51), channel_id=1, source_target_pairs={{4,0},{8,4},{12,8},{16,12},{20,16},{24,20},{28,24},{32,28},{36,32}... | collective-permute-start | bytes 73736 | tf_op jit(solution)/shard_map/ppermute | solution.py:404
  57.7 3.5 %collective-permute-done.3.below_ref = bf16[32,384]{1,0:T(8,128)(2,1)S(1)} collective-permute-done((bf16[32,384]{1,0:T(8,128)(2,1)S(1)}, bf16[32,384]{1,0:T(8,128)(2,1)S(1)}, u32[]{:S(2)}, u32[]{:S(2)}) %collective-permute-start.3) | collective-permute-done | bytes 24608 | tf_op jit(solution)/shard_map/ppermute | solution.py:404
  61.2 5.1 %conv.1.local_ref = f32[32,64,256]{2,1,0:T(8,128)S(1)} custom-call(bf16[384,192]{1,0:T(8,128)(2,1)S(1)} %fusion.13.matrix_ref, bf16[2048,256]{1,0:T(8,128)(2,1)} %bitcast.109, bf16[2048,128]{1,0:T(8,128)(2,1)} %copy-done.8, bf16[32,384]{1,0:T(8,128)(2,1)S(1)} %collective-permute-done.2.above_ref, bf16[32,384]{1,0:T(8,128)(2,1)S(1)} %collective-permute-done.3.below_ref, ...), custom_call_target="tpu_custom_call" | custom-call | tf_op jit(solution)/shard_map/conv/pallas_call | solution.py:338
  67.1 21.1 %all_to_all.40 = bf16[16,2,64,256]{3,2,1,0:T(8,128)(2,1)S(1)} all-to-all(bf16[16,2,64,256]{3,2,1,0:T(8,128)(2,1)S(1)} %to_field.2), channel_id=1, replica_groups=mesh['dp'=4,'gx'=16,'gy'=4] {'gx'}, dimensions={0} | all-to-all | bytes 2097152 | tf_op jit(solution)/shard_map/all_to_all | solution.py:458
  88.2 1.9 %gate_both.1 = (bf16[32,64,256]{2,1,0:T(8,128)(2,1)}, f32[32,64,256]{2,1,0:T(8,128)}) custom-call(f32[32,64,256]{2,1,0:T(8,128)S(1)} %conv.1.local_ref, bf16[32,64,256]{2,1,0:T(8,128)(2,1)S(1)} %bitcast.101, bf16[32,64,256]{2,1,0:T(8,128)(2,1)S(1)} %bitcast.102), custom_call_target="tpu_custom_call" | custom-call | tf_op jit(solution)/shard_map/gate_both/pallas_call | solution.py:239
  90.1 4.8 %all-to-all-start.4 = ((bf16[16,2,64,256]{3,2,1,0:T(8,128)(2,1)}), bf16[16,2,64,256]{3,2,1,0:T(8,128)(2,1)S(1)}, u32[]{:S(2)}, u32[]{:S(2)}) async-start(bf16[16,2,64,256]{3,2,1,0:T(8,128)(2,1)} %bitcast.14), calls=%async_computation.4 | async-start | bytes 2097152 | tf_op jit(solution)/shard_map/all_to_all | solution.py:458
  95.9 3.5 %collective-permute-start.4 = (bf16[32,256]{1,0:T(8,128)(2,1)S(1)}, bf16[32,256]{1,0:T(8,128)(2,1)S(1)}, u32[]{:S(2)}, u32[]{:S(2)}) collective-permute-start(bf16[32,256]{1,0:T(8,128)(2,1)S(1)} %bitcast.119), channel_id=1, source_target_pairs={{0,4},{4,8},{8,12},{12,16},{16,20},{20,24},{24,28},{28,32},{32,36}... | collective-permute-start | bytes 49160 | tf_op jit(solution)/shard_map/ppermute | solution.py:404
  99.5 1.9 %collective-permute-start.5 = (bf16[32,256]{1,0:T(8,128)(2,1)S(1)}, bf16[32,256]{1,0:T(8,128)(2,1)S(1)}, u32[]{:S(2)}, u32[]{:S(2)}) collective-permute-start(bf16[32,256]{1,0:T(8,128)(2,1)S(1)} %bitcast.117), channel_id=1, source_target_pairs={{4,0},{8,4},{12,8},{16,12},{20,16},{24,20},{28,24},{32,28},{36,32}... | collective-permute-start | bytes 49160 | tf_op jit(solution)/shard_map/ppermute | solution.py:404
  101.4 9.4 %all-to-all-done.4.block_ref = bf16[16,2,64,256]{3,2,1,0:T(8,128)(2,1)S(1)} async-done(((bf16[16,2,64,256]{3,2,1,0:T(8,128)(2,1)}), bf16[16,2,64,256]{3,2,1,0:T(8,128)(2,1)S(1)}, u32[]{:S(2)}, u32[]{:S(2)}) %all-to-all-start.4) | async-done | bytes 1048608 | tf_op jit(solution)/shard_map/all_to_all | solution.py:458
  110.8 1.7 to_modes.3
  112.5 8.5 %all-to-all-start.5 = ((bf16[64,8,128]{2,1,0:T(8,128)(2,1)}), bf16[64,8,128]{2,1,0:T(8,128)(2,1)S(1)}, u32[]{:S(2)}, u32[]{:S(2)}) async-start(bf16[64,8,128]{2,1,0:T(8,128)(2,1)} %to_modes.3), calls=%async_computation.5 | async-start | bytes 262144 | tf_op jit(solution)/shard_map/all_to_all | solution.py:458
  121.3 2.1 %pad_maximum_fusion.1 = bf16[66,32,256]{2,0,1:T(8,128)(2,1)S(1)} fusion(bf16[1,32,256]{2,0,1:T(2,128)(2,1)S(1)} %copy.43, bf16[64,32,256]{2,0,1:T(8,128)(2,1)} %bitcast.16, bf16[1,32,256]{2,0,1:T(2,128)(2,1)S(1)} %copy.42), kind=kLoop, calls=%fused_computation.6 | loop fusion | flops 3244032 | bytes 2162688 | tf_op jit(solution)/shard_map/concatenate | solution.py:413
  125.1 7.1 %all-to-all-done.5.parts_ref = bf16[64,8,128]{2,1,0:T(8,128)(2,1)S(1)} async-done(((bf16[64,8,128]{2,1,0:T(8,128)(2,1)}), bf16[64,8,128]{2,1,0:T(8,128)(2,1)S(1)}, u32[]{:S(2)}, u32[]{:S(2)}) %all-to-all-start.5) | async-done | bytes 131104 | tf_op jit(solution)/shard_map/all_to_all | solution.py:458
  133.3 4.7 %all-to-all-start.6 = ((bf16[64,8,128]{2,1,0:T(8,128)(2,1)}), bf16[64,8,128]{2,1,0:T(8,128)(2,1)S(1)}, u32[]{:S(2)}, u32[]{:S(2)}) async-start(bf16[64,8,128]{2,1,0:T(8,128)(2,1)} %get-tuple-element.64), calls=%async_computation.6 | async-start | bytes 262144 | tf_op jit(solution)/shard_map/all_to_all | solution.py:458
  138.0 4.2 %collective-permute-start.7 = (bf16[1,2112]{1,0:T(2,128)(2,1)S(1)}, bf16[1,2112]{1,0:T(2,128)(2,1)S(1)}, u32[]{:S(2)}, u32[]{:S(2)}) collective-permute-start(bf16[1,2112]{1,0:T(2,128)(2,1)S(1)} %get-tuple-element.93), channel_id=1, source_target_pairs={{0,1},{1,2},{2,3},{4,5},{5,6},{6,7},{8,9},{9,10},{10,11},{12,13},{... | collective-permute-start | bytes 12680 | tf_op jit(solution)/shard_map/ppermute | solution.py:404
  143.5 5.8 %all-to-all-done.6.spec_ref = bf16[64,8,128]{2,1,0:T(8,128)(2,1)S(1)} async-done(((bf16[64,8,128]{2,1,0:T(8,128)(2,1)}), bf16[64,8,128]{2,1,0:T(8,128)(2,1)S(1)}, u32[]{:S(2)}, u32[]{:S(2)}) %all-to-all-start.6) | async-done | bytes 131104 | tf_op jit(solution)/shard_map/all_to_all | solution.py:458
  149.3 1.7 to_field.3
  151.0 3.9 %all-to-all-start.7 = ((bf16[16,2,64,256]{3,2,1,0:T(8,128)(2,1)}), bf16[16,2,64,256]{3,2,1,0:T(8,128)(2,1)S(1)}, u32[]{:S(2)}, u32[]{:S(2)}) async-start(bf16[16,2,64,256]{3,2,1,0:T(8,128)(2,1)} %to_field.3), calls=%async_computation.7 | async-start | bytes 2097152 | tf_op jit(solution)/shard_map/all_to_all | solution.py:458
  155.3 5.0 %conv_stacked.1.local_ref = f32[32,64,256]{2,1,0:T(8,128)S(1)} custom-call(bf16[384,192]{1,0:T(8,128)(2,1)S(1)} %fusion.16.matrix_ref, bf16[2112,256]{1,0:T(8,128)(2,1)} %bitcast.106, bf16[2112,128]{1,0:T(8,128)(2,1)S(1)} %convolution_convert_fusion.side_ref, f32[32,128]{1,0:T(8,128)S(1)} %broadcast_in_dim.25.bias_ref), custom_call_target="tpu_custom_call" | custom-call | tf_op jit(solution)/shard_map/conv_stacked/pallas_call | solution.py:66
  161.7 2.4 %pad_maximum_fusion = f32[32,32,2,2,128]{4,3,2,1,0:T(2,128)} fusion(f32[32,32,1,2,128]{4,3,2,1,0:T(2,128)S(1)} %get-tuple-element.88, f32[32,32,1,2,128]{4,3,2,1,0:T(2,128)S(1)} %get-tuple-element.87), kind=kLoop, calls=%fused_computation.5 | loop fusion | flops 524288 | bytes 4194304 | tf_op jit(solution)/shard_map/stack | solution.py:471
  164.1 6.7 %all-to-all-done.7 = bf16[16,2,64,256]{3,2,1,0:T(8,128)(2,1)S(1)} async-done(((bf16[16,2,64,256]{3,2,1,0:T(8,128)(2,1)}), bf16[16,2,64,256]{3,2,1,0:T(8,128)(2,1)S(1)}, u32[]{:S(2)}, u32[]{:S(2)}) %all-to-all-start.7) | async-done | bytes 1048608 | tf_op jit(solution)/shard_map/all_to_all | solution.py:458
  170.8 1.4 add_field.1
  (71 shorter events, 10.7 us)
Async XLA Ops:
  0.6 7.5 %copy-start.6 = (bf16[1,32,64,256]{3,2,1,0:T(8,128)(2,1)S(1)}, bf16[1,32,64,256]{3,2,1,0:T(8,128)(2,1)}, u32[]{:S(2)}) copy-start(bf16[1,32,64,256]{3,2,1,0:T(8,128)(2,1)} %param.10) | copy-start | bytes 3145732
  0.6 8.1 %copy-start.10 = (bf16[2,256]{1,0:T(2,128)(2,1)S(1)}, bf16[2,256]{1,0:T(2,128)(2,1)}, u32[]{:S(2)}) copy-start(bf16[2,256]{1,0:T(2,128)(2,1)} %constant.15.clone) | copy-start | bytes 3076
  0.7 23.5 %all-to-all-start = ((bf16[16,2,64,256]{3,2,1,0:T(8,128)(2,1)}), bf16[16,2,64,256]{3,2,1,0:T(8,128)(2,1)S(1)}, u32[]{:S(2)}, u32[]{:S(2)}) async-start(bf16[16,2,64,256]{3,2,1,0:T(8,128)(2,1)} %bitcast.110), calls=%async_computation | async-start | bytes 2097152 | tf_op jit(solution)/shard_map/all_to_all | solution.py:458
  8.1 7.4 %copy-start.9 = (bf16[9,32,32]{2,1,0:T(8,128)(2,1)S(1)}, bf16[9,32,32]{2,1,0:T(8,128)(2,1)}, u32[]{:S(2)}) copy-start(bf16[9,32,32]{2,1,0:T(8,128)(2,1)} %param.12) | copy-start | bytes 55300
  8.7 7.0 %copy-start.5 = (bf16[1,32,64,256]{3,1,2,0:T(8,128)(2,1)}, bf16[1,32,64,256]{3,1,2,0:T(8,128)(2,1)S(1)}, u32[]{:S(2)}) copy-start(bf16[1,32,64,256]{3,1,2,0:T(8,128)(2,1)S(1)} %copy.82) | copy-start | bytes 3145732
  8.8 15.4 %copy-start.1 = (bf16[256,1536]{1,0:T(8,128)(2,1)S(1)}, bf16[256,1536]{1,0:T(8,128)(2,1)}, u32[]{:S(2)}) copy-start(bf16[256,1536]{1,0:T(8,128)(2,1)} %constant.13.clone.table_ref) | copy-start | bytes 2359300
  9.2 16.6 %collective-permute-start.1 = (bf16[1,2048]{1,0:T(2,128)(2,1)S(1)}, bf16[1,2048]{1,0:T(2,128)(2,1)S(1)}, u32[]{:S(2)}, u32[]{:S(2)}) collective-permute-start(bf16[1,2048]{1,0:T(2,128)(2,1)S(1)} %get-tuple-element.95), channel_id=1, source_target_pairs={{0,1},{1,2},{2,3},{4,5},{5,6},{6,7},{8,9},{9,10},{10,11},{12,13},{... | collective-permute-start | bytes 12296 | tf_op jit(solution)/shard_map/ppermute | solution.py:404
  14.2 11.6 %collective-permute-start = (bf16[1,2048]{1,0:T(2,128)(2,1)S(1)}, bf16[1,2048]{1,0:T(2,128)(2,1)S(1)}, u32[]{:S(2)}, u32[]{:S(2)}) collective-permute-start(bf16[1,2048]{1,0:T(2,128)(2,1)S(1)} %get-tuple-element.96), channel_id=1, source_target_pairs={{1,0},{2,1},{3,2},{5,4},{6,5},{7,6},{9,8},{10,9},{11,10},{13,12},{... | collective-permute-start | bytes 12296 | tf_op jit(solution)/shard_map/ppermute | solution.py:404
  15.9 19.3 %copy-start.11 = (bf16[2,128]{1,0:T(2,128)(2,1)S(1)}, bf16[2,128]{1,0:T(2,128)(2,1)}, u32[]{:S(2)}) copy-start(bf16[2,128]{1,0:T(2,128)(2,1)} %constant.16.clone) | copy-start | bytes 1540
  24.1 37.0 %copy-start.12 = (f32[32]{0:T(128)S(1)}, f32[32]{0:T(128)}, u32[]{:S(2)}) copy-start(f32[32]{0:T(128)} %param.13) | copy-start | bytes 388
  25.8 20.6 %all-to-all-start.1 = ((bf16[64,8,128]{2,1,0:T(8,128)(2,1)}), bf16[64,8,128]{2,1,0:T(8,128)(2,1)S(1)}, u32[]{:S(2)}, u32[]{:S(2)}) async-start(bf16[64,8,128]{2,1,0:T(8,128)(2,1)} %to_modes.2), calls=%async_computation.1 | async-start | bytes 262144 | tf_op jit(solution)/shard_map/all_to_all | solution.py:458
  35.6 25.6 %copy-start.8 = (bf16[2048,128]{1,0:T(8,128)(2,1)}, bf16[2048,128]{1,0:T(8,128)(2,1)S(1)}, u32[]{:S(2)}) copy-start(bf16[2048,128]{1,0:T(8,128)(2,1)S(1)} %convolution_convert_fusion.2.side_hbm) | copy-start | bytes 1572868
  47.5 18.9 %copy-start = (bf16[1536,256]{1,0:T(8,128)(2,1)S(1)}, bf16[1536,256]{1,0:T(8,128)(2,1)}, u32[]{:S(2)}) copy-start(bf16[1536,256]{1,0:T(8,128)(2,1)} %constant.14.clone.table_ref) | copy-start | bytes 2359300
  47.5 18.9 %all-to-all-start.2 = ((bf16[64,8,128]{2,1,0:T(8,128)(2,1)}), bf16[64,8,128]{2,1,0:T(8,128)(2,1)S(1)}, u32[]{:S(2)}, u32[]{:S(2)}) async-start(bf16[64,8,128]{2,1,0:T(8,128)(2,1)} %get-tuple-element.48), calls=%async_computation.2 | async-start | bytes 262144 | tf_op jit(solution)/shard_map/all_to_all | solution.py:458
  52.1 5.5 %collective-permute-start.2 = (bf16[32,384]{1,0:T(8,128)(2,1)S(1)}, bf16[32,384]{1,0:T(8,128)(2,1)S(1)}, u32[]{:S(2)}, u32[]{:S(2)}) collective-permute-start(bf16[32,384]{1,0:T(8,128)(2,1)S(1)} %get-tuple-element.50), channel_id=1, source_target_pairs={{0,4},{4,8},{8,12},{12,16},{16,20},{20,24},{24,28},{28,32},{32,36}... | collective-permute-start | bytes 73736 | tf_op jit(solution)/shard_map/ppermute | solution.py:404
  55.7 5.4 %collective-permute-start.3 = (bf16[32,384]{1,0:T(8,128)(2,1)S(1)}, bf16[32,384]{1,0:T(8,128)(2,1)S(1)}, u32[]{:S(2)}, u32[]{:S(2)}) collective-permute-start(bf16[32,384]{1,0:T(8,128)(2,1)S(1)} %get-tuple-element.51), channel_id=1, source_target_pairs={{4,0},{8,4},{12,8},{16,12},{20,16},{24,20},{28,24},{32,28},{36,32}... | collective-permute-start | bytes 73736 | tf_op jit(solution)/shard_map/ppermute | solution.py:404
  66.4 21.8 %copy-start.3 = (bf16[1,32,64,256]{3,2,1,0:T(8,128)(2,1)S(1)}, bf16[1,32,64,256]{3,2,1,0:T(8,128)(2,1)}, u32[]{:S(2)}) copy-start(bf16[1,32,64,256]{3,2,1,0:T(8,128)(2,1)} %param.14) | copy-start | bytes 3145732
  90.1 20.7 %copy-start.2 = (bf16[256,1536]{1,0:T(8,128)(2,1)S(1)}, bf16[256,1536]{1,0:T(8,128)(2,1)}, u32[]{:S(2)}) copy-start(bf16[256,1536]{1,0:T(8,128)(2,1)} %constant.13.clone.table_ref) | copy-start | bytes 2359300
  90.1 20.7 %all-to-all-start.4 = ((bf16[16,2,64,256]{3,2,1,0:T(8,128)(2,1)}), bf16[16,2,64,256]{3,2,1,0:T(8,128)(2,1)S(1)}, u32[]{:S(2)}, u32[]{:S(2)}) async-start(bf16[16,2,64,256]{3,2,1,0:T(8,128)(2,1)} %bitcast.14), calls=%async_computation.4 | async-start | bytes 2097152 | tf_op jit(solution)/shard_map/all_to_all | solution.py:458
  95.9 16.5 %collective-permute-start.4 = (bf16[32,256]{1,0:T(8,128)(2,1)S(1)}, bf16[32,256]{1,0:T(8,128)(2,1)S(1)}, u32[]{:S(2)}, u32[]{:S(2)}) collective-permute-start(bf16[32,256]{1,0:T(8,128)(2,1)S(1)} %bitcast.119), channel_id=1, source_target_pairs={{0,4},{4,8},{8,12},{12,16},{16,20},{20,24},{24,28},{28,32},{32,36}... | collective-permute-start | bytes 49160 | tf_op jit(solution)/shard_map/ppermute | solution.py:404
  99.5 13.0 %collective-permute-start.5 = (bf16[32,256]{1,0:T(8,128)(2,1)S(1)}, bf16[32,256]{1,0:T(8,128)(2,1)S(1)}, u32[]{:S(2)}, u32[]{:S(2)}) collective-permute-start(bf16[32,256]{1,0:T(8,128)(2,1)S(1)} %bitcast.117), channel_id=1, source_target_pairs={{4,0},{8,4},{12,8},{16,12},{20,16},{24,20},{28,24},{32,28},{36,32}... | collective-permute-start | bytes 49160 | tf_op jit(solution)/shard_map/ppermute | solution.py:404
  112.5 19.7 %all-to-all-start.5 = ((bf16[64,8,128]{2,1,0:T(8,128)(2,1)}), bf16[64,8,128]{2,1,0:T(8,128)(2,1)S(1)}, u32[]{:S(2)}, u32[]{:S(2)}) async-start(bf16[64,8,128]{2,1,0:T(8,128)(2,1)} %to_modes.3), calls=%async_computation.5 | async-start | bytes 262144 | tf_op jit(solution)/shard_map/all_to_all | solution.py:458
  121.3 2.5 %copy-start.7 = (bf16[32,32,2,2,128]{4,3,2,1,0:T(2,128)(2,1)S(1)}, bf16[32,32,2,2,128]{4,3,2,1,0:T(2,128)(2,1)}, u32[]{:S(2)}) copy-start(bf16[32,32,2,2,128]{4,3,2,1,0:T(2,128)(2,1)} %param.11) | copy-start | bytes 3145732
  123.8 1.0 copy-start.4
  133.3 16.0 %all-to-all-start.6 = ((bf16[64,8,128]{2,1,0:T(8,128)(2,1)}), bf16[64,8,128]{2,1,0:T(8,128)(2,1)S(1)}, u32[]{:S(2)}, u32[]{:S(2)}) async-start(bf16[64,8,128]{2,1,0:T(8,128)(2,1)} %get-tuple-element.64), calls=%async_computation.6 | async-start | bytes 262144 | tf_op jit(solution)/shard_map/all_to_all | solution.py:458
  138.0 13.0 %collective-permute-start.7 = (bf16[1,2112]{1,0:T(2,128)(2,1)S(1)}, bf16[1,2112]{1,0:T(2,128)(2,1)S(1)}, u32[]{:S(2)}, u32[]{:S(2)}) collective-permute-start(bf16[1,2112]{1,0:T(2,128)(2,1)S(1)} %get-tuple-element.93), channel_id=1, source_target_pairs={{0,1},{1,2},{2,3},{4,5},{5,6},{6,7},{8,9},{9,10},{10,11},{12,13},{... | collective-permute-start | bytes 12680 | tf_op jit(solution)/shard_map/ppermute | solution.py:404
  142.2 8.8 %collective-permute-start.6 = (bf16[1,2112]{1,0:T(2,128)(2,1)S(1)}, bf16[1,2112]{1,0:T(2,128)(2,1)S(1)}, u32[]{:S(2)}, u32[]{:S(2)}) collective-permute-start(bf16[1,2112]{1,0:T(2,128)(2,1)S(1)} %get-tuple-element.94), channel_id=1, source_target_pairs={{1,0},{2,1},{3,2},{5,4},{6,5},{7,6},{9,8},{10,9},{11,10},{13,12},{... | collective-permute-start | bytes 12680 | tf_op jit(solution)/shard_map/ppermute | solution.py:404
  151.0 19.8 %all-to-all-start.7 = ((bf16[16,2,64,256]{3,2,1,0:T(8,128)(2,1)}), bf16[16,2,64,256]{3,2,1,0:T(8,128)(2,1)S(1)}, u32[]{:S(2)}, u32[]{:S(2)}) async-start(bf16[16,2,64,256]{3,2,1,0:T(8,128)(2,1)} %to_field.3), calls=%async_computation.7 | async-start | bytes 2097152 | tf_op jit(solution)/shard_map/all_to_all | solution.py:458

commit v12 on v10

--- a/solution.py
+++ b/solution.py
@@ -215,7 +215,7 @@
     return jnp.transpose(split, (2, 3, 0, 1, 4)).reshape(slots, 2, -1, kept)
 
 
-CHUNK = 4
+CHUNK = 2
 
 
 def gate_kernel(local_ref, field_ref, up_ref, grad_out, act_out, grad_ref, act_ref, sems):

time: 167 us -> 167 us (level)
  no operation moved by 1% of the time
where the time goes in v12:
time: 167 us; the launch traced here: 166 us
  starting transfers between devices  65.4 us (39%)
  waiting for transfers between devices  47.2 us (28%)
  Pallas kernels  21.5 us (13%)
  blocking collectives  18.4 us (11%)
  other arithmetic  5.96 us (4%)
  local copies, waits for them, and re-layouts  4.96 us (3%)
    all_to_all x7, waiting for transfers between devices, exchange(): return lax.all_to_all(value, axes, split_axis=0, concat_axis=0, tiled=True)  47.1 us
    all_to_all x7, starting transfers between devices, exchange(): return lax.all_to_all(value, axes, split_axis=0, concat_axis=0, tiled=True)  42.7 us
    ppermute x8, starting transfers between devices, swap(): return lax.ppermute(value, axis, pairs)  22.7 us
    all_to_all x1, blocking collectives, exchange(): return lax.all_to_all(value, axes, split_axis=0, concat_axis=0, tiled=True)  18.4 us
    pallas_call x7, Pallas kernels, on_chip(): pl.pallas_call(kernel, in_specs=[spec] * len(values), out_specs=[spec] *...  12.9 us
    pallas_call x1, Pallas kernels, conv(): pl.pallas_call(conv_kernel, in_specs=[vmem, hbm, hbm, vmem, vmem, vmem],...  5.15 us
    another operation x2, other arithmetic, weight_grads(): return jnp.stack([grad_real, grad_imag], axis=2)  3.62 us
  transfers between devices with their start and end apart: 15, of which 7 were waited for; matrix products, arithmetic and copies ran while one was open for 7% of the time, Pallas kernels for 10%

profile of v12, /device:TPU:1, one launch (start us, length us, event | category | flops | bytes accessed | tf_op | source)
XLA Modules:
  0.0 166.2 jit_solution(2936652777947002434)
XLA Ops:
  0.7 7.5 %all-to-all-start = ((bf16[16,2,64,256]{3,2,1,0:T(8,128)(2,1)}), bf16[16,2,64,256]{3,2,1,0:T(8,128)(2,1)S(1)}, u32[]{:S(2)}, u32[]{:S(2)}) async-start(bf16[16,2,64,256]{3,2,1,0:T(8,128)(2,1)} %bitcast.110), calls=%async_computation | async-start | bytes 2097152 | tf_op jit(solution)/shard_map/all_to_all | solution.py:458
  9.2 5.1 %collective-permute-start.1 = (bf16[1,2048]{1,0:T(2,128)(2,1)S(1)}, bf16[1,2048]{1,0:T(2,128)(2,1)S(1)}, u32[]{:S(2)}, u32[]{:S(2)}) collective-permute-start(bf16[1,2048]{1,0:T(2,128)(2,1)S(1)} %get-tuple-element.95), channel_id=1, source_target_pairs={{0,1},{1,2},{2,3},{4,5},{5,6},{6,7},{8,9},{9,10},{10,11},{12,13},{... | collective-permute-start | bytes 12296 | tf_op jit(solution)/shard_map/ppermute | solution.py:404
  14.2 1.3 collective-permute-start
  15.9 1.4 copy.78
  17.3 6.9 %all-to-all-done.block_ref = bf16[16,2,64,256]{3,2,1,0:T(8,128)(2,1)S(1)} async-done(((bf16[16,2,64,256]{3,2,1,0:T(8,128)(2,1)}), bf16[16,2,64,256]{3,2,1,0:T(8,128)(2,1)S(1)}, u32[]{:S(2)}, u32[]{:S(2)}) %all-to-all-start) | async-done | bytes 1048608 | tf_op jit(solution)/shard_map/all_to_all | solution.py:458
  24.1 1.7 %to_modes.2 = bf16[64,8,128]{2,1,0:T(8,128)(2,1)} custom-call(bf16[16,2,64,256]{3,2,1,0:T(8,128)(2,1)S(1)} %all-to-all-done.block_ref, bf16[256,1536]{1,0:T(8,128)(2,1)S(1)} %copy-done.1), custom_call_target="tpu_custom_call" | custom-call | tf_op jit(solution)/shard_map/to_modes/pallas_call | solution.py:66
  25.8 9.4 %all-to-all-start.1 = ((bf16[64,8,128]{2,1,0:T(8,128)(2,1)}), bf16[64,8,128]{2,1,0:T(8,128)(2,1)S(1)}, u32[]{:S(2)}, u32[]{:S(2)}) async-start(bf16[64,8,128]{2,1,0:T(8,128)(2,1)} %to_modes.2), calls=%async_computation.1 | async-start | bytes 262144 | tf_op jit(solution)/shard_map/all_to_all | solution.py:458
  35.6 3.5 %collective-permute-start.2 = (bf16[32,384]{1,0:T(8,128)(2,1)S(1)}, bf16[32,384]{1,0:T(8,128)(2,1)S(1)}, u32[]{:S(2)}, u32[]{:S(2)}) collective-permute-start(bf16[32,384]{1,0:T(8,128)(2,1)S(1)} %pad_maximum_fusion.2), channel_id=1, source_target_pairs={{0,4},{4,8},{8,12},{12,16},{16,20},{20,24},{24,28},{28,32},{32,36}... | collective-permute-start | bytes 73736 | tf_op jit(solution)/shard_map/ppermute | solution.py:404
  39.2 1.9 %collective-permute-start.3 = (bf16[32,384]{1,0:T(8,128)(2,1)S(1)}, bf16[32,384]{1,0:T(8,128)(2,1)S(1)}, u32[]{:S(2)}, u32[]{:S(2)}) collective-permute-start(bf16[32,384]{1,0:T(8,128)(2,1)S(1)} %pad_maximum_fusion.3), channel_id=1, source_target_pairs={{4,0},{8,4},{12,8},{16,12},{20,16},{24,20},{28,24},{32,28},{36,32}... | collective-permute-start | bytes 73736 | tf_op jit(solution)/shard_map/ppermute | solution.py:404
  41.1 5.3 %all-to-all-done.1.parts_ref = bf16[64,8,128]{2,1,0:T(8,128)(2,1)S(1)} async-done(((bf16[64,8,128]{2,1,0:T(8,128)(2,1)}), bf16[64,8,128]{2,1,0:T(8,128)(2,1)S(1)}, u32[]{:S(2)}, u32[]{:S(2)}) %all-to-all-start.1) | async-done | bytes 131104 | tf_op jit(solution)/shard_map/all_to_all | solution.py:458
  47.5 7.5 %all-to-all-start.2 = ((bf16[64,8,128]{2,1,0:T(8,128)(2,1)}), bf16[64,8,128]{2,1,0:T(8,128)(2,1)S(1)}, u32[]{:S(2)}, u32[]{:S(2)}) async-start(bf16[64,8,128]{2,1,0:T(8,128)(2,1)} %get-tuple-element.48), calls=%async_computation.2 | async-start | bytes 262144 | tf_op jit(solution)/shard_map/all_to_all | solution.py:458
  55.1 5.1 %conv.1.local_ref = f32[32,64,256]{2,1,0:T(8,128)S(1)} custom-call(bf16[384,192]{1,0:T(8,128)(2,1)S(1)} %fusion.13.matrix_ref, bf16[2048,256]{1,0:T(8,128)(2,1)} %bitcast.109, bf16[2048,128]{1,0:T(8,128)(2,1)} %copy-done.8, bf16[32,384]{1,0:T(8,128)(2,1)S(1)} %collective-permute-done.2.above_ref, bf16[32,384]{1,0:T(8,128)(2,1)S(1)} %collective-permute-done.3.below_ref, ...), custom_call_target="tpu_custom_call" | custom-call | tf_op jit(solution)/shard_map/conv/pallas_call | solution.py:338
  60.3 6.0 %all-to-all-done.2.spec_ref = bf16[64,8,128]{2,1,0:T(8,128)(2,1)S(1)} async-done(((bf16[64,8,128]{2,1,0:T(8,128)(2,1)}), bf16[64,8,128]{2,1,0:T(8,128)(2,1)S(1)}, u32[]{:S(2)}, u32[]{:S(2)}) %all-to-all-start.2) | async-done | bytes 131104 | tf_op jit(solution)/shard_map/all_to_all | solution.py:458
  66.9 18.4 %all_to_all.40 = bf16[16,2,64,256]{3,2,1,0:T(8,128)(2,1)S(1)} all-to-all(bf16[16,2,64,256]{3,2,1,0:T(8,128)(2,1)S(1)} %to_field.2), channel_id=1, replica_groups=mesh['dp'=4,'gx'=16,'gy'=4] {'gx'}, dimensions={0} | all-to-all | bytes 2097152 | tf_op jit(solution)/shard_map/all_to_all | solution.py:458
  85.3 2.0 %gate_both.1 = (bf16[32,64,256]{2,1,0:T(8,128)(2,1)}, f32[32,64,256]{2,1,0:T(8,128)}) custom-call(f32[32,64,256]{2,1,0:T(8,128)S(1)} %conv.1.local_ref, bf16[32,64,256]{2,1,0:T(8,128)(2,1)S(1)} %bitcast.101, bf16[32,64,256]{2,1,0:T(8,128)(2,1)S(1)} %bitcast.102), custom_call_target="tpu_custom_call" | custom-call | tf_op jit(solution)/shard_map/gate_both/pallas_call | solution.py:239
  87.3 4.8 %all-to-all-start.4 = ((bf16[16,2,64,256]{3,2,1,0:T(8,128)(2,1)}), bf16[16,2,64,256]{3,2,1,0:T(8,128)(2,1)S(1)}, u32[]{:S(2)}, u32[]{:S(2)}) async-start(bf16[16,2,64,256]{3,2,1,0:T(8,128)(2,1)} %bitcast.14), calls=%async_computation.4 | async-start | bytes 2097152 | tf_op jit(solution)/shard_map/all_to_all | solution.py:458
  93.2 3.5 %collective-permute-start.4 = (bf16[32,256]{1,0:T(8,128)(2,1)S(1)}, bf16[32,256]{1,0:T(8,128)(2,1)S(1)}, u32[]{:S(2)}, u32[]{:S(2)}) collective-permute-start(bf16[32,256]{1,0:T(8,128)(2,1)S(1)} %bitcast.119), channel_id=1, source_target_pairs={{0,4},{4,8},{8,12},{12,16},{16,20},{20,24},{24,28},{28,32},{32,36}... | collective-permute-start | bytes 49160 | tf_op jit(solution)/shard_map/ppermute | solution.py:404
  96.7 1.9 %collective-permute-start.5 = (bf16[32,256]{1,0:T(8,128)(2,1)S(1)}, bf16[32,256]{1,0:T(8,128)(2,1)S(1)}, u32[]{:S(2)}, u32[]{:S(2)}) collective-permute-start(bf16[32,256]{1,0:T(8,128)(2,1)S(1)} %bitcast.117), channel_id=1, source_target_pairs={{4,0},{8,4},{12,8},{16,12},{20,16},{24,20},{28,24},{32,28},{36,32}... | collective-permute-start | bytes 49160 | tf_op jit(solution)/shard_map/ppermute | solution.py:404
  98.6 9.4 %all-to-all-done.4.block_ref = bf16[16,2,64,256]{3,2,1,0:T(8,128)(2,1)S(1)} async-done(((bf16[16,2,64,256]{3,2,1,0:T(8,128)(2,1)}), bf16[16,2,64,256]{3,2,1,0:T(8,128)(2,1)S(1)}, u32[]{:S(2)}, u32[]{:S(2)}) %all-to-all-start.4) | async-done | bytes 1048608 | tf_op jit(solution)/shard_map/all_to_all | solution.py:458
  108.0 1.7 %to_modes.3 = bf16[64,8,128]{2,1,0:T(8,128)(2,1)} custom-call(bf16[16,2,64,256]{3,2,1,0:T(8,128)(2,1)S(1)} %all-to-all-done.4.block_ref, bf16[256,1536]{1,0:T(8,128)(2,1)S(1)} %copy-done.2), custom_call_target="tpu_custom_call" | custom-call | tf_op jit(solution)/shard_map/to_modes/pallas_call | solution.py:66
  109.7 4.9 %all-to-all-start.5 = ((bf16[64,8,128]{2,1,0:T(8,128)(2,1)}), bf16[64,8,128]{2,1,0:T(8,128)(2,1)S(1)}, u32[]{:S(2)}, u32[]{:S(2)}) async-start(bf16[64,8,128]{2,1,0:T(8,128)(2,1)} %to_modes.3), calls=%async_computation.5 | async-start | bytes 262144 | tf_op jit(solution)/shard_map/all_to_all | solution.py:458
  115.0 2.1 %pad_maximum_fusion.1 = bf16[66,32,256]{2,0,1:T(8,128)(2,1)S(1)} fusion(bf16[1,32,256]{2,0,1:T(2,128)(2,1)S(1)} %copy.43, bf16[64,32,256]{2,0,1:T(8,128)(2,1)} %bitcast.16, bf16[1,32,256]{2,0,1:T(2,128)(2,1)S(1)} %copy.42), kind=kLoop, calls=%fused_computation.6 | loop fusion | flops 3244032 | bytes 2162688 | tf_op jit(solution)/shard_map/concatenate | solution.py:413
  118.8 7.1 %all-to-all-done.5.parts_ref = bf16[64,8,128]{2,1,0:T(8,128)(2,1)S(1)} async-done(((bf16[64,8,128]{2,1,0:T(8,128)(2,1)}), bf16[64,8,128]{2,1,0:T(8,128)(2,1)S(1)}, u32[]{:S(2)}, u32[]{:S(2)}) %all-to-all-start.5) | async-done | bytes 131104 | tf_op jit(solution)/shard_map/all_to_all | solution.py:458
  127.0 4.7 %all-to-all-start.6 = ((bf16[64,8,128]{2,1,0:T(8,128)(2,1)}), bf16[64,8,128]{2,1,0:T(8,128)(2,1)S(1)}, u32[]{:S(2)}, u32[]{:S(2)}) async-start(bf16[64,8,128]{2,1,0:T(8,128)(2,1)} %get-tuple-element.64), calls=%async_computation.6 | async-start | bytes 262144 | tf_op jit(solution)/shard_map/all_to_all | solution.py:458
  131.8 4.2 %collective-permute-start.7 = (bf16[1,2112]{1,0:T(2,128)(2,1)S(1)}, bf16[1,2112]{1,0:T(2,128)(2,1)S(1)}, u32[]{:S(2)}, u32[]{:S(2)}) collective-permute-start(bf16[1,2112]{1,0:T(2,128)(2,1)S(1)} %get-tuple-element.93), channel_id=1, source_target_pairs={{0,1},{1,2},{2,3},{4,5},{5,6},{6,7},{8,9},{9,10},{10,11},{12,13},{... | collective-permute-start | bytes 12680 | tf_op jit(solution)/shard_map/ppermute | solution.py:404
  137.3 5.8 %all-to-all-done.6.spec_ref = bf16[64,8,128]{2,1,0:T(8,128)(2,1)S(1)} async-done(((bf16[64,8,128]{2,1,0:T(8,128)(2,1)}), bf16[64,8,128]{2,1,0:T(8,128)(2,1)S(1)}, u32[]{:S(2)}, u32[]{:S(2)}) %all-to-all-start.6) | async-done | bytes 131104 | tf_op jit(solution)/shard_map/all_to_all | solution.py:458
  143.0 1.7 %to_field.3 = bf16[16,2,64,256]{3,2,1,0:T(8,128)(2,1)} custom-call(bf16[64,8,128]{2,1,0:T(8,128)(2,1)S(1)} %all-to-all-done.6.spec_ref, bf16[1536,256]{1,0:T(8,128)(2,1)S(1)} %copy-done), custom_call_target="tpu_custom_call" | custom-call | tf_op jit(solution)/shard_map/to_field/pallas_call | solution.py:66
  144.7 3.9 %all-to-all-start.7 = ((bf16[16,2,64,256]{3,2,1,0:T(8,128)(2,1)}), bf16[16,2,64,256]{3,2,1,0:T(8,128)(2,1)S(1)}, u32[]{:S(2)}, u32[]{:S(2)}) async-start(bf16[16,2,64,256]{3,2,1,0:T(8,128)(2,1)} %to_field.3), calls=%async_computation.7 | async-start | bytes 2097152 | tf_op jit(solution)/shard_map/all_to_all | solution.py:458
  149.0 5.0 %conv_stacked.1.local_ref = f32[32,64,256]{2,1,0:T(8,128)S(1)} custom-call(bf16[384,192]{1,0:T(8,128)(2,1)S(1)} %fusion.16.matrix_ref, bf16[2112,256]{1,0:T(8,128)(2,1)} %bitcast.106, bf16[2112,128]{1,0:T(8,128)(2,1)S(1)} %convolution_convert_fusion.side_ref, f32[32,128]{1,0:T(8,128)S(1)} %broadcast_in_dim.25.bias_ref), custom_call_target="tpu_custom_call" | custom-call | tf_op jit(solution)/shard_map/conv_stacked/pallas_call | solution.py:66
  155.4 2.4 %pad_maximum_fusion = f32[32,32,2,2,128]{4,3,2,1,0:T(2,128)} fusion(f32[32,32,1,2,128]{4,3,2,1,0:T(2,128)S(1)} %get-tuple-element.88, f32[32,32,1,2,128]{4,3,2,1,0:T(2,128)S(1)} %get-tuple-element.87), kind=kLoop, calls=%fused_computation.5 | loop fusion | flops 524288 | bytes 4194304 | tf_op jit(solution)/shard_map/stack | solution.py:471
  157.8 6.7 %all-to-all-done.7 = bf16[16,2,64,256]{3,2,1,0:T(8,128)(2,1)S(1)} async-done(((bf16[16,2,64,256]{3,2,1,0:T(8,128)(2,1)}), bf16[16,2,64,256]{3,2,1,0:T(8,128)(2,1)S(1)}, u32[]{:S(2)}, u32[]{:S(2)}) %all-to-all-start.7) | async-done | bytes 1048608 | tf_op jit(solution)/shard_map/all_to_all | solution.py:458
  164.6 1.4 add_field.1
  (70 shorter events, 10.7 us)
Async XLA Ops:
  0.6 7.5 %copy-start.6 = (bf16[1,32,64,256]{3,2,1,0:T(8,128)(2,1)S(1)}, bf16[1,32,64,256]{3,2,1,0:T(8,128)(2,1)}, u32[]{:S(2)}) copy-start(bf16[1,32,64,256]{3,2,1,0:T(8,128)(2,1)} %param.10) | copy-start | bytes 3145732
  0.6 8.1 %copy-start.10 = (bf16[2,256]{1,0:T(2,128)(2,1)S(1)}, bf16[2,256]{1,0:T(2,128)(2,1)}, u32[]{:S(2)}) copy-start(bf16[2,256]{1,0:T(2,128)(2,1)} %constant.15.clone) | copy-start | bytes 3076
  0.7 23.5 %all-to-all-start = ((bf16[16,2,64,256]{3,2,1,0:T(8,128)(2,1)}), bf16[16,2,64,256]{3,2,1,0:T(8,128)(2,1)S(1)}, u32[]{:S(2)}, u32[]{:S(2)}) async-start(bf16[16,2,64,256]{3,2,1,0:T(8,128)(2,1)} %bitcast.110), calls=%async_computation | async-start | bytes 2097152 | tf_op jit(solution)/shard_map/all_to_all | solution.py:458
  8.1 7.4 %copy-start.9 = (bf16[9,32,32]{2,1,0:T(8,128)(2,1)S(1)}, bf16[9,32,32]{2,1,0:T(8,128)(2,1)}, u32[]{:S(2)}) copy-start(bf16[9,32,32]{2,1,0:T(8,128)(2,1)} %param.12) | copy-start | bytes 55300
  8.7 7.0 %copy-start.5 = (bf16[1,32,64,256]{3,1,2,0:T(8,128)(2,1)}, bf16[1,32,64,256]{3,1,2,0:T(8,128)(2,1)S(1)}, u32[]{:S(2)}) copy-start(bf16[1,32,64,256]{3,1,2,0:T(8,128)(2,1)S(1)} %copy.82) | copy-start | bytes 3145732
  8.8 15.4 %copy-start.1 = (bf16[256,1536]{1,0:T(8,128)(2,1)S(1)}, bf16[256,1536]{1,0:T(8,128)(2,1)}, u32[]{:S(2)}) copy-start(bf16[256,1536]{1,0:T(8,128)(2,1)} %constant.13.clone.table_ref) | copy-start | bytes 2359300
  9.2 16.6 %collective-permute-start.1 = (bf16[1,2048]{1,0:T(2,128)(2,1)S(1)}, bf16[1,2048]{1,0:T(2,128)(2,1)S(1)}, u32[]{:S(2)}, u32[]{:S(2)}) collective-permute-start(bf16[1,2048]{1,0:T(2,128)(2,1)S(1)} %get-tuple-element.95), channel_id=1, source_target_pairs={{0,1},{1,2},{2,3},{4,5},{5,6},{6,7},{8,9},{9,10},{10,11},{12,13},{... | collective-permute-start | bytes 12296 | tf_op jit(solution)/shard_map/ppermute | solution.py:404
  14.2 11.6 %collective-permute-start = (bf16[1,2048]{1,0:T(2,128)(2,1)S(1)}, bf16[1,2048]{1,0:T(2,128)(2,1)S(1)}, u32[]{:S(2)}, u32[]{:S(2)}) collective-permute-start(bf16[1,2048]{1,0:T(2,128)(2,1)S(1)} %get-tuple-element.96), channel_id=1, source_target_pairs={{1,0},{2,1},{3,2},{5,4},{6,5},{7,6},{9,8},{10,9},{11,10},{13,12},{... | collective-permute-start | bytes 12296 | tf_op jit(solution)/shard_map/ppermute | solution.py:404
  15.9 19.3 %copy-start.11 = (bf16[2,128]{1,0:T(2,128)(2,1)S(1)}, bf16[2,128]{1,0:T(2,128)(2,1)}, u32[]{:S(2)}) copy-start(bf16[2,128]{1,0:T(2,128)(2,1)} %constant.16.clone) | copy-start | bytes 1540
  24.1 30.9 %copy-start.12 = (f32[32]{0:T(128)S(1)}, f32[32]{0:T(128)}, u32[]{:S(2)}) copy-start(f32[32]{0:T(128)} %param.13) | copy-start | bytes 388
  25.8 20.6 %all-to-all-start.1 = ((bf16[64,8,128]{2,1,0:T(8,128)(2,1)}), bf16[64,8,128]{2,1,0:T(8,128)(2,1)S(1)}, u32[]{:S(2)}, u32[]{:S(2)}) async-start(bf16[64,8,128]{2,1,0:T(8,128)(2,1)} %to_modes.2), calls=%async_computation.1 | async-start | bytes 262144 | tf_op jit(solution)/shard_map/all_to_all | solution.py:458
  35.6 19.4 %copy-start.8 = (bf16[2048,128]{1,0:T(8,128)(2,1)}, bf16[2048,128]{1,0:T(8,128)(2,1)S(1)}, u32[]{:S(2)}) copy-start(bf16[2048,128]{1,0:T(8,128)(2,1)S(1)} %convolution_convert_fusion.2.side_hbm) | copy-start | bytes 1572868
  35.6 11.9 %collective-permute-start.2 = (bf16[32,384]{1,0:T(8,128)(2,1)S(1)}, bf16[32,384]{1,0:T(8,128)(2,1)S(1)}, u32[]{:S(2)}, u32[]{:S(2)}) collective-permute-start(bf16[32,384]{1,0:T(8,128)(2,1)S(1)} %pad_maximum_fusion.2), channel_id=1, source_target_pairs={{0,4},{4,8},{8,12},{12,16},{16,20},{20,24},{24,28},{28,32},{32,36}... | collective-permute-start | bytes 73736 | tf_op jit(solution)/shard_map/ppermute | solution.py:404
  39.2 8.3 %collective-permute-start.3 = (bf16[32,384]{1,0:T(8,128)(2,1)S(1)}, bf16[32,384]{1,0:T(8,128)(2,1)S(1)}, u32[]{:S(2)}, u32[]{:S(2)}) collective-permute-start(bf16[32,384]{1,0:T(8,128)(2,1)S(1)} %pad_maximum_fusion.3), channel_id=1, source_target_pairs={{4,0},{8,4},{12,8},{16,12},{20,16},{24,20},{28,24},{32,28},{36,32}... | collective-permute-start | bytes 73736 | tf_op jit(solution)/shard_map/ppermute | solution.py:404
  47.5 18.7 %copy-start = (bf16[1536,256]{1,0:T(8,128)(2,1)S(1)}, bf16[1536,256]{1,0:T(8,128)(2,1)}, u32[]{:S(2)}) copy-start(bf16[1536,256]{1,0:T(8,128)(2,1)} %constant.14.clone.table_ref) | copy-start | bytes 2359300
  47.5 18.7 %all-to-all-start.2 = ((bf16[64,8,128]{2,1,0:T(8,128)(2,1)}), bf16[64,8,128]{2,1,0:T(8,128)(2,1)S(1)}, u32[]{:S(2)}, u32[]{:S(2)}) async-start(bf16[64,8,128]{2,1,0:T(8,128)(2,1)} %get-tuple-element.48), calls=%async_computation.2 | async-start | bytes 262144 | tf_op jit(solution)/shard_map/all_to_all | solution.py:458
  66.2 19.1 %copy-start.3 = (bf16[1,32,64,256]{3,2,1,0:T(8,128)(2,1)S(1)}, bf16[1,32,64,256]{3,2,1,0:T(8,128)(2,1)}, u32[]{:S(2)}) copy-start(bf16[1,32,64,256]{3,2,1,0:T(8,128)(2,1)} %param.14) | copy-start | bytes 3145732
  87.3 20.7 %copy-start.2 = (bf16[256,1536]{1,0:T(8,128)(2,1)S(1)}, bf16[256,1536]{1,0:T(8,128)(2,1)}, u32[]{:S(2)}) copy-start(bf16[256,1536]{1,0:T(8,128)(2,1)} %constant.13.clone.table_ref) | copy-start | bytes 2359300
  87.3 20.7 %all-to-all-start.4 = ((bf16[16,2,64,256]{3,2,1,0:T(8,128)(2,1)}), bf16[16,2,64,256]{3,2,1,0:T(8,128)(2,1)S(1)}, u32[]{:S(2)}, u32[]{:S(2)}) async-start(bf16[16,2,64,256]{3,2,1,0:T(8,128)(2,1)} %bitcast.14), calls=%async_computation.4 | async-start | bytes 2097152 | tf_op jit(solution)/shard_map/all_to_all | solution.py:458
  93.2 16.5 %collective-permute-start.4 = (bf16[32,256]{1,0:T(8,128)(2,1)S(1)}, bf16[32,256]{1,0:T(8,128)(2,1)S(1)}, u32[]{:S(2)}, u32[]{:S(2)}) collective-permute-start(bf16[32,256]{1,0:T(8,128)(2,1)S(1)} %bitcast.119), channel_id=1, source_target_pairs={{0,4},{4,8},{8,12},{12,16},{16,20},{20,24},{24,28},{28,32},{32,36}... | collective-permute-start | bytes 49160 | tf_op jit(solution)/shard_map/ppermute | solution.py:404
  96.7 13.0 %collective-permute-start.5 = (bf16[32,256]{1,0:T(8,128)(2,1)S(1)}, bf16[32,256]{1,0:T(8,128)(2,1)S(1)}, u32[]{:S(2)}, u32[]{:S(2)}) collective-permute-start(bf16[32,256]{1,0:T(8,128)(2,1)S(1)} %bitcast.117), channel_id=1, source_target_pairs={{4,0},{8,4},{12,8},{16,12},{20,16},{24,20},{28,24},{32,28},{36,32}... | collective-permute-start | bytes 49160 | tf_op jit(solution)/shard_map/ppermute | solution.py:404
  109.7 16.3 %all-to-all-start.5 = ((bf16[64,8,128]{2,1,0:T(8,128)(2,1)}), bf16[64,8,128]{2,1,0:T(8,128)(2,1)S(1)}, u32[]{:S(2)}, u32[]{:S(2)}) async-start(bf16[64,8,128]{2,1,0:T(8,128)(2,1)} %to_modes.3), calls=%async_computation.5 | async-start | bytes 262144 | tf_op jit(solution)/shard_map/all_to_all | solution.py:458
  115.0 2.5 %copy-start.7 = (bf16[32,32,2,2,128]{4,3,2,1,0:T(2,128)(2,1)S(1)}, bf16[32,32,2,2,128]{4,3,2,1,0:T(2,128)(2,1)}, u32[]{:S(2)}) copy-start(bf16[32,32,2,2,128]{4,3,2,1,0:T(2,128)(2,1)} %param.11) | copy-start | bytes 3145732
  117.4 1.0 copy-start.4
  127.0 16.0 %all-to-all-start.6 = ((bf16[64,8,128]{2,1,0:T(8,128)(2,1)}), bf16[64,8,128]{2,1,0:T(8,128)(2,1)S(1)}, u32[]{:S(2)}, u32[]{:S(2)}) async-start(bf16[64,8,128]{2,1,0:T(8,128)(2,1)} %get-tuple-element.64), calls=%async_computation.6 | async-start | bytes 262144 | tf_op jit(solution)/shard_map/all_to_all | solution.py:458
  131.8 13.0 %collective-permute-start.7 = (bf16[1,2112]{1,0:T(2,128)(2,1)S(1)}, bf16[1,2112]{1,0:T(2,128)(2,1)S(1)}, u32[]{:S(2)}, u32[]{:S(2)}) collective-permute-start(bf16[1,2112]{1,0:T(2,128)(2,1)S(1)} %get-tuple-element.93), channel_id=1, source_target_pairs={{0,1},{1,2},{2,3},{4,5},{5,6},{6,7},{8,9},{9,10},{10,11},{12,13},{... | collective-permute-start | bytes 12680 | tf_op jit(solution)/shard_map/ppermute | solution.py:404
  136.0 8.8 %collective-permute-start.6 = (bf16[1,2112]{1,0:T(2,128)(2,1)S(1)}, bf16[1,2112]{1,0:T(2,128)(2,1)S(1)}, u32[]{:S(2)}, u32[]{:S(2)}) collective-permute-start(bf16[1,2112]{1,0:T(2,128)(2,1)S(1)} %get-tuple-element.94), channel_id=1, source_target_pairs={{1,0},{2,1},{3,2},{5,4},{6,5},{7,6},{9,8},{10,9},{11,10},{13,12},{... | collective-permute-start | bytes 12680 | tf_op jit(solution)/shard_map/ppermute | solution.py:404
  144.7 19.8 %all-to-all-start.7 = ((bf16[16,2,64,256]{3,2,1,0:T(8,128)(2,1)}), bf16[16,2,64,256]{3,2,1,0:T(8,128)(2,1)S(1)}, u32[]{:S(2)}, u32[]{:S(2)}) async-start(bf16[16,2,64,256]{3,2,1,0:T(8,128)(2,1)} %to_field.3), calls=%async_computation.7 | async-start | bytes 2097152 | tf_op jit(solution)/shard_map/all_to_all | solution.py:458

commit v13 on v12

--- a/solution.py
+++ b/solution.py
@@ -215,7 +215,7 @@
     return jnp.transpose(split, (2, 3, 0, 1, 4)).reshape(slots, 2, -1, kept)
 
 
-CHUNK = 2
+CHUNK = 8
 
 
 def gate_kernel(local_ref, field_ref, up_ref, grad_out, act_out, grad_ref, act_ref, sems):

time: 167 us -> 167 us (level)
  no operation moved by 1% of the time
where the time goes in v13:
time: 167 us; the launch traced here: 166 us
  starting transfers between devices  65.4 us (39%)
  waiting for transfers between devices  47.2 us (28%)
  Pallas kernels  21.4 us (13%)
  blocking collectives  18.4 us (11%)
  other arithmetic  5.96 us (4%)
  local copies, waits for them, and re-layouts  4.96 us (3%)
    all_to_all x7, waiting for transfers between devices, exchange(): return lax.all_to_all(value, axes, split_axis=0, concat_axis=0, tiled=True)  47.1 us
    all_to_all x7, starting transfers between devices, exchange(): return lax.all_to_all(value, axes, split_axis=0, concat_axis=0, tiled=True)  42.7 us
    ppermute x8, starting transfers between devices, swap(): return lax.ppermute(value, axis, pairs)  22.7 us
    all_to_all x1, blocking collectives, exchange(): return lax.all_to_all(value, axes, split_axis=0, concat_axis=0, tiled=True)  18.4 us
    pallas_call x7, Pallas kernels, on_chip(): pl.pallas_call(kernel, in_specs=[spec] * len(values), out_specs=[spec] *...  12.9 us
    pallas_call x1, Pallas kernels, conv(): pl.pallas_call(conv_kernel, in_specs=[vmem, hbm, hbm, vmem, vmem, vmem],...  5.15 us
    another operation x2, other arithmetic, weight_grads(): return jnp.stack([grad_real, grad_imag], axis=2)  3.62 us
  transfers between devices with their start and end apart: 15, of which 7 were waited for; matrix products, arithmetic and copies ran while one was open for 7% of the time, Pallas kernels for 10%

profile of v13, /device:TPU:1, one launch (start us, length us, event | category | flops | bytes accessed | tf_op | source)
XLA Modules:
  0.0 166.1 jit_solution(3564236152028275290)
XLA Ops:
  0.7 7.5 %all-to-all-start = ((bf16[16,2,64,256]{3,2,1,0:T(8,128)(2,1)}), bf16[16,2,64,256]{3,2,1,0:T(8,128)(2,1)S(1)}, u32[]{:S(2)}, u32[]{:S(2)}) async-start(bf16[16,2,64,256]{3,2,1,0:T(8,128)(2,1)} %bitcast.110), calls=%async_computation | async-start | bytes 2097152 | tf_op jit(solution)/shard_map/all_to_all | solution.py:458
  9.2 5.1 %collective-permute-start.1 = (bf16[1,2048]{1,0:T(2,128)(2,1)S(1)}, bf16[1,2048]{1,0:T(2,128)(2,1)S(1)}, u32[]{:S(2)}, u32[]{:S(2)}) collective-permute-start(bf16[1,2048]{1,0:T(2,128)(2,1)S(1)} %get-tuple-element.95), channel_id=1, source_target_pairs={{0,1},{1,2},{2,3},{4,5},{5,6},{6,7},{8,9},{9,10},{10,11},{12,13},{... | collective-permute-start | bytes 12296 | tf_op jit(solution)/shard_map/ppermute | solution.py:404
  14.2 1.3 collective-permute-start
  15.9 1.4 copy.78
  17.3 6.9 %all-to-all-done.block_ref = bf16[16,2,64,256]{3,2,1,0:T(8,128)(2,1)S(1)} async-done(((bf16[16,2,64,256]{3,2,1,0:T(8,128)(2,1)}), bf16[16,2,64,256]{3,2,1,0:T(8,128)(2,1)S(1)}, u32[]{:S(2)}, u32[]{:S(2)}) %all-to-all-start) | async-done | bytes 1048608 | tf_op jit(solution)/shard_map/all_to_all | solution.py:458
  24.1 1.7 %to_modes.2 = bf16[64,8,128]{2,1,0:T(8,128)(2,1)} custom-call(bf16[16,2,64,256]{3,2,1,0:T(8,128)(2,1)S(1)} %all-to-all-done.block_ref, bf16[256,1536]{1,0:T(8,128)(2,1)S(1)} %copy-done.1), custom_call_target="tpu_custom_call" | custom-call | tf_op jit(solution)/shard_map/to_modes/pallas_call | solution.py:66
  25.8 9.4 %all-to-all-start.1 = ((bf16[64,8,128]{2,1,0:T(8,128)(2,1)}), bf16[64,8,128]{2,1,0:T(8,128)(2,1)S(1)}, u32[]{:S(2)}, u32[]{:S(2)}) async-start(bf16[64,8,128]{2,1,0:T(8,128)(2,1)} %to_modes.2), calls=%async_computation.1 | async-start | bytes 262144 | tf_op jit(solution)/shard_map/all_to_all | solution.py:458
  35.6 3.5 %collective-permute-start.2 = (bf16[32,384]{1,0:T(8,128)(2,1)S(1)}, bf16[32,384]{1,0:T(8,128)(2,1)S(1)}, u32[]{:S(2)}, u32[]{:S(2)}) collective-permute-start(bf16[32,384]{1,0:T(8,128)(2,1)S(1)} %pad_maximum_fusion.2), channel_id=1, source_target_pairs={{0,4},{4,8},{8,12},{12,16},{16,20},{20,24},{24,28},{28,32},{32,36}... | collective-permute-start | bytes 73736 | tf_op jit(solution)/shard_map/ppermute | solution.py:404
  39.2 1.9 %collective-permute-start.3 = (bf16[32,384]{1,0:T(8,128)(2,1)S(1)}, bf16[32,384]{1,0:T(8,128)(2,1)S(1)}, u32[]{:S(2)}, u32[]{:S(2)}) collective-permute-start(bf16[32,384]{1,0:T(8,128)(2,1)S(1)} %pad_maximum_fusion.3), channel_id=1, source_target_pairs={{4,0},{8,4},{12,8},{16,12},{20,16},{24,20},{28,24},{32,28},{36,32}... | collective-permute-start | bytes 73736 | tf_op jit(solution)/shard_map/ppermute | solution.py:404
  41.1 5.3 %all-to-all-done.1.parts_ref = bf16[64,8,128]{2,1,0:T(8,128)(2,1)S(1)} async-done(((bf16[64,8,128]{2,1,0:T(8,128)(2,1)}), bf16[64,8,128]{2,1,0:T(8,128)(2,1)S(1)}, u32[]{:S(2)}, u32[]{:S(2)}) %all-to-all-start.1) | async-done | bytes 131104 | tf_op jit(solution)/shard_map/all_to_all | solution.py:458
  47.5 7.5 %all-to-all-start.2 = ((bf16[64,8,128]{2,1,0:T(8,128)(2,1)}), bf16[64,8,128]{2,1,0:T(8,128)(2,1)S(1)}, u32[]{:S(2)}, u32[]{:S(2)}) async-start(bf16[64,8,128]{2,1,0:T(8,128)(2,1)} %get-tuple-element.48), calls=%async_computation.2 | async-start | bytes 262144 | tf_op jit(solution)/shard_map/all_to_all | solution.py:458
  55.1 5.1 %conv.1.local_ref = f32[32,64,256]{2,1,0:T(8,128)S(1)} custom-call(bf16[384,192]{1,0:T(8,128)(2,1)S(1)} %fusion.13.matrix_ref, bf16[2048,256]{1,0:T(8,128)(2,1)} %bitcast.109, bf16[2048,128]{1,0:T(8,128)(2,1)} %copy-done.8, bf16[32,384]{1,0:T(8,128)(2,1)S(1)} %collective-permute-done.2.above_ref, bf16[32,384]{1,0:T(8,128)(2,1)S(1)} %collective-permute-done.3.below_ref, ...), custom_call_target="tpu_custom_call" | custom-call | tf_op jit(solution)/shard_map/conv/pallas_call | solution.py:338
  60.3 6.0 %all-to-all-done.2.spec_ref = bf16[64,8,128]{2,1,0:T(8,128)(2,1)S(1)} async-done(((bf16[64,8,128]{2,1,0:T(8,128)(2,1)}), bf16[64,8,128]{2,1,0:T(8,128)(2,1)S(1)}, u32[]{:S(2)}, u32[]{:S(2)}) %all-to-all-start.2) | async-done | bytes 131104 | tf_op jit(solution)/shard_map/all_to_all | solution.py:458
  66.9 18.4 %all_to_all.40 = bf16[16,2,64,256]{3,2,1,0:T(8,128)(2,1)S(1)} all-to-all(bf16[16,2,64,256]{3,2,1,0:T(8,128)(2,1)S(1)} %to_field.2), channel_id=1, replica_groups=mesh['dp'=4,'gx'=16,'gy'=4] {'gx'}, dimensions={0} | all-to-all | bytes 2097152 | tf_op jit(solution)/shard_map/all_to_all | solution.py:458
  85.3 2.0 %gate_both.1 = (bf16[32,64,256]{2,1,0:T(8,128)(2,1)}, f32[32,64,256]{2,1,0:T(8,128)}) custom-call(f32[32,64,256]{2,1,0:T(8,128)S(1)} %conv.1.local_ref, bf16[32,64,256]{2,1,0:T(8,128)(2,1)S(1)} %bitcast.101, bf16[32,64,256]{2,1,0:T(8,128)(2,1)S(1)} %bitcast.102), custom_call_target="tpu_custom_call" | custom-call | tf_op jit(solution)/shard_map/gate_both/pallas_call | solution.py:239
  87.3 4.8 %all-to-all-start.4 = ((bf16[16,2,64,256]{3,2,1,0:T(8,128)(2,1)}), bf16[16,2,64,256]{3,2,1,0:T(8,128)(2,1)S(1)}, u32[]{:S(2)}, u32[]{:S(2)}) async-start(bf16[16,2,64,256]{3,2,1,0:T(8,128)(2,1)} %bitcast.14), calls=%async_computation.4 | async-start | bytes 2097152 | tf_op jit(solution)/shard_map/all_to_all | solution.py:458
  93.1 3.5 %collective-permute-start.4 = (bf16[32,256]{1,0:T(8,128)(2,1)S(1)}, bf16[32,256]{1,0:T(8,128)(2,1)S(1)}, u32[]{:S(2)}, u32[]{:S(2)}) collective-permute-start(bf16[32,256]{1,0:T(8,128)(2,1)S(1)} %bitcast.119), channel_id=1, source_target_pairs={{0,4},{4,8},{8,12},{12,16},{16,20},{20,24},{24,28},{28,32},{32,36}... | collective-permute-start | bytes 49160 | tf_op jit(solution)/shard_map/ppermute | solution.py:404
  96.7 1.9 %collective-permute-start.5 = (bf16[32,256]{1,0:T(8,128)(2,1)S(1)}, bf16[32,256]{1,0:T(8,128)(2,1)S(1)}, u32[]{:S(2)}, u32[]{:S(2)}) collective-permute-start(bf16[32,256]{1,0:T(8,128)(2,1)S(1)} %bitcast.117), channel_id=1, source_target_pairs={{4,0},{8,4},{12,8},{16,12},{20,16},{24,20},{28,24},{32,28},{36,32}... | collective-permute-start | bytes 49160 | tf_op jit(solution)/shard_map/ppermute | solution.py:404
  98.6 9.4 %all-to-all-done.4.block_ref = bf16[16,2,64,256]{3,2,1,0:T(8,128)(2,1)S(1)} async-done(((bf16[16,2,64,256]{3,2,1,0:T(8,128)(2,1)}), bf16[16,2,64,256]{3,2,1,0:T(8,128)(2,1)S(1)}, u32[]{:S(2)}, u32[]{:S(2)}) %all-to-all-start.4) | async-done | bytes 1048608 | tf_op jit(solution)/shard_map/all_to_all | solution.py:458
  108.0 1.7 %to_modes.3 = bf16[64,8,128]{2,1,0:T(8,128)(2,1)} custom-call(bf16[16,2,64,256]{3,2,1,0:T(8,128)(2,1)S(1)} %all-to-all-done.4.block_ref, bf16[256,1536]{1,0:T(8,128)(2,1)S(1)} %copy-done.2), custom_call_target="tpu_custom_call" | custom-call | tf_op jit(solution)/shard_map/to_modes/pallas_call | solution.py:66
  109.7 4.9 %all-to-all-start.5 = ((bf16[64,8,128]{2,1,0:T(8,128)(2,1)}), bf16[64,8,128]{2,1,0:T(8,128)(2,1)S(1)}, u32[]{:S(2)}, u32[]{:S(2)}) async-start(bf16[64,8,128]{2,1,0:T(8,128)(2,1)} %to_modes.3), calls=%async_computation.5 | async-start | bytes 262144 | tf_op jit(solution)/shard_map/all_to_all | solution.py:458
  115.0 2.1 %pad_maximum_fusion.1 = bf16[66,32,256]{2,0,1:T(8,128)(2,1)S(1)} fusion(bf16[1,32,256]{2,0,1:T(2,128)(2,1)S(1)} %copy.43, bf16[64,32,256]{2,0,1:T(8,128)(2,1)} %bitcast.16, bf16[1,32,256]{2,0,1:T(2,128)(2,1)S(1)} %copy.42), kind=kLoop, calls=%fused_computation.6 | loop fusion | flops 3244032 | bytes 2162688 | tf_op jit(solution)/shard_map/concatenate | solution.py:413
  118.8 7.1 %all-to-all-done.5.parts_ref = bf16[64,8,128]{2,1,0:T(8,128)(2,1)S(1)} async-done(((bf16[64,8,128]{2,1,0:T(8,128)(2,1)}), bf16[64,8,128]{2,1,0:T(8,128)(2,1)S(1)}, u32[]{:S(2)}, u32[]{:S(2)}) %all-to-all-start.5) | async-done | bytes 131104 | tf_op jit(solution)/shard_map/all_to_all | solution.py:458
  127.0 4.7 %all-to-all-start.6 = ((bf16[64,8,128]{2,1,0:T(8,128)(2,1)}), bf16[64,8,128]{2,1,0:T(8,128)(2,1)S(1)}, u32[]{:S(2)}, u32[]{:S(2)}) async-start(bf16[64,8,128]{2,1,0:T(8,128)(2,1)} %get-tuple-element.64), calls=%async_computation.6 | async-start | bytes 262144 | tf_op jit(solution)/shard_map/all_to_all | solution.py:458
  131.8 4.2 %collective-permute-start.7 = (bf16[1,2112]{1,0:T(2,128)(2,1)S(1)}, bf16[1,2112]{1,0:T(2,128)(2,1)S(1)}, u32[]{:S(2)}, u32[]{:S(2)}) collective-permute-start(bf16[1,2112]{1,0:T(2,128)(2,1)S(1)} %get-tuple-element.93), channel_id=1, source_target_pairs={{0,1},{1,2},{2,3},{4,5},{5,6},{6,7},{8,9},{9,10},{10,11},{12,13},{... | collective-permute-start | bytes 12680 | tf_op jit(solution)/shard_map/ppermute | solution.py:404
  137.2 5.8 %all-to-all-done.6.spec_ref = bf16[64,8,128]{2,1,0:T(8,128)(2,1)S(1)} async-done(((bf16[64,8,128]{2,1,0:T(8,128)(2,1)}), bf16[64,8,128]{2,1,0:T(8,128)(2,1)S(1)}, u32[]{:S(2)}, u32[]{:S(2)}) %all-to-all-start.6) | async-done | bytes 131104 | tf_op jit(solution)/shard_map/all_to_all | solution.py:458
  143.0 1.7 %to_field.3 = bf16[16,2,64,256]{3,2,1,0:T(8,128)(2,1)} custom-call(bf16[64,8,128]{2,1,0:T(8,128)(2,1)S(1)} %all-to-all-done.6.spec_ref, bf16[1536,256]{1,0:T(8,128)(2,1)S(1)} %copy-done), custom_call_target="tpu_custom_call" | custom-call | tf_op jit(solution)/shard_map/to_field/pallas_call | solution.py:66
  144.7 3.9 %all-to-all-start.7 = ((bf16[16,2,64,256]{3,2,1,0:T(8,128)(2,1)}), bf16[16,2,64,256]{3,2,1,0:T(8,128)(2,1)S(1)}, u32[]{:S(2)}, u32[]{:S(2)}) async-start(bf16[16,2,64,256]{3,2,1,0:T(8,128)(2,1)} %to_field.3), calls=%async_computation.7 | async-start | bytes 2097152 | tf_op jit(solution)/shard_map/all_to_all | solution.py:458
  149.0 5.0 %conv_stacked.1.local_ref = f32[32,64,256]{2,1,0:T(8,128)S(1)} custom-call(bf16[384,192]{1,0:T(8,128)(2,1)S(1)} %fusion.16.matrix_ref, bf16[2112,256]{1,0:T(8,128)(2,1)} %bitcast.106, bf16[2112,128]{1,0:T(8,128)(2,1)S(1)} %convolution_convert_fusion.side_ref, f32[32,128]{1,0:T(8,128)S(1)} %broadcast_in_dim.25.bias_ref), custom_call_target="tpu_custom_call" | custom-call | tf_op jit(solution)/shard_map/conv_stacked/pallas_call | solution.py:66
  155.4 2.4 %pad_maximum_fusion = f32[32,32,2,2,128]{4,3,2,1,0:T(2,128)} fusion(f32[32,32,1,2,128]{4,3,2,1,0:T(2,128)S(1)} %get-tuple-element.88, f32[32,32,1,2,128]{4,3,2,1,0:T(2,128)S(1)} %get-tuple-element.87), kind=kLoop, calls=%fused_computation.5 | loop fusion | flops 524288 | bytes 4194304 | tf_op jit(solution)/shard_map/stack | solution.py:471
  157.8 6.7 %all-to-all-done.7 = bf16[16,2,64,256]{3,2,1,0:T(8,128)(2,1)S(1)} async-done(((bf16[16,2,64,256]{3,2,1,0:T(8,128)(2,1)}), bf16[16,2,64,256]{3,2,1,0:T(8,128)(2,1)S(1)}, u32[]{:S(2)}, u32[]{:S(2)}) %all-to-all-start.7) | async-done | bytes 1048608 | tf_op jit(solution)/shard_map/all_to_all | solution.py:458
  164.5 1.4 add_field.1
  (70 shorter events, 10.7 us)
Async XLA Ops:
  0.6 7.5 %copy-start.6 = (bf16[1,32,64,256]{3,2,1,0:T(8,128)(2,1)S(1)}, bf16[1,32,64,256]{3,2,1,0:T(8,128)(2,1)}, u32[]{:S(2)}) copy-start(bf16[1,32,64,256]{3,2,1,0:T(8,128)(2,1)} %param.10) | copy-start | bytes 3145732
  0.6 8.1 %copy-start.10 = (bf16[2,256]{1,0:T(2,128)(2,1)S(1)}, bf16[2,256]{1,0:T(2,128)(2,1)}, u32[]{:S(2)}) copy-start(bf16[2,256]{1,0:T(2,128)(2,1)} %constant.15.clone) | copy-start | bytes 3076
  0.7 23.5 %all-to-all-start = ((bf16[16,2,64,256]{3,2,1,0:T(8,128)(2,1)}), bf16[16,2,64,256]{3,2,1,0:T(8,128)(2,1)S(1)}, u32[]{:S(2)}, u32[]{:S(2)}) async-start(bf16[16,2,64,256]{3,2,1,0:T(8,128)(2,1)} %bitcast.110), calls=%async_computation | async-start | bytes 2097152 | tf_op jit(solution)/shard_map/all_to_all | solution.py:458
  8.1 7.4 %copy-start.9 = (bf16[9,32,32]{2,1,0:T(8,128)(2,1)S(1)}, bf16[9,32,32]{2,1,0:T(8,128)(2,1)}, u32[]{:S(2)}) copy-start(bf16[9,32,32]{2,1,0:T(8,128)(2,1)} %param.12) | copy-start | bytes 55300
  8.7 7.0 %copy-start.5 = (bf16[1,32,64,256]{3,1,2,0:T(8,128)(2,1)}, bf16[1,32,64,256]{3,1,2,0:T(8,128)(2,1)S(1)}, u32[]{:S(2)}) copy-start(bf16[1,32,64,256]{3,1,2,0:T(8,128)(2,1)S(1)} %copy.82) | copy-start | bytes 3145732
  8.8 15.4 %copy-start.1 = (bf16[256,1536]{1,0:T(8,128)(2,1)S(1)}, bf16[256,1536]{1,0:T(8,128)(2,1)}, u32[]{:S(2)}) copy-start(bf16[256,1536]{1,0:T(8,128)(2,1)} %constant.13.clone.table_ref) | copy-start | bytes 2359300
  9.2 16.6 %collective-permute-start.1 = (bf16[1,2048]{1,0:T(2,128)(2,1)S(1)}, bf16[1,2048]{1,0:T(2,128)(2,1)S(1)}, u32[]{:S(2)}, u32[]{:S(2)}) collective-permute-start(bf16[1,2048]{1,0:T(2,128)(2,1)S(1)} %get-tuple-element.95), channel_id=1, source_target_pairs={{0,1},{1,2},{2,3},{4,5},{5,6},{6,7},{8,9},{9,10},{10,11},{12,13},{... | collective-permute-start | bytes 12296 | tf_op jit(solution)/shard_map/ppermute | solution.py:404
  14.2 11.6 %collective-permute-start = (bf16[1,2048]{1,0:T(2,128)(2,1)S(1)}, bf16[1,2048]{1,0:T(2,128)(2,1)S(1)}, u32[]{:S(2)}, u32[]{:S(2)}) collective-permute-start(bf16[1,2048]{1,0:T(2,128)(2,1)S(1)} %get-tuple-element.96), channel_id=1, source_target_pairs={{1,0},{2,1},{3,2},{5,4},{6,5},{7,6},{9,8},{10,9},{11,10},{13,12},{... | collective-permute-start | bytes 12296 | tf_op jit(solution)/shard_map/ppermute | solution.py:404
  15.9 19.3 %copy-start.11 = (bf16[2,128]{1,0:T(2,128)(2,1)S(1)}, bf16[2,128]{1,0:T(2,128)(2,1)}, u32[]{:S(2)}) copy-start(bf16[2,128]{1,0:T(2,128)(2,1)} %constant.16.clone) | copy-start | bytes 1540
  24.1 30.9 %copy-start.12 = (f32[32]{0:T(128)S(1)}, f32[32]{0:T(128)}, u32[]{:S(2)}) copy-start(f32[32]{0:T(128)} %param.13) | copy-start | bytes 388
  25.8 20.6 %all-to-all-start.1 = ((bf16[64,8,128]{2,1,0:T(8,128)(2,1)}), bf16[64,8,128]{2,1,0:T(8,128)(2,1)S(1)}, u32[]{:S(2)}, u32[]{:S(2)}) async-start(bf16[64,8,128]{2,1,0:T(8,128)(2,1)} %to_modes.2), calls=%async_computation.1 | async-start | bytes 262144 | tf_op jit(solution)/shard_map/all_to_all | solution.py:458
  35.6 19.4 %copy-start.8 = (bf16[2048,128]{1,0:T(8,128)(2,1)}, bf16[2048,128]{1,0:T(8,128)(2,1)S(1)}, u32[]{:S(2)}) copy-start(bf16[2048,128]{1,0:T(8,128)(2,1)S(1)} %convolution_convert_fusion.2.side_hbm) | copy-start | bytes 1572868
  35.6 11.9 %collective-permute-start.2 = (bf16[32,384]{1,0:T(8,128)(2,1)S(1)}, bf16[32,384]{1,0:T(8,128)(2,1)S(1)}, u32[]{:S(2)}, u32[]{:S(2)}) collective-permute-start(bf16[32,384]{1,0:T(8,128)(2,1)S(1)} %pad_maximum_fusion.2), channel_id=1, source_target_pairs={{0,4},{4,8},{8,12},{12,16},{16,20},{20,24},{24,28},{28,32},{32,36}... | collective-permute-start | bytes 73736 | tf_op jit(solution)/shard_map/ppermute | solution.py:404
  39.2 8.3 %collective-permute-start.3 = (bf16[32,384]{1,0:T(8,128)(2,1)S(1)}, bf16[32,384]{1,0:T(8,128)(2,1)S(1)}, u32[]{:S(2)}, u32[]{:S(2)}) collective-permute-start(bf16[32,384]{1,0:T(8,128)(2,1)S(1)} %pad_maximum_fusion.3), channel_id=1, source_target_pairs={{4,0},{8,4},{12,8},{16,12},{20,16},{24,20},{28,24},{32,28},{36,32}... | collective-permute-start | bytes 73736 | tf_op jit(solution)/shard_map/ppermute | solution.py:404
  47.5 18.7 %copy-start = (bf16[1536,256]{1,0:T(8,128)(2,1)S(1)}, bf16[1536,256]{1,0:T(8,128)(2,1)}, u32[]{:S(2)}) copy-start(bf16[1536,256]{1,0:T(8,128)(2,1)} %constant.14.clone.table_ref) | copy-start | bytes 2359300
  47.5 18.7 %all-to-all-start.2 = ((bf16[64,8,128]{2,1,0:T(8,128)(2,1)}), bf16[64,8,128]{2,1,0:T(8,128)(2,1)S(1)}, u32[]{:S(2)}, u32[]{:S(2)}) async-start(bf16[64,8,128]{2,1,0:T(8,128)(2,1)} %get-tuple-element.48), calls=%async_computation.2 | async-start | bytes 262144 | tf_op jit(solution)/shard_map/all_to_all | solution.py:458
  66.2 19.1 %copy-start.3 = (bf16[1,32,64,256]{3,2,1,0:T(8,128)(2,1)S(1)}, bf16[1,32,64,256]{3,2,1,0:T(8,128)(2,1)}, u32[]{:S(2)}) copy-start(bf16[1,32,64,256]{3,2,1,0:T(8,128)(2,1)} %param.14) | copy-start | bytes 3145732
  87.3 20.7 %copy-start.2 = (bf16[256,1536]{1,0:T(8,128)(2,1)S(1)}, bf16[256,1536]{1,0:T(8,128)(2,1)}, u32[]{:S(2)}) copy-start(bf16[256,1536]{1,0:T(8,128)(2,1)} %constant.13.clone.table_ref) | copy-start | bytes 2359300
  87.3 20.7 %all-to-all-start.4 = ((bf16[16,2,64,256]{3,2,1,0:T(8,128)(2,1)}), bf16[16,2,64,256]{3,2,1,0:T(8,128)(2,1)S(1)}, u32[]{:S(2)}, u32[]{:S(2)}) async-start(bf16[16,2,64,256]{3,2,1,0:T(8,128)(2,1)} %bitcast.14), calls=%async_computation.4 | async-start | bytes 2097152 | tf_op jit(solution)/shard_map/all_to_all | solution.py:458
  93.1 16.5 %collective-permute-start.4 = (bf16[32,256]{1,0:T(8,128)(2,1)S(1)}, bf16[32,256]{1,0:T(8,128)(2,1)S(1)}, u32[]{:S(2)}, u32[]{:S(2)}) collective-permute-start(bf16[32,256]{1,0:T(8,128)(2,1)S(1)} %bitcast.119), channel_id=1, source_target_pairs={{0,4},{4,8},{8,12},{12,16},{16,20},{20,24},{24,28},{28,32},{32,36}... | collective-permute-start | bytes 49160 | tf_op jit(solution)/shard_map/ppermute | solution.py:404
  96.7 13.0 %collective-permute-start.5 = (bf16[32,256]{1,0:T(8,128)(2,1)S(1)}, bf16[32,256]{1,0:T(8,128)(2,1)S(1)}, u32[]{:S(2)}, u32[]{:S(2)}) collective-permute-start(bf16[32,256]{1,0:T(8,128)(2,1)S(1)} %bitcast.117), channel_id=1, source_target_pairs={{4,0},{8,4},{12,8},{16,12},{20,16},{24,20},{28,24},{32,28},{36,32}... | collective-permute-start | bytes 49160 | tf_op jit(solution)/shard_map/ppermute | solution.py:404
  109.7 16.2 %all-to-all-start.5 = ((bf16[64,8,128]{2,1,0:T(8,128)(2,1)}), bf16[64,8,128]{2,1,0:T(8,128)(2,1)S(1)}, u32[]{:S(2)}, u32[]{:S(2)}) async-start(bf16[64,8,128]{2,1,0:T(8,128)(2,1)} %to_modes.3), calls=%async_computation.5 | async-start | bytes 262144 | tf_op jit(solution)/shard_map/all_to_all | solution.py:458
  115.0 2.5 %copy-start.7 = (bf16[32,32,2,2,128]{4,3,2,1,0:T(2,128)(2,1)S(1)}, bf16[32,32,2,2,128]{4,3,2,1,0:T(2,128)(2,1)}, u32[]{:S(2)}) copy-start(bf16[32,32,2,2,128]{4,3,2,1,0:T(2,128)(2,1)} %param.11) | copy-start | bytes 3145732
  117.4 1.0 copy-start.4
  127.0 16.0 %all-to-all-start.6 = ((bf16[64,8,128]{2,1,0:T(8,128)(2,1)}), bf16[64,8,128]{2,1,0:T(8,128)(2,1)S(1)}, u32[]{:S(2)}, u32[]{:S(2)}) async-start(bf16[64,8,128]{2,1,0:T(8,128)(2,1)} %get-tuple-element.64), calls=%async_computation.6 | async-start | bytes 262144 | tf_op jit(solution)/shard_map/all_to_all | solution.py:458
  131.8 13.0 %collective-permute-start.7 = (bf16[1,2112]{1,0:T(2,128)(2,1)S(1)}, bf16[1,2112]{1,0:T(2,128)(2,1)S(1)}, u32[]{:S(2)}, u32[]{:S(2)}) collective-permute-start(bf16[1,2112]{1,0:T(2,128)(2,1)S(1)} %get-tuple-element.93), channel_id=1, source_target_pairs={{0,1},{1,2},{2,3},{4,5},{5,6},{6,7},{8,9},{9,10},{10,11},{12,13},{... | collective-permute-start | bytes 12680 | tf_op jit(solution)/shard_map/ppermute | solution.py:404
  135.9 8.8 %collective-permute-start.6 = (bf16[1,2112]{1,0:T(2,128)(2,1)S(1)}, bf16[1,2112]{1,0:T(2,128)(2,1)S(1)}, u32[]{:S(2)}, u32[]{:S(2)}) collective-permute-start(bf16[1,2112]{1,0:T(2,128)(2,1)S(1)} %get-tuple-element.94), channel_id=1, source_target_pairs={{1,0},{2,1},{3,2},{5,4},{6,5},{7,6},{9,8},{10,9},{11,10},{13,12},{... | collective-permute-start | bytes 12680 | tf_op jit(solution)/shard_map/ppermute | solution.py:404
  144.7 19.8 %all-to-all-start.7 = ((bf16[16,2,64,256]{3,2,1,0:T(8,128)(2,1)}), bf16[16,2,64,256]{3,2,1,0:T(8,128)(2,1)S(1)}, u32[]{:S(2)}, u32[]{:S(2)}) async-start(bf16[16,2,64,256]{3,2,1,0:T(8,128)(2,1)} %to_field.3), calls=%async_computation.7 | async-start | bytes 2097152 | tf_op jit(solution)/shard_map/all_to_all | solution.py:458
